TPU v7x, 32 devices: a whole 2x2x4 slice. The times are simulated.
32 devices in a mesh: dp: 8 (over y, x, core), expert: 4 (over z).
Axes of the slice: x: 2, y: 2, z: 4, core: 2. Of those that a mesh axis runs over, the one named last changes fastest.
Arguments:
- tokens: bfloat16 [8192, 2048], P(('dp', 'expert')), may hold values from -6 to 6
- cotangent: bfloat16 [8192, 2048], P(('dp', 'expert')), may hold values from -6 to 6
- gain_one: bfloat16 [2048], P(('dp', 'expert')), may hold values from 0.5 to 1.5
- gain_two: bfloat16 [2048], P(('dp', 'expert')), may hold values from 0.5 to 1.5
- kv_weight: bfloat16 [2048, 4096], P(('dp', 'expert')), may hold values from -0.125 to 0.125
- att_router: bfloat16 [2048, 4], P(('dp', 'expert')), may hold values from -0.09375 to 0.09375
- ffn_router: bfloat16 [2048, 4], P(('dp', 'expert')), may hold values from -0.09375 to 0.09375
- query_weight: bfloat16 [4, 2048, 2048], P('expert', 'dp'), may hold values from -0.125 to 0.125
- output_weight: bfloat16 [4, 2048, 2048], P('expert', 'dp'), may hold values from -1 to 1
- gate_weight: bfloat16 [4, 2048, 5632], P('expert', 'dp'), may hold values from -0.125 to 0.125
- up_weight: bfloat16 [4, 2048, 5632], P('expert', 'dp'), may hold values from -0.125 to 0.125
- down_weight: bfloat16 [4, 5632, 2048], P('expert', 'dp'), may hold values from -0.078125 to 0.078125
- leaf_parent: int32 [8, 8], P('dp'), may hold values from 1 to 4, as said below
- att_route: int32 [8192, 2], P(('dp', 'expert')), may hold values from 0 to 3, all different within a row; in each aligned block of 256 rows (0 to 255, 256 to 511, ...) at most 160 rows name the same one
- ffn_route: int32 [8192, 2], P(('dp', 'expert')), may hold values from 0 to 3, all different within a row; in each aligned block of 256 rows (0 to 255, 256 to 511, ...) at most 160 rows name the same one
Outputs:
- layer_out: bfloat16 [8192, 2048], P(('dp', 'expert'))
- input_grad: float32 [8192, 2048], P(('dp', 'expert'))
- gain_one_grad: float32 [2048], P(('dp', 'expert'))
- gain_two_grad: float32 [2048], P(('dp', 'expert'))
- kv_grad: float32 [2048, 4096], P(('dp', 'expert'))
- att_router_grad: float32 [2048, 4], P(('dp', 'expert'))
- ffn_router_grad: float32 [2048, 4], P(('dp', 'expert'))
- query_grad: float32 [4, 2048, 2048], P('expert', 'dp')
- output_grad: float32 [4, 2048, 2048], P('expert', 'dp')
- gate_grad: float32 [4, 2048, 5632], P('expert', 'dp')
- up_grad: float32 [4, 2048, 5632], P('expert', 'dp')
- down_grad: float32 [4, 5632, 2048], P('expert', 'dp')
Inputs may be any that keep to these rules, and one draw needn't show every extreme that they name: leaf_parent[t, l] is the branch segment that leaf l of tree t continues; each branch has exactly two leaves. `att_route`: each row names two different experts; among the 256 rows of one device no expert is named by more than 160 rows, a bound that some block reaches. `ffn_route`: each row names two different experts; among the 256 rows of one device no expert is named by more than 160 rows, a bound that some block reaches.
All inputs are finite; a program needn't handle non-finite values.
Results may differ from a plain program's by a relative error of at most 0.019.
Values may be sent and summed in bfloat16 or wider, within the bound.
No kernel may reach another device: no remote copies, remote signals or barrier semaphores. Data moves between devices by JAX's collectives and lax.ppermute only.
A program may use at most 448 MiB of HBM per device.

v0:
```python
import jax
import jax.numpy as jnp
from jax import lax
from jax.sharding import PartitionSpec as P

HEADS = 16
HEAD = 128
TRUNK = 512
BRANCH = 64
LEAF = 32


norm_eps = 1e-05
highest = lax.Precision.HIGHEST
masked_score = -1e30


def layout(row_index):
    past_trunk = row_index - TRUNK
    in_branch = (row_index >= TRUNK) & (past_trunk < 4 * BRANCH)
    leaf_offset = past_trunk - 4 * BRANCH
    segment = jnp.where(
        row_index < TRUNK,
        0,
        jnp.where(in_branch, 1 + past_trunk // BRANCH, 5 + leaf_offset // LEAF),
    )
    position = jnp.where(
        row_index < TRUNK,
        row_index,
        jnp.where(in_branch, TRUNK + past_trunk % BRANCH, TRUNK + BRANCH + leaf_offset % LEAF),
    )
    return (segment, position)


def visible(query_index, query_segment, key_index, key_segment, parents):
    leaf_slot = query_segment - 5
    branch_of = jnp.sum(
        jnp.where(
            leaf_slot[:, None] == jnp.arange(8, dtype=jnp.int32)[None, :], parents[None, :], 0
        ),
        1,
    )
    ancestor = jnp.where(query_segment >= 5, branch_of, -1)
    same_segment = (key_segment[None, :] == query_segment[:, None]) & (
        key_index[None, :] <= query_index[:, None]
    )
    from_trunk = (key_segment[None, :] == 0) & (query_segment[:, None] > 0)
    from_branch = key_segment[None, :] == ancestor[:, None]
    return same_segment | from_trunk | from_branch


def rotary_tables(position):
    half_width = HEAD // 2
    frequency = 10000.0 ** (-2.0 * jnp.arange(half_width, dtype=jnp.float32) / HEAD)
    angle = position.astype(jnp.float32)[:, None] * frequency[None, :]
    return (jnp.cos(angle), jnp.sin(angle))


def rotate(vector, cosine, sine_table):
    length = vector.shape[0]
    heads_view = vector.reshape(length, HEADS, HEAD)
    lead_half = heads_view[..., : HEAD // 2]
    tail_half = heads_view[..., HEAD // 2 :]
    cos_part = cosine[:, None, :]
    sin_part = sine_table[:, None, :]
    turned = jnp.concatenate(
        [lead_half * cos_part - tail_half * sin_part, tail_half * cos_part + lead_half * sin_part],
        -1,
    )
    return turned.reshape(length, HEADS * HEAD)


def rotate_back(grad_in, cosine, sine_table):
    length = grad_in.shape[0]
    heads_view = grad_in.reshape(length, HEADS, HEAD)
    lead_half = heads_view[..., : HEAD // 2]
    tail_half = heads_view[..., HEAD // 2 :]
    cos_part = cosine[:, None, :]
    sin_part = sine_table[:, None, :]
    turned = jnp.concatenate(
        [lead_half * cos_part + tail_half * sin_part, tail_half * cos_part - lead_half * sin_part],
        -1,
    )
    return turned.reshape(length, HEADS * HEAD)


def slot_targets(routes, capacity, experts):
    flat_routes = routes.reshape(-1)
    picks = (flat_routes[:, None] == jnp.arange(experts, dtype=jnp.int32)[None, :]).astype(
        jnp.int32
    )
    earlier = jnp.cumsum(picks, 0) - picks
    return (flat_routes * capacity + jnp.sum(earlier * picks, 1)).reshape(routes.shape)


def placement_of(routes, capacity, experts):
    target = slot_targets(routes, capacity, experts)
    slots_all = jnp.arange(experts * capacity, dtype=jnp.int32)
    return (slots_all[:, None, None] == target[None, :, :]).astype(jnp.bfloat16)


def slot_sources(group_routes, capacity, experts, row_count, own_expert):
    sources = group_routes.shape[0] // row_count
    per_source = group_routes.reshape(sources, row_count, 2)
    targets = jax.vmap(lambda source_routes: slot_targets(source_routes, capacity, experts))(
        per_source
    )
    wanted = own_expert * capacity + jnp.arange(capacity, dtype=jnp.int32)
    hits = targets[:, None, :, :] == wanted[None, :, None, None]
    token_ids = (
        jnp.arange(sources, dtype=jnp.int32)[:, None] * row_count
        + jnp.arange(row_count, dtype=jnp.int32)[None, :]
    )
    found = jnp.sum(jnp.where(hits, token_ids[:, None, :, None], 0), (2, 3))
    return found.reshape(-1)


def gate_weights(logits, routes, experts):
    picks = (routes[:, :, None] == jnp.arange(experts, dtype=jnp.int32)[None, None, :]).astype(
        jnp.float32
    )
    chosen = jnp.sum(picks * logits[:, None, :], -1)
    return (jax.nn.softmax(chosen, -1), picks)


def router_back(gates, picks, picked, stream_grad):
    gate_grad = jnp.sum(picked * stream_grad[:, None, :], 2)
    chosen_grad = gates * (gate_grad - jnp.sum(gates * gate_grad, 1, keepdims=True))
    return jnp.sum(picks * chosen_grad[:, :, None], 1)


def send_rows(place, values, experts, capacity):
    packed = jnp.dot(jnp.sum(place, 2), values, preferred_element_type=jnp.float32).astype(
        jnp.bfloat16
    )
    return packed.reshape(experts, capacity, -1)


def send_grads(place, grads_in, experts, capacity):
    packed = jnp.einsum("srk,rkd->sd", place, grads_in, preferred_element_type=jnp.float32).astype(
        jnp.bfloat16
    )
    return packed.reshape(experts, capacity, -1)


def take_back(place, returned):
    flat_back = returned.reshape(place.shape[0], -1)
    return jnp.einsum("srk,sd->rkd", place, flat_back, preferred_element_type=jnp.float32)


def to_owner(packed):
    return lax.all_to_all(packed, "expert", split_axis=0, concat_axis=0, tiled=True)


def to_source(packed):
    return lax.all_to_all(packed, "expert", split_axis=0, concat_axis=0, tiled=True)


def expert_weights(query_weight, output_weight, gate_weight, up_weight, down_weight):
    gathered = (
        lax.all_gather(query_weight, "dp", axis=1, tiled=True),
        lax.all_gather(output_weight, "dp", axis=1, tiled=True),
        lax.all_gather(gate_weight, "dp", axis=1, tiled=True),
        lax.all_gather(up_weight, "dp", axis=1, tiled=True),
        lax.all_gather(down_weight, "dp", axis=1, tiled=True),
    )
    return tuple((member[0] for member in gathered))


def attention_scores(queries, key_block, key_mask, score_scale):
    length = queries.shape[0]
    raw_scores = (
        jnp.einsum(
            "qhd,khd->hqk",
            queries.reshape(length, HEADS, HEAD),
            key_block.reshape(key_block.shape[0], HEADS, HEAD),
            preferred_element_type=jnp.float32,
        )
        * score_scale
    )
    return jnp.where(key_mask[None], raw_scores, masked_score)


def norm_back(stream, inverse, gain, grad_in):
    scaled = grad_in * gain
    return inverse * scaled - stream * inverse**3 * jnp.mean(scaled * stream, -1, keepdims=True)


def body(
    tokens,
    cotangent,
    gain_one,
    gain_two,
    kv_weight,
    att_router,
    ffn_router,
    query_weight,
    output_weight,
    gate_weight,
    up_weight,
    down_weight,
    leaf_parent,
    att_route,
    ffn_route,
):
    row_count = tokens.shape[0]
    model_width = tokens.shape[1]
    experts = att_router.shape[1]
    capacity = row_count * 5 // (2 * experts)
    head_width = HEADS * HEAD
    score_scale = HEAD ** (-0.5)
    parents = leaf_parent[0]
    own_expert = lax.axis_index("expert")
    shared = (
        lax.all_gather(gain_one, ("dp", "expert"), axis=0, tiled=True),
        lax.all_gather(gain_two, ("dp", "expert"), axis=0, tiled=True),
        lax.all_gather(kv_weight, ("dp", "expert"), axis=0, tiled=True),
        lax.all_gather(att_router, ("dp", "expert"), axis=0, tiled=True),
        lax.all_gather(ffn_router, ("dp", "expert"), axis=0, tiled=True),
    )
    gain_first = shared[0].astype(jnp.float32)
    gain_second = shared[1].astype(jnp.float32)
    kv_all = shared[2]
    att_all = shared[3]
    ffn_all = shared[4]
    query_all, output_all, gate_all, up_all, down_all = expert_weights(
        query_weight, output_weight, gate_weight, up_weight, down_weight
    )
    own_index = own_expert * row_count + jnp.arange(row_count, dtype=jnp.int32)
    _, own_position = layout(own_index)
    own_cos, own_sin = rotary_tables(own_position)
    inputs = tokens.astype(jnp.float32)
    inverse_one = lax.rsqrt(jnp.mean(inputs * inputs, -1, keepdims=True) + norm_eps)
    normed_one = (inputs * inverse_one * gain_first).astype(jnp.bfloat16)
    kv_raw = jnp.dot(normed_one, kv_all, preferred_element_type=jnp.float32)
    kv_local = jnp.concatenate(
        [rotate(kv_raw[:, :head_width], own_cos, own_sin), kv_raw[:, head_width:]], 1
    ).astype(jnp.bfloat16)
    kv_group = lax.all_gather(kv_local, "expert", axis=0, tiled=True)
    route_group = lax.all_gather(att_route, "expert", axis=0, tiled=True)
    key_block = kv_group[:, :head_width]
    value_block = kv_group[:, head_width:]
    key_index = jnp.arange(kv_group.shape[0], dtype=jnp.int32)
    key_segment, _ = layout(key_index)
    att_logits = jnp.dot(normed_one, att_all, preferred_element_type=jnp.float32)
    att_gate, att_picks = gate_weights(att_logits, att_route, experts)
    att_place = placement_of(att_route, capacity, experts)
    query_rows = to_owner(send_rows(att_place, normed_one, experts, capacity)).reshape(
        -1, model_width
    )
    query_index = slot_sources(route_group, capacity, experts, row_count, own_expert)
    query_segment, query_position = layout(query_index)
    query_cos, query_sin = rotary_tables(query_position)
    key_mask = visible(query_index, query_segment, key_index, key_segment, parents)
    queries = rotate(
        jnp.dot(query_rows, query_all, preferred_element_type=jnp.float32), query_cos, query_sin
    ).astype(jnp.bfloat16)
    scores = attention_scores(queries, key_block, key_mask, score_scale)
    row_peak = jnp.max(scores, -1, keepdims=True)
    exponent = jnp.exp(scores - row_peak)
    row_total = jnp.sum(exponent, -1, keepdims=True)
    log_total = row_peak + jnp.log(row_total)
    value_heads = value_block.reshape(-1, HEADS, HEAD)
    attended = (
        jnp.einsum(
            "hqk,khd->qhd",
            (exponent / row_total).astype(jnp.bfloat16),
            value_heads,
            preferred_element_type=jnp.float32,
        )
        .reshape(-1, head_width)
        .astype(jnp.bfloat16)
    )
    att_branch = jnp.dot(attended, output_all, preferred_element_type=jnp.float32).astype(
        jnp.bfloat16
    )
    att_picked = take_back(att_place, to_source(att_branch.reshape(experts, capacity, -1)))
    mixed_stream = inputs + jnp.sum(att_gate[:, :, None] * att_picked, 1)
    inverse_two = lax.rsqrt(jnp.mean(mixed_stream * mixed_stream, -1, keepdims=True) + norm_eps)
    normed_two = (mixed_stream * inverse_two * gain_second).astype(jnp.bfloat16)
    ffn_logits = jnp.dot(normed_two, ffn_all, preferred_element_type=jnp.float32)
    ffn_gate, ffn_picks = gate_weights(ffn_logits, ffn_route, experts)
    ffn_place = placement_of(ffn_route, capacity, experts)
    ffn_rows = to_owner(send_rows(ffn_place, normed_two, experts, capacity)).reshape(
        -1, model_width
    )
    gate_value = jnp.dot(ffn_rows, gate_all, preferred_element_type=jnp.float32)
    up_value = jnp.dot(ffn_rows, up_all, preferred_element_type=jnp.float32)
    hidden = (jax.nn.silu(gate_value) * up_value).astype(jnp.bfloat16)
    ffn_branch = jnp.dot(hidden, down_all, preferred_element_type=jnp.float32).astype(jnp.bfloat16)
    ffn_picked = take_back(ffn_place, to_source(ffn_branch.reshape(experts, capacity, -1)))
    result = mixed_stream + jnp.sum(ffn_gate[:, :, None] * ffn_picked, 1)
    grad_out = cotangent.astype(jnp.float32)
    ffn_logit_grad = router_back(ffn_gate, ffn_picks, ffn_picked, grad_out)
    ffn_branch_grad = (ffn_gate[:, :, None] * grad_out[:, None, :]).astype(jnp.bfloat16)
    ffn_grad_rows = to_owner(send_grads(ffn_place, ffn_branch_grad, experts, capacity)).reshape(
        -1, model_width
    )
    query_all, output_all, gate_all, up_all, down_all = expert_weights(
        query_weight, output_weight, gate_weight, up_weight, down_weight
    )
    hidden_grad = jnp.dot(ffn_grad_rows, down_all.T, preferred_element_type=jnp.float32)
    sigmoid_gate = jax.nn.sigmoid(gate_value)
    gate_grad = (
        hidden_grad * up_value * sigmoid_gate * (1.0 + gate_value * (1.0 - sigmoid_gate))
    ).astype(jnp.bfloat16)
    up_grad = (hidden_grad * gate_value * sigmoid_gate).astype(jnp.bfloat16)
    ffn_rows_grad = (
        jnp.dot(gate_grad, gate_all.T, preferred_element_type=jnp.float32)
        + jnp.dot(up_grad, up_all.T, preferred_element_type=jnp.float32)
    ).astype(jnp.bfloat16)
    ffn_rows_back = to_source(ffn_rows_grad.reshape(experts, capacity, -1)).reshape(
        experts * capacity, -1
    )
    gate_part = jnp.dot(ffn_rows.T, gate_grad, preferred_element_type=jnp.float32)
    up_part = jnp.dot(ffn_rows.T, up_grad, preferred_element_type=jnp.float32)
    down_part = jnp.dot(hidden.T, ffn_grad_rows, preferred_element_type=jnp.float32)
    gate_sum, up_sum, down_sum = (
        lax.psum_scatter(
            gate_part.astype(jnp.bfloat16), "dp", scatter_dimension=0, tiled=True
        ).astype(jnp.float32),
        lax.psum_scatter(
            up_part.astype(jnp.bfloat16), "dp", scatter_dimension=0, tiled=True
        ).astype(jnp.float32),
        lax.psum_scatter(
            down_part.astype(jnp.bfloat16), "dp", scatter_dimension=0, tiled=True
        ).astype(jnp.float32),
    )
    normed_two_grad = jnp.einsum(
        "srk,sd->rd", ffn_place, ffn_rows_back, preferred_element_type=jnp.float32
    ) + jnp.dot(ffn_logit_grad, ffn_all.astype(jnp.float32).T, precision=highest)
    gain_two_part = jnp.sum(normed_two_grad * mixed_stream * inverse_two, 0)
    mixed_grad = grad_out + norm_back(mixed_stream, inverse_two, gain_second, normed_two_grad)
    att_logit_grad = router_back(att_gate, att_picks, att_picked, mixed_grad)
    att_branch_grad = (att_gate[:, :, None] * mixed_grad[:, None, :]).astype(jnp.bfloat16)
    att_grad_rows = to_owner(send_grads(att_place, att_branch_grad, experts, capacity)).reshape(
        -1, model_width
    )
    attended_grad = jnp.dot(att_grad_rows, output_all.T, preferred_element_type=jnp.float32).astype(
        jnp.bfloat16
    )
    output_part = jnp.dot(attended.T, att_grad_rows, preferred_element_type=jnp.float32)
    scores_again = attention_scores(queries, key_block, key_mask, score_scale)
    probs_full = jnp.exp(scores_again - log_total)
    attended_heads = attended_grad.reshape(-1, HEADS, HEAD)
    prob_grad = jnp.einsum(
        "qhd,khd->hqk", attended_heads, value_heads, preferred_element_type=jnp.float32
    )
    row_delta = jnp.sum(probs_full * prob_grad, -1, keepdims=True)
    score_grad = (probs_full * (prob_grad - row_delta)).astype(jnp.bfloat16)
    key_heads = key_block.reshape(-1, HEADS, HEAD)
    query_heads = queries.reshape(-1, HEADS, HEAD)
    query_grad_full = (
        jnp.einsum(
            "hqk,khd->qhd", score_grad, key_heads, preferred_element_type=jnp.float32
        ).reshape(-1, head_width)
        * score_scale
    )
    key_grad_part = (
        jnp.einsum(
            "hqk,qhd->khd", score_grad, query_heads, preferred_element_type=jnp.float32
        ).reshape(-1, head_width)
        * score_scale
    )
    value_grad_part = jnp.einsum(
        "hqk,qhd->khd",
        probs_full.astype(jnp.bfloat16),
        attended_heads,
        preferred_element_type=jnp.float32,
    ).reshape(-1, head_width)
    query_raw_grad = rotate_back(query_grad_full, query_cos, query_sin).astype(jnp.bfloat16)
    query_part = jnp.dot(query_rows.T, query_raw_grad, preferred_element_type=jnp.float32)
    att_rows_grad = jnp.dot(query_raw_grad, query_all.T, preferred_element_type=jnp.float32).astype(
        jnp.bfloat16
    )
    att_rows_back = to_source(att_rows_grad.reshape(experts, capacity, -1)).reshape(
        experts * capacity, -1
    )
    query_sum, output_sum = (
        lax.psum_scatter(
            query_part.astype(jnp.bfloat16), "dp", scatter_dimension=0, tiled=True
        ).astype(jnp.float32),
        lax.psum_scatter(
            output_part.astype(jnp.bfloat16), "dp", scatter_dimension=0, tiled=True
        ).astype(jnp.float32),
    )
    kv_grad_local = lax.psum_scatter(
        jnp.concatenate([key_grad_part, value_grad_part], 1).astype(jnp.bfloat16),
        "expert",
        scatter_dimension=0,
        tiled=True,
    ).astype(jnp.float32)
    kv_raw_grad = jnp.concatenate(
        [
            rotate_back(kv_grad_local[:, :head_width], own_cos, own_sin),
            kv_grad_local[:, head_width:],
        ],
        1,
    ).astype(jnp.bfloat16)
    kv_part = jnp.dot(normed_one.T, kv_raw_grad, preferred_element_type=jnp.float32)
    normed_one_grad = (
        jnp.dot(kv_raw_grad, kv_all.T, preferred_element_type=jnp.float32)
        + jnp.einsum("srk,sd->rd", att_place, att_rows_back, preferred_element_type=jnp.float32)
        + jnp.dot(att_logit_grad, att_all.astype(jnp.float32).T, precision=highest)
    )
    gain_one_part = jnp.sum(normed_one_grad * inputs * inverse_one, 0)
    input_grad = mixed_grad + norm_back(inputs, inverse_one, gain_first, normed_one_grad)
    att_router_part = jnp.dot(normed_one.astype(jnp.float32).T, att_logit_grad, precision=highest)
    ffn_router_part = jnp.dot(normed_two.astype(jnp.float32).T, ffn_logit_grad, precision=highest)
    shared_sums = (
        lax.psum_scatter(gain_one_part, ("dp", "expert"), scatter_dimension=0, tiled=True),
        lax.psum_scatter(gain_two_part, ("dp", "expert"), scatter_dimension=0, tiled=True),
        lax.psum_scatter(kv_part, ("dp", "expert"), scatter_dimension=0, tiled=True),
        lax.psum_scatter(att_router_part, ("dp", "expert"), scatter_dimension=0, tiled=True),
        lax.psum_scatter(ffn_router_part, ("dp", "expert"), scatter_dimension=0, tiled=True),
    )
    return (
        result.astype(jnp.bfloat16),
        input_grad,
        shared_sums[0],
        shared_sums[1],
        shared_sums[2],
        shared_sums[3],
        shared_sums[4],
        query_sum[None],
        output_sum[None],
        gate_sum[None],
        up_sum[None],
        down_sum[None],
    )


def solution(mesh):
    in_specs = (
        P(("dp", "expert"), None),
        P(("dp", "expert"), None),
        P(("dp", "expert")),
        P(("dp", "expert")),
        P(("dp", "expert"), None),
        P(("dp", "expert"), None),
        P(("dp", "expert"), None),
        P("expert", "dp", None),
        P("expert", "dp", None),
        P("expert", "dp", None),
        P("expert", "dp", None),
        P("expert", "dp", None),
        P("dp", None),
        P(("dp", "expert"), None),
        P(("dp", "expert"), None),
    )
    out_specs = (
        P(("dp", "expert"), None),
        P(("dp", "expert"), None),
        P(("dp", "expert")),
        P(("dp", "expert")),
        P(("dp", "expert"), None),
        P(("dp", "expert"), None),
        P(("dp", "expert"), None),
        P("expert", "dp", None),
        P("expert", "dp", None),
        P("expert", "dp", None),
        P("expert", "dp", None),
        P("expert", "dp", None),
    )
    return jax.shard_map(body, mesh=mesh, in_specs=in_specs, out_specs=out_specs, check_vma=False)
```

profile of v0, /device:TPU:0, one launch (start us, length us, event | category | flops | bytes accessed | tf_op | source)
XLA Modules:
  0.0 2927.9 jit_solution(2531565768638693867)
XLA Ops:
  10.4 43.7 %all-reduce.5 = (bf16[2048]{0:T(1024)(128)(2,1)S(1)}, bf16[2048]{0:T(1024)(128)(2,1)}) all-reduce(bf16[2048]{0:T(1024)(128)(2,1)S(1)} %dynamic-update-slice, bf16[2048]{0:T(1024)(128)(2,1)S(1)} %dynamic-update-slice.1), channel_id=1, replica_groups=mesh['dp'=8,'expert'=4] {'dp','expert'}, use_global_device_ids=true, to_apply=%add | all-reduce | flops 4096 | bytes 16384
  56.8 72.6 %all-gather.10.cloned.1.call-done = bf16[2048,4096]{1,0:T(8,128)(2,1)} async-done(((bf16[64,4096]{1,0:T(8,128)(2,1)}), bf16[2048,4096]{1,0:T(8,128)(2,1)}) %all-gather.10.cloned.1.call-update) | async-done | bytes 16777232 | tf_op jit(solution)/shard_map/all_gather | solution.py:217
  154.4 117.2 %all_gather.45 = s32[1024,2]{0,1:T(2,128)S(1)} all-gather(s32[256,2]{0,1:T(2,128)S(1)} %copy-done.58), channel_id=1, replica_groups=mesh['dp'=8,'expert'=4] {'expert'}, dimensions={0}, use_global_device_ids=true | all-gather | bytes 10240 | tf_op jit(solution)/shard_map/all_gather | solution.py:240
  306.3 44.0 %all-gather.12.cloned.1.call-done = bf16[1024,4096]{1,0:T(8,128)(2,1)} async-done(((bf16[256,4096]{1,0:T(8,128)(2,1)}), bf16[1024,4096]{1,0:T(8,128)(2,1)}) %all-gather.12.cloned.1.call-update) | async-done | bytes 8388624 | tf_op jit(solution)/shard_map/all_gather | solution.py:239
  362.8 21.0 fusion.18
  403.2 22.6 fusion.63
  440.9 116.7 %all-gather = bf16[32,64,4]{1,2,0:T(4,128)(2,1)S(1)} all-gather(bf16[1,64,4]{1,2,0:T(4,128)(2,1)S(1)} %bitcast.253), channel_id=1, replica_groups=mesh['dp'=8,'expert'=4] {'dp','expert'}, dimensions={0}, use_global_device_ids=true | all-gather | bytes 16896 | tf_op jit(solution)/shard_map/all_gather | solution.py:218
  557.8 63.6 %all-gather.1 = bf16[32,64,4]{1,2,0:T(4,128)(2,1)S(1)} all-gather(bf16[1,64,4]{1,2,0:T(4,128)(2,1)S(1)} %bitcast.254), channel_id=1, replica_groups=mesh['dp'=8,'expert'=4] {'dp','expert'}, dimensions={0}, use_global_device_ids=true | all-gather | bytes 16896 | tf_op jit(solution)/shard_map/all_gather | solution.py:219
  645.8 51.7 %all-to-all-done.4 = bf16[4,160,2048]{2,1,0:T(8,128)(2,1)} async-done(((bf16[4,160,2048]{2,1,0:T(8,128)(2,1)}), bf16[4,160,2048]{2,1,0:T(8,128)(2,1)}, u32[]{:S(2)}, u32[]{:S(2)}) %all-to-all-start.4) | async-done | bytes 2621472 | tf_op jit(solution)/shard_map/all_to_all | solution.py:152
  701.4 23.1 fusion.2
  724.5 35.8 %all-to-all-done.2 = bf16[4,160,2048]{2,1,0:T(8,128)(2,1)S(1)} async-done(((bf16[4,160,2048]{2,1,0:T(8,128)(2,1)}), bf16[4,160,2048]{2,1,0:T(8,128)(2,1)S(1)}, u32[]{:S(2)}, u32[]{:S(2)}) %all-to-all-start.2) | async-done | bytes 2621472 | tf_op jit(solution)/shard_map/all_to_all | solution.py:152
  760.3 23.4 fusion.8
  783.7 31.9 %multiply_convert_fusion.2 = (bf16[640,5632]{1,0:T(8,128)(2,1)}, bf16[640,5632]{1,0:T(8,128)(2,1)}, bf16[640,5632]{1,0:T(8,128)(2,1)}) fusion(f32[640,5632]{1,0:T(8,128)} %fusion.2, f32[640,5632]{1,0:T(8,128)} %fusion.8, bf16[640,2048]{1,0:T(8,128)(2,1)S(1)} %bitcast.236, bf16[1,2048,5632]{2,1,0:T(8,128)(2,1)} %all-gather.18.cloned.1.call-done), kind=kOutput, calls=%fused_computation.28 | convolution fusion | flops 14821621760 | bytes 76152832 | tf_op jit(solution)/shard_map/dot_general | solution.py:287
  815.6 21.2 fusion.35
  840.5 20.4 fusion.6
  861.0 21.3 add_convert_fusion
  912.2 52.8 %all-to-all-done.5 = bf16[4,160,2048]{2,1,0:T(8,128)(2,1)} async-done(((bf16[4,160,2048]{2,1,0:T(8,128)(2,1)}), bf16[4,160,2048]{2,1,0:T(8,128)(2,1)}, u32[]{:S(2)}, u32[]{:S(2)}) %all-to-all-start.5) | async-done | bytes 2621472 | tf_op jit(solution)/shard_map/all_to_all | solution.py:156
  978.9 58.9 %all-to-all-done.6 = bf16[4,160,2048]{2,1,0:T(8,128)(2,1)S(1)} async-done(((bf16[4,160,2048]{2,1,0:T(8,128)(2,1)}), bf16[4,160,2048]{2,1,0:T(8,128)(2,1)S(1)}, u32[]{:S(2)}, u32[]{:S(2)}) %all-to-all-start.6) | async-done | bytes 2621472 | tf_op jit(solution)/shard_map/all_to_all | solution.py:152
  1072.2 35.9 %multiply_reduce_fusion = (f32[16,640]{1,0:T(8,128)S(1)}, f32[16,640,1024]{2,1,0:T(8,128)}) fusion(f32[16,640]{1,0:T(8,128)S(1)} %log_add_fusion, f32[16,640,1024]{2,1,0:T(8,128)} %get-tuple-element.54, pred[640,1024]{1,0:T(8,128)(4,1)S(1)} %copy-done.6, bf16[640,16,128]{0,2,1:T(8,128)(2,1)S(1)} %bitcast.224, bf16[128,16,8,128]{3,2,1,0:T(8,128)(2,1)} %get-tuple-element.29), kind=kOutput, calls=%fused_computation.1 | convolution fusion | flops 2736773120 | bytes 91439104 | tf_op jit(solution)/shard_map/qhd,khd->hqk/dot_general | solution.py:346
  1108.1 34.7 %multiply_convert_fusion = bf16[16,640,1024]{2,1,0:T(8,128)(2,1)} fusion(f32[16,640,1024]{2,1,0:T(8,128)} %get-tuple-element.59, f32[16,640]{1,0:T(8,128)S(1)} %get-tuple-element.58, f32[16,640]{1,0:T(8,128)S(1)} %log_add_fusion, f32[16,640,1024]{2,1,0:T(8,128)} %get-tuple-element.54, pred[640,1024]{1,0:T(8,128)(4,1)S(1)} %copy-done.6), kind=kLoop, calls=%fused_computation | loop fusion | flops 62914560 | bytes 105594880 | tf_op jit(solution)/shard_map/convert_element_type | solution.py:350
  1212.9 25.7 convolution_convert_fusion
  1240.4 24.5 convolution_convert_fusion.2
  1265.0 24.4 convolution_convert_fusion.1
  1348.2 122.7 %reduce-scatter.30.cloned.1.call-done = f32[64,4]{1,0:T(8,128)} async-done(((f32[2048,4]{1,0:T(8,128)}), f32[64,4]{1,0:T(8,128)}) %reduce-scatter.30.cloned.1.call-update) | async-done | bytes 1040
  1472.3 137.3 %reduce-scatter.28.cloned.1.call-done = f32[64,4]{1,0:T(8,128)} async-done(((f32[2048,4]{1,0:T(8,128)}), f32[64,4]{1,0:T(8,128)}) %reduce-scatter.28.cloned.1.call-update) | async-done | bytes 1040
  1611.0 70.1 %reduce-scatter.20.cloned.1.call-done = bf16[256,2048]{1,0:T(8,128)(2,1)} async-done(((bf16[2048,2048]{1,0:T(8,128)(2,1)}), bf16[256,2048]{1,0:T(8,128)(2,1)}) %reduce-scatter.20.cloned.1.call-update) | async-done | bytes 1048592 | tf_op jit(solution)/shard_map/reduce_scatter | solution.py:383
  1683.9 72.1 %reduce-scatter.18.cloned.1.call-done = bf16[256,2048]{1,0:T(8,128)(2,1)} async-done(((bf16[2048,2048]{1,0:T(8,128)(2,1)}), bf16[256,2048]{1,0:T(8,128)(2,1)}) %reduce-scatter.18.cloned.1.call-update) | async-done | bytes 1048592 | tf_op jit(solution)/shard_map/reduce_scatter | solution.py:380
  1779.5 40.0 %all-reduce.4 = (f32[2048]{0:T(1024)S(1)}, f32[2048]{0:T(1024)S(1)}) all-reduce(f32[2048]{0:T(1024)S(1)} %get-tuple-element.16, f32[2048]{0:T(1024)S(1)} %copy-done.64), channel_id=3, replica_groups=mesh['dp'=8,'expert'=4] {'dp','expert'}, use_global_device_ids=true, to_apply=%region_36.37.clone | all-reduce | flops 4096 | bytes 32768
  1824.1 82.6 %reduce-scatter.26.cloned.1.call-done = bf16[704,2048]{1,0:T(8,128)(2,1)} async-done(((bf16[5632,2048]{1,0:T(8,128)(2,1)}), bf16[704,2048]{1,0:T(8,128)(2,1)}) %reduce-scatter.26.cloned.1.call-update) | async-done | bytes 2883600 | tf_op jit(solution)/shard_map/reduce_scatter | solution.py:325
  1911.8 144.7 %reduce-scatter.22.cloned.1.call-done = bf16[256,5632]{1,0:T(8,128)(2,1)} async-done(((bf16[2048,5632]{1,0:T(8,128)(2,1)}), bf16[256,5632]{1,0:T(8,128)(2,1)}) %reduce-scatter.22.cloned.1.call-update) | async-done | bytes 2883600 | tf_op jit(solution)/shard_map/reduce_scatter | solution.py:319
  2061.5 144.8 %reduce-scatter.24.cloned.1.call-done = bf16[256,5632]{1,0:T(8,128)(2,1)} async-done(((bf16[2048,5632]{1,0:T(8,128)(2,1)}), bf16[256,5632]{1,0:T(8,128)(2,1)}) %reduce-scatter.24.cloned.1.call-update) | async-done | bytes 2883600 | tf_op jit(solution)/shard_map/reduce_scatter | solution.py:322
  2211.4 709.6 %reduce-scatter.16.cloned.1.call-done = f32[64,4096]{1,0:T(8,128)} async-done(((f32[2048,4096]{1,0:T(8,128)}), f32[64,4096]{1,0:T(8,128)}) %reduce-scatter.16.cloned.1.call-update) | async-done | bytes 1048592 | tf_op jit(solution)/shard_map/reduce_scatter | solution.py:413
  (381 shorter events, 401.2 us)
Async XLA Ops:
  7.2 122.2 %copy-start = (bf16[256,2048]{1,0:T(8,128)(2,1)S(1)}, bf16[256,2048]{1,0:T(8,128)(2,1)}, u32[]{:S(2)}) copy-start(bf16[256,2048]{1,0:T(8,128)(2,1)} %param.15) | copy-start | bytes 3145732
  7.2 122.2 %all-gather.10.cloned.1.call-start = ((), (), s32[]{:S(2)}) async-start(), calls=%async_computation.17 | async-start | bytes 17301504 | tf_op jit(solution)/shard_map/all_gather | solution.py:217
  7.9 273.9 %all-gather.14.cloned.1.call-start = ((), (), s32[]{:S(2)}) async-start(), calls=%async_computation.19 | async-start | bytes 9437184 | tf_op jit(solution)/shard_map/all_gather | solution.py:161
  8.7 341.6 %all-gather.12.cloned.1.call-start = ((), (), s32[]{:S(2)}) async-start(), calls=%async_computation.18 | async-start | bytes 10485760 | tf_op jit(solution)/shard_map/all_gather | solution.py:239
  54.1 570.9 %copy-start.38 = (f32[2048]{0:T(1024)}, f32[2048]{0:T(1024)S(1)}, u32[]{:S(2)}) copy-start(f32[2048]{0:T(1024)S(1)} %convert_element_type.184) | copy-start | bytes 24580
  56.3 568.8 %copy-start.53 = (f32[256]{0:T(256)}, f32[256]{0:T(256)S(1)}, u32[]{:S(2)}) copy-start(f32[256]{0:T(256)S(1)} %get-tuple-element.50) | copy-start | bytes 3076
  141.4 284.3 %all-gather.16.cloned.1.call-start = ((), (), s32[]{:S(2)}) async-start(), calls=%async_computation.20 | async-start | bytes 9437184 | tf_op jit(solution)/shard_map/all_gather | solution.py:162
  142.0 559.4 %all-gather.22.cloned.1.call-start = ((), (), s32[]{:S(2)}) async-start(), calls=%async_computation.23 | async-start | bytes 25952256 | tf_op jit(solution)/shard_map/all_gather | solution.py:165
  142.6 581.9 %all-gather.20.cloned.1.call-start = ((), (), s32[]{:S(2)}) async-start(), calls=%async_computation.22 | async-start | bytes 25952256 | tf_op jit(solution)/shard_map/all_gather | solution.py:164
  143.2 640.5 %all-gather.18.cloned.1.call-start = ((), (), s32[]{:S(2)}) async-start(), calls=%async_computation.21 | async-start | bytes 25952256 | tf_op jit(solution)/shard_map/all_gather | solution.py:163
  146.3 479.3 %copy-start.62 = (s32[256,2]{0,1:T(2,128)}, s32[256,2]{0,1:T(2,128)S(1)}, u32[]{:S(2)}) copy-start(s32[256,2]{0,1:T(2,128)S(1)} %multiply_add_fusion.1) | copy-start | bytes 6148
  149.8 144.5 %all-to-all-start = ((bf16[4,160,2048]{2,1,0:T(8,128)(2,1)}), bf16[4,160,2048]{2,1,0:T(8,128)(2,1)}, u32[]{:S(2)}, u32[]{:S(2)}) async-start(bf16[4,160,2048]{2,1,0:T(8,128)(2,1)} %bitcast.225), calls=%async_computation | async-start | bytes 5242880 | tf_op jit(solution)/shard_map/all_to_all | solution.py:152
  154.4 125.3 %copy-start.88 = (s32[1,8]{1,0:T(1,128)S(1)}, s32[1,8]{1,0:T(1,128)}, u32[]{:S(2)}) copy-start(s32[1,8]{1,0:T(1,128)} %param.27) | copy-start | bytes 100
  435.7 187.8 %copy-start.17 = (bf16[256,2048]{1,0:T(8,128)(2,1)S(1)}, bf16[256,2048]{1,0:T(8,128)(2,1)}, u32[]{:S(2)}) copy-start(bf16[256,2048]{1,0:T(8,128)(2,1)} %param.16) | copy-start | bytes 3145732
  435.7 189.9 %all-to-all-start.1 = ((bf16[4,160,2048]{2,1,0:T(8,128)(2,1)}), bf16[4,160,2048]{2,1,0:T(8,128)(2,1)}, u32[]{:S(2)}, u32[]{:S(2)}) async-start(bf16[4,160,2048]{2,1,0:T(8,128)(2,1)} %bitcast.243), calls=%async_computation.1 | async-start | bytes 5242880 | tf_op jit(solution)/shard_map/all_to_all | solution.py:156
  440.9 191.6 %copy-start.47 = (f32[2048]{0:T(1024)}, f32[2048]{0:T(1024)S(1)}, u32[]{:S(2)}) copy-start(f32[2048]{0:T(1024)S(1)} %convert_element_type.201) | copy-start | bytes 24580
  637.8 59.7 %all-to-all-start.4 = ((bf16[4,160,2048]{2,1,0:T(8,128)(2,1)}), bf16[4,160,2048]{2,1,0:T(8,128)(2,1)}, u32[]{:S(2)}, u32[]{:S(2)}) async-start(bf16[4,160,2048]{2,1,0:T(8,128)(2,1)} %bitcast.248), calls=%async_computation.4 | async-start | bytes 5242880 | tf_op jit(solution)/shard_map/all_to_all | solution.py:152
  697.5 62.8 %all-to-all-start.2 = ((bf16[4,160,2048]{2,1,0:T(8,128)(2,1)}), bf16[4,160,2048]{2,1,0:T(8,128)(2,1)S(1)}, u32[]{:S(2)}, u32[]{:S(2)}) async-start(bf16[4,160,2048]{2,1,0:T(8,128)(2,1)} %bitcast.226), calls=%async_computation.2 | async-start | bytes 5242880 | tf_op jit(solution)/shard_map/all_to_all | solution.py:152
  836.9 62.6 %all-to-all-start.3 = ((bf16[4,160,2048]{2,1,0:T(8,128)(2,1)}), bf16[4,160,2048]{2,1,0:T(8,128)(2,1)S(1)}, u32[]{:S(2)}, u32[]{:S(2)}) async-start(bf16[4,160,2048]{2,1,0:T(8,128)(2,1)} %bitcast.246), calls=%async_computation.3 | async-start | bytes 5242880 | tf_op jit(solution)/shard_map/all_to_all | solution.py:156
  901.0 64.0 %all-to-all-start.5 = ((bf16[4,160,2048]{2,1,0:T(8,128)(2,1)}), bf16[4,160,2048]{2,1,0:T(8,128)(2,1)}, u32[]{:S(2)}, u32[]{:S(2)}) async-start(bf16[4,160,2048]{2,1,0:T(8,128)(2,1)} %bitcast.30), calls=%async_computation.5 | async-start | bytes 5242880 | tf_op jit(solution)/shard_map/all_to_all | solution.py:156
  975.0 62.8 %all-to-all-start.6 = ((bf16[4,160,2048]{2,1,0:T(8,128)(2,1)}), bf16[4,160,2048]{2,1,0:T(8,128)(2,1)S(1)}, u32[]{:S(2)}, u32[]{:S(2)}) async-start(bf16[4,160,2048]{2,1,0:T(8,128)(2,1)} %bitcast.247), calls=%async_computation.6 | async-start | bytes 5242880 | tf_op jit(solution)/shard_map/all_to_all | solution.py:152
  978.8 327.4 %reduce-scatter.14.cloned.1.call-start = ((), (), s32[]{:S(2)}) async-start(), calls=%async_computation.24 | async-start | bytes 10485760 | tf_op jit(solution)/shard_map/reduce_scatter | solution.py:387
  1163.1 307.8 %reduce-scatter.30.cloned.1.call-start = ((), (), s32[]{:S(2)}) async-start(), calls=%async_computation.32 | async-start | bytes 1081344
  1169.8 439.8 %reduce-scatter.28.cloned.1.call-start = ((), (), s32[]{:S(2)}) async-start(), calls=%async_computation.31 | async-start | bytes 1081344
  1172.2 508.9 %reduce-scatter.20.cloned.1.call-start = ((), (), s32[]{:S(2)}) async-start(), calls=%async_computation.27 | async-start | bytes 9437184 | tf_op jit(solution)/shard_map/reduce_scatter | solution.py:383
  1183.4 572.6 %reduce-scatter.18.cloned.1.call-start = ((), (), s32[]{:S(2)}) async-start(), calls=%async_computation.26 | async-start | bytes 9437184 | tf_op jit(solution)/shard_map/reduce_scatter | solution.py:380
  1212.9 693.8 %reduce-scatter.26.cloned.1.call-start = ((), (), s32[]{:S(2)}) async-start(), calls=%async_computation.30 | async-start | bytes 25952256 | tf_op jit(solution)/shard_map/reduce_scatter | solution.py:325
  1238.6 817.9 %reduce-scatter.22.cloned.1.call-start = ((), (), s32[]{:S(2)}) async-start(), calls=%async_computation.28 | async-start | bytes 25952256 | tf_op jit(solution)/shard_map/reduce_scatter | solution.py:319
  1265.0 941.4 %reduce-scatter.24.cloned.1.call-start = ((), (), s32[]{:S(2)}) async-start(), calls=%async_computation.29 | async-start | bytes 25952256 | tf_op jit(solution)/shard_map/reduce_scatter | solution.py:322
  1289.5 1631.5 %reduce-scatter.16.cloned.1.call-start = ((), (), s32[]{:S(2)}) async-start(), calls=%async_computation.25 | async-start | bytes 34603008 | tf_op jit(solution)/shard_map/reduce_scatter | solution.py:413
  1343.6 428.3 %all-to-all-start.7 = ((bf16[4,160,2048]{2,1,0:T(8,128)(2,1)}), bf16[4,160,2048]{2,1,0:T(8,128)(2,1)}, u32[]{:S(2)}, u32[]{:S(2)}) async-start(bf16[4,160,2048]{2,1,0:T(8,128)(2,1)} %bitcast.244), calls=%async_computation.8 | async-start | bytes 5242880 | tf_op jit(solution)/shard_map/all_to_all | solution.py:156
  1611.0 147.8 %copy-start.16 = (bf16[256,2048]{0,1:T(8,128)(2,1)S(1)}, bf16[256,2048]{0,1:T(8,128)(2,1)}, u32[]{:S(2)}) copy-start(bf16[256,2048]{0,1:T(8,128)(2,1)} %get-tuple-element.40) | copy-start | bytes 3145732
  (81 other events, 1366.1 us)
Sparse Core Ops, SparseCore 0:
  11.0 118.3 all-gather.9
  131.3 52.5 all-gather.13
  186.0 164.2 all-gather.11
  352.0 52.2 all-gather.15
  406.1 116.3 all-gather.21
  524.2 116.5 all-gather.19
  642.7 116.3 all-gather.17
  1163.2 142.9 reduce-scatter.13
  1308.5 162.3 reduce-scatter.29
  1473.6 135.9 reduce-scatter.27
  1613.1 68.0 reduce-scatter.19
  1684.5 71.5 reduce-scatter.17
  1759.6 146.9 reduce-scatter.25
  1910.2 146.3 reduce-scatter.21
  2060.0 146.3 reduce-scatter.23
  2209.1 711.8 reduce-scatter.15
where the time goes:
time: 2940 us; the launch traced here: 2930 us
  waiting for transfers between devices  1840 us (63%)
  matrix products  480 us (16%)
  blocking collectives  381 us (13%)
  other arithmetic  119 us (4%)
  local copies, waits for them, and re-layouts  59.4 us (2%)
  starting transfers between devices  35.3 us (1%)
    reduce_scatter x1, waiting for transfers between devices, body(): lax.psum_scatter(kv_part, ('dp', 'expert'), scatter_dimension=0, tiled=True)  710 us
    unnamed x18, waiting for transfers between devices  264 us
    all_to_all x4, waiting for transfers between devices, to_owner(): lax.all_to_all(packed, 'expert', split_axis=0, concat_axis=0, tiled=True)  146 us
    reduce_scatter x1, waiting for transfers between devices, body(): lax.psum_scatter(up_part.astype(jnp.bfloat16), 'dp', scatter_dimension=0,...  145 us
    reduce_scatter x1, waiting for transfers between devices, body(): lax.psum_scatter(gate_part.astype(jnp.bfloat16), 'dp', scatter_dimension=...  145 us
    all_gather x1, blocking collectives, body(): route_group = lax.all_gather(att_route, 'expert', axis=0, tiled=True)  117 us
    all_gather x1, blocking collectives, body(): lax.all_gather(att_router, ('dp', 'expert'), axis=0, tiled=True)  117 us
    unnamed x2, blocking collectives  83.7 us
  transfers between devices with their start and end apart: 24, of which 16 were waited for; matrix products, arithmetic and copies ran while one was open for 16% of the time, Pallas kernels for 0%

commit v1 on v0

v1 whole, which is shorter than its diff:
```python
import jax
import jax.numpy as jnp
from jax import lax
from jax.sharding import PartitionSpec as P

HEADS = 16
HEAD = 128
TRUNK = 512
BRANCH = 64
LEAF = 32
PAD = 128


norm_eps = 1e-05
highest = lax.Precision.HIGHEST
masked_score = -1e30
score_scale = HEAD ** (-0.5)
bf16 = jnp.bfloat16
f32 = jnp.float32


def layout(row_index):
    past_trunk = row_index - TRUNK
    in_branch = (row_index >= TRUNK) & (past_trunk < 4 * BRANCH)
    leaf_offset = past_trunk - 4 * BRANCH
    segment = jnp.where(
        row_index < TRUNK,
        0,
        jnp.where(in_branch, 1 + past_trunk // BRANCH, 5 + leaf_offset // LEAF),
    )
    position = jnp.where(
        row_index < TRUNK,
        row_index,
        jnp.where(in_branch, TRUNK + past_trunk % BRANCH, TRUNK + BRANCH + leaf_offset % LEAF),
    )
    return (segment, position)


def visible(query_index, query_segment, key_index, key_segment, parents):
    leaf_slot = query_segment - 5
    branch_of = jnp.sum(
        jnp.where(
            leaf_slot[:, None] == jnp.arange(8, dtype=jnp.int32)[None, :], parents[None, :], 0
        ),
        1,
    )
    ancestor = jnp.where(query_segment >= 5, branch_of, -1)
    same_segment = (key_segment[None, :] == query_segment[:, None]) & (
        key_index[None, :] <= query_index[:, None]
    )
    from_trunk = (key_segment[None, :] == 0) & (query_segment[:, None] > 0)
    from_branch = key_segment[None, :] == ancestor[:, None]
    return same_segment | from_trunk | from_branch


def rotary_tables(position):
    half_width = HEAD // 2
    frequency = 10000.0 ** (-2.0 * jnp.arange(half_width, dtype=f32) / HEAD)
    angle = position.astype(f32)[:, None] * frequency[None, :]
    return (jnp.cos(angle), jnp.sin(angle))


def rotate(vector, cosine, sine_table):
    length, width = vector.shape
    heads_view = vector.reshape(length, width // HEAD, HEAD)
    lead_half = heads_view[..., : HEAD // 2]
    tail_half = heads_view[..., HEAD // 2 :]
    cos_part = cosine[:, None, :]
    sin_part = sine_table[:, None, :]
    turned = jnp.concatenate(
        [lead_half * cos_part - tail_half * sin_part, tail_half * cos_part + lead_half * sin_part],
        -1,
    )
    return turned.reshape(length, width)


def rotate_back(grad_in, cosine, sine_table):
    return rotate(grad_in, cosine, -sine_table)


def mm(left, right):
    return jnp.dot(left, right, preferred_element_type=f32)


def mm_tn(left, right):
    return lax.dot_general(left, right, (((0,), (0,)), ((), ())), preferred_element_type=f32)


def mm_nt(left, right):
    return lax.dot_general(left, right, (((1,), (1,)), ((), ())), preferred_element_type=f32)


def earlier_count(named):
    rows = named.shape[0]
    before = jnp.tril(jnp.ones((rows, rows), bf16), -1)
    return mm(before, named.astype(bf16)).astype(jnp.int32)


def placement_of(routes, capacity, experts):
    picks = (routes[:, :, None] == jnp.arange(experts, dtype=jnp.int32)[None, None, :]).astype(
        jnp.int32
    )
    rank = earlier_count(jnp.sum(picks, 1))
    target = routes * capacity + jnp.sum(picks * rank[:, None, :], 2)
    slots_all = jnp.arange(experts * capacity, dtype=jnp.int32)
    return (target.T[:, :, None] == slots_all[None, None, :]).astype(bf16)


def gate_weights(logits, routes, experts):
    picks = (routes[:, :, None] == jnp.arange(experts, dtype=jnp.int32)[None, None, :]).astype(f32)
    chosen = jnp.sum(picks * logits[:, None, :], -1)
    return (jax.nn.softmax(chosen, -1), picks)


def router_back(gates, picks, picked, stream_grad):
    gate_grad = jnp.sum(picked * stream_grad[None], 2).T
    chosen_grad = gates * (gate_grad - jnp.sum(gates * gate_grad, 1, keepdims=True))
    return jnp.sum(picks * chosen_grad[:, :, None], 1)


def send_rows(place, values, experts):
    packed = mm_tn(place[0] + place[1], values).astype(bf16)
    return packed.reshape(experts, -1, values.shape[1])


def send_grads(place, gates, grad_in, experts):
    scaled = (gates.T[:, :, None] * grad_in[None]).astype(bf16)
    packed = (mm_tn(place[0], scaled[0]) + mm_tn(place[1], scaled[1])).astype(bf16)
    return packed.reshape(experts, -1, grad_in.shape[1])


def take_back(place, returned):
    flat_back = returned.reshape(place.shape[2], -1)
    return jnp.stack([mm(place[0], flat_back), mm(place[1], flat_back)])


def exchange(packed):
    return lax.all_to_all(packed, "expert", split_axis=0, concat_axis=0, tiled=True)


def ring_step(block, experts):
    return lax.ppermute(block, "expert", [(i, (i + 1) % experts) for i in range(experts)])


def ring_gather(block, experts):
    blocks = [block]
    for _ in range(experts - 1):
        blocks.append(ring_step(blocks[-1], experts))
    return blocks


def norm_back(stream, inverse, gain, grad_in):
    scaled = grad_in * gain
    return inverse * scaled - stream * inverse**3 * jnp.mean(scaled * stream, -1, keepdims=True)


def group_scores(queries, keys):
    heads = queries.shape[1] // HEAD
    return (
        jnp.einsum(
            "qhd,khd->hqk",
            queries.reshape(-1, heads, HEAD),
            keys.reshape(-1, heads, HEAD),
            preferred_element_type=f32,
        )
        * score_scale
    )


def attend(queries, keys, values, key_mask):
    heads = queries.shape[1] // HEAD
    scores = jnp.where(key_mask[None], group_scores(queries, keys), masked_score)
    row_peak = jnp.max(scores, -1, keepdims=True)
    exponent = jnp.exp(scores - row_peak)
    row_total = jnp.sum(exponent, -1, keepdims=True)
    attended = jnp.einsum(
        "hqk,khd->qhd",
        (exponent / row_total).astype(bf16),
        values.reshape(-1, heads, HEAD),
        preferred_element_type=f32,
    ).reshape(queries.shape)
    return (attended.astype(bf16), row_peak + jnp.log(row_total))


def attend_back(queries, keys, values, key_mask, log_total, attended, attended_grad):
    heads = queries.shape[1] // HEAD
    scores = jnp.where(key_mask[None], group_scores(queries, keys), masked_score)
    probs = jnp.exp(scores - log_total)
    grad_heads = attended_grad.reshape(-1, heads, HEAD)
    value_heads = values.reshape(-1, heads, HEAD)
    prob_grad = jnp.einsum("qhd,khd->hqk", grad_heads, value_heads, preferred_element_type=f32)
    row_delta = jnp.sum(
        grad_heads.astype(f32) * attended.reshape(-1, heads, HEAD).astype(f32), -1
    ).T[:, :, None]
    score_grad = (probs * (prob_grad - row_delta)).astype(bf16)
    query_grad = jnp.einsum(
        "hqk,khd->qhd", score_grad, keys.reshape(-1, heads, HEAD), preferred_element_type=f32
    ).reshape(queries.shape)
    key_grad = jnp.einsum(
        "hqk,qhd->khd", score_grad, queries.reshape(-1, heads, HEAD), preferred_element_type=f32
    ).reshape(keys.shape)
    value_grad = jnp.einsum(
        "hqk,qhd->khd", probs.astype(bf16), grad_heads, preferred_element_type=f32
    ).reshape(values.shape)
    return (query_grad * score_scale, key_grad * score_scale, value_grad)


def gather_dp(weight):
    return lax.all_gather(weight[0], "dp", axis=0, tiled=True)


def reduce_dp(part):
    return lax.psum_scatter(part, "dp", scatter_dimension=0, tiled=True)


def body(
    tokens,
    cotangent,
    gain_one,
    gain_two,
    kv_weight,
    att_router,
    ffn_router,
    query_weight,
    output_weight,
    gate_weight,
    up_weight,
    down_weight,
    leaf_parent,
    att_route,
    ffn_route,
):
    row_count, model_width = tokens.shape
    experts = att_router.shape[1]
    capacity = row_count * 5 // (2 * experts)
    head_width = HEADS * HEAD
    width = head_width // experts
    shard_rows = kv_weight.shape[0]
    parents = leaf_parent[0]
    own = lax.axis_index("expert")
    backs = [(own - k) % experts for k in range(experts)]

    small = jnp.concatenate(
        [
            att_router,
            ffn_router,
            gain_one[:, None],
            gain_two[:, None],
            jnp.zeros((shard_rows, PAD - 2 * experts - 2), bf16),
        ],
        1,
    )
    bundle = jnp.concatenate(
        [
            kv_weight.reshape(shard_rows, 2, experts, width)
            .transpose(2, 0, 1, 3)
            .reshape(experts, shard_rows, 2 * width),
            jnp.broadcast_to(small[None], (experts, shard_rows, PAD)),
        ],
        2,
    )
    bundle = exchange(bundle).reshape(experts * shard_rows, 2 * width + PAD)
    bundle = lax.all_gather(bundle, "dp", axis=0, tiled=True)
    kv_all = bundle[:, : 2 * width]
    att_all = bundle[:, 2 * width : 2 * width + experts]
    ffn_all = bundle[:, 2 * width + experts : 2 * width + 2 * experts]
    gain_first = bundle[:, 2 * width + 2 * experts].astype(f32)
    gain_second = bundle[:, 2 * width + 2 * experts + 1].astype(f32)

    query_all = gather_dp(query_weight)
    output_all = gather_dp(output_weight)
    gate_all = gather_dp(gate_weight)
    up_all = gather_dp(up_weight)
    down_all = gather_dp(down_weight)

    tagged = jnp.concatenate(
        [tokens, att_route.astype(bf16), jnp.zeros((row_count, PAD - 2), bf16)], 1
    )
    tree = jnp.zeros((experts * row_count, model_width + PAD), bf16)
    for k, block in enumerate(ring_gather(tagged, experts)):
        tree = lax.dynamic_update_slice_in_dim(tree, block, backs[k] * row_count, 0)
    tree_tokens = tree[:, :model_width].astype(f32)
    tree_routes = tree[:, model_width : model_width + 2].astype(jnp.int32)
    tree_index = jnp.arange(experts * row_count, dtype=jnp.int32)
    tree_segment, tree_position = layout(tree_index)
    tree_cos, tree_sin = rotary_tables(tree_position)
    tree_inverse = lax.rsqrt(jnp.mean(tree_tokens * tree_tokens, -1, keepdims=True) + norm_eps)
    normed_tree = (tree_tokens * tree_inverse * gain_first).astype(bf16)
    inputs = tokens.astype(f32)
    own_start = own * row_count
    inverse_one = lax.dynamic_slice_in_dim(tree_inverse, own_start, row_count, 0)
    normed_one = lax.dynamic_slice_in_dim(normed_tree, own_start, row_count, 0)

    kv_raw = mm(normed_tree, kv_all)
    kv_own = jnp.concatenate(
        [rotate(kv_raw[:, :width], tree_cos, tree_sin), kv_raw[:, width:]], 1
    ).astype(bf16)
    kv_blocks = ring_gather(kv_own, experts)

    named = jnp.any(tree_routes == own, 1).reshape(experts, row_count)
    rank = earlier_count(named.T).T
    slots = jnp.arange(capacity, dtype=jnp.int32)
    chosen = named[:, None, :] & (rank[:, None, :] == slots[None, :, None])
    chosen_index = tree_index.reshape(experts, 1, row_count)
    query_index = jnp.sum(jnp.where(chosen, chosen_index, 0), 2).reshape(-1)
    chosen = chosen.astype(bf16)
    query_rows = (
        jnp.einsum(
            "ksr,krd->ksd",
            chosen,
            normed_tree.reshape(experts, row_count, model_width),
            preferred_element_type=f32,
        )
        .astype(bf16)
        .reshape(-1, model_width)
    )
    query_segment, query_position = layout(query_index)
    query_cos, query_sin = rotary_tables(query_position)
    key_mask = visible(query_index, query_segment, tree_index, tree_segment, parents)
    queries = rotate(mm(query_rows, query_all), query_cos, query_sin).astype(bf16)

    attended = jnp.zeros(queries.shape, bf16)
    saved = []
    for k in range(experts):
        start = backs[k] * width
        group_queries = lax.dynamic_slice_in_dim(queries, start, width, 1)
        keys, values = kv_blocks[k][:, :width], kv_blocks[k][:, width:]
        group_attended, log_total = attend(group_queries, keys, values, key_mask)
        attended = lax.dynamic_update_slice_in_dim(attended, group_attended, start, 1)
        saved.append((group_queries, keys, values, key_mask, log_total, group_attended))
    att_branch = mm(attended, output_all).astype(bf16)
    att_back = exchange(att_branch.reshape(experts, capacity, -1))

    att_logits = mm(normed_one, att_all)
    att_gate, att_picks = gate_weights(att_logits, att_route, experts)
    att_place = placement_of(att_route, capacity, experts)
    att_picked = take_back(att_place, att_back)
    mixed_stream = inputs + jnp.sum(att_gate.T[:, :, None] * att_picked, 0)
    inverse_two = lax.rsqrt(jnp.mean(mixed_stream * mixed_stream, -1, keepdims=True) + norm_eps)
    normed_two = (mixed_stream * inverse_two * gain_second).astype(bf16)
    ffn_logits = mm(normed_two, ffn_all)
    ffn_gate, ffn_picks = gate_weights(ffn_logits, ffn_route, experts)
    ffn_place = placement_of(ffn_route, capacity, experts)
    ffn_rows = exchange(send_rows(ffn_place, normed_two, experts)).reshape(-1, model_width)
    grad_out = cotangent.astype(f32)
    ffn_grad_rows = exchange(send_grads(ffn_place, ffn_gate, grad_out, experts)).reshape(
        -1, model_width
    )
    gate_value = mm(ffn_rows, gate_all)
    up_value = mm(ffn_rows, up_all)
    sigmoid_gate = jax.nn.sigmoid(gate_value)
    hidden = (gate_value * sigmoid_gate * up_value).astype(bf16)
    down_part = mm_tn(hidden, ffn_grad_rows).astype(bf16)
    down_sum = reduce_dp(down_part)
    ffn_branch = mm(hidden, down_all).astype(bf16)
    ffn_picked = take_back(ffn_place, exchange(ffn_branch.reshape(experts, capacity, -1)))
    result = mixed_stream + jnp.sum(ffn_gate.T[:, :, None] * ffn_picked, 0)
    ffn_logit_grad = router_back(ffn_gate, ffn_picks, ffn_picked, grad_out)
    hidden_grad = mm_nt(ffn_grad_rows, down_all)
    gate_grad = (
        hidden_grad * up_value * sigmoid_gate * (1.0 + gate_value * (1.0 - sigmoid_gate))
    ).astype(bf16)
    up_grad = (hidden_grad * gate_value * sigmoid_gate).astype(bf16)
    ffn_rows_grad = (mm_nt(gate_grad, gate_all) + mm_nt(up_grad, up_all)).astype(bf16)
    ffn_rows_back = exchange(ffn_rows_grad.reshape(experts, capacity, -1)).reshape(
        experts * capacity, -1
    )
    gate_sum = reduce_dp(mm_tn(ffn_rows, gate_grad).astype(bf16))
    up_sum = reduce_dp(mm_tn(ffn_rows, up_grad).astype(bf16))
    normed_two_grad = mm(ffn_place[0] + ffn_place[1], ffn_rows_back) + jnp.dot(
        ffn_logit_grad, ffn_all.astype(f32).T, precision=highest
    )
    gain_two_part = jnp.sum(normed_two_grad * mixed_stream * inverse_two, 0)
    mixed_grad = grad_out + norm_back(mixed_stream, inverse_two, gain_second, normed_two_grad)

    att_logit_grad = router_back(att_gate, att_picks, att_picked, mixed_grad)
    att_grad_rows = exchange(send_grads(att_place, att_gate, mixed_grad, experts)).reshape(
        -1, model_width
    )
    attended_grad = mm_nt(att_grad_rows, output_all).astype(bf16)
    output_sum = reduce_dp(mm_tn(attended, att_grad_rows).astype(bf16))
    query_grad = jnp.zeros(queries.shape, f32)
    kv_grad = None
    for step in range(1, experts + 1):
        k = step % experts
        start = backs[k] * width
        group_grad = lax.dynamic_slice_in_dim(attended_grad, start, width, 1)
        group_query_grad, key_grad, value_grad = attend_back(*saved[k], group_grad)
        query_grad = lax.dynamic_update_slice_in_dim(query_grad, group_query_grad, start, 1)
        part = jnp.concatenate([key_grad, value_grad], 1)
        if kv_grad is not None:
            part = part + kv_grad.astype(f32)
        kv_grad = part if k == 0 else ring_step(part.astype(bf16), experts)
    query_raw_grad = rotate_back(query_grad, query_cos, query_sin).astype(bf16)
    query_sum = reduce_dp(mm_tn(query_rows, query_raw_grad).astype(bf16))
    att_rows_grad = mm_nt(query_raw_grad, query_all).astype(bf16)
    kv_raw_grad = jnp.concatenate(
        [rotate_back(kv_grad[:, :width], tree_cos, tree_sin), kv_grad[:, width:]], 1
    ).astype(bf16)
    tree_grad = mm_nt(kv_raw_grad, kv_all).reshape(experts, row_count, -1) + jnp.einsum(
        "ksr,ksd->krd",
        chosen,
        att_rows_grad.reshape(experts, capacity, -1),
        preferred_element_type=f32,
    )
    normed_one_grad = None
    for step in range(1, experts + 1):
        k = step % experts
        part = lax.dynamic_index_in_dim(tree_grad, backs[k], 0, keepdims=False)
        if normed_one_grad is not None:
            part = part + normed_one_grad.astype(f32)
        normed_one_grad = part if k == 0 else ring_step(part.astype(bf16), experts)
    normed_one_grad = normed_one_grad + jnp.dot(
        att_logit_grad, att_all.astype(f32).T, precision=highest
    )
    gain_one_part = jnp.sum(normed_one_grad * inputs * inverse_one, 0)
    input_grad = mixed_grad + norm_back(inputs, inverse_one, gain_first, normed_one_grad)
    att_router_part = lax.dot_general(
        normed_one.astype(f32), att_logit_grad, (((0,), (0,)), ((), ())), precision=highest
    )
    ffn_router_part = lax.dot_general(
        normed_two.astype(f32), ffn_logit_grad, (((0,), (0,)), ((), ())), precision=highest
    )
    shared_part = jnp.concatenate(
        [
            mm_tn(normed_tree, kv_raw_grad).astype(bf16),
            att_router_part.astype(bf16),
            ffn_router_part.astype(bf16),
            gain_one_part[:, None].astype(bf16),
            gain_two_part[:, None].astype(bf16),
            jnp.zeros((model_width, PAD - 2 * experts - 2), bf16),
        ],
        1,
    )
    shared_sum = exchange(reduce_dp(shared_part).reshape(experts, shard_rows, -1)).astype(f32)
    kv_sum = (
        shared_sum[:, :, : 2 * width]
        .reshape(experts, shard_rows, 2, width)
        .transpose(1, 2, 0, 3)
        .reshape(shard_rows, 2 * head_width)
    )
    small_sum = jnp.sum(shared_sum[:, :, 2 * width :], 0)
    return (
        result.astype(bf16),
        input_grad,
        small_sum[:, 2 * experts],
        small_sum[:, 2 * experts + 1],
        kv_sum,
        small_sum[:, :experts],
        small_sum[:, experts : 2 * experts],
        query_sum.astype(f32)[None],
        output_sum.astype(f32)[None],
        gate_sum.astype(f32)[None],
        up_sum.astype(f32)[None],
        down_sum.astype(f32)[None],
    )

def solution(mesh):
    in_specs = (
        P(("dp", "expert"), None),
        P(("dp", "expert"), None),
        P(("dp", "expert")),
        P(("dp", "expert")),
        P(("dp", "expert"), None),
        P(("dp", "expert"), None),
        P(("dp", "expert"), None),
        P("expert", "dp", None),
        P("expert", "dp", None),
        P("expert", "dp", None),
        P("expert", "dp", None),
        P("expert", "dp", None),
        P("dp", None),
        P(("dp", "expert"), None),
        P(("dp", "expert"), None),
    )
    out_specs = (
        P(("dp", "expert"), None),
        P(("dp", "expert"), None),
        P(("dp", "expert")),
        P(("dp", "expert")),
        P(("dp", "expert"), None),
        P(("dp", "expert"), None),
        P(("dp", "expert"), None),
        P("expert", "dp", None),
        P("expert", "dp", None),
        P("expert", "dp", None),
        P("expert", "dp", None),
        P("expert", "dp", None),
    )
    return jax.shard_map(body, mesh=mesh, in_specs=in_specs, out_specs=out_specs, check_vma=False)
```

time: 2940 us -> 1840 us (0.63)
  waiting for transfers between devices: 1840 us -> 1110 us
  blocking collectives: 381 us -> 22 us
  local copies, waits for them, and re-layouts: 59.4 us -> 125 us
  matrix products: 480 us -> 443 us
  other arithmetic: 119 us -> 88.4 us
    reduce_scatter x7 -> x6, waiting for transfers between devices: 1240 us -> 519 us  [reduce_dp(): return lax.psum_scatter(part, 'dp', scatter_dimension=0, tiled=True)]
    ppermute x0 -> x12, waiting for transfers between devices: none -> 320 us  [ring_step(): lax.ppermute(block, 'expert', [(i, (i + 1) % experts) for i in range(expe...]
    all_gather x3 -> x0, blocking collectives: 298 us -> none  [the longest x1 117 us: body(): route_group = lax.all_gather(att_route, 'expert', axis=0, tiled=True)]
    unnamed x18 -> x12, waiting for transfers between devices: 264 us -> 2.56 us
    all_gather x7 -> x6, waiting for transfers between devices: 117 us -> 0.05 us  [the longest x5 0.03 us: gather_dp(): return lax.all_gather(weight[0], 'dp', axis=0, tiled=True)]
    unnamed x2 -> x0, blocking collectives: 83.7 us -> none
    all_to_all x8 -> x7, waiting for transfers between devices: 216 us -> 267 us  [exchange(): lax.all_to_all(packed, 'expert', split_axis=0, concat_axis=0, tiled=True)]
    dot_general x36 -> x63, matrix products: 475 us -> 443 us  [the longest x11 115 us: mm_tn(): lax.dot_general(left, right, (((0,), (0,)), ((), ())), preferred_element_...]
  transfers between devices with their start and end apart: 24 -> 31, of which waited for: 16 -> 23; matrix products, arithmetic and copies ran while one was open for 16% -> 24% of each run, Pallas kernels for 0% -> 0%
where the time goes in v1:
time: 1840 us
  waiting for transfers between devices  1110 us (60%)
  matrix products  443 us (24%)
  local copies, waits for them, and re-layouts  125 us (7%)
  other arithmetic  88.4 us (5%)
  starting transfers between devices  32.3 us (2%)
  blocking collectives  22 us (1%)
    reduce_scatter x6, waiting for transfers between devices, reduce_dp(): return lax.psum_scatter(part, 'dp', scatter_dimension=0, tiled=True)  519 us
    ppermute x12, waiting for transfers between devices, ring_step(): lax.ppermute(block, 'expert', [(i, (i + 1) % experts) for i in range(expe...  320 us
    all_to_all x7, waiting for transfers between devices, exchange(): lax.all_to_all(packed, 'expert', split_axis=0, concat_axis=0, tiled=True)  267 us
    dot_general x11, matrix products, mm_tn(): lax.dot_general(left, right, (((0,), (0,)), ((), ())), preferred_element_...  115 us
    dot_general x16, matrix products, mm(): return jnp.dot(left, right, preferred_element_type=f32)  113 us
    dot_general x6, matrix products, mm_nt(): lax.dot_general(left, right, (((1,), (1,)), ((), ())), preferred_element_...  86.9 us
    unnamed x344, local copies, waits for them, and re-layouts  42.8 us
  transfers between devices with their start and end apart: 31, of which 23 were waited for; matrix products, arithmetic and copies ran while one was open for 24% of the time, Pallas kernels for 0%

profile of v1, /device:TPU:0, one launch (start us, length us, event | category | flops | bytes accessed | tf_op | source)
XLA Modules:
  0.0 1836.4 jit_solution(14085059543342084127)
XLA Ops:
  12.7 22.0 %all_to_all.40 = bf16[4,64,1152]{2,1,0:T(8,128)(2,1)S(1)} all-to-all(bf16[4,64,1152]{2,1,0:T(8,128)(2,1)S(1)} %pad_maximum_fusion.10), channel_id=1, replica_groups=mesh['dp'=8,'expert'=4] {'expert'}, dimensions={0} | all-to-all | bytes 1179648 | tf_op jit(solution)/shard_map/all_to_all | solution.py:138
  41.9 27.0 %collective-permute-done = bf16[256,2176]{1,0:T(8,128)(2,1)} collective-permute-done((bf16[256,2176]{1,0:T(8,128)(2,1)S(1)}, bf16[256,2176]{1,0:T(8,128)(2,1)}, u32[]{:S(2)}, u32[]{:S(2)}) %collective-permute-start) | collective-permute-done | bytes 1114144 | tf_op jit(solution)/shard_map/ppermute | solution.py:142
  71.9 23.7 %collective-permute-done.1 = bf16[256,2176]{1,0:T(8,128)(2,1)} collective-permute-done((bf16[256,2176]{1,0:T(8,128)(2,1)}, bf16[256,2176]{1,0:T(8,128)(2,1)}, u32[]{:S(2)}, u32[]{:S(2)}) %collective-permute-start.1) | collective-permute-done | bytes 1114144 | tf_op jit(solution)/shard_map/ppermute | solution.py:142
  99.2 22.5 %collective-permute-done.2 = bf16[256,2176]{1,0:T(8,128)(2,1)S(1)} collective-permute-done((bf16[256,2176]{1,0:T(8,128)(2,1)}, bf16[256,2176]{1,0:T(8,128)(2,1)S(1)}, u32[]{:S(2)}, u32[]{:S(2)}) %collective-permute-start.2) | collective-permute-done | bytes 1114144 | tf_op jit(solution)/shard_map/ppermute | solution.py:142
  149.8 44.5 %collective-permute-done.3 = bf16[1024,1024]{0,1:T(8,128)(2,1)} collective-permute-done((bf16[1024,1024]{0,1:T(8,128)(2,1)}, bf16[1024,1024]{0,1:T(8,128)(2,1)}, u32[]{:S(2)}, u32[]{:S(2)}) %collective-permute-start.3) | collective-permute-done | bytes 2097184 | tf_op jit(solution)/shard_map/ppermute | solution.py:142
  205.6 34.2 %collective-permute-done.4 = bf16[1024,1024]{0,1:T(8,128)(2,1)} collective-permute-done((bf16[1024,1024]{0,1:T(8,128)(2,1)}, bf16[1024,1024]{0,1:T(8,128)(2,1)}, u32[]{:S(2)}, u32[]{:S(2)}) %collective-permute-start.4) | collective-permute-done | bytes 2097184 | tf_op jit(solution)/shard_map/ppermute | solution.py:142
  293.7 17.2 fusion.15
  370.7 46.8 %all-to-all-done.1 = bf16[4,160,2048]{2,1,0:T(8,128)(2,1)S(1)} async-done(((bf16[4,160,2048]{2,1,0:T(8,128)(2,1)}), bf16[4,160,2048]{2,1,0:T(8,128)(2,1)S(1)}, u32[]{:S(2)}, u32[]{:S(2)}) %all-to-all-start.1) | async-done | bytes 2621472 | tf_op jit(solution)/shard_map/all_to_all | solution.py:138
  436.5 56.5 %all-to-all-done.4 = bf16[4,160,2048]{2,1,0:T(8,128)(2,1)} async-done(((bf16[4,160,2048]{2,1,0:T(8,128)(2,1)}), bf16[4,160,2048]{2,1,0:T(8,128)(2,1)}, u32[]{:S(2)}, u32[]{:S(2)}) %all-to-all-start.4) | async-done | bytes 2621472 | tf_op jit(solution)/shard_map/all_to_all | solution.py:138
  497.1 23.0 %fusion = f32[640,5632]{1,0:T(8,128)} fusion(bf16[640,2048]{1,0:T(8,128)(2,1)} %bitcast.61, bf16[1,5632,2048]{2,1,0:T(8,128)(2,1)} %all-gather.22.cloned.1.call-done), kind=kOutput, calls=%fused_computation | convolution fusion | flops 14763950080 | bytes 40108032 | tf_op jit(solution)/shard_map/dot_general | solution.py:90
  520.2 35.9 %all-to-all-done.2 = bf16[4,160,2048]{2,1,0:T(8,128)(2,1)S(1)} async-done(((bf16[4,160,2048]{2,1,0:T(8,128)(2,1)}), bf16[4,160,2048]{2,1,0:T(8,128)(2,1)S(1)}, u32[]{:S(2)}, u32[]{:S(2)}) %all-to-all-start.2) | async-done | bytes 2621472 | tf_op jit(solution)/shard_map/all_to_all | solution.py:138
  556.0 23.4 %fusion.6 = f32[640,5632]{1,0:T(8,128)} fusion(bf16[640,2048]{1,0:T(8,128)(2,1)S(1)} %bitcast.384, bf16[1,2048,5632]{2,1,0:T(8,128)(2,1)} %all-gather.20.cloned.1.call-done), kind=kOutput, calls=%fused_computation.6 | convolution fusion | flops 14763950080 | bytes 40108032 | tf_op jit(solution)/shard_map/dot_general | solution.py:82
  579.4 31.9 %multiply_convert_fusion.1 = (bf16[640,5632]{1,0:T(8,128)(2,1)}, bf16[640,5632]{1,0:T(8,128)(2,1)}, bf16[640,5632]{1,0:T(8,128)(2,1)}) fusion(f32[640,5632]{1,0:T(8,128)} %fusion, f32[640,5632]{1,0:T(8,128)} %fusion.6, bf16[640,2048]{1,0:T(8,128)(2,1)S(1)} %bitcast.385, bf16[1,2048,5632]{2,1,0:T(8,128)(2,1)} %all-gather.18.cloned.1.call-done), kind=kOutput, calls=%fused_computation.16 | convolution fusion | flops 14821621760 | bytes 76152832 | tf_op jit(solution)/shard_map/dot_general | solution.py:82
  611.3 21.2 %fusion.60 = bf16[640,2048]{1,0:T(8,128)(2,1)} fusion(bf16[640,5632]{1,0:T(8,128)(2,1)} %get-tuple-element.70, bf16[1,5632,2048]{2,1,0:T(8,128)(2,1)} %all-gather.22.cloned.1.call-done), kind=kOutput, calls=%fused_computation.104 | convolution fusion | flops 14765260800 | bytes 32899072 | tf_op jit(solution)/shard_map/dot_general | solution.py:82
  636.2 20.5 %fusion.4 = f32[640,2048]{1,0:T(8,128)S(1)} fusion(bf16[640,5632]{1,0:T(8,128)(2,1)} %get-tuple-element.71, bf16[1,2048,5632]{2,1,0:T(8,128)(2,1)} %all-gather.20.cloned.1.call-done), kind=kOutput, calls=%fused_computation.4 | convolution fusion | flops 14763950080 | bytes 35520512 | tf_op jit(solution)/shard_map/dot_general | solution.py:90
  656.6 21.3 %add_convert_fusion.1 = bf16[640,2048]{1,0:T(8,128)(2,1)} fusion(f32[640,2048]{1,0:T(8,128)S(1)} %fusion.4, bf16[640,5632]{1,0:T(8,128)(2,1)} %get-tuple-element.69, bf16[1,2048,5632]{2,1,0:T(8,128)(2,1)} %all-gather.18.cloned.1.call-done), kind=kOutput, calls=%fused_computation.66 | convolution fusion | flops 14766571520 | bytes 38141952 | tf_op jit(solution)/shard_map/dot_general | solution.py:90
  677.9 17.2 all-to-all-done.3
  707.3 51.6 %all-to-all-done.5 = bf16[4,160,2048]{2,1,0:T(8,128)(2,1)} async-done(((bf16[4,160,2048]{2,1,0:T(8,128)(2,1)}), bf16[4,160,2048]{2,1,0:T(8,128)(2,1)}, u32[]{:S(2)}, u32[]{:S(2)}) %all-to-all-start.5) | async-done | bytes 2621472 | tf_op jit(solution)/shard_map/all_to_all | solution.py:138
  773.9 58.7 %all-to-all-done.6 = bf16[4,160,2048]{2,1,0:T(8,128)(2,1)S(1)} async-done(((bf16[4,160,2048]{2,1,0:T(8,128)(2,1)}), bf16[4,160,2048]{2,1,0:T(8,128)(2,1)S(1)}, u32[]{:S(2)}, u32[]{:S(2)}) %all-to-all-start.6) | async-done | bytes 2621472 | tf_op jit(solution)/shard_map/all_to_all | solution.py:138
  918.7 30.0 %collective-permute-done.6 = bf16[1024,1024]{0,1:T(8,128)(2,1)} collective-permute-done((bf16[1024,1024]{0,1:T(8,128)(2,1)}, bf16[1024,1024]{0,1:T(8,128)(2,1)}, u32[]{:S(2)}, u32[]{:S(2)}) %collective-permute-start.6) | collective-permute-done | bytes 2097184 | tf_op jit(solution)/shard_map/ppermute | solution.py:142
  965.8 35.7 %collective-permute-done.7 = bf16[1024,1024]{0,1:T(8,128)(2,1)} collective-permute-done((bf16[1024,1024]{0,1:T(8,128)(2,1)}, bf16[1024,1024]{0,1:T(8,128)(2,1)}, u32[]{:S(2)}, u32[]{:S(2)}) %collective-permute-start.7) | collective-permute-done | bytes 2097184 | tf_op jit(solution)/shard_map/ppermute | solution.py:142
  1014.6 36.5 %collective-permute-done.8 = bf16[1024,1024]{0,1:T(8,128)(2,1)S(1)} collective-permute-done((bf16[1024,1024]{0,1:T(8,128)(2,1)S(1)}, bf16[1024,1024]{0,1:T(8,128)(2,1)S(1)}, u32[]{:S(2)}, u32[]{:S(2)}) %collective-permute-start.8) | collective-permute-done | bytes 2097184 | tf_op jit(solution)/shard_map/ppermute | solution.py:142
  1075.2 23.4 %collective-permute-done.9 = bf16[256,2048]{1,0:T(8,128)(2,1)S(1)} collective-permute-done((bf16[256,2048]{1,0:T(8,128)(2,1)S(1)}, bf16[256,2048]{1,0:T(8,128)(2,1)S(1)}, u32[]{:S(2)}, u32[]{:S(2)}) %collective-permute-start.9) | collective-permute-done | bytes 1048608 | tf_op jit(solution)/shard_map/ppermute | solution.py:142
  1104.5 18.8 %collective-permute-done.10 = bf16[256,2048]{1,0:T(8,128)(2,1)S(1)} collective-permute-done((bf16[256,2048]{1,0:T(8,128)(2,1)S(1)}, bf16[256,2048]{1,0:T(8,128)(2,1)S(1)}, u32[]{:S(2)}, u32[]{:S(2)}) %collective-permute-start.10) | collective-permute-done | bytes 1048608 | tf_op jit(solution)/shard_map/ppermute | solution.py:142
  1150.7 22.7 %concatenate.61 = bf16[2048,1152]{0,1:T(8,128)(2,1)} concatenate(bf16[2048,1024]{0,1:T(8,128)(2,1)} %convolution_convert_fusion.5, bf16[2048,4]{0,1:T(4,128)(2,1)S(1)} %convolution_convert_fusion.9, bf16[2048,4]{0,1:T(4,128)(2,1)S(1)} %convolution_convert_fusion.8, bf16[2048,1]{0,1:T(2,128)(2,1)S(1)} %convert_element_type.459, bf16[2048,1]{0,1:T(2,128)(2,1)S(1)} %convert_element_type.461, ...), dimensions={1} | concatenate | bytes 9437184 | tf_op jit(solution)/shard_map/concatenate | solution.py:424
  1196.3 25.4 %convolution_convert_fusion = bf16[5632,2048]{1,0:T(8,128)(2,1)} fusion(bf16[640,5632]{1,0:T(8,128)(2,1)} %get-tuple-element.70, bf16[640,2048]{1,0:T(8,128)(2,1)} %bitcast.61), kind=kOutput, calls=%fused_computation.12 | convolution fusion | flops 14775484416 | bytes 32899072 | tf_op jit(solution)/shard_map/dot_general | solution.py:86
  1222.0 25.6 %convolution_convert_fusion.1 = bf16[2048,5632]{1,0:T(8,128)(2,1)} fusion(bf16[640,2048]{1,0:T(8,128)(2,1)} %bitcast.386, bf16[640,5632]{1,0:T(8,128)(2,1)} %get-tuple-element.71), kind=kOutput, calls=%fused_computation.13 | convolution fusion | flops 14775484416 | bytes 32899072 | tf_op jit(solution)/shard_map/dot_general | solution.py:86
  1247.9 25.5 %convolution_convert_fusion.2 = bf16[2048,5632]{1,0:T(8,128)(2,1)} fusion(bf16[640,2048]{1,0:T(8,128)(2,1)} %bitcast.387, bf16[640,5632]{1,0:T(8,128)(2,1)} %get-tuple-element.69), kind=kOutput, calls=%fused_computation.14 | convolution fusion | flops 14775484416 | bytes 32899072 | tf_op jit(solution)/shard_map/dot_general | solution.py:86
  1302.4 72.2 %reduce-scatter.11.cloned.1.call-done = bf16[256,2048]{1,0:T(8,128)(2,1)} async-done(((bf16[2048,2048]{1,0:T(8,128)(2,1)}), bf16[256,2048]{1,0:T(8,128)(2,1)}) %reduce-scatter.11.cloned.1.call-update) | async-done | bytes 1048592 | tf_op jit(solution)/shard_map/reduce_scatter | solution.py:213
  1382.9 141.5 %reduce-scatter.17.cloned.1.call-done = bf16[704,2048]{1,0:T(8,128)(2,1)} async-done(((bf16[5632,2048]{1,0:T(8,128)(2,1)}), bf16[704,2048]{1,0:T(8,128)(2,1)}) %reduce-scatter.17.cloned.1.call-update) | async-done | bytes 2883600 | tf_op jit(solution)/shard_map/reduce_scatter | solution.py:213
  1529.5 144.9 %reduce-scatter.15.cloned.1.call-done = bf16[256,5632]{1,0:T(8,128)(2,1)} async-done(((bf16[2048,5632]{1,0:T(8,128)(2,1)}), bf16[256,5632]{1,0:T(8,128)(2,1)}) %reduce-scatter.15.cloned.1.call-update) | async-done | bytes 2883600 | tf_op jit(solution)/shard_map/reduce_scatter | solution.py:213
  1679.5 144.8 %reduce-scatter.13.cloned.1.call-done = bf16[256,5632]{1,0:T(8,128)(2,1)} async-done(((bf16[2048,5632]{1,0:T(8,128)(2,1)}), bf16[256,5632]{1,0:T(8,128)(2,1)}) %reduce-scatter.13.cloned.1.call-update) | async-done | bytes 2883600 | tf_op jit(solution)/shard_map/reduce_scatter | solution.py:213
  (607 shorter events, 472.8 us)
Async XLA Ops:
  7.2 117.7 %all-gather.12.cloned.1.call-start = ((), (), s32[]{:S(2)}) async-start(), calls=%async_computation.14 | async-start | bytes 5308416 | tf_op jit(solution)/shard_map/all_gather | solution.py:263
  35.9 207.7 %all-gather.14.cloned.1.call-start = ((), (), s32[]{:S(2)}) async-start(), calls=%async_computation.21 | async-start | bytes 9437184 | tf_op jit(solution)/shard_map/all_gather | solution.py:209
  36.6 314.1 %all-gather.16.cloned.1.call-start = ((), (), s32[]{:S(2)}) async-start(), calls=%async_computation.22 | async-start | bytes 9437184 | tf_op jit(solution)/shard_map/all_gather | solution.py:209
  37.4 459.8 %all-gather.22.cloned.1.call-start = ((), (), s32[]{:S(2)}) async-start(), calls=%async_computation.25 | async-start | bytes 25952256 | tf_op jit(solution)/shard_map/all_gather | solution.py:209
  37.9 518.1 %all-gather.20.cloned.1.call-start = ((), (), s32[]{:S(2)}) async-start(), calls=%async_computation.24 | async-start | bytes 25952256 | tf_op jit(solution)/shard_map/all_gather | solution.py:209
  38.5 540.9 %all-gather.18.cloned.1.call-start = ((), (), s32[]{:S(2)}) async-start(), calls=%async_computation.23 | async-start | bytes 25952256 | tf_op jit(solution)/shard_map/all_gather | solution.py:209
  41.4 27.5 %collective-permute-start = (bf16[256,2176]{1,0:T(8,128)(2,1)S(1)}, bf16[256,2176]{1,0:T(8,128)(2,1)}, u32[]{:S(2)}, u32[]{:S(2)}) collective-permute-start(bf16[256,2176]{1,0:T(8,128)(2,1)S(1)} %concatenate.48), channel_id=1, source_target_pairs={{0,1},{1,2},{2,3},{3,0},{4,5},{5,6},{6,7},{7,4},{8,9},{9,10},{10,1... | collective-permute-start | bytes 3342344 | tf_op jit(solution)/shard_map/ppermute | solution.py:142
  68.9 26.8 %collective-permute-start.1 = (bf16[256,2176]{1,0:T(8,128)(2,1)}, bf16[256,2176]{1,0:T(8,128)(2,1)}, u32[]{:S(2)}, u32[]{:S(2)}) collective-permute-start(bf16[256,2176]{1,0:T(8,128)(2,1)} %collective-permute-done), channel_id=1, source_target_pairs={{0,1},{1,2},{2,3},{3,0},{4,5},{5,6},{6,7},{7,4},{8,9},{9,10},{10,1... | collective-permute-start | bytes 3342344 | tf_op jit(solution)/shard_map/ppermute | solution.py:142
  95.7 26.0 %collective-permute-start.2 = (bf16[256,2176]{1,0:T(8,128)(2,1)}, bf16[256,2176]{1,0:T(8,128)(2,1)S(1)}, u32[]{:S(2)}, u32[]{:S(2)}) collective-permute-start(bf16[256,2176]{1,0:T(8,128)(2,1)} %collective-permute-done.1), channel_id=1, source_target_pairs={{0,1},{1,2},{2,3},{3,0},{4,5},{5,6},{6,7},{7,4},{8,9},{9,10},{10,1... | collective-permute-start | bytes 3342344 | tf_op jit(solution)/shard_map/ppermute | solution.py:142
  147.9 46.4 %collective-permute-start.3 = (bf16[1024,1024]{0,1:T(8,128)(2,1)}, bf16[1024,1024]{0,1:T(8,128)(2,1)}, u32[]{:S(2)}, u32[]{:S(2)}) collective-permute-start(bf16[1024,1024]{0,1:T(8,128)(2,1)} %pad_maximum_fusion.3), channel_id=1, source_target_pairs={{0,1},{1,2},{2,3},{3,0},{4,5},{5,6},{6,7},{7,4},{8,9},{9,10},{10,1... | collective-permute-start | bytes 6291464 | tf_op jit(solution)/shard_map/ppermute | solution.py:142
  194.3 45.5 %collective-permute-start.4 = (bf16[1024,1024]{0,1:T(8,128)(2,1)}, bf16[1024,1024]{0,1:T(8,128)(2,1)}, u32[]{:S(2)}, u32[]{:S(2)}) collective-permute-start(bf16[1024,1024]{0,1:T(8,128)(2,1)} %collective-permute-done.3), channel_id=1, source_target_pairs={{0,1},{1,2},{2,3},{3,0},{4,5},{5,6},{6,7},{7,4},{8,9},{9,10},{10,1... | collective-permute-start | bytes 6291464 | tf_op jit(solution)/shard_map/ppermute | solution.py:142
  197.1 147.7 %copy-start.31 = (pred[640,1024]{1,0:T(8,128)(4,1)}, pred[640,1024]{1,0:T(8,128)(4,1)S(1)}, u32[]{:S(2)}) copy-start(pred[640,1024]{1,0:T(8,128)(4,1)S(1)} %fusion.71) | copy-start | bytes 1966084
  239.8 45.0 %collective-permute-start.5 = (bf16[1024,1024]{0,1:T(8,128)(2,1)}, bf16[1024,1024]{0,1:T(8,128)(2,1)}, u32[]{:S(2)}, u32[]{:S(2)}) collective-permute-start(bf16[1024,1024]{0,1:T(8,128)(2,1)} %collective-permute-done.4), channel_id=1, source_target_pairs={{0,1},{1,2},{2,3},{3,0},{4,5},{5,6},{6,7},{7,4},{8,9},{9,10},{10,1... | collective-permute-start | bytes 6291464 | tf_op jit(solution)/shard_map/ppermute | solution.py:142
  360.6 56.9 %all-to-all-start.1 = ((bf16[4,160,2048]{2,1,0:T(8,128)(2,1)}), bf16[4,160,2048]{2,1,0:T(8,128)(2,1)S(1)}, u32[]{:S(2)}, u32[]{:S(2)}) async-start(bf16[4,160,2048]{2,1,0:T(8,128)(2,1)} %bitcast.393), calls=%async_computation.1 | async-start | bytes 5242880 | tf_op jit(solution)/shard_map/all_to_all | solution.py:138
  429.3 63.8 %all-to-all-start.4 = ((bf16[4,160,2048]{2,1,0:T(8,128)(2,1)}), bf16[4,160,2048]{2,1,0:T(8,128)(2,1)}, u32[]{:S(2)}, u32[]{:S(2)}) async-start(bf16[4,160,2048]{2,1,0:T(8,128)(2,1)} %bitcast.350), calls=%async_computation.4 | async-start | bytes 5242880 | tf_op jit(solution)/shard_map/all_to_all | solution.py:138
  493.0 63.0 %all-to-all-start.2 = ((bf16[4,160,2048]{2,1,0:T(8,128)(2,1)}), bf16[4,160,2048]{2,1,0:T(8,128)(2,1)S(1)}, u32[]{:S(2)}, u32[]{:S(2)}) async-start(bf16[4,160,2048]{2,1,0:T(8,128)(2,1)} %bitcast.48), calls=%async_computation.2 | async-start | bytes 5242880 | tf_op jit(solution)/shard_map/all_to_all | solution.py:138
  632.5 62.6 %all-to-all-start.3 = ((bf16[4,160,2048]{2,1,0:T(8,128)(2,1)}), bf16[4,160,2048]{2,1,0:T(8,128)(2,1)S(1)}, u32[]{:S(2)}, u32[]{:S(2)}) async-start(bf16[4,160,2048]{2,1,0:T(8,128)(2,1)} %bitcast.394), calls=%async_computation.3 | async-start | bytes 5242880 | tf_op jit(solution)/shard_map/all_to_all | solution.py:138
  695.1 63.8 %all-to-all-start.5 = ((bf16[4,160,2048]{2,1,0:T(8,128)(2,1)}), bf16[4,160,2048]{2,1,0:T(8,128)(2,1)}, u32[]{:S(2)}, u32[]{:S(2)}) async-start(bf16[4,160,2048]{2,1,0:T(8,128)(2,1)} %bitcast.392), calls=%async_computation.5 | async-start | bytes 5242880 | tf_op jit(solution)/shard_map/all_to_all | solution.py:138
  769.8 62.8 %all-to-all-start.6 = ((bf16[4,160,2048]{2,1,0:T(8,128)(2,1)}), bf16[4,160,2048]{2,1,0:T(8,128)(2,1)S(1)}, u32[]{:S(2)}, u32[]{:S(2)}) async-start(bf16[4,160,2048]{2,1,0:T(8,128)(2,1)} %bitcast.67), calls=%async_computation.6 | async-start | bytes 5242880 | tf_op jit(solution)/shard_map/all_to_all | solution.py:138
  773.6 505.0 %reduce-scatter.7.cloned.1.call-start = ((), (), s32[]{:S(2)}) async-start(), calls=%async_computation.15 | async-start | bytes 5308416 | tf_op jit(solution)/shard_map/reduce_scatter | solution.py:213
  899.8 49.0 %collective-permute-start.6 = (bf16[1024,1024]{0,1:T(8,128)(2,1)}, bf16[1024,1024]{0,1:T(8,128)(2,1)}, u32[]{:S(2)}, u32[]{:S(2)}) collective-permute-start(bf16[1024,1024]{0,1:T(8,128)(2,1)} %pad_maximum_fusion.4), channel_id=1, source_target_pairs={{0,1},{1,2},{2,3},{3,0},{4,5},{5,6},{6,7},{7,4},{8,9},{9,10},{10,1... | collective-permute-start | bytes 6291464 | tf_op jit(solution)/shard_map/ppermute | solution.py:142
  953.2 48.3 %collective-permute-start.7 = (bf16[1024,1024]{0,1:T(8,128)(2,1)}, bf16[1024,1024]{0,1:T(8,128)(2,1)}, u32[]{:S(2)}, u32[]{:S(2)}) collective-permute-start(bf16[1024,1024]{0,1:T(8,128)(2,1)} %fusion.50), channel_id=1, source_target_pairs={{0,1},{1,2},{2,3},{3,0},{4,5},{5,6},{6,7},{7,4},{8,9},{9,10},{10,1... | collective-permute-start | bytes 6291464 | tf_op jit(solution)/shard_map/ppermute | solution.py:142
  1004.2 47.0 %collective-permute-start.8 = (bf16[1024,1024]{0,1:T(8,128)(2,1)S(1)}, bf16[1024,1024]{0,1:T(8,128)(2,1)S(1)}, u32[]{:S(2)}, u32[]{:S(2)}) collective-permute-start(bf16[1024,1024]{0,1:T(8,128)(2,1)S(1)} %fusion.49), channel_id=1, source_target_pairs={{0,1},{1,2},{2,3},{3,0},{4,5},{5,6},{6,7},{7,4},{8,9},{9,10},{10,1... | collective-permute-start | bytes 6291464 | tf_op jit(solution)/shard_map/ppermute | solution.py:142
  1075.2 23.5 %collective-permute-start.9 = (bf16[256,2048]{1,0:T(8,128)(2,1)S(1)}, bf16[256,2048]{1,0:T(8,128)(2,1)S(1)}, u32[]{:S(2)}, u32[]{:S(2)}) collective-permute-start(bf16[256,2048]{1,0:T(8,128)(2,1)S(1)} %fusion.88), channel_id=1, source_target_pairs={{0,1},{1,2},{2,3},{3,0},{4,5},{5,6},{6,7},{7,4},{8,9},{9,10},{10,1... | collective-permute-start | bytes 3145736 | tf_op jit(solution)/shard_map/ppermute | solution.py:142
  1100.5 22.8 %collective-permute-start.10 = (bf16[256,2048]{1,0:T(8,128)(2,1)S(1)}, bf16[256,2048]{1,0:T(8,128)(2,1)S(1)}, u32[]{:S(2)}, u32[]{:S(2)}) collective-permute-start(bf16[256,2048]{1,0:T(8,128)(2,1)S(1)} %fusion.78), channel_id=1, source_target_pairs={{0,1},{1,2},{2,3},{3,0},{4,5},{5,6},{6,7},{7,4},{8,9},{9,10},{10,1... | collective-permute-start | bytes 3145736 | tf_op jit(solution)/shard_map/ppermute | solution.py:142
  1125.2 21.7 %collective-permute-start.11 = (bf16[256,2048]{1,0:T(8,128)(2,1)S(1)}, bf16[256,2048]{1,0:T(8,128)(2,1)S(1)}, u32[]{:S(2)}, u32[]{:S(2)}) collective-permute-start(bf16[256,2048]{1,0:T(8,128)(2,1)S(1)} %fusion.79), channel_id=1, source_target_pairs={{0,1},{1,2},{2,3},{3,0},{4,5},{5,6},{6,7},{7,4},{8,9},{9,10},{10,1... | collective-permute-start | bytes 3145736 | tf_op jit(solution)/shard_map/ppermute | solution.py:142
  1173.4 126.2 %reduce-scatter.9.cloned.1.call-start = ((), (), s32[]{:S(2)}) async-start(), calls=%async_computation.16 | async-start | bytes 9437184 | tf_op jit(solution)/shard_map/reduce_scatter | solution.py:213
  1184.7 189.9 %reduce-scatter.11.cloned.1.call-start = ((), (), s32[]{:S(2)}) async-start(), calls=%async_computation.17 | async-start | bytes 9437184 | tf_op jit(solution)/shard_map/reduce_scatter | solution.py:213
  1196.3 328.1 %reduce-scatter.17.cloned.1.call-start = ((), (), s32[]{:S(2)}) async-start(), calls=%async_computation.20 | async-start | bytes 25952256 | tf_op jit(solution)/shard_map/reduce_scatter | solution.py:213
  1221.8 452.6 %reduce-scatter.15.cloned.1.call-start = ((), (), s32[]{:S(2)}) async-start(), calls=%async_computation.19 | async-start | bytes 25952256 | tf_op jit(solution)/shard_map/reduce_scatter | solution.py:213
  1247.7 576.6 %reduce-scatter.13.cloned.1.call-start = ((), (), s32[]{:S(2)}) async-start(), calls=%async_computation.18 | async-start | bytes 25952256 | tf_op jit(solution)/shard_map/reduce_scatter | solution.py:213
  1280.8 96.6 %all-to-all-start.7 = ((bf16[4,64,1152]{2,1,0:T(8,128)(2,1)}), bf16[4,64,1152]{2,1,0:T(8,128)(2,1)S(1)}, u32[]{:S(2)}, u32[]{:S(2)}) async-start(bf16[4,64,1152]{2,1,0:T(8,128)(2,1)} %bitcast.114), calls=%async_computation.8 | async-start | bytes 1179648 | tf_op jit(solution)/shard_map/all_to_all | solution.py:138
  (167 other events, 2369.6 us)
Sparse Core Ops, SparseCore 0:
  36.0 38.7 all-gather.11
  76.7 54.2 all-gather.13
  132.9 54.2 all-gather.15
  188.9 116.3 all-gather.21
  307.0 116.3 all-gather.19
  425.1 116.3 all-gather.17
  1173.5 50.9 reduce-scatter.6
  1228.0 71.5 reduce-scatter.8
  1303.1 71.4 reduce-scatter.10
  1378.1 146.3 reduce-scatter.16
  1528.0 146.3 reduce-scatter.14
  1677.9 146.3 reduce-scatter.12

commit v2 on v1

--- a/solution.py
+++ b/solution.py
@@ -136,6 +136,16 @@
 
 def exchange(packed):
     return lax.all_to_all(packed, "expert", split_axis=0, concat_axis=0, tiled=True)
+
+
+def exchange_direct(packed, experts, own):
+    received = jnp.zeros(packed.shape, packed.dtype)
+    for k in range(experts):
+        block = lax.dynamic_index_in_dim(packed, (own + k) % experts, 0)
+        if k:
+            block = lax.ppermute(block, "expert", [(i, (i + k) % experts) for i in range(experts)])
+        received = lax.dynamic_update_slice_in_dim(received, block, (own - k) % experts, 0)
+    return received
 
 
 def ring_step(block, experts):
@@ -259,7 +269,7 @@
         ],
         2,
     )
-    bundle = exchange(bundle).reshape(experts * shard_rows, 2 * width + PAD)
+    bundle = exchange_direct(bundle, experts, own).reshape(experts * shard_rows, 2 * width + PAD)
     bundle = lax.all_gather(bundle, "dp", axis=0, tiled=True)
     kv_all = bundle[:, : 2 * width]
     att_all = bundle[:, 2 * width : 2 * width + experts]
@@ -324,7 +334,10 @@
     for k in range(experts):
         start = backs[k] * width
         group_queries = lax.dynamic_slice_in_dim(queries, start, width, 1)
-        keys, values = kv_blocks[k][:, :width], kv_blocks[k][:, width:]
+        kv_block = kv_blocks[k]
+        if k:
+            kv_block, attended = lax.optimization_barrier((kv_block, attended))
+        keys, values = kv_block[:, :width], kv_block[:, width:]
         group_attended, log_total = attend(group_queries, keys, values, key_mask)
         attended = lax.dynamic_update_slice_in_dim(attended, group_attended, start, 1)
         saved.append((group_queries, keys, values, key_mask, log_total, group_attended))
@@ -343,30 +356,42 @@
     ffn_place = placement_of(ffn_route, capacity, experts)
     ffn_rows = exchange(send_rows(ffn_place, normed_two, experts)).reshape(-1, model_width)
     grad_out = cotangent.astype(f32)
-    ffn_grad_rows = exchange(send_grads(ffn_place, ffn_gate, grad_out, experts)).reshape(
-        -1, model_width
-    )
+    ffn_rows, packed_grads = lax.optimization_barrier(
+        (ffn_rows, send_grads(ffn_place, ffn_gate, grad_out, experts))
+    )
+    ffn_grad_rows = exchange(packed_grads).reshape(-1, model_width)
     gate_value = mm(ffn_rows, gate_all)
     up_value = mm(ffn_rows, up_all)
     sigmoid_gate = jax.nn.sigmoid(gate_value)
     hidden = (gate_value * sigmoid_gate * up_value).astype(bf16)
     down_part = mm_tn(hidden, ffn_grad_rows).astype(bf16)
+    down_part, hidden, ffn_grad_rows = lax.optimization_barrier((down_part, hidden, ffn_grad_rows))
     down_sum = reduce_dp(down_part)
     ffn_branch = mm(hidden, down_all).astype(bf16)
-    ffn_picked = take_back(ffn_place, exchange(ffn_branch.reshape(experts, capacity, -1)))
-    result = mixed_stream + jnp.sum(ffn_gate.T[:, :, None] * ffn_picked, 0)
-    ffn_logit_grad = router_back(ffn_gate, ffn_picks, ffn_picked, grad_out)
+    ffn_branch, ffn_grad_rows = lax.optimization_barrier((ffn_branch, ffn_grad_rows))
+    ffn_back = exchange(ffn_branch.reshape(experts, capacity, -1))
     hidden_grad = mm_nt(ffn_grad_rows, down_all)
     gate_grad = (
         hidden_grad * up_value * sigmoid_gate * (1.0 + gate_value * (1.0 - sigmoid_gate))
     ).astype(bf16)
     up_grad = (hidden_grad * gate_value * sigmoid_gate).astype(bf16)
     ffn_rows_grad = (mm_nt(gate_grad, gate_all) + mm_nt(up_grad, up_all)).astype(bf16)
+    ffn_rows_grad, gate_grad, up_grad, ffn_back = lax.optimization_barrier(
+        (ffn_rows_grad, gate_grad, up_grad, ffn_back)
+    )
+    ffn_picked = take_back(ffn_place, ffn_back)
+    result = mixed_stream + jnp.sum(ffn_gate.T[:, :, None] * ffn_picked, 0)
+    ffn_logit_grad = router_back(ffn_gate, ffn_picks, ffn_picked, grad_out)
     ffn_rows_back = exchange(ffn_rows_grad.reshape(experts, capacity, -1)).reshape(
         experts * capacity, -1
     )
-    gate_sum = reduce_dp(mm_tn(ffn_rows, gate_grad).astype(bf16))
-    up_sum = reduce_dp(mm_tn(ffn_rows, up_grad).astype(bf16))
+    gate_part = mm_tn(ffn_rows, gate_grad).astype(bf16)
+    up_part = mm_tn(ffn_rows, up_grad).astype(bf16)
+    gate_part, up_part, ffn_rows_back = lax.optimization_barrier(
+        (gate_part, up_part, ffn_rows_back)
+    )
+    gate_sum = reduce_dp(gate_part)
+    up_sum = reduce_dp(up_part)
     normed_two_grad = mm(ffn_place[0] + ffn_place[1], ffn_rows_back) + jnp.dot(
         ffn_logit_grad, ffn_all.astype(f32).T, precision=highest
     )
@@ -377,8 +402,9 @@
     att_grad_rows = exchange(send_grads(att_place, att_gate, mixed_grad, experts)).reshape(
         -1, model_width
     )
+    att_grad_rows, down_sum = lax.optimization_barrier((att_grad_rows, down_sum))
     attended_grad = mm_nt(att_grad_rows, output_all).astype(bf16)
-    output_sum = reduce_dp(mm_tn(attended, att_grad_rows).astype(bf16))
+    output_part = mm_tn(attended, att_grad_rows).astype(bf16)
     query_grad = jnp.zeros(queries.shape, f32)
     kv_grad = None
     for step in range(1, experts + 1):
@@ -388,11 +414,17 @@
         group_query_grad, key_grad, value_grad = attend_back(*saved[k], group_grad)
         query_grad = lax.dynamic_update_slice_in_dim(query_grad, group_query_grad, start, 1)
         part = jnp.concatenate([key_grad, value_grad], 1)
+        if step == 2:
+            kv_grad, output_part = lax.optimization_barrier((kv_grad, output_part))
+        if k == 0:
+            query_raw_grad = rotate_back(query_grad, query_cos, query_sin).astype(bf16)
+            query_part = mm_tn(query_rows, query_raw_grad).astype(bf16)
+            kv_grad, query_part = lax.optimization_barrier((kv_grad, query_part))
         if kv_grad is not None:
             part = part + kv_grad.astype(f32)
         kv_grad = part if k == 0 else ring_step(part.astype(bf16), experts)
-    query_raw_grad = rotate_back(query_grad, query_cos, query_sin).astype(bf16)
-    query_sum = reduce_dp(mm_tn(query_rows, query_raw_grad).astype(bf16))
+    output_sum = reduce_dp(output_part)
+    query_sum = reduce_dp(query_part)
     att_rows_grad = mm_nt(query_raw_grad, query_all).astype(bf16)
     kv_raw_grad = jnp.concatenate(
         [rotate_back(kv_grad[:, :width], tree_cos, tree_sin), kv_grad[:, width:]], 1
@@ -432,6 +464,7 @@
         ],
         1,
     )
+    shared_part, query_sum = lax.optimization_barrier((shared_part, query_sum))
     shared_sum = exchange(reduce_dp(shared_part).reshape(experts, shard_rows, -1)).astype(f32)
     kv_sum = (
         shared_sum[:, :, : 2 * width]

time: 1840 us -> 1530 us (0.83)
  waiting for transfers between devices: 1110 us -> 825 us
  blocking collectives: 22 us -> 0 us
    reduce_scatter x6, waiting for transfers between devices: 519 us -> 338 us  [reduce_dp(): return lax.psum_scatter(part, 'dp', scatter_dimension=0, tiled=True)]
    all_to_all x7, waiting for transfers between devices: 267 us -> 172 us  [exchange(): lax.all_to_all(packed, 'expert', split_axis=0, concat_axis=0, tiled=True)]
    all_to_all x1 -> x0, blocking collectives: 22 us -> none  [exchange(): lax.all_to_all(packed, 'expert', split_axis=0, concat_axis=0, tiled=True)]
    dot_general x4, matrix products: 30.8 us -> 9.77 us  [group_scores(): jnp.einsum('qhd,khd->hqk', queries.reshape(-1, heads, HEAD), keys.reshape...]
    unnamed x344 -> x334, local copies, waits for them, and re-layouts: 42.8 us -> 40.2 us
  transfers between devices with their start and end apart: 31 -> 34, of which waited for: 23 -> 22; matrix products, arithmetic and copies ran while one was open for 24% -> 34% of each run, Pallas kernels for 0% -> 0%
where the time goes in v2:
time: 1530 us; the launch traced here: 1520 us
  waiting for transfers between devices  825 us (54%)
  matrix products  430 us (28%)
  local copies, waits for them, and re-layouts  122 us (8%)
  other arithmetic  84.7 us (6%)
  starting transfers between devices  45.5 us (3%)
  between operations  17.3 us (1%)
    reduce_scatter x6, waiting for transfers between devices, reduce_dp(): return lax.psum_scatter(part, 'dp', scatter_dimension=0, tiled=True)  338 us
    ppermute x12, waiting for transfers between devices, ring_step(): lax.ppermute(block, 'expert', [(i, (i + 1) % experts) for i in range(expe...  302 us
    all_to_all x7, waiting for transfers between devices, exchange(): lax.all_to_all(packed, 'expert', split_axis=0, concat_axis=0, tiled=True)  172 us
    dot_general x11, matrix products, mm_tn(): lax.dot_general(left, right, (((0,), (0,)), ((), ())), preferred_element_...  111 us
    dot_general x16, matrix products, mm(): return jnp.dot(left, right, preferred_element_type=f32)  111 us
    dot_general x6, matrix products, mm_nt(): lax.dot_general(left, right, (((1,), (1,)), ((), ())), preferred_element_...  93.7 us
    unnamed x334, local copies, waits for them, and re-layouts  40.2 us
    all_to_all x7, starting transfers between devices, exchange(): lax.all_to_all(packed, 'expert', split_axis=0, concat_axis=0, tiled=True)  31 us
  transfers between devices with their start and end apart: 34, of which 22 were waited for; matrix products, arithmetic and copies ran while one was open for 34% of the time, Pallas kernels for 0%

profile of v2, /device:TPU:0, one launch (start us, length us, event | category | flops | bytes accessed | tf_op | source)
XLA Modules:
  0.0 1523.9 jit_solution(12758596327748847969)
XLA Ops:
  37.2 24.9 %collective-permute-done = bf16[256,2176]{1,0:T(8,128)(2,1)} collective-permute-done((bf16[256,2176]{1,0:T(8,128)(2,1)S(1)}, bf16[256,2176]{1,0:T(8,128)(2,1)}, u32[]{:S(2)}, u32[]{:S(2)}) %collective-permute-start) | collective-permute-done | bytes 1114144 | tf_op jit(solution)/shard_map/ppermute | solution.py:152
  66.9 22.3 %collective-permute-done.1 = bf16[256,2176]{1,0:T(8,128)(2,1)} collective-permute-done((bf16[256,2176]{1,0:T(8,128)(2,1)}, bf16[256,2176]{1,0:T(8,128)(2,1)}, u32[]{:S(2)}, u32[]{:S(2)}) %collective-permute-start.1) | collective-permute-done | bytes 1114144 | tf_op jit(solution)/shard_map/ppermute | solution.py:152
  93.2 22.1 %collective-permute-done.2 = bf16[256,2176]{1,0:T(8,128)(2,1)S(1)} collective-permute-done((bf16[256,2176]{1,0:T(8,128)(2,1)}, bf16[256,2176]{1,0:T(8,128)(2,1)S(1)}, u32[]{:S(2)}, u32[]{:S(2)}) %collective-permute-start.2) | collective-permute-done | bytes 1114144 | tf_op jit(solution)/shard_map/ppermute | solution.py:152
  144.7 45.2 %collective-permute-done.6 = bf16[1024,1024]{0,1:T(8,128)(2,1)} collective-permute-done((bf16[1024,1024]{0,1:T(8,128)(2,1)}, bf16[1024,1024]{0,1:T(8,128)(2,1)}, u32[]{:S(2)}, u32[]{:S(2)}) %collective-permute-start.6) | collective-permute-done | bytes 2097184 | tf_op jit(solution)/shard_map/ppermute | solution.py:152
  198.9 37.1 %collective-permute-done.7 = bf16[1024,1024]{0,1:T(8,128)(2,1)} collective-permute-done((bf16[1024,1024]{0,1:T(8,128)(2,1)}, bf16[1024,1024]{0,1:T(8,128)(2,1)}, u32[]{:S(2)}, u32[]{:S(2)}) %collective-permute-start.7) | collective-permute-done | bytes 2097184 | tf_op jit(solution)/shard_map/ppermute | solution.py:152
  235.9 11.7 copy.252
  247.7 9.9 fusion.216
  311.8 10.5 fusion.66
  330.7 51.8 %all-to-all-done = bf16[4,160,2048]{2,1,0:T(8,128)(2,1)S(1)} async-done(((bf16[4,160,2048]{2,1,0:T(8,128)(2,1)}), bf16[4,160,2048]{2,1,0:T(8,128)(2,1)S(1)}, u32[]{:S(2)}, u32[]{:S(2)}) %all-to-all-start) | async-done | bytes 2621472 | tf_op jit(solution)/shard_map/all_to_all | solution.py:138
  402.7 51.7 %all-to-all-done.1 = bf16[4,160,2048]{2,1,0:T(8,128)(2,1)} async-done(((bf16[4,160,2048]{2,1,0:T(8,128)(2,1)}), bf16[4,160,2048]{2,1,0:T(8,128)(2,1)}, u32[]{:S(2)}, u32[]{:S(2)}) %all-to-all-start.1) | async-done | bytes 2621472 | tf_op jit(solution)/shard_map/all_to_all | solution.py:138
  458.1 23.3 %fusion.10 = f32[640,5632]{1,0:T(8,128)} fusion(bf16[640,2048]{1,0:T(8,128)(2,1)} %bitcast.47, bf16[1,2048,5632]{2,1,0:T(8,128)(2,1)} %all-gather.18.cloned.1.call-done), kind=kOutput, calls=%fused_computation.10 | convolution fusion | flops 14763950080 | bytes 40108032 | tf_op jit(solution)/shard_map/dot_general | solution.py:82
  481.4 28.5 %multiply_convert_fusion.2 = (bf16[640,5632]{1,0:T(8,128)(2,1)}, f32[640,5632]{1,0:T(8,128)}) fusion(f32[640,5632]{1,0:T(8,128)} %fusion.10, bf16[640,2048]{1,0:T(8,128)(2,1)} %bitcast.47, bf16[1,2048,5632]{2,1,0:T(8,128)(2,1)} %all-gather.20.cloned.1.call-done), kind=kOutput, calls=%fused_computation.17 | convolution fusion | flops 14785576960 | bytes 61734912 | tf_op jit(solution)/shard_map/dot_general | solution.py:82
  517.0 25.8 %convolution_convert_fusion = bf16[5632,2048]{1,0:T(8,128)(2,1)} fusion(bf16[640,5632]{1,0:T(8,128)(2,1)} %get-tuple-element.48, bf16[640,2048]{1,0:T(8,128)(2,1)S(1)} %bitcast.374), kind=kOutput, calls=%fused_computation.12 | convolution fusion | flops 14775484416 | bytes 32899072 | tf_op jit(solution)/shard_map/dot_general | solution.py:86
  542.9 22.5 %fusion.60 = bf16[640,2048]{1,0:T(8,128)(2,1)} fusion(bf16[640,5632]{1,0:T(8,128)(2,1)} %get-tuple-element.48, bf16[1,5632,2048]{2,1,0:T(8,128)(2,1)} %all-gather.22.cloned.1.call-done), kind=kOutput, calls=%fused_computation.104 | convolution fusion | flops 14765260800 | bytes 32899072 | tf_op jit(solution)/shard_map/dot_general | solution.py:82
  569.2 31.5 %multiply_convert_fusion.1 = (bf16[640,5632]{1,0:T(8,128)(2,1)}, bf16[640,5632]{1,0:T(8,128)(2,1)}) fusion(f32[640,5632]{1,0:T(8,128)} %fusion.10, f32[640,5632]{1,0:T(8,128)} %get-tuple-element.177, bf16[640,2048]{1,0:T(8,128)(2,1)} %bitcast.375, bf16[1,5632,2048]{2,1,0:T(8,128)(2,1)} %all-gather.22.cloned.1.call-done), kind=kOutput, calls=%fused_computation.16 | convolution fusion | flops 14810808320 | bytes 68943872 | tf_op jit(solution)/shard_map/dot_general | solution.py:90
  600.7 21.0 %fusion.4 = f32[640,2048]{1,0:T(8,128)S(1)} fusion(bf16[640,5632]{1,0:T(8,128)(2,1)} %get-tuple-element.54, bf16[1,2048,5632]{2,1,0:T(8,128)(2,1)} %all-gather.20.cloned.1.call-done), kind=kOutput, calls=%fused_computation.4 | convolution fusion | flops 14763950080 | bytes 35520512 | tf_op jit(solution)/shard_map/dot_general | solution.py:90
  621.8 19.2 %add_convert_fusion.1 = bf16[640,2048]{1,0:T(8,128)(2,1)} fusion(f32[640,2048]{1,0:T(8,128)S(1)} %fusion.4, bf16[640,5632]{1,0:T(8,128)(2,1)S(1)} %copy-done.146, bf16[1,2048,5632]{2,1,0:T(8,128)(2,1)} %all-gather.18.cloned.1.call-done), kind=kOutput, calls=%fused_computation.66 | convolution fusion | flops 14766571520 | bytes 38141952 | tf_op jit(solution)/shard_map/dot_general | solution.py:90
  646.5 25.7 %convolution_convert_fusion.1 = bf16[2048,5632]{1,0:T(8,128)(2,1)} fusion(bf16[640,2048]{1,0:T(8,128)(2,1)} %bitcast.47, bf16[640,5632]{1,0:T(8,128)(2,1)} %get-tuple-element.54), kind=kOutput, calls=%fused_computation.13 | convolution fusion | flops 14775484416 | bytes 32899072 | tf_op jit(solution)/shard_map/dot_general | solution.py:86
  676.5 26.0 %convolution_convert_fusion.2 = bf16[2048,5632]{1,0:T(8,128)(2,1)} fusion(bf16[640,2048]{1,0:T(8,128)(2,1)} %bitcast.47, bf16[640,5632]{1,0:T(8,128)(2,1)} %get-tuple-element.53), kind=kOutput, calls=%fused_computation.14 | convolution fusion | flops 14775484416 | bytes 32899072 | tf_op jit(solution)/shard_map/dot_general | solution.py:86
  722.7 58.8 %all-to-all-done.5 = bf16[4,160,2048]{2,1,0:T(8,128)(2,1)S(1)} async-done(((bf16[4,160,2048]{2,1,0:T(8,128)(2,1)}), bf16[4,160,2048]{2,1,0:T(8,128)(2,1)S(1)}, u32[]{:S(2)}, u32[]{:S(2)}) %all-to-all-start.5) | async-done | bytes 2621472 | tf_op jit(solution)/shard_map/all_to_all | solution.py:138
  879.6 25.3 %collective-permute-done.9 = bf16[1024,1024]{0,1:T(8,128)(2,1)} collective-permute-done((bf16[1024,1024]{0,1:T(8,128)(2,1)}, bf16[1024,1024]{0,1:T(8,128)(2,1)}, u32[]{:S(2)}, u32[]{:S(2)}) %collective-permute-start.9) | collective-permute-done | bytes 2097184 | tf_op jit(solution)/shard_map/ppermute | solution.py:152
  920.5 35.3 %collective-permute-done.10 = bf16[1024,1024]{0,1:T(8,128)(2,1)S(1)} collective-permute-done((bf16[1024,1024]{0,1:T(8,128)(2,1)S(1)}, bf16[1024,1024]{0,1:T(8,128)(2,1)S(1)}, u32[]{:S(2)}, u32[]{:S(2)}) %collective-permute-start.10) | collective-permute-done | bytes 2097184 | tf_op jit(solution)/shard_map/ppermute | solution.py:152
  964.0 9.1 convolution_convert_fusion.3
  973.1 31.8 %collective-permute-done.11 = bf16[1024,1024]{0,1:T(8,128)(2,1)S(1)} collective-permute-done((bf16[1024,1024]{0,1:T(8,128)(2,1)}, bf16[1024,1024]{0,1:T(8,128)(2,1)S(1)}, u32[]{:S(2)}, u32[]{:S(2)}) %collective-permute-start.11) | collective-permute-done | bytes 2097184 | tf_op jit(solution)/shard_map/ppermute | solution.py:152
  1048.7 22.9 %collective-permute-done.12 = bf16[256,2048]{1,0:T(8,128)(2,1)S(1)} collective-permute-done((bf16[256,2048]{1,0:T(8,128)(2,1)S(1)}, bf16[256,2048]{1,0:T(8,128)(2,1)S(1)}, u32[]{:S(2)}, u32[]{:S(2)}) %collective-permute-start.12) | collective-permute-done | bytes 1048608 | tf_op jit(solution)/shard_map/ppermute | solution.py:152
  1073.7 21.6 %collective-permute-done.13 = bf16[256,2048]{1,0:T(8,128)(2,1)S(1)} collective-permute-done((bf16[256,2048]{1,0:T(8,128)(2,1)S(1)}, bf16[256,2048]{1,0:T(8,128)(2,1)S(1)}, u32[]{:S(2)}, u32[]{:S(2)}) %collective-permute-start.13) | collective-permute-done | bytes 1048608 | tf_op jit(solution)/shard_map/ppermute | solution.py:152
  1103.1 13.7 collective-permute-done.14
  1121.0 22.9 %concatenate.61 = bf16[2048,1152]{0,1:T(8,128)(2,1)} concatenate(bf16[2048,1024]{0,1:T(8,128)(2,1)} %convolution_convert_fusion.5, bf16[2048,4]{0,1:T(4,128)(2,1)S(1)} %convolution_convert_fusion.9, bf16[2048,4]{0,1:T(4,128)(2,1)S(1)} %convolution_convert_fusion.8, bf16[2048,1]{0,1:T(2,128)(2,1)S(1)} %convert_element_type.464, bf16[2048,1]{0,1:T(2,128)(2,1)S(1)} %convert_element_type.466, ...), dimensions={1} | concatenate | bytes 9437184 | tf_op jit(solution)/shard_map/concatenate | solution.py:456
  1149.6 75.3 %reduce-scatter.17.cloned.1.call-done = bf16[256,5632]{1,0:T(8,128)(2,1)} async-done(((bf16[2048,5632]{1,0:T(8,128)(2,1)}), bf16[256,5632]{1,0:T(8,128)(2,1)}) %reduce-scatter.17.cloned.1.call-update) | async-done | bytes 2883600 | tf_op jit(solution)/shard_map/reduce_scatter | solution.py:223
  1229.8 144.8 %reduce-scatter.15.cloned.1.call-done = bf16[256,5632]{1,0:T(8,128)(2,1)} async-done(((bf16[2048,5632]{1,0:T(8,128)(2,1)}), bf16[256,5632]{1,0:T(8,128)(2,1)}) %reduce-scatter.15.cloned.1.call-update) | async-done | bytes 2883600 | tf_op jit(solution)/shard_map/reduce_scatter | solution.py:223
  1381.8 50.1 %reduce-scatter.11.cloned.1.call-done = bf16[256,1152]{0,1:T(8,128)(2,1)} async-done(((bf16[2048,1152]{0,1:T(8,128)(2,1)}), bf16[256,1152]{0,1:T(8,128)(2,1)}) %reduce-scatter.11.cloned.1.call-update) | async-done | bytes 589840 | tf_op jit(solution)/shard_map/reduce_scatter | solution.py:223
  1438.5 68.1 %reduce-scatter.13.cloned.1.call-done = bf16[256,2048]{1,0:T(8,128)(2,1)} async-done(((bf16[2048,2048]{1,0:T(8,128)(2,1)}), bf16[256,2048]{1,0:T(8,128)(2,1)}) %reduce-scatter.13.cloned.1.call-update) | async-done | bytes 1048592 | tf_op jit(solution)/shard_map/reduce_scatter | solution.py:223
  (604 shorter events, 416.3 us)
Async XLA Ops:
  7.2 111.3 %all-gather.12.cloned.1.call-start = ((), (), s32[]{:S(2)}) async-start(), calls=%async_computation.13 | async-start | bytes 5308416 | tf_op jit(solution)/shard_map/all_gather | solution.py:273
  16.0 12.3 collective-permute-start.4
  29.2 206.7 %all-gather.14.cloned.1.call-start = ((), (), s32[]{:S(2)}) async-start(), calls=%async_computation.20 | async-start | bytes 9437184 | tf_op jit(solution)/shard_map/all_gather | solution.py:219
  29.9 281.9 %all-gather.16.cloned.1.call-start = ((), (), s32[]{:S(2)}) async-start(), calls=%async_computation.21 | async-start | bytes 9437184 | tf_op jit(solution)/shard_map/all_gather | solution.py:219
  30.7 427.4 %all-gather.18.cloned.1.call-start = ((), (), s32[]{:S(2)}) async-start(), calls=%async_computation.22 | async-start | bytes 25952256 | tf_op jit(solution)/shard_map/all_gather | solution.py:219
  31.3 450.1 %all-gather.20.cloned.1.call-start = ((), (), s32[]{:S(2)}) async-start(), calls=%async_computation.23 | async-start | bytes 25952256 | tf_op jit(solution)/shard_map/all_gather | solution.py:219
  31.8 511.0 %all-gather.22.cloned.1.call-start = ((), (), s32[]{:S(2)}) async-start(), calls=%async_computation.24 | async-start | bytes 25952256 | tf_op jit(solution)/shard_map/all_gather | solution.py:219
  33.6 28.6 %collective-permute-start = (bf16[256,2176]{1,0:T(8,128)(2,1)S(1)}, bf16[256,2176]{1,0:T(8,128)(2,1)}, u32[]{:S(2)}, u32[]{:S(2)}) collective-permute-start(bf16[256,2176]{1,0:T(8,128)(2,1)S(1)} %concatenate.48), channel_id=1, source_target_pairs={{0,1},{1,2},{2,3},{3,0},{4,5},{5,6},{6,7},{7,4},{8,9},{9,10},{10,1... | collective-permute-start | bytes 3342344 | tf_op jit(solution)/shard_map/ppermute | solution.py:152
  62.1 27.0 %collective-permute-start.1 = (bf16[256,2176]{1,0:T(8,128)(2,1)}, bf16[256,2176]{1,0:T(8,128)(2,1)}, u32[]{:S(2)}, u32[]{:S(2)}) collective-permute-start(bf16[256,2176]{1,0:T(8,128)(2,1)} %collective-permute-done), channel_id=1, source_target_pairs={{0,1},{1,2},{2,3},{3,0},{4,5},{5,6},{6,7},{7,4},{8,9},{9,10},{10,1... | collective-permute-start | bytes 3342344 | tf_op jit(solution)/shard_map/ppermute | solution.py:152
  89.1 26.2 %collective-permute-start.2 = (bf16[256,2176]{1,0:T(8,128)(2,1)}, bf16[256,2176]{1,0:T(8,128)(2,1)S(1)}, u32[]{:S(2)}, u32[]{:S(2)}) collective-permute-start(bf16[256,2176]{1,0:T(8,128)(2,1)} %collective-permute-done.1), channel_id=1, source_target_pairs={{0,1},{1,2},{2,3},{3,0},{4,5},{5,6},{6,7},{7,4},{8,9},{9,10},{10,1... | collective-permute-start | bytes 3342344 | tf_op jit(solution)/shard_map/ppermute | solution.py:152
  143.4 46.5 %collective-permute-start.6 = (bf16[1024,1024]{0,1:T(8,128)(2,1)}, bf16[1024,1024]{0,1:T(8,128)(2,1)}, u32[]{:S(2)}, u32[]{:S(2)}) collective-permute-start(bf16[1024,1024]{0,1:T(8,128)(2,1)} %pad_maximum_fusion.3), channel_id=1, source_target_pairs={{0,1},{1,2},{2,3},{3,0},{4,5},{5,6},{6,7},{7,4},{8,9},{9,10},{10,1... | collective-permute-start | bytes 6291464 | tf_op jit(solution)/shard_map/ppermute | solution.py:152
  189.9 46.0 %collective-permute-start.7 = (bf16[1024,1024]{0,1:T(8,128)(2,1)}, bf16[1024,1024]{0,1:T(8,128)(2,1)}, u32[]{:S(2)}, u32[]{:S(2)}) collective-permute-start(bf16[1024,1024]{0,1:T(8,128)(2,1)} %collective-permute-done.6), channel_id=1, source_target_pairs={{0,1},{1,2},{2,3},{3,0},{4,5},{5,6},{6,7},{7,4},{8,9},{9,10},{10,1... | collective-permute-start | bytes 6291464 | tf_op jit(solution)/shard_map/ppermute | solution.py:152
  235.9 62.2 %collective-permute-start.8 = (bf16[1024,1024]{0,1:T(8,128)(2,1)}, bf16[1024,1024]{0,1:T(8,128)(2,1)}, u32[]{:S(2)}, u32[]{:S(2)}) collective-permute-start(bf16[1024,1024]{0,1:T(8,128)(2,1)} %collective-permute-done.7), channel_id=1, source_target_pairs={{0,1},{1,2},{2,3},{3,0},{4,5},{5,6},{6,7},{7,4},{8,9},{9,10},{10,1... | collective-permute-start | bytes 6291464 | tf_op jit(solution)/shard_map/ppermute | solution.py:152
  322.4 60.0 %all-to-all-start = ((bf16[4,160,2048]{2,1,0:T(8,128)(2,1)}), bf16[4,160,2048]{2,1,0:T(8,128)(2,1)S(1)}, u32[]{:S(2)}, u32[]{:S(2)}) async-start(bf16[4,160,2048]{2,1,0:T(8,128)(2,1)} %bitcast.379), calls=%async_computation | async-start | bytes 5242880 | tf_op jit(solution)/shard_map/all_to_all | solution.py:138
  390.5 63.8 %all-to-all-start.1 = ((bf16[4,160,2048]{2,1,0:T(8,128)(2,1)}), bf16[4,160,2048]{2,1,0:T(8,128)(2,1)}, u32[]{:S(2)}, u32[]{:S(2)}) async-start(bf16[4,160,2048]{2,1,0:T(8,128)(2,1)} %bitcast.46), calls=%async_computation.1 | async-start | bytes 5242880 | tf_op jit(solution)/shard_map/all_to_all | solution.py:138
  454.4 62.6 %all-to-all-start.2 = ((bf16[4,160,2048]{2,1,0:T(8,128)(2,1)}), bf16[4,160,2048]{2,1,0:T(8,128)(2,1)S(1)}, u32[]{:S(2)}, u32[]{:S(2)}) async-start(bf16[4,160,2048]{2,1,0:T(8,128)(2,1)} %bitcast.336), calls=%async_computation.2 | async-start | bytes 5242880 | tf_op jit(solution)/shard_map/all_to_all | solution.py:138
  458.0 323.4 %reduce-scatter.7.cloned.1.call-start = ((), (), s32[]{:S(2)}) async-start(), calls=%async_computation.14 | async-start | bytes 25952256 | tf_op jit(solution)/shard_map/reduce_scatter | solution.py:223
  565.3 75.7 %all-to-all-start.3 = ((bf16[4,160,2048]{2,1,0:T(8,128)(2,1)}), bf16[4,160,2048]{2,1,0:T(8,128)(2,1)S(1)}, u32[]{:S(2)}, u32[]{:S(2)}) async-start(bf16[4,160,2048]{2,1,0:T(8,128)(2,1)} %bitcast.380), calls=%async_computation.3 | async-start | bytes 5242880 | tf_op jit(solution)/shard_map/all_to_all | solution.py:138
  641.0 64.0 %all-to-all-start.4 = ((bf16[4,160,2048]{2,1,0:T(8,128)(2,1)}), bf16[4,160,2048]{2,1,0:T(8,128)(2,1)}, u32[]{:S(2)}, u32[]{:S(2)}) async-start(bf16[4,160,2048]{2,1,0:T(8,128)(2,1)} %bitcast.378), calls=%async_computation.4 | async-start | bytes 5242880 | tf_op jit(solution)/shard_map/all_to_all | solution.py:138
  718.7 62.8 %all-to-all-start.5 = ((bf16[4,160,2048]{2,1,0:T(8,128)(2,1)}), bf16[4,160,2048]{2,1,0:T(8,128)(2,1)S(1)}, u32[]{:S(2)}, u32[]{:S(2)}) async-start(bf16[4,160,2048]{2,1,0:T(8,128)(2,1)} %bitcast.65), calls=%async_computation.5 | async-start | bytes 5242880 | tf_op jit(solution)/shard_map/all_to_all | solution.py:138
  722.5 421.3 %reduce-scatter.9.cloned.1.call-start = ((), (), s32[]{:S(2)}) async-start(), calls=%async_computation.15 | async-start | bytes 9437184 | tf_op jit(solution)/shard_map/reduce_scatter | solution.py:223
  856.1 48.8 %collective-permute-start.9 = (bf16[1024,1024]{0,1:T(8,128)(2,1)}, bf16[1024,1024]{0,1:T(8,128)(2,1)}, u32[]{:S(2)}, u32[]{:S(2)}) collective-permute-start(bf16[1024,1024]{0,1:T(8,128)(2,1)} %pad_maximum_fusion.4), channel_id=1, source_target_pairs={{0,1},{1,2},{2,3},{3,0},{4,5},{5,6},{6,7},{7,4},{8,9},{9,10},{10,1... | collective-permute-start | bytes 6291464 | tf_op jit(solution)/shard_map/ppermute | solution.py:152
  908.0 47.8 %collective-permute-start.10 = (bf16[1024,1024]{0,1:T(8,128)(2,1)S(1)}, bf16[1024,1024]{0,1:T(8,128)(2,1)S(1)}, u32[]{:S(2)}, u32[]{:S(2)}) collective-permute-start(bf16[1024,1024]{0,1:T(8,128)(2,1)S(1)} %fusion.50), channel_id=1, source_target_pairs={{0,1},{1,2},{2,3},{3,0},{4,5},{5,6},{6,7},{7,4},{8,9},{9,10},{10,1... | collective-permute-start | bytes 6291464 | tf_op jit(solution)/shard_map/ppermute | solution.py:152
  958.0 46.9 %collective-permute-start.11 = (bf16[1024,1024]{0,1:T(8,128)(2,1)}, bf16[1024,1024]{0,1:T(8,128)(2,1)S(1)}, u32[]{:S(2)}, u32[]{:S(2)}) collective-permute-start(bf16[1024,1024]{0,1:T(8,128)(2,1)} %fusion.49), channel_id=1, source_target_pairs={{0,1},{1,2},{2,3},{3,0},{4,5},{5,6},{6,7},{7,4},{8,9},{9,10},{10,1... | collective-permute-start | bytes 6291464 | tf_op jit(solution)/shard_map/ppermute | solution.py:152
  1006.3 218.6 %reduce-scatter.17.cloned.1.call-start = ((), (), s32[]{:S(2)}) async-start(), calls=%async_computation.19 | async-start | bytes 25952256 | tf_op jit(solution)/shard_map/reduce_scatter | solution.py:223
  1007.0 367.7 %reduce-scatter.15.cloned.1.call-start = ((), (), s32[]{:S(2)}) async-start(), calls=%async_computation.18 | async-start | bytes 25952256 | tf_op jit(solution)/shard_map/reduce_scatter | solution.py:223
  1007.6 424.2 %reduce-scatter.11.cloned.1.call-start = ((), (), s32[]{:S(2)}) async-start(), calls=%async_computation.16 | async-start | bytes 5308416 | tf_op jit(solution)/shard_map/reduce_scatter | solution.py:223
  1048.7 23.0 %collective-permute-start.12 = (bf16[256,2048]{1,0:T(8,128)(2,1)S(1)}, bf16[256,2048]{1,0:T(8,128)(2,1)S(1)}, u32[]{:S(2)}, u32[]{:S(2)}) collective-permute-start(bf16[256,2048]{1,0:T(8,128)(2,1)S(1)} %fusion.88), channel_id=1, source_target_pairs={{0,1},{1,2},{2,3},{3,0},{4,5},{5,6},{6,7},{7,4},{8,9},{9,10},{10,1... | collective-permute-start | bytes 3145736 | tf_op jit(solution)/shard_map/ppermute | solution.py:152
  1072.0 23.3 %collective-permute-start.13 = (bf16[256,2048]{1,0:T(8,128)(2,1)S(1)}, bf16[256,2048]{1,0:T(8,128)(2,1)S(1)}, u32[]{:S(2)}, u32[]{:S(2)}) collective-permute-start(bf16[256,2048]{1,0:T(8,128)(2,1)S(1)} %fusion.78), channel_id=1, source_target_pairs={{0,1},{1,2},{2,3},{3,0},{4,5},{5,6},{6,7},{7,4},{8,9},{9,10},{10,1... | collective-permute-start | bytes 3145736 | tf_op jit(solution)/shard_map/ppermute | solution.py:152
  1095.5 21.3 %collective-permute-start.14 = (bf16[256,2048]{1,0:T(8,128)(2,1)S(1)}, bf16[256,2048]{1,0:T(8,128)(2,1)S(1)}, u32[]{:S(2)}, u32[]{:S(2)}) collective-permute-start(bf16[256,2048]{1,0:T(8,128)(2,1)S(1)} %fusion.79), channel_id=1, source_target_pairs={{0,1},{1,2},{2,3},{3,0},{4,5},{5,6},{6,7},{7,4},{8,9},{9,10},{10,1... | collective-permute-start | bytes 3145736 | tf_op jit(solution)/shard_map/ppermute | solution.py:152
  1143.8 362.8 %reduce-scatter.13.cloned.1.call-start = ((), (), s32[]{:S(2)}) async-start(), calls=%async_computation.17 | async-start | bytes 9437184 | tf_op jit(solution)/shard_map/reduce_scatter | solution.py:223
  1433.9 77.1 %all-to-all-start.6 = ((bf16[4,64,1152]{2,1,0:T(8,128)(2,1)}), bf16[4,64,1152]{2,1,0:T(8,128)(2,1)S(1)}, u32[]{:S(2)}, u32[]{:S(2)}) async-start(bf16[4,64,1152]{2,1,0:T(8,128)(2,1)} %bitcast.112), calls=%async_computation.9 | async-start | bytes 1179648 | tf_op jit(solution)/shard_map/all_to_all | solution.py:138
  (165 other events, 2487.7 us)
Sparse Core Ops, SparseCore 0:
  29.3 41.1 all-gather.11
  72.3 54.2 all-gather.13
  128.5 54.2 all-gather.15
  184.6 116.3 all-gather.17
  302.6 116.3 all-gather.19
  420.8 116.3 all-gather.21
  542.9 144.3 reduce-scatter.6
  1005.1 69.6 reduce-scatter.8
  1078.4 146.3 reduce-scatter.16
  1228.3 146.3 reduce-scatter.14
  1378.1 53.6 reduce-scatter.10
  1435.1 71.4 reduce-scatter.12

commit v3 on v2

--- a/solution.py
+++ b/solution.py
@@ -221,6 +221,37 @@
 
 def reduce_dp(part):
     return lax.psum_scatter(part, "dp", scatter_dimension=0, tiled=True)
+
+
+def swap(block, bit):
+    return lax.ppermute(block, "dp", [(i, i ^ bit) for i in range(8)])
+
+
+def bit_of(value, bit):
+    return (value // bit) % 2
+
+
+def halves(block, axis, bit):
+    pick = bit_of(lax.axis_index("dp"), bit)
+    kept = lax.dynamic_index_in_dim(block, pick, axis, keepdims=False)
+    sent = lax.dynamic_index_in_dim(block, 1 - pick, axis, keepdims=False)
+    return (kept.astype(f32), sent.astype(bf16))
+
+
+def fold(block, axis, bit):
+    kept, sent = halves(block, axis, bit)
+    return kept + swap(sent, bit).astype(f32)
+
+
+def reduce_swaps(part):
+    if lax.axis_size("dp") != 8:
+        return reduce_dp(part).astype(f32)
+    rows, columns = part.shape
+    grid = fold(part.reshape(2, 2, 2, rows // 8, columns), 2, 1).astype(bf16)
+    left, right = grid[..., : columns // 2], grid[..., columns // 2 :]
+    left = fold(fold(left, 1, 2).astype(bf16), 0, 4)
+    right = fold(fold(right, 0, 4).astype(bf16), 0, 2)
+    return jnp.concatenate([left, right], 1)
 
 
 def body(
@@ -416,15 +447,17 @@
         part = jnp.concatenate([key_grad, value_grad], 1)
         if step == 2:
             kv_grad, output_part = lax.optimization_barrier((kv_grad, output_part))
+            output_sum = reduce_swaps(output_part)
         if k == 0:
             query_raw_grad = rotate_back(query_grad, query_cos, query_sin).astype(bf16)
             query_part = mm_tn(query_rows, query_raw_grad).astype(bf16)
-            kv_grad, query_part = lax.optimization_barrier((kv_grad, query_part))
+            kv_grad, query_part, output_sum = lax.optimization_barrier(
+                (kv_grad, query_part, output_sum)
+            )
+            query_sum = reduce_swaps(query_part)
         if kv_grad is not None:
             part = part + kv_grad.astype(f32)
         kv_grad = part if k == 0 else ring_step(part.astype(bf16), experts)
-    output_sum = reduce_dp(output_part)
-    query_sum = reduce_dp(query_part)
     att_rows_grad = mm_nt(query_raw_grad, query_all).astype(bf16)
     kv_raw_grad = jnp.concatenate(
         [rotate_back(kv_grad[:, :width], tree_cos, tree_sin), kv_grad[:, width:]], 1
@@ -442,29 +475,35 @@
         if normed_one_grad is not None:
             part = part + normed_one_grad.astype(f32)
         normed_one_grad = part if k == 0 else ring_step(part.astype(bf16), experts)
+    normed_one_grad, query_sum = lax.optimization_barrier((normed_one_grad, query_sum))
     normed_one_grad = normed_one_grad + jnp.dot(
         att_logit_grad, att_all.astype(f32).T, precision=highest
     )
     gain_one_part = jnp.sum(normed_one_grad * inputs * inverse_one, 0)
     input_grad = mixed_grad + norm_back(inputs, inverse_one, gain_first, normed_one_grad)
     att_router_part = lax.dot_general(
-        normed_one.astype(f32), att_logit_grad, (((0,), (0,)), ((), ())), precision=highest
+        att_logit_grad, normed_one.astype(f32), (((0,), (0,)), ((), ())), precision=highest
     )
     ffn_router_part = lax.dot_general(
-        normed_two.astype(f32), ffn_logit_grad, (((0,), (0,)), ((), ())), precision=highest
-    )
+        ffn_logit_grad, normed_two.astype(f32), (((0,), (0,)), ((), ())), precision=highest
+    )
+    small_part = jnp.concatenate(
+        [
+            att_router_part,
+            ffn_router_part,
+            gain_one_part[None],
+            gain_two_part[None],
+            jnp.zeros((PAD - 2 * experts - 2, model_width), f32),
+        ],
+        0,
+    ).astype(bf16)
     shared_part = jnp.concatenate(
         [
             mm_tn(normed_tree, kv_raw_grad).astype(bf16),
-            att_router_part.astype(bf16),
-            ffn_router_part.astype(bf16),
-            gain_one_part[:, None].astype(bf16),
-            gain_two_part[:, None].astype(bf16),
-            jnp.zeros((model_width, PAD - 2 * experts - 2), bf16),
+            mm_tn(small_part, jnp.eye(PAD, dtype=bf16)).astype(bf16),
         ],
         1,
     )
-    shared_part, query_sum = lax.optimization_barrier((shared_part, query_sum))
     shared_sum = exchange(reduce_dp(shared_part).reshape(experts, shard_rows, -1)).astype(f32)
     kv_sum = (
         shared_sum[:, :, : 2 * width]

time: 1530 us -> 1270 us (0.83)
  waiting for transfers between devices: 825 us -> 540 us
  local copies, waits for them, and re-layouts: 122 us -> 101 us
  other arithmetic: 84.7 us -> 102 us
    reduce_scatter x6 -> x4, waiting for transfers between devices: 338 us -> 37.2 us  [reduce_dp(): return lax.psum_scatter(part, 'dp', scatter_dimension=0, tiled=True)]
    ppermute x0 -> x10, waiting for transfers between devices: none -> 71.4 us  [swap(): return lax.ppermute(block, 'dp', [(i, i ^ bit) for i in range(8)])]
    ppermute x12, waiting for transfers between devices: 302 us -> 234 us  [ring_step(): lax.ppermute(block, 'expert', [(i, (i + 1) % experts) for i in range(expe...]
    concatenate x1, local copies, waits for them, and re-layouts: 22.9 us -> 5.48 us  [body(): jnp.concatenate([att_router_part, ffn_router_part, gain_one_part[None], g...]
    dot_general x11 -> x12, matrix products: 111 us -> 120 us  [mm_tn(): lax.dot_general(left, right, (((0,), (0,)), ((), ())), preferred_element_...]
    unnamed x334 -> x324, local copies, waits for them, and re-layouts: 40.2 us -> 35.8 us
  transfers between devices with their start and end apart: 34 -> 42, of which waited for: 22 -> 24; matrix products, arithmetic and copies ran while one was open for 34% -> 48% of each run, Pallas kernels for 0% -> 0%
where the time goes in v3:
time: 1270 us; the launch traced here: 1260 us
  waiting for transfers between devices  540 us (43%)
  matrix products  445 us (35%)
  other arithmetic  102 us (8%)
  local copies, waits for them, and re-layouts  101 us (8%)
  starting transfers between devices  57.3 us (5%)
  between operations  17.4 us (1%)
    ppermute x12, waiting for transfers between devices, ring_step(): lax.ppermute(block, 'expert', [(i, (i + 1) % experts) for i in range(expe...  234 us
    all_to_all x7, waiting for transfers between devices, exchange(): lax.all_to_all(packed, 'expert', split_axis=0, concat_axis=0, tiled=True)  186 us
    dot_general x12, matrix products, mm_tn(): lax.dot_general(left, right, (((0,), (0,)), ((), ())), preferred_element_...  120 us
    dot_general x16, matrix products, mm(): return jnp.dot(left, right, preferred_element_type=f32)  112 us
    dot_general x6, matrix products, mm_nt(): lax.dot_general(left, right, (((1,), (1,)), ((), ())), preferred_element_...  97.9 us
    ppermute x10, waiting for transfers between devices, swap(): return lax.ppermute(block, 'dp', [(i, i ^ bit) for i in range(8)])  71.4 us
    reduce_scatter x4, waiting for transfers between devices, reduce_dp(): return lax.psum_scatter(part, 'dp', scatter_dimension=0, tiled=True)  37.2 us
    unnamed x324, local copies, waits for them, and re-layouts  35.8 us
  transfers between devices with their start and end apart: 42, of which 24 were waited for; matrix products, arithmetic and copies ran while one was open for 48% of the time, Pallas kernels for 0%

profile of v3, /device:TPU:0, one launch (start us, length us, event | category | flops | bytes accessed | tf_op | source)
XLA Modules:
  0.0 1263.2 jit_solution(3252472521404319360)
XLA Ops:
  37.2 24.9 %collective-permute-done = bf16[256,2176]{1,0:T(8,128)(2,1)} collective-permute-done((bf16[256,2176]{1,0:T(8,128)(2,1)S(1)}, bf16[256,2176]{1,0:T(8,128)(2,1)}, u32[]{:S(2)}, u32[]{:S(2)}) %collective-permute-start) | collective-permute-done | bytes 1114144 | tf_op jit(solution)/shard_map/ppermute | solution.py:152
  66.8 22.3 %collective-permute-done.1 = bf16[256,2176]{1,0:T(8,128)(2,1)} collective-permute-done((bf16[256,2176]{1,0:T(8,128)(2,1)}, bf16[256,2176]{1,0:T(8,128)(2,1)}, u32[]{:S(2)}, u32[]{:S(2)}) %collective-permute-start.1) | collective-permute-done | bytes 1114144 | tf_op jit(solution)/shard_map/ppermute | solution.py:152
  93.5 22.1 %collective-permute-done.2 = bf16[256,2176]{1,0:T(8,128)(2,1)S(1)} collective-permute-done((bf16[256,2176]{1,0:T(8,128)(2,1)}, bf16[256,2176]{1,0:T(8,128)(2,1)S(1)}, u32[]{:S(2)}, u32[]{:S(2)}) %collective-permute-start.2) | collective-permute-done | bytes 1114144 | tf_op jit(solution)/shard_map/ppermute | solution.py:152
  145.2 45.0 %collective-permute-done.6 = bf16[1024,1024]{0,1:T(8,128)(2,1)} collective-permute-done((bf16[1024,1024]{0,1:T(8,128)(2,1)}, bf16[1024,1024]{0,1:T(8,128)(2,1)}, u32[]{:S(2)}, u32[]{:S(2)}) %collective-permute-start.6) | collective-permute-done | bytes 2097184 | tf_op jit(solution)/shard_map/ppermute | solution.py:152
  199.1 37.1 %collective-permute-done.7 = bf16[1024,1024]{0,1:T(8,128)(2,1)} collective-permute-done((bf16[1024,1024]{0,1:T(8,128)(2,1)}, bf16[1024,1024]{0,1:T(8,128)(2,1)}, u32[]{:S(2)}, u32[]{:S(2)}) %collective-permute-start.7) | collective-permute-done | bytes 2097184 | tf_op jit(solution)/shard_map/ppermute | solution.py:152
  236.2 11.7 copy.262
  247.9 9.9 fusion.221
  312.1 10.6 fusion.68
  330.8 52.0 %all-to-all-done = bf16[4,160,2048]{2,1,0:T(8,128)(2,1)S(1)} async-done(((bf16[4,160,2048]{2,1,0:T(8,128)(2,1)}), bf16[4,160,2048]{2,1,0:T(8,128)(2,1)S(1)}, u32[]{:S(2)}, u32[]{:S(2)}) %all-to-all-start) | async-done | bytes 2621472 | tf_op jit(solution)/shard_map/all_to_all | solution.py:138
  403.0 51.7 %all-to-all-done.1 = bf16[4,160,2048]{2,1,0:T(8,128)(2,1)} async-done(((bf16[4,160,2048]{2,1,0:T(8,128)(2,1)}), bf16[4,160,2048]{2,1,0:T(8,128)(2,1)}, u32[]{:S(2)}, u32[]{:S(2)}) %all-to-all-start.1) | async-done | bytes 2621472 | tf_op jit(solution)/shard_map/all_to_all | solution.py:138
  458.4 23.2 %fusion.10 = f32[640,5632]{1,0:T(8,128)} fusion(bf16[640,2048]{1,0:T(8,128)(2,1)} %bitcast.47, bf16[1,2048,5632]{2,1,0:T(8,128)(2,1)} %all-gather.18.cloned.1.call-done), kind=kOutput, calls=%fused_computation.10 | convolution fusion | flops 14763950080 | bytes 40108032 | tf_op jit(solution)/shard_map/dot_general | solution.py:82
  481.6 28.5 %multiply_convert_fusion.2 = (bf16[640,5632]{1,0:T(8,128)(2,1)}, f32[640,5632]{1,0:T(8,128)}) fusion(f32[640,5632]{1,0:T(8,128)} %fusion.10, bf16[640,2048]{1,0:T(8,128)(2,1)} %bitcast.47, bf16[1,2048,5632]{2,1,0:T(8,128)(2,1)} %all-gather.20.cloned.1.call-done), kind=kOutput, calls=%fused_computation.17 | convolution fusion | flops 14785576960 | bytes 61734912 | tf_op jit(solution)/shard_map/dot_general | solution.py:82
  517.3 25.7 %convolution_convert_fusion = bf16[5632,2048]{1,0:T(8,128)(2,1)} fusion(bf16[640,5632]{1,0:T(8,128)(2,1)} %get-tuple-element.49, bf16[640,2048]{1,0:T(8,128)(2,1)S(1)} %bitcast.428), kind=kOutput, calls=%fused_computation.12 | convolution fusion | flops 14775484416 | bytes 32899072 | tf_op jit(solution)/shard_map/dot_general | solution.py:86
  543.1 22.6 %fusion.62 = bf16[640,2048]{1,0:T(8,128)(2,1)} fusion(bf16[640,5632]{1,0:T(8,128)(2,1)} %get-tuple-element.49, bf16[1,5632,2048]{2,1,0:T(8,128)(2,1)} %all-gather.22.cloned.1.call-done), kind=kOutput, calls=%fused_computation.111 | convolution fusion | flops 14765260800 | bytes 32899072 | tf_op jit(solution)/shard_map/dot_general | solution.py:82
  569.9 31.4 %multiply_convert_fusion.1 = (bf16[640,5632]{1,0:T(8,128)(2,1)}, bf16[640,5632]{1,0:T(8,128)(2,1)}) fusion(f32[640,5632]{1,0:T(8,128)} %fusion.10, f32[640,5632]{1,0:T(8,128)} %get-tuple-element.183, bf16[640,2048]{1,0:T(8,128)(2,1)} %bitcast.429, bf16[1,5632,2048]{2,1,0:T(8,128)(2,1)} %all-gather.22.cloned.1.call-done), kind=kOutput, calls=%fused_computation.16 | convolution fusion | flops 14810808320 | bytes 68943872 | tf_op jit(solution)/shard_map/dot_general | solution.py:90
  601.3 21.0 %fusion.4 = f32[640,2048]{1,0:T(8,128)S(1)} fusion(bf16[640,5632]{1,0:T(8,128)(2,1)} %get-tuple-element.55, bf16[1,2048,5632]{2,1,0:T(8,128)(2,1)} %all-gather.20.cloned.1.call-done), kind=kOutput, calls=%fused_computation.4 | convolution fusion | flops 14763950080 | bytes 35520512 | tf_op jit(solution)/shard_map/dot_general | solution.py:90
  622.3 19.2 %add_convert_fusion.1 = bf16[640,2048]{1,0:T(8,128)(2,1)} fusion(f32[640,2048]{1,0:T(8,128)S(1)} %fusion.4, bf16[640,5632]{1,0:T(8,128)(2,1)S(1)} %copy-done.143, bf16[1,2048,5632]{2,1,0:T(8,128)(2,1)} %all-gather.18.cloned.1.call-done), kind=kOutput, calls=%fused_computation.70 | convolution fusion | flops 14766571520 | bytes 38141952 | tf_op jit(solution)/shard_map/dot_general | solution.py:90
  646.7 25.9 %convolution_convert_fusion.1 = bf16[2048,5632]{1,0:T(8,128)(2,1)} fusion(bf16[640,2048]{1,0:T(8,128)(2,1)} %bitcast.47, bf16[640,5632]{1,0:T(8,128)(2,1)} %get-tuple-element.55), kind=kOutput, calls=%fused_computation.13 | convolution fusion | flops 14775484416 | bytes 32899072 | tf_op jit(solution)/shard_map/dot_general | solution.py:86
  672.6 26.2 %convolution_convert_fusion.2 = bf16[2048,5632]{1,0:T(8,128)(2,1)} fusion(bf16[640,2048]{1,0:T(8,128)(2,1)} %bitcast.47, bf16[640,5632]{1,0:T(8,128)(2,1)} %get-tuple-element.54), kind=kOutput, calls=%fused_computation.14 | convolution fusion | flops 14775484416 | bytes 32899072 | tf_op jit(solution)/shard_map/dot_general | solution.py:86
  730.6 57.1 %all-to-all-done.5 = bf16[4,160,2048]{2,1,0:T(8,128)(2,1)S(1)} async-done(((bf16[4,160,2048]{2,1,0:T(8,128)(2,1)}), bf16[4,160,2048]{2,1,0:T(8,128)(2,1)S(1)}, u32[]{:S(2)}, u32[]{:S(2)}) %all-to-all-start.5) | async-done | bytes 2621472 | tf_op jit(solution)/shard_map/all_to_all | solution.py:138
  867.1 11.5 fusion.65
  878.6 12.9 %convolution_convert_fusion.4 = bf16[2048,2048]{1,0:T(8,128)(2,1)} fusion(bf16[640,2048]{0,1:T(8,128)(2,1)} %copy-done.58, bf16[640,2048]{1,0:T(8,128)(2,1)S(1)} %bitcast.427), kind=kOutput, calls=%fused_computation.63 | convolution fusion | flops 5372903424 | bytes 13631488 | tf_op jit(solution)/shard_map/dot_general | solution.py:86
  902.5 11.8 convolution_convert_fusion.3
  920.0 8.8 fusion.39
  937.1 30.9 %collective-permute-done.10 = bf16[1024,1024]{0,1:T(8,128)(2,1)} collective-permute-done((bf16[1024,1024]{0,1:T(8,128)(2,1)}, bf16[1024,1024]{0,1:T(8,128)(2,1)}, u32[]{:S(2)}, u32[]{:S(2)}) %collective-permute-start.10) | collective-permute-done | bytes 2097184 | tf_op jit(solution)/shard_map/ppermute | solution.py:152
  985.1 22.2 %collective-permute-done.15 = bf16[2,256,1024]{2,1,0:T(8,128)(2,1)S(1)} collective-permute-done((bf16[2,256,1024]{2,1,0:T(8,128)(2,1)S(1)}, bf16[2,256,1024]{2,1,0:T(8,128)(2,1)S(1)}, u32[]{:S(2)}, u32[]{:S(2)}) %collective-permute-start.15) | collective-permute-done | bytes 1048608 | tf_op jit(solution)/shard_map/ppermute | solution.py:227
  1010.7 17.4 %collective-permute-done.14 = bf16[256,1024]{1,0:T(8,128)(2,1)S(1)} collective-permute-done((bf16[256,1024]{1,0:T(8,128)(2,1)S(1)}, bf16[256,1024]{1,0:T(8,128)(2,1)S(1)}, u32[]{:S(2)}, u32[]{:S(2)}) %collective-permute-start.14) | collective-permute-done | bytes 524320 | tf_op jit(solution)/shard_map/ppermute | solution.py:227
  1057.4 27.3 %collective-permute-done.17 = bf16[256,2048]{1,0:T(8,128)(2,1)S(1)} collective-permute-done((bf16[256,2048]{1,0:T(8,128)(2,1)S(1)}, bf16[256,2048]{1,0:T(8,128)(2,1)S(1)}, u32[]{:S(2)}, u32[]{:S(2)}) %collective-permute-start.17) | collective-permute-done | bytes 1048608 | tf_op jit(solution)/shard_map/ppermute | solution.py:152
  1087.1 24.5 %collective-permute-done.18 = bf16[256,2048]{1,0:T(8,128)(2,1)S(1)} collective-permute-done((bf16[256,2048]{1,0:T(8,128)(2,1)S(1)}, bf16[256,2048]{1,0:T(8,128)(2,1)S(1)}, u32[]{:S(2)}, u32[]{:S(2)}) %collective-permute-start.18) | collective-permute-done | bytes 1048608 | tf_op jit(solution)/shard_map/ppermute | solution.py:152
  1126.2 14.5 %collective-permute-done.21 = bf16[2,256,1024]{2,1,0:T(8,128)(2,1)S(1)} collective-permute-done((bf16[2,256,1024]{2,1,0:T(8,128)(2,1)S(1)}, bf16[2,256,1024]{2,1,0:T(8,128)(2,1)S(1)}, u32[]{:S(2)}, u32[]{:S(2)}) %collective-permute-start.21) | collective-permute-done | bytes 1048608 | tf_op jit(solution)/shard_map/ppermute | solution.py:227
  1188.8 37.2 %reduce-scatter.7.cloned.1.call-done = bf16[256,1152]{0,1:T(8,128)(2,1)} async-done(((bf16[2048,1152]{0,1:T(8,128)(2,1)}), bf16[256,1152]{0,1:T(8,128)(2,1)}) %reduce-scatter.7.cloned.1.call-update) | async-done | bytes 589840 | tf_op jit(solution)/shard_map/reduce_scatter | solution.py:223
  1236.9 11.6 all-to-all-done.6
  (632 shorter events, 446.9 us)
Async XLA Ops:
  7.2 111.6 %all-gather.12.cloned.1.call-start = ((), (), s32[]{:S(2)}) async-start(), calls=%async_computation.11 | async-start | bytes 5308416 | tf_op jit(solution)/shard_map/all_gather | solution.py:304
  29.2 207.0 %all-gather.14.cloned.1.call-start = ((), (), s32[]{:S(2)}) async-start(), calls=%async_computation.16 | async-start | bytes 9437184 | tf_op jit(solution)/shard_map/all_gather | solution.py:219
  29.9 282.1 %all-gather.16.cloned.1.call-start = ((), (), s32[]{:S(2)}) async-start(), calls=%async_computation.17 | async-start | bytes 9437184 | tf_op jit(solution)/shard_map/all_gather | solution.py:219
  30.7 427.7 %all-gather.18.cloned.1.call-start = ((), (), s32[]{:S(2)}) async-start(), calls=%async_computation.18 | async-start | bytes 25952256 | tf_op jit(solution)/shard_map/all_gather | solution.py:219
  31.3 450.4 %all-gather.20.cloned.1.call-start = ((), (), s32[]{:S(2)}) async-start(), calls=%async_computation.19 | async-start | bytes 25952256 | tf_op jit(solution)/shard_map/all_gather | solution.py:219
  31.8 511.2 %all-gather.22.cloned.1.call-start = ((), (), s32[]{:S(2)}) async-start(), calls=%async_computation.20 | async-start | bytes 25952256 | tf_op jit(solution)/shard_map/all_gather | solution.py:219
  33.6 28.6 %collective-permute-start = (bf16[256,2176]{1,0:T(8,128)(2,1)S(1)}, bf16[256,2176]{1,0:T(8,128)(2,1)}, u32[]{:S(2)}, u32[]{:S(2)}) collective-permute-start(bf16[256,2176]{1,0:T(8,128)(2,1)S(1)} %concatenate.58), channel_id=1, source_target_pairs={{0,1},{1,2},{2,3},{3,0},{4,5},{5,6},{6,7},{7,4},{8,9},{9,10},{10,1... | collective-permute-start | bytes 3342344 | tf_op jit(solution)/shard_map/ppermute | solution.py:152
  62.1 27.0 %collective-permute-start.1 = (bf16[256,2176]{1,0:T(8,128)(2,1)}, bf16[256,2176]{1,0:T(8,128)(2,1)}, u32[]{:S(2)}, u32[]{:S(2)}) collective-permute-start(bf16[256,2176]{1,0:T(8,128)(2,1)} %collective-permute-done), channel_id=1, source_target_pairs={{0,1},{1,2},{2,3},{3,0},{4,5},{5,6},{6,7},{7,4},{8,9},{9,10},{10,1... | collective-permute-start | bytes 3342344 | tf_op jit(solution)/shard_map/ppermute | solution.py:152
  143.9 46.3 %collective-permute-start.6 = (bf16[1024,1024]{0,1:T(8,128)(2,1)}, bf16[1024,1024]{0,1:T(8,128)(2,1)}, u32[]{:S(2)}, u32[]{:S(2)}) collective-permute-start(bf16[1024,1024]{0,1:T(8,128)(2,1)} %pad_maximum_fusion.4), channel_id=1, source_target_pairs={{0,1},{1,2},{2,3},{3,0},{4,5},{5,6},{6,7},{7,4},{8,9},{9,10},{10,1... | collective-permute-start | bytes 6291464 | tf_op jit(solution)/shard_map/ppermute | solution.py:152
  190.2 45.9 %collective-permute-start.7 = (bf16[1024,1024]{0,1:T(8,128)(2,1)}, bf16[1024,1024]{0,1:T(8,128)(2,1)}, u32[]{:S(2)}, u32[]{:S(2)}) collective-permute-start(bf16[1024,1024]{0,1:T(8,128)(2,1)} %collective-permute-done.6), channel_id=1, source_target_pairs={{0,1},{1,2},{2,3},{3,0},{4,5},{5,6},{6,7},{7,4},{8,9},{9,10},{10,1... | collective-permute-start | bytes 6291464 | tf_op jit(solution)/shard_map/ppermute | solution.py:152
  236.2 62.2 %collective-permute-start.8 = (bf16[1024,1024]{0,1:T(8,128)(2,1)}, bf16[1024,1024]{0,1:T(8,128)(2,1)}, u32[]{:S(2)}, u32[]{:S(2)}) collective-permute-start(bf16[1024,1024]{0,1:T(8,128)(2,1)} %collective-permute-done.7), channel_id=1, source_target_pairs={{0,1},{1,2},{2,3},{3,0},{4,5},{5,6},{6,7},{7,4},{8,9},{9,10},{10,1... | collective-permute-start | bytes 6291464 | tf_op jit(solution)/shard_map/ppermute | solution.py:152
  322.7 60.1 %all-to-all-start = ((bf16[4,160,2048]{2,1,0:T(8,128)(2,1)}), bf16[4,160,2048]{2,1,0:T(8,128)(2,1)S(1)}, u32[]{:S(2)}, u32[]{:S(2)}) async-start(bf16[4,160,2048]{2,1,0:T(8,128)(2,1)} %bitcast.430), calls=%async_computation | async-start | bytes 5242880 | tf_op jit(solution)/shard_map/all_to_all | solution.py:138
  390.9 63.8 %all-to-all-start.1 = ((bf16[4,160,2048]{2,1,0:T(8,128)(2,1)}), bf16[4,160,2048]{2,1,0:T(8,128)(2,1)}, u32[]{:S(2)}, u32[]{:S(2)}) async-start(bf16[4,160,2048]{2,1,0:T(8,128)(2,1)} %bitcast.46), calls=%async_computation.1 | async-start | bytes 5242880 | tf_op jit(solution)/shard_map/all_to_all | solution.py:138
  454.6 62.6 %all-to-all-start.2 = ((bf16[4,160,2048]{2,1,0:T(8,128)(2,1)}), bf16[4,160,2048]{2,1,0:T(8,128)(2,1)S(1)}, u32[]{:S(2)}, u32[]{:S(2)}) async-start(bf16[4,160,2048]{2,1,0:T(8,128)(2,1)} %bitcast.388), calls=%async_computation.2 | async-start | bytes 5242880 | tf_op jit(solution)/shard_map/all_to_all | solution.py:138
  458.3 329.4 %reduce-scatter.5.cloned.1.call-start = ((), (), s32[]{:S(2)}) async-start(), calls=%async_computation.12 | async-start | bytes 25952256 | tf_op jit(solution)/shard_map/reduce_scatter | solution.py:223
  565.6 75.9 %all-to-all-start.3 = ((bf16[4,160,2048]{2,1,0:T(8,128)(2,1)}), bf16[4,160,2048]{2,1,0:T(8,128)(2,1)S(1)}, u32[]{:S(2)}, u32[]{:S(2)}) async-start(bf16[4,160,2048]{2,1,0:T(8,128)(2,1)} %bitcast.434), calls=%async_computation.3 | async-start | bytes 5242880 | tf_op jit(solution)/shard_map/all_to_all | solution.py:138
  641.5 63.6 %all-to-all-start.4 = ((bf16[4,160,2048]{2,1,0:T(8,128)(2,1)}), bf16[4,160,2048]{2,1,0:T(8,128)(2,1)}, u32[]{:S(2)}, u32[]{:S(2)}) async-start(bf16[4,160,2048]{2,1,0:T(8,128)(2,1)} %bitcast.433), calls=%async_computation.4 | async-start | bytes 5242880 | tf_op jit(solution)/shard_map/all_to_all | solution.py:138
  646.7 531.4 %reduce-scatter.11.cloned.1.call-start = ((), (), s32[]{:S(2)}) async-start(), calls=%async_computation.15 | async-start | bytes 25952256 | tf_op jit(solution)/shard_map/reduce_scatter | solution.py:223
  725.9 61.8 %all-to-all-start.5 = ((bf16[4,160,2048]{2,1,0:T(8,128)(2,1)}), bf16[4,160,2048]{2,1,0:T(8,128)(2,1)S(1)}, u32[]{:S(2)}, u32[]{:S(2)}) async-start(bf16[4,160,2048]{2,1,0:T(8,128)(2,1)} %bitcast.65), calls=%async_computation.5 | async-start | bytes 5242880 | tf_op jit(solution)/shard_map/all_to_all | solution.py:138
  729.8 453.6 %reduce-scatter.9.cloned.1.call-start = ((), (), s32[]{:S(2)}) async-start(), calls=%async_computation.14 | async-start | bytes 25952256 | tf_op jit(solution)/shard_map/reduce_scatter | solution.py:223
  730.6 495.4 %reduce-scatter.7.cloned.1.call-start = ((), (), s32[]{:S(2)}) async-start(), calls=%async_computation.13 | async-start | bytes 5308416 | tf_op jit(solution)/shard_map/reduce_scatter | solution.py:223
  820.4 71.2 %collective-permute-start.9 = (bf16[1024,1024]{0,1:T(8,128)(2,1)}, bf16[1024,1024]{0,1:T(8,128)(2,1)}, u32[]{:S(2)}, u32[]{:S(2)}) collective-permute-start(bf16[1024,1024]{0,1:T(8,128)(2,1)} %pad_maximum_fusion.5), channel_id=1, source_target_pairs={{0,1},{1,2},{2,3},{3,0},{4,5},{5,6},{6,7},{7,4},{8,9},{9,10},{10,1... | collective-permute-start | bytes 6291464 | tf_op jit(solution)/shard_map/ppermute | solution.py:152
  896.8 32.1 %collective-permute-start.12 = (bf16[2,2,256,2048]{3,2,1,0:T(8,128)(2,1)}, bf16[2,2,256,2048]{3,2,1,0:T(8,128)(2,1)}, u32[]{:S(2)}, u32[]{:S(2)}) collective-permute-start(bf16[2,2,256,2048]{3,2,1,0:T(8,128)(2,1)} %dynamic-slice_bitcast_fusion.1), channel_id=1, source_target_pairs={{0,4},{4,0},{8,12},{12,8},{16,20},{20,16},{24,28},{28,24},{1,5},{5... | collective-permute-start | bytes 12582920 | tf_op jit(solution)/shard_map/ppermute | solution.py:227
  918.3 49.7 %collective-permute-start.10 = (bf16[1024,1024]{0,1:T(8,128)(2,1)}, bf16[1024,1024]{0,1:T(8,128)(2,1)}, u32[]{:S(2)}, u32[]{:S(2)}) collective-permute-start(bf16[1024,1024]{0,1:T(8,128)(2,1)} %fusion.52), channel_id=1, source_target_pairs={{0,1},{1,2},{2,3},{3,0},{4,5},{5,6},{6,7},{7,4},{8,9},{9,10},{10,1... | collective-permute-start | bytes 6291464 | tf_op jit(solution)/shard_map/ppermute | solution.py:152
  935.3 46.5 %collective-permute-start.13 = (bf16[2,256,1024]{2,1,0:T(8,128)(2,1)S(1)}, bf16[2,256,1024]{2,1,0:T(8,128)(2,1)}, u32[]{:S(2)}, u32[]{:S(2)}) collective-permute-start(bf16[2,256,1024]{2,1,0:T(8,128)(2,1)S(1)} %dynamic-slice_bitcast_fusion.5), channel_id=1, source_target_pairs={{0,8},{4,12},{8,0},{12,4},{16,24},{20,28},{24,16},{28,20},{1,9},{5... | collective-permute-start | bytes 3145736 | tf_op jit(solution)/shard_map/ppermute | solution.py:227
  971.9 61.6 %collective-permute-start.11 = (bf16[1024,1024]{0,1:T(8,128)(2,1)}, bf16[1024,1024]{0,1:T(8,128)(2,1)S(1)}, u32[]{:S(2)}, u32[]{:S(2)}) collective-permute-start(bf16[1024,1024]{0,1:T(8,128)(2,1)} %fusion.51), channel_id=1, source_target_pairs={{0,1},{1,2},{2,3},{3,0},{4,5},{5,6},{6,7},{7,4},{8,9},{9,10},{10,1... | collective-permute-start | bytes 6291464 | tf_op jit(solution)/shard_map/ppermute | solution.py:152
  972.2 35.1 %collective-permute-start.15 = (bf16[2,256,1024]{2,1,0:T(8,128)(2,1)S(1)}, bf16[2,256,1024]{2,1,0:T(8,128)(2,1)S(1)}, u32[]{:S(2)}, u32[]{:S(2)}) collective-permute-start(bf16[2,256,1024]{2,1,0:T(8,128)(2,1)S(1)} %dynamic-slice_bitcast_fusion.4), channel_id=1, source_target_pairs={{0,16},{4,20},{8,24},{12,28},{16,0},{20,4},{24,8},{28,12},{1,17},{... | collective-permute-start | bytes 3145736 | tf_op jit(solution)/shard_map/ppermute | solution.py:227
  983.6 44.5 %collective-permute-start.14 = (bf16[256,1024]{1,0:T(8,128)(2,1)S(1)}, bf16[256,1024]{1,0:T(8,128)(2,1)S(1)}, u32[]{:S(2)}, u32[]{:S(2)}) collective-permute-start(bf16[256,1024]{1,0:T(8,128)(2,1)S(1)} %dynamic-slice_bitcast_fusion.9), channel_id=1, source_target_pairs={{0,16},{4,20},{8,24},{12,28},{16,0},{20,4},{24,8},{28,12},{1,17},{... | collective-permute-start | bytes 1572872 | tf_op jit(solution)/shard_map/ppermute | solution.py:227
  1049.0 63.0 %collective-permute-start.20 = (bf16[2,2,256,2048]{3,2,1,0:T(8,128)(2,1)S(1)}, bf16[2,2,256,2048]{3,2,1,0:T(8,128)(2,1)S(1)}, u32[]{:S(2)}, u32[]{:S(2)}) collective-permute-start(bf16[2,2,256,2048]{3,2,1,0:T(8,128)(2,1)S(1)} %dynamic-slice_bitcast_fusion), channel_id=1, source_target_pairs={{0,4},{4,0},{8,12},{12,8},{16,20},{20,16},{24,28},{28,24},{1,5},{5... | collective-permute-start | bytes 12582920 | tf_op jit(solution)/shard_map/ppermute | solution.py:227
  1057.4 27.4 %collective-permute-start.17 = (bf16[256,2048]{1,0:T(8,128)(2,1)S(1)}, bf16[256,2048]{1,0:T(8,128)(2,1)S(1)}, u32[]{:S(2)}, u32[]{:S(2)}) collective-permute-start(bf16[256,2048]{1,0:T(8,128)(2,1)S(1)} %fusion.93), channel_id=1, source_target_pairs={{0,1},{1,2},{2,3},{3,0},{4,5},{5,6},{6,7},{7,4},{8,9},{9,10},{10,1... | collective-permute-start | bytes 3145736 | tf_op jit(solution)/shard_map/ppermute | solution.py:152
  1085.1 26.5 %collective-permute-start.18 = (bf16[256,2048]{1,0:T(8,128)(2,1)S(1)}, bf16[256,2048]{1,0:T(8,128)(2,1)S(1)}, u32[]{:S(2)}, u32[]{:S(2)}) collective-permute-start(bf16[256,2048]{1,0:T(8,128)(2,1)S(1)} %fusion.84), channel_id=1, source_target_pairs={{0,1},{1,2},{2,3},{3,0},{4,5},{5,6},{6,7},{7,4},{8,9},{9,10},{10,1... | collective-permute-start | bytes 3145736 | tf_op jit(solution)/shard_map/ppermute | solution.py:152
  1111.9 31.8 %collective-permute-start.19 = (bf16[256,2048]{1,0:T(8,128)(2,1)S(1)}, bf16[256,2048]{1,0:T(8,128)(2,1)}, u32[]{:S(2)}, u32[]{:S(2)}) collective-permute-start(bf16[256,2048]{1,0:T(8,128)(2,1)S(1)} %fusion.85), channel_id=1, source_target_pairs={{0,1},{1,2},{2,3},{3,0},{4,5},{5,6},{6,7},{7,4},{8,9},{9,10},{10,1... | collective-permute-start | bytes 3145736 | tf_op jit(solution)/shard_map/ppermute | solution.py:152
  (168 other events, 2511.5 us)
Sparse Core Ops, SparseCore 0:
  29.3 41.1 all-gather.11
  72.3 54.2 all-gather.13
  128.5 54.2 all-gather.15
  184.6 116.3 all-gather.17
  302.6 116.3 all-gather.19
  420.8 116.3 all-gather.21
  543.1 144.5 reduce-scatter.4
  705.3 145.5 reduce-scatter.10
  854.6 185.8 reduce-scatter.8
  1173.1 52.8 reduce-scatter.6

commit v4 on v3

--- a/solution.py
+++ b/solution.py
@@ -112,8 +112,7 @@
     return (jax.nn.softmax(chosen, -1), picks)
 
 
-def router_back(gates, picks, picked, stream_grad):
-    gate_grad = jnp.sum(picked * stream_grad[None], 2).T
+def router_back(gates, picks, gate_grad):
     chosen_grad = gates * (gate_grad - jnp.sum(gates * gate_grad, 1, keepdims=True))
     return jnp.sum(picks * chosen_grad[:, :, None], 1)
 
@@ -127,6 +126,14 @@
     scaled = (gates.T[:, :, None] * grad_in[None]).astype(bf16)
     packed = (mm_tn(place[0], scaled[0]) + mm_tn(place[1], scaled[1])).astype(bf16)
     return packed.reshape(experts, -1, grad_in.shape[1])
+
+
+def as_columns(values):
+    high = lax.reduce_precision(values, 8, 7)
+    rest = values - high
+    middle = lax.reduce_precision(rest, 8, 7)
+    columns = jnp.stack([high, middle, rest - middle], 1).astype(bf16)
+    return jnp.pad(columns, ((0, 0), (0, PAD - 3)))
 
 
 def take_back(place, returned):
@@ -336,7 +343,6 @@
     kv_own = jnp.concatenate(
         [rotate(kv_raw[:, :width], tree_cos, tree_sin), kv_raw[:, width:]], 1
     ).astype(bf16)
-    kv_blocks = ring_gather(kv_own, experts)
 
     named = jnp.any(tree_routes == own, 1).reshape(experts, row_count)
     rank = earlier_count(named.T).T
@@ -362,12 +368,19 @@
 
     attended = jnp.zeros(queries.shape, bf16)
     saved = []
+    kv_block = kv_own
+    kv_next = ring_step(kv_own, experts)
     for k in range(experts):
+        if k:
+            kv_block = kv_next
+            if k == 1:
+                kv_block, queries = lax.optimization_barrier((kv_block, queries))
+            else:
+                kv_block, attended = lax.optimization_barrier((kv_block, attended))
+            if k < experts - 1:
+                kv_next = ring_step(kv_block, experts)
         start = backs[k] * width
         group_queries = lax.dynamic_slice_in_dim(queries, start, width, 1)
-        kv_block = kv_blocks[k]
-        if k:
-            kv_block, attended = lax.optimization_barrier((kv_block, attended))
         keys, values = kv_block[:, :width], kv_block[:, width:]
         group_attended, log_total = attend(group_queries, keys, values, key_mask)
         attended = lax.dynamic_update_slice_in_dim(attended, group_attended, start, 1)
@@ -387,32 +400,38 @@
     ffn_place = placement_of(ffn_route, capacity, experts)
     ffn_rows = exchange(send_rows(ffn_place, normed_two, experts)).reshape(-1, model_width)
     grad_out = cotangent.astype(f32)
-    ffn_rows, packed_grads = lax.optimization_barrier(
-        (ffn_rows, send_grads(ffn_place, ffn_gate, grad_out, experts))
-    )
-    ffn_grad_rows = exchange(packed_grads).reshape(-1, model_width)
+    slot_gate = jnp.sum(ffn_place.astype(f32) * ffn_gate.T[:, :, None], (0, 1))
+    packed_grads = jnp.concatenate(
+        [
+            send_rows(ffn_place, cotangent, experts),
+            as_columns(slot_gate).reshape(experts, capacity, PAD),
+        ],
+        2,
+    )
+    ffn_rows, packed_grads = lax.optimization_barrier((ffn_rows, packed_grads))
+    received_grads = exchange(packed_grads).reshape(experts * capacity, -1)
+    out_rows = received_grads[:, :model_width]
+    row_gate = jnp.sum(received_grads[:, model_width:].astype(f32), 1, keepdims=True)
+    ffn_grad_rows = (row_gate * out_rows.astype(f32)).astype(bf16)
     gate_value = mm(ffn_rows, gate_all)
     up_value = mm(ffn_rows, up_all)
     sigmoid_gate = jax.nn.sigmoid(gate_value)
     hidden = (gate_value * sigmoid_gate * up_value).astype(bf16)
     down_part = mm_tn(hidden, ffn_grad_rows).astype(bf16)
-    down_part, hidden, ffn_grad_rows = lax.optimization_barrier((down_part, hidden, ffn_grad_rows))
+    down_part, hidden, out_rows = lax.optimization_barrier((down_part, hidden, out_rows))
     down_sum = reduce_dp(down_part)
-    ffn_branch = mm(hidden, down_all).astype(bf16)
-    ffn_branch, ffn_grad_rows = lax.optimization_barrier((ffn_branch, ffn_grad_rows))
-    ffn_back = exchange(ffn_branch.reshape(experts, capacity, -1))
-    hidden_grad = mm_nt(ffn_grad_rows, down_all)
+    hidden_pull = mm_nt(out_rows, down_all)
+    row_pull = jnp.sum(hidden.astype(f32) * hidden_pull, 1)
+    hidden_grad = row_gate * hidden_pull
     gate_grad = (
         hidden_grad * up_value * sigmoid_gate * (1.0 + gate_value * (1.0 - sigmoid_gate))
     ).astype(bf16)
     up_grad = (hidden_grad * gate_value * sigmoid_gate).astype(bf16)
     ffn_rows_grad = (mm_nt(gate_grad, gate_all) + mm_nt(up_grad, up_all)).astype(bf16)
-    ffn_rows_grad, gate_grad, up_grad, ffn_back = lax.optimization_barrier(
-        (ffn_rows_grad, gate_grad, up_grad, ffn_back)
-    )
-    ffn_picked = take_back(ffn_place, ffn_back)
-    result = mixed_stream + jnp.sum(ffn_gate.T[:, :, None] * ffn_picked, 0)
-    ffn_logit_grad = router_back(ffn_gate, ffn_picks, ffn_picked, grad_out)
+    ffn_rows_grad = jnp.concatenate([ffn_rows_grad, as_columns(row_pull)], 1)
+    ffn_rows_grad, gate_grad, up_grad = lax.optimization_barrier(
+        (ffn_rows_grad, gate_grad, up_grad)
+    )
     ffn_rows_back = exchange(ffn_rows_grad.reshape(experts, capacity, -1)).reshape(
         experts * capacity, -1
     )
@@ -423,19 +442,26 @@
     )
     gate_sum = reduce_dp(gate_part)
     up_sum = reduce_dp(up_part)
-    normed_two_grad = mm(ffn_place[0] + ffn_place[1], ffn_rows_back) + jnp.dot(
+    gate_pull = jnp.sum(take_back(ffn_place, ffn_rows_back[:, model_width:]), 2).T
+    ffn_logit_grad = router_back(ffn_gate, ffn_picks, gate_pull)
+    normed_two_grad = mm(ffn_place[0] + ffn_place[1], ffn_rows_back[:, :model_width]) + jnp.dot(
         ffn_logit_grad, ffn_all.astype(f32).T, precision=highest
     )
     gain_two_part = jnp.sum(normed_two_grad * mixed_stream * inverse_two, 0)
     mixed_grad = grad_out + norm_back(mixed_stream, inverse_two, gain_second, normed_two_grad)
 
-    att_logit_grad = router_back(att_gate, att_picks, att_picked, mixed_grad)
-    att_grad_rows = exchange(send_grads(att_place, att_gate, mixed_grad, experts)).reshape(
-        -1, model_width
-    )
+    att_logit_grad = router_back(
+        att_gate, att_picks, jnp.sum(att_picked * mixed_grad[None], 2).T
+    )
+    packed_grads, hidden = lax.optimization_barrier(
+        (send_grads(att_place, att_gate, mixed_grad, experts), hidden)
+    )
+    ffn_branch = mm(hidden, down_all).astype(bf16)
+    att_grad_rows, ffn_branch = lax.optimization_barrier((exchange(packed_grads), ffn_branch))
+    att_grad_rows = att_grad_rows.reshape(-1, model_width)
+    ffn_back = exchange(ffn_branch.reshape(experts, capacity, -1))
     att_grad_rows, down_sum = lax.optimization_barrier((att_grad_rows, down_sum))
     attended_grad = mm_nt(att_grad_rows, output_all).astype(bf16)
-    output_part = mm_tn(attended, att_grad_rows).astype(bf16)
     query_grad = jnp.zeros(queries.shape, f32)
     kv_grad = None
     for step in range(1, experts + 1):
@@ -445,19 +471,24 @@
         group_query_grad, key_grad, value_grad = attend_back(*saved[k], group_grad)
         query_grad = lax.dynamic_update_slice_in_dim(query_grad, group_query_grad, start, 1)
         part = jnp.concatenate([key_grad, value_grad], 1)
-        if step == 2:
-            kv_grad, output_part = lax.optimization_barrier((kv_grad, output_part))
-            output_sum = reduce_swaps(output_part)
-        if k == 0:
-            query_raw_grad = rotate_back(query_grad, query_cos, query_sin).astype(bf16)
-            query_part = mm_tn(query_rows, query_raw_grad).astype(bf16)
-            kv_grad, query_part, output_sum = lax.optimization_barrier(
-                (kv_grad, query_part, output_sum)
-            )
-            query_sum = reduce_swaps(query_part)
         if kv_grad is not None:
             part = part + kv_grad.astype(f32)
-        kv_grad = part if k == 0 else ring_step(part.astype(bf16), experts)
+        if k == 0:
+            kv_grad = part
+            continue
+        part = part.astype(bf16)
+        if step == 2:
+            part, att_grad_rows, ffn_back = lax.optimization_barrier(
+                (part, att_grad_rows, ffn_back)
+            )
+        if step == experts - 1:
+            part, query_rows = lax.optimization_barrier((part, query_rows))
+        kv_grad = ring_step(part, experts)
+    ffn_picked = take_back(ffn_place, ffn_back)
+    result = mixed_stream + jnp.sum(ffn_gate.T[:, :, None] * ffn_picked, 0)
+    output_sum = reduce_swaps(mm_tn(attended, att_grad_rows).astype(bf16))
+    query_raw_grad = rotate_back(query_grad, query_cos, query_sin).astype(bf16)
+    query_sum = reduce_swaps(mm_tn(query_rows, query_raw_grad).astype(bf16))
     att_rows_grad = mm_nt(query_raw_grad, query_all).astype(bf16)
     kv_raw_grad = jnp.concatenate(
         [rotate_back(kv_grad[:, :width], tree_cos, tree_sin), kv_grad[:, width:]], 1
@@ -468,19 +499,10 @@
         att_rows_grad.reshape(experts, capacity, -1),
         preferred_element_type=f32,
     )
-    normed_one_grad = None
-    for step in range(1, experts + 1):
-        k = step % experts
-        part = lax.dynamic_index_in_dim(tree_grad, backs[k], 0, keepdims=False)
-        if normed_one_grad is not None:
-            part = part + normed_one_grad.astype(f32)
-        normed_one_grad = part if k == 0 else ring_step(part.astype(bf16), experts)
-    normed_one_grad, query_sum = lax.optimization_barrier((normed_one_grad, query_sum))
-    normed_one_grad = normed_one_grad + jnp.dot(
-        att_logit_grad, att_all.astype(f32).T, precision=highest
-    )
-    gain_one_part = jnp.sum(normed_one_grad * inputs * inverse_one, 0)
-    input_grad = mixed_grad + norm_back(inputs, inverse_one, gain_first, normed_one_grad)
+    router_grad = jnp.dot(att_logit_grad, att_all.astype(f32).T, precision=highest)
+    gain_one_part = jnp.sum(router_grad * inputs * inverse_one, 0) + jnp.sum(
+        tree_grad.reshape(tree_tokens.shape) * tree_tokens * tree_inverse, 0
+    )
     att_router_part = lax.dot_general(
         att_logit_grad, normed_one.astype(f32), (((0,), (0,)), ((), ())), precision=highest
     )
@@ -504,6 +526,20 @@
         ],
         1,
     )
+    normed_one_grad = None
+    for step in range(1, experts + 1):
+        k = step % experts
+        part = lax.dynamic_index_in_dim(tree_grad, backs[k], 0, keepdims=False)
+        if normed_one_grad is not None:
+            part = part + normed_one_grad.astype(f32)
+        normed_one_grad = part if k == 0 else ring_step(part.astype(bf16), experts)
+        if step == 1:
+            normed_one_grad, output_sum = lax.optimization_barrier((normed_one_grad, output_sum))
+    normed_one_grad, query_sum, shared_part = lax.optimization_barrier(
+        (normed_one_grad, query_sum, shared_part)
+    )
+    normed_one_grad = normed_one_grad + router_grad
+    input_grad = mixed_grad + norm_back(inputs, inverse_one, gain_first, normed_one_grad)
     shared_sum = exchange(reduce_dp(shared_part).reshape(experts, shard_rows, -1)).astype(f32)
     kv_sum = (
         shared_sum[:, :, : 2 * width]

time: 1270 us -> 1250 us (0.984)
  waiting for transfers between devices: 540 us -> 415 us
  blocking collectives: 0 us -> 66.5 us
  local copies, waits for them, and re-layouts: 101 us -> 123 us
  other arithmetic: 102 us -> 116 us
    all_to_all x0 -> x1, blocking collectives: none -> 66.5 us  [exchange(): lax.all_to_all(packed, 'expert', split_axis=0, concat_axis=0, tiled=True)]
    ppermute x10, waiting for transfers between devices: 71.4 us -> 15.2 us  [swap(): return lax.ppermute(block, 'dp', [(i, i ^ bit) for i in range(8)])]
    all_to_all x7 -> x6, waiting for transfers between devices: 186 us -> 148 us  [exchange(): lax.all_to_all(packed, 'expert', split_axis=0, concat_axis=0, tiled=True)]
    ppermute x12, waiting for transfers between devices: 234 us -> 208 us  [ring_step(): lax.ppermute(block, 'expert', [(i, (i + 1) % experts) for i in range(expe...]
    dot_general x16 -> x18, matrix products: 112 us -> 120 us  [mm(): return jnp.dot(left, right, preferred_element_type=f32)]
    dot_general x12 -> x11, matrix products: 120 us -> 112 us  [mm_tn(): lax.dot_general(left, right, (((0,), (0,)), ((), ())), preferred_element_...]
    unnamed x324 -> x377, local copies, waits for them, and re-layouts: 35.8 us -> 43.6 us
    all_to_all x7 -> x6, starting transfers between devices: 31 us -> 25.4 us  [exchange(): lax.all_to_all(packed, 'expert', split_axis=0, concat_axis=0, tiled=True)]
  transfers between devices with their start and end apart: 42 -> 41, of which waited for: 24 -> 23; matrix products, arithmetic and copies ran while one was open for 48% -> 52% of each run, Pallas kernels for 0% -> 0%
where the time goes in v4:
time: 1250 us
  matrix products  456 us (36%)
  waiting for transfers between devices  415 us (33%)
  local copies, waits for them, and re-layouts  123 us (10%)
  other arithmetic  116 us (9%)
  blocking collectives  66.5 us (5%)
  starting transfers between devices  53 us (4%)
  between operations  17.7 us (1%)
    ppermute x12, waiting for transfers between devices, ring_step(): lax.ppermute(block, 'expert', [(i, (i + 1) % experts) for i in range(expe...  208 us
    all_to_all x6, waiting for transfers between devices, exchange(): lax.all_to_all(packed, 'expert', split_axis=0, concat_axis=0, tiled=True)  148 us
    dot_general x18, matrix products, mm(): return jnp.dot(left, right, preferred_element_type=f32)  120 us
    dot_general x11, matrix products, mm_tn(): lax.dot_general(left, right, (((0,), (0,)), ((), ())), preferred_element_...  112 us
    dot_general x6, matrix products, mm_nt(): lax.dot_general(left, right, (((1,), (1,)), ((), ())), preferred_element_...  103 us
    all_to_all x1, blocking collectives, exchange(): lax.all_to_all(packed, 'expert', split_axis=0, concat_axis=0, tiled=True)  66.5 us
    unnamed x377, local copies, waits for them, and re-layouts  43.6 us
    dot_general x4, matrix products, attend_back(): jnp.einsum('qhd,khd->hqk', grad_heads, value_heads, preferred_element_typ...  32.2 us
  transfers between devices with their start and end apart: 41, of which 23 were waited for; matrix products, arithmetic and copies ran while one was open for 52% of the time, Pallas kernels for 0%

profile of v4, /device:TPU:0, one launch (start us, length us, event | category | flops | bytes accessed | tf_op | source)
XLA Modules:
  0.0 1246.9 jit_solution(13157242885729667679)
XLA Ops:
  38.4 24.9 %collective-permute-done = bf16[256,2176]{1,0:T(8,128)(2,1)} collective-permute-done((bf16[256,2176]{1,0:T(8,128)(2,1)S(1)}, bf16[256,2176]{1,0:T(8,128)(2,1)}, u32[]{:S(2)}, u32[]{:S(2)}) %collective-permute-start) | collective-permute-done | bytes 1114144 | tf_op jit(solution)/shard_map/ppermute | solution.py:159
  68.2 22.1 %collective-permute-done.1 = bf16[256,2176]{1,0:T(8,128)(2,1)} collective-permute-done((bf16[256,2176]{1,0:T(8,128)(2,1)}, bf16[256,2176]{1,0:T(8,128)(2,1)}, u32[]{:S(2)}, u32[]{:S(2)}) %collective-permute-start.1) | collective-permute-done | bytes 1114144 | tf_op jit(solution)/shard_map/ppermute | solution.py:159
  94.2 22.1 %collective-permute-done.2 = bf16[256,2176]{1,0:T(8,128)(2,1)S(1)} collective-permute-done((bf16[256,2176]{1,0:T(8,128)(2,1)}, bf16[256,2176]{1,0:T(8,128)(2,1)S(1)}, u32[]{:S(2)}, u32[]{:S(2)}) %collective-permute-start.2) | collective-permute-done | bytes 1114144 | tf_op jit(solution)/shard_map/ppermute | solution.py:159
  150.4 12.4 copy.272
  162.8 10.1 fusion.233
  173.9 20.6 %collective-permute-done.6 = bf16[1024,1024]{0,1:T(8,128)(2,1)} collective-permute-done((bf16[1024,1024]{0,1:T(8,128)(2,1)}, bf16[1024,1024]{0,1:T(8,128)(2,1)}, u32[]{:S(2)}, u32[]{:S(2)}) %collective-permute-start.6) | collective-permute-done | bytes 2097184 | tf_op jit(solution)/shard_map/ppermute | solution.py:159
  223.1 17.2 %collective-permute-done.7 = bf16[1024,1024]{0,1:T(8,128)(2,1)} collective-permute-done((bf16[1024,1024]{0,1:T(8,128)(2,1)}, bf16[1024,1024]{0,1:T(8,128)(2,1)}, u32[]{:S(2)}, u32[]{:S(2)}) %collective-permute-start.7) | collective-permute-done | bytes 2097184 | tf_op jit(solution)/shard_map/ppermute | solution.py:159
  253.9 31.2 %collective-permute-done.8 = bf16[1024,1024]{0,1:T(8,128)(2,1)S(1)} collective-permute-done((bf16[1024,1024]{0,1:T(8,128)(2,1)}, bf16[1024,1024]{0,1:T(8,128)(2,1)S(1)}, u32[]{:S(2)}, u32[]{:S(2)}) %collective-permute-start.8) | collective-permute-done | bytes 2097184 | tf_op jit(solution)/shard_map/ppermute | solution.py:159
  296.9 10.3 fusion.72
  316.3 48.7 %all-to-all-done = bf16[4,160,2048]{2,1,0:T(8,128)(2,1)S(1)} async-done(((bf16[4,160,2048]{2,1,0:T(8,128)(2,1)}), bf16[4,160,2048]{2,1,0:T(8,128)(2,1)S(1)}, u32[]{:S(2)}, u32[]{:S(2)}) %all-to-all-start) | async-done | bytes 2621472 | tf_op jit(solution)/shard_map/all_to_all | solution.py:145
  386.5 51.6 %all-to-all-done.1 = bf16[4,160,2048]{2,1,0:T(8,128)(2,1)} async-done(((bf16[4,160,2048]{2,1,0:T(8,128)(2,1)}), bf16[4,160,2048]{2,1,0:T(8,128)(2,1)}, u32[]{:S(2)}, u32[]{:S(2)}) %all-to-all-start.1) | async-done | bytes 2621472 | tf_op jit(solution)/shard_map/all_to_all | solution.py:145
  438.1 66.5 %all_to_all.35 = bf16[4,160,2176]{2,1,0:T(8,128)(2,1)S(1)} all-to-all(bf16[4,160,2176]{2,1,0:T(8,128)(2,1)} %pad_maximum_fusion.2), channel_id=1, replica_groups=mesh['dp'=8,'expert'=4] {'expert'}, dimensions={0} | all-to-all | bytes 5570560 | tf_op jit(solution)/shard_map/all_to_all | solution.py:145
  506.7 23.3 %fusion.10 = f32[640,5632]{1,0:T(8,128)} fusion(bf16[640,2048]{1,0:T(8,128)(2,1)} %bitcast.47, bf16[1,2048,5632]{2,1,0:T(8,128)(2,1)} %all-gather.18.cloned.1.call-done), kind=kOutput, calls=%fused_computation.10 | convolution fusion | flops 14763950080 | bytes 40108032 | tf_op jit(solution)/shard_map/dot_general | solution.py:82
  530.0 28.5 %multiply_convert_fusion.2 = (bf16[640,5632]{1,0:T(8,128)(2,1)}, f32[640,5632]{1,0:T(8,128)}) fusion(f32[640,5632]{1,0:T(8,128)} %fusion.10, bf16[640,2048]{1,0:T(8,128)(2,1)} %bitcast.47, bf16[1,2048,5632]{2,1,0:T(8,128)(2,1)} %all-gather.20.cloned.1.call-done), kind=kOutput, calls=%fused_computation.18 | convolution fusion | flops 14785576960 | bytes 61734912 | tf_op jit(solution)/shard_map/dot_general | solution.py:82
  558.5 24.9 %convolution_convert_fusion = bf16[5632,2048]{1,0:T(8,128)(2,1)} fusion(bf16[640,5632]{1,0:T(8,128)(2,1)} %get-tuple-element.60, f32[640]{0:T(1024)S(1)} %convert_reduce_fusion.2, bf16[640,2176]{1,0:T(8,128)(2,1)S(1)} %bitcast.390), kind=kOutput, calls=%fused_computation.12 | convolution fusion | flops 14779416576 | bytes 32903168 | tf_op jit(solution)/shard_map/dot_general | solution.py:86
  585.1 38.2 %multiply_convert_fusion.1 = (bf16[640,5632]{1,0:T(8,128)(2,1)}, bf16[640,5632]{1,0:T(8,128)(2,1)}, f32[640]{0:T(1024)S(1)}) fusion(f32[640,5632]{1,0:T(8,128)} %fusion.10, f32[640,5632]{1,0:T(8,128)} %get-tuple-element.192, f32[640]{0:T(1024)S(1)} %convert_reduce_fusion.2, bf16[640,5632]{1,0:T(8,128)(2,1)} %get-tuple-element.60, ...), kind=kOutput, calls=%fused_computation.17 | convolution fusion | flops 14825225216 | bytes 76157952 | tf_op jit(solution)/shard_map/dot_general | solution.py:90
  623.5 20.6 %fusion.4 = f32[640,2048]{1,0:T(8,128)S(1)} fusion(bf16[640,5632]{1,0:T(8,128)(2,1)} %get-tuple-element.56, bf16[1,2048,5632]{2,1,0:T(8,128)(2,1)} %all-gather.20.cloned.1.call-done), kind=kOutput, calls=%fused_computation.4 | convolution fusion | flops 14763950080 | bytes 35520512 | tf_op jit(solution)/shard_map/dot_general | solution.py:90
  644.2 18.8 %add_convert_fusion.1 = bf16[640,2048]{1,0:T(8,128)(2,1)S(1)} fusion(f32[640,2048]{1,0:T(8,128)S(1)} %fusion.4, bf16[640,5632]{1,0:T(8,128)(2,1)S(1)} %copy-done.164, bf16[1,2048,5632]{2,1,0:T(8,128)(2,1)} %all-gather.18.cloned.1.call-done), kind=kOutput, calls=%fused_computation.75 | convolution fusion | flops 14766571520 | bytes 38141952 | tf_op jit(solution)/shard_map/dot_general | solution.py:90
  668.5 26.2 %convolution_convert_fusion.1 = bf16[2048,5632]{1,0:T(8,128)(2,1)} fusion(bf16[640,2048]{1,0:T(8,128)(2,1)} %bitcast.47, bf16[640,5632]{1,0:T(8,128)(2,1)} %get-tuple-element.56), kind=kOutput, calls=%fused_computation.13 | convolution fusion | flops 14775484416 | bytes 32899072 | tf_op jit(solution)/shard_map/dot_general | solution.py:86
  694.7 26.1 %convolution_convert_fusion.2 = bf16[2048,5632]{1,0:T(8,128)(2,1)} fusion(bf16[640,2048]{1,0:T(8,128)(2,1)} %bitcast.47, bf16[640,5632]{1,0:T(8,128)(2,1)} %get-tuple-element.55), kind=kOutput, calls=%fused_computation.14 | convolution fusion | flops 14775484416 | bytes 32899072 | tf_op jit(solution)/shard_map/dot_general | solution.py:86
  720.8 11.2 all-to-all-done.3
  756.7 24.1 %fusion.66 = bf16[640,2048]{1,0:T(8,128)(2,1)} fusion(bf16[640,5632]{1,0:T(8,128)(2,1)} %get-tuple-element.60, bf16[1,5632,2048]{2,1,0:T(8,128)(2,1)} %all-gather.22.cloned.1.call-done), kind=kOutput, calls=%fused_computation.114 | convolution fusion | flops 14765260800 | bytes 32899072 | tf_op jit(solution)/shard_map/dot_general | solution.py:82
  789.5 25.3 %all-to-all-done.4 = bf16[4,160,2048]{2,1,0:T(8,128)(2,1)S(1)} async-done(((bf16[4,160,2048]{2,1,0:T(8,128)(2,1)}), bf16[4,160,2048]{2,1,0:T(8,128)(2,1)S(1)}, u32[]{:S(2)}, u32[]{:S(2)}) %all-to-all-start.4) | async-done | bytes 2621472 | tf_op jit(solution)/shard_map/all_to_all | solution.py:145
  872.8 10.8 multiply_convert_fusion.3
  910.9 9.6 fusion.38
  931.8 9.9 fusion.69
  965.1 28.9 %collective-permute-done.10 = bf16[1024,1024]{0,1:T(8,128)(2,1)S(1)} collective-permute-done((bf16[1024,1024]{0,1:T(8,128)(2,1)}, bf16[1024,1024]{0,1:T(8,128)(2,1)S(1)}, u32[]{:S(2)}, u32[]{:S(2)}) %collective-permute-start.10) | collective-permute-done | bytes 2097184 | tf_op jit(solution)/shard_map/ppermute | solution.py:159
  1010.2 31.4 %collective-permute-done.11 = bf16[1024,1024]{0,1:T(8,128)(2,1)S(1)} collective-permute-done((bf16[1024,1024]{0,1:T(8,128)(2,1)S(1)}, bf16[1024,1024]{0,1:T(8,128)(2,1)S(1)}, u32[]{:S(2)}, u32[]{:S(2)}) %collective-permute-start.11) | collective-permute-done | bytes 2097184 | tf_op jit(solution)/shard_map/ppermute | solution.py:159
  1073.3 10.8 convolution_convert_fusion.5
  1113.8 9.6 collective-permute-done.18
  1177.5 31.9 %reduce-scatter.7.cloned.1.call-done = bf16[256,1152]{0,1:T(8,128)(2,1)} async-done(((bf16[2048,1152]{0,1:T(8,128)(2,1)}), bf16[256,1152]{0,1:T(8,128)(2,1)}) %reduce-scatter.7.cloned.1.call-update) | async-done | bytes 589840 | tf_op jit(solution)/shard_map/reduce_scatter | solution.py:230
  1220.4 11.6 all-to-all-done.6
  (701 shorter events, 469.8 us)
Async XLA Ops:
  7.2 115.3 %all-gather.12.cloned.1.call-start = ((), (), s32[]{:S(2)}) async-start(), calls=%async_computation.11 | async-start | bytes 5308416 | tf_op jit(solution)/shard_map/all_gather | solution.py:311
  29.2 121.2 %all-gather.14.cloned.1.call-start = ((), (), s32[]{:S(2)}) async-start(), calls=%async_computation.16 | async-start | bytes 9437184 | tf_op jit(solution)/shard_map/all_gather | solution.py:226
  29.9 266.9 %all-gather.16.cloned.1.call-start = ((), (), s32[]{:S(2)}) async-start(), calls=%async_computation.17 | async-start | bytes 9437184 | tf_op jit(solution)/shard_map/all_gather | solution.py:226
  30.7 476.0 %all-gather.18.cloned.1.call-start = ((), (), s32[]{:S(2)}) async-start(), calls=%async_computation.18 | async-start | bytes 25952256 | tf_op jit(solution)/shard_map/all_gather | solution.py:226
  31.3 498.7 %all-gather.20.cloned.1.call-start = ((), (), s32[]{:S(2)}) async-start(), calls=%async_computation.19 | async-start | bytes 25952256 | tf_op jit(solution)/shard_map/all_gather | solution.py:226
  31.8 551.6 %all-gather.22.cloned.1.call-start = ((), (), s32[]{:S(2)}) async-start(), calls=%async_computation.20 | async-start | bytes 25952256 | tf_op jit(solution)/shard_map/all_gather | solution.py:226
  34.7 28.6 %collective-permute-start = (bf16[256,2176]{1,0:T(8,128)(2,1)S(1)}, bf16[256,2176]{1,0:T(8,128)(2,1)}, u32[]{:S(2)}, u32[]{:S(2)}) collective-permute-start(bf16[256,2176]{1,0:T(8,128)(2,1)S(1)} %concatenate.65), channel_id=1, source_target_pairs={{0,1},{1,2},{2,3},{3,0},{4,5},{5,6},{6,7},{7,4},{8,9},{9,10},{10,1... | collective-permute-start | bytes 3342344 | tf_op jit(solution)/shard_map/ppermute | solution.py:159
  63.3 27.0 %collective-permute-start.1 = (bf16[256,2176]{1,0:T(8,128)(2,1)}, bf16[256,2176]{1,0:T(8,128)(2,1)}, u32[]{:S(2)}, u32[]{:S(2)}) collective-permute-start(bf16[256,2176]{1,0:T(8,128)(2,1)} %collective-permute-done), channel_id=1, source_target_pairs={{0,1},{1,2},{2,3},{3,0},{4,5},{5,6},{6,7},{7,4},{8,9},{9,10},{10,1... | collective-permute-start | bytes 3342344 | tf_op jit(solution)/shard_map/ppermute | solution.py:159
  90.3 26.0 %collective-permute-start.2 = (bf16[256,2176]{1,0:T(8,128)(2,1)}, bf16[256,2176]{1,0:T(8,128)(2,1)S(1)}, u32[]{:S(2)}, u32[]{:S(2)}) collective-permute-start(bf16[256,2176]{1,0:T(8,128)(2,1)} %collective-permute-done.1), channel_id=1, source_target_pairs={{0,1},{1,2},{2,3},{3,0},{4,5},{5,6},{6,7},{7,4},{8,9},{9,10},{10,1... | collective-permute-start | bytes 3342344 | tf_op jit(solution)/shard_map/ppermute | solution.py:159
  148.0 46.5 %collective-permute-start.6 = (bf16[1024,1024]{0,1:T(8,128)(2,1)}, bf16[1024,1024]{0,1:T(8,128)(2,1)}, u32[]{:S(2)}, u32[]{:S(2)}) collective-permute-start(bf16[1024,1024]{0,1:T(8,128)(2,1)} %pad_maximum_fusion.5), channel_id=1, source_target_pairs={{0,1},{1,2},{2,3},{3,0},{4,5},{5,6},{6,7},{7,4},{8,9},{9,10},{10,1... | collective-permute-start | bytes 6291464 | tf_op jit(solution)/shard_map/ppermute | solution.py:159
  194.5 45.8 %collective-permute-start.7 = (bf16[1024,1024]{0,1:T(8,128)(2,1)}, bf16[1024,1024]{0,1:T(8,128)(2,1)}, u32[]{:S(2)}, u32[]{:S(2)}) collective-permute-start(bf16[1024,1024]{0,1:T(8,128)(2,1)} %collective-permute-done.6), channel_id=1, source_target_pairs={{0,1},{1,2},{2,3},{3,0},{4,5},{5,6},{6,7},{7,4},{8,9},{9,10},{10,1... | collective-permute-start | bytes 6291464 | tf_op jit(solution)/shard_map/ppermute | solution.py:159
  240.3 44.7 %collective-permute-start.8 = (bf16[1024,1024]{0,1:T(8,128)(2,1)}, bf16[1024,1024]{0,1:T(8,128)(2,1)S(1)}, u32[]{:S(2)}, u32[]{:S(2)}) collective-permute-start(bf16[1024,1024]{0,1:T(8,128)(2,1)} %collective-permute-done.7), channel_id=1, source_target_pairs={{0,1},{1,2},{2,3},{3,0},{4,5},{5,6},{6,7},{7,4},{8,9},{9,10},{10,1... | collective-permute-start | bytes 6291464 | tf_op jit(solution)/shard_map/ppermute | solution.py:159
  307.2 57.8 %all-to-all-start = ((bf16[4,160,2048]{2,1,0:T(8,128)(2,1)}), bf16[4,160,2048]{2,1,0:T(8,128)(2,1)S(1)}, u32[]{:S(2)}, u32[]{:S(2)}) async-start(bf16[4,160,2048]{2,1,0:T(8,128)(2,1)} %bitcast.440), calls=%async_computation | async-start | bytes 5242880 | tf_op jit(solution)/shard_map/all_to_all | solution.py:145
  374.5 63.6 %all-to-all-start.1 = ((bf16[4,160,2048]{2,1,0:T(8,128)(2,1)}), bf16[4,160,2048]{2,1,0:T(8,128)(2,1)}, u32[]{:S(2)}, u32[]{:S(2)}) async-start(bf16[4,160,2048]{2,1,0:T(8,128)(2,1)} %bitcast.46), calls=%async_computation.1 | async-start | bytes 5242880 | tf_op jit(solution)/shard_map/all_to_all | solution.py:145
  379.1 440.4 %reduce-scatter.5.cloned.1.call-start = ((), (), s32[]{:S(2)}) async-start(), calls=%async_computation.12 | async-start | bytes 25952256 | tf_op jit(solution)/shard_map/reduce_scatter | solution.py:230
  664.7 67.3 %all-to-all-start.3 = ((bf16[4,160,2176]{2,1,0:T(8,128)(2,1)}), bf16[4,160,2176]{2,1,0:T(8,128)(2,1)S(1)}, u32[]{:S(2)}, u32[]{:S(2)}) async-start(bf16[4,160,2176]{2,1,0:T(8,128)(2,1)} %bitcast.54), calls=%async_computation.3 | async-start | bytes 5570560 | tf_op jit(solution)/shard_map/all_to_all | solution.py:145
  668.5 498.1 %reduce-scatter.11.cloned.1.call-start = ((), (), s32[]{:S(2)}) async-start(), calls=%async_computation.15 | async-start | bytes 25952256 | tf_op jit(solution)/shard_map/reduce_scatter | solution.py:230
  752.1 62.7 %all-to-all-start.4 = ((bf16[4,160,2048]{2,1,0:T(8,128)(2,1)}), bf16[4,160,2048]{2,1,0:T(8,128)(2,1)S(1)}, u32[]{:S(2)}, u32[]{:S(2)}) async-start(bf16[4,160,2048]{2,1,0:T(8,128)(2,1)} %bitcast.62), calls=%async_computation.4 | async-start | bytes 5242880 | tf_op jit(solution)/shard_map/all_to_all | solution.py:145
  756.0 415.9 %reduce-scatter.9.cloned.1.call-start = ((), (), s32[]{:S(2)}) async-start(), calls=%async_computation.14 | async-start | bytes 25952256 | tf_op jit(solution)/shard_map/reduce_scatter | solution.py:230
  814.8 131.3 %all-to-all-start.5 = ((bf16[4,160,2048]{2,1,0:T(8,128)(2,1)}), bf16[4,160,2048]{2,1,0:T(8,128)(2,1)}, u32[]{:S(2)}, u32[]{:S(2)}) async-start(bf16[4,160,2048]{2,1,0:T(8,128)(2,1)} %bitcast.437), calls=%async_computation.6 | async-start | bytes 5242880 | tf_op jit(solution)/shard_map/all_to_all | solution.py:145
  819.4 390.0 %reduce-scatter.7.cloned.1.call-start = ((), (), s32[]{:S(2)}) async-start(), calls=%async_computation.13 | async-start | bytes 5308416 | tf_op jit(solution)/shard_map/reduce_scatter | solution.py:230
  850.3 91.5 %collective-permute-start.9 = (bf16[1024,1024]{0,1:T(8,128)(2,1)}, bf16[1024,1024]{0,1:T(8,128)(2,1)}, u32[]{:S(2)}, u32[]{:S(2)}) collective-permute-start(bf16[1024,1024]{0,1:T(8,128)(2,1)} %pad_maximum_fusion.6), channel_id=1, source_target_pairs={{0,1},{1,2},{2,3},{3,0},{4,5},{5,6},{6,7},{7,4},{8,9},{9,10},{10,1... | collective-permute-start | bytes 6291464 | tf_op jit(solution)/shard_map/ppermute | solution.py:159
  946.1 47.8 %collective-permute-start.10 = (bf16[1024,1024]{0,1:T(8,128)(2,1)}, bf16[1024,1024]{0,1:T(8,128)(2,1)S(1)}, u32[]{:S(2)}, u32[]{:S(2)}) collective-permute-start(bf16[1024,1024]{0,1:T(8,128)(2,1)} %fusion.54), channel_id=1, source_target_pairs={{0,1},{1,2},{2,3},{3,0},{4,5},{5,6},{6,7},{7,4},{8,9},{9,10},{10,1... | collective-permute-start | bytes 6291464 | tf_op jit(solution)/shard_map/ppermute | solution.py:159
  960.9 93.5 %collective-permute-start.13 = (bf16[2,2,256,2048]{3,2,1,0:T(8,128)(2,1)}, bf16[2,2,256,2048]{3,2,1,0:T(8,128)(2,1)}, u32[]{:S(2)}, u32[]{:S(2)}) collective-permute-start(bf16[2,2,256,2048]{3,2,1,0:T(8,128)(2,1)} %dynamic-slice_bitcast_fusion.1), channel_id=1, source_target_pairs={{0,4},{4,0},{8,12},{12,8},{16,20},{20,16},{24,28},{28,24},{1,5},{5... | collective-permute-start | bytes 12582920 | tf_op jit(solution)/shard_map/ppermute | solution.py:234
  994.8 46.8 %collective-permute-start.11 = (bf16[1024,1024]{0,1:T(8,128)(2,1)S(1)}, bf16[1024,1024]{0,1:T(8,128)(2,1)S(1)}, u32[]{:S(2)}, u32[]{:S(2)}) collective-permute-start(bf16[1024,1024]{0,1:T(8,128)(2,1)S(1)} %fusion.56), channel_id=1, source_target_pairs={{0,1},{1,2},{2,3},{3,0},{4,5},{5,6},{6,7},{7,4},{8,9},{9,10},{10,1... | collective-permute-start | bytes 6291464 | tf_op jit(solution)/shard_map/ppermute | solution.py:159
  1010.2 91.0 %collective-permute-start.20 = (bf16[2,2,256,2048]{3,2,1,0:T(8,128)(2,1)}, bf16[2,2,256,2048]{3,2,1,0:T(8,128)(2,1)}, u32[]{:S(2)}, u32[]{:S(2)}) collective-permute-start(bf16[2,2,256,2048]{3,2,1,0:T(8,128)(2,1)} %dynamic-slice_bitcast_fusion), channel_id=1, source_target_pairs={{0,4},{4,0},{8,12},{12,8},{16,20},{20,16},{24,28},{28,24},{1,5},{5... | collective-permute-start | bytes 12582920 | tf_op jit(solution)/shard_map/ppermute | solution.py:234
  1061.4 22.6 %collective-permute-start.14 = (bf16[2,256,1024]{2,1,0:T(8,128)(2,1)}, bf16[2,256,1024]{2,1,0:T(8,128)(2,1)}, u32[]{:S(2)}, u32[]{:S(2)}) collective-permute-start(bf16[2,256,1024]{2,1,0:T(8,128)(2,1)} %dynamic-slice_bitcast_fusion.5), channel_id=1, source_target_pairs={{0,8},{4,12},{8,0},{12,4},{16,24},{20,28},{24,16},{28,20},{1,9},{5... | collective-permute-start | bytes 3145736 | tf_op jit(solution)/shard_map/ppermute | solution.py:234
  1063.0 23.8 %collective-permute-start.16 = (bf16[2,256,1024]{2,1,0:T(8,128)(2,1)S(1)}, bf16[2,256,1024]{2,1,0:T(8,128)(2,1)}, u32[]{:S(2)}, u32[]{:S(2)}) collective-permute-start(bf16[2,256,1024]{2,1,0:T(8,128)(2,1)S(1)} %dynamic-slice_bitcast_fusion.4), channel_id=1, source_target_pairs={{0,16},{4,20},{8,24},{12,28},{16,0},{20,4},{24,8},{28,12},{1,17},{... | collective-permute-start | bytes 3145736 | tf_op jit(solution)/shard_map/ppermute | solution.py:234
  1072.6 27.3 %collective-permute-start.12 = (bf16[256,2048]{1,0:T(8,128)(2,1)S(1)}, bf16[256,2048]{1,0:T(8,128)(2,1)S(1)}, u32[]{:S(2)}, u32[]{:S(2)}) collective-permute-start(bf16[256,2048]{1,0:T(8,128)(2,1)S(1)} %fusion.101), channel_id=1, source_target_pairs={{0,1},{1,2},{2,3},{3,0},{4,5},{5,6},{6,7},{7,4},{8,9},{9,10},{10,1... | collective-permute-start | bytes 3145736 | tf_op jit(solution)/shard_map/ppermute | solution.py:159
  1101.2 22.1 %collective-permute-start.18 = (bf16[256,2048]{1,0:T(8,128)(2,1)}, bf16[256,2048]{1,0:T(8,128)(2,1)}, u32[]{:S(2)}, u32[]{:S(2)}) collective-permute-start(bf16[256,2048]{1,0:T(8,128)(2,1)} %fusion.92), channel_id=1, source_target_pairs={{0,1},{1,2},{2,3},{3,0},{4,5},{5,6},{6,7},{7,4},{8,9},{9,10},{10,1... | collective-permute-start | bytes 3145736 | tf_op jit(solution)/shard_map/ppermute | solution.py:159
  1112.3 23.4 %collective-permute-start.23 = (bf16[2,256,1024]{2,1,0:T(8,128)(2,1)S(1)}, bf16[2,256,1024]{2,1,0:T(8,128)(2,1)S(1)}, u32[]{:S(2)}, u32[]{:S(2)}) collective-permute-start(bf16[2,256,1024]{2,1,0:T(8,128)(2,1)S(1)} %dynamic-slice_bitcast_fusion.2), channel_id=1, source_target_pairs={{0,16},{4,20},{8,24},{12,28},{16,0},{20,4},{24,8},{28,12},{1,17},{... | collective-permute-start | bytes 3145736 | tf_op jit(solution)/shard_map/ppermute | solution.py:234
  1126.5 24.1 %collective-permute-start.19 = (bf16[256,2048]{1,0:T(8,128)(2,1)}, bf16[256,2048]{1,0:T(8,128)(2,1)}, u32[]{:S(2)}, u32[]{:S(2)}) collective-permute-start(bf16[256,2048]{1,0:T(8,128)(2,1)} %fusion.93), channel_id=1, source_target_pairs={{0,1},{1,2},{2,3},{3,0},{4,5},{5,6},{6,7},{7,4},{8,9},{9,10},{10,1... | collective-permute-start | bytes 3145736 | tf_op jit(solution)/shard_map/ppermute | solution.py:159
  (193 other events, 2179.1 us)
Sparse Core Ops, SparseCore 0:
  29.3 41.1 all-gather.11
  72.3 54.2 all-gather.13
  128.5 54.2 all-gather.15
  184.6 116.3 all-gather.17
  302.6 116.3 all-gather.19
  420.7 116.3 all-gather.21
  583.5 145.2 reduce-scatter.4
  733.8 145.1 reduce-scatter.10
  882.7 146.3 reduce-scatter.8
  1154.5 54.8 reduce-scatter.6

commit v5 on v4

--- a/solution.py
+++ b/solution.py
@@ -409,14 +409,15 @@
         2,
     )
     ffn_rows, packed_grads = lax.optimization_barrier((ffn_rows, packed_grads))
-    received_grads = exchange(packed_grads).reshape(experts * capacity, -1)
-    out_rows = received_grads[:, :model_width]
-    row_gate = jnp.sum(received_grads[:, model_width:].astype(f32), 1, keepdims=True)
-    ffn_grad_rows = (row_gate * out_rows.astype(f32)).astype(bf16)
     gate_value = mm(ffn_rows, gate_all)
     up_value = mm(ffn_rows, up_all)
     sigmoid_gate = jax.nn.sigmoid(gate_value)
     hidden = (gate_value * sigmoid_gate * up_value).astype(bf16)
+    received_grads, hidden = lax.optimization_barrier((exchange(packed_grads), hidden))
+    received_grads = received_grads.reshape(experts * capacity, -1)
+    out_rows = received_grads[:, :model_width]
+    row_gate = jnp.sum(received_grads[:, model_width:].astype(f32), 1, keepdims=True)
+    ffn_grad_rows = (row_gate * out_rows.astype(f32)).astype(bf16)
     down_part = mm_tn(hidden, ffn_grad_rows).astype(bf16)
     down_part, hidden, out_rows = lax.optimization_barrier((down_part, hidden, out_rows))
     down_sum = reduce_dp(down_part)
@@ -467,7 +468,9 @@
     for step in range(1, experts + 1):
         k = step % experts
         start = backs[k] * width
-        group_grad = lax.dynamic_slice_in_dim(attended_grad, start, width, 1)
+        group_grad = lax.dynamic_slice_in_dim(
+            attended_grad if step < 4 else late_grad, start, width, 1
+        )
         group_query_grad, key_grad, value_grad = attend_back(*saved[k], group_grad)
         query_grad = lax.dynamic_update_slice_in_dim(query_grad, group_query_grad, start, 1)
         part = jnp.concatenate([key_grad, value_grad], 1)
@@ -478,8 +481,8 @@
             continue
         part = part.astype(bf16)
         if step == 2:
-            part, att_grad_rows, ffn_back = lax.optimization_barrier(
-                (part, att_grad_rows, ffn_back)
+            part, att_grad_rows, ffn_back, late_grad = lax.optimization_barrier(
+                (part, att_grad_rows, ffn_back, attended_grad)
             )
         if step == experts - 1:
             part, query_rows = lax.optimization_barrier((part, query_rows))
@@ -533,14 +536,16 @@
         if normed_one_grad is not None:
             part = part + normed_one_grad.astype(f32)
         normed_one_grad = part if k == 0 else ring_step(part.astype(bf16), experts)
+        if step == experts - 1:
+            normed_one_grad, shared_part = lax.optimization_barrier(
+                (normed_one_grad, reduce_dp(shared_part))
+            )
         if step == 1:
             normed_one_grad, output_sum = lax.optimization_barrier((normed_one_grad, output_sum))
-    normed_one_grad, query_sum, shared_part = lax.optimization_barrier(
-        (normed_one_grad, query_sum, shared_part)
-    )
+    normed_one_grad, query_sum = lax.optimization_barrier((normed_one_grad, query_sum))
     normed_one_grad = normed_one_grad + router_grad
     input_grad = mixed_grad + norm_back(inputs, inverse_one, gain_first, normed_one_grad)
-    shared_sum = exchange(reduce_dp(shared_part).reshape(experts, shard_rows, -1)).astype(f32)
+    shared_sum = exchange(shared_part.reshape(experts, shard_rows, -1)).astype(f32)
     kv_sum = (
         shared_sum[:, :, : 2 * width]
         .reshape(experts, shard_rows, 2, width)

time: 1250 us -> 1190 us (0.952)
  blocking collectives: 66.5 us -> 0 us
  waiting for transfers between devices: 415 us -> 391 us
    all_to_all x1 -> x0, blocking collectives: 66.5 us -> none  [exchange(): lax.all_to_all(packed, 'expert', split_axis=0, concat_axis=0, tiled=True)]
    reduce_scatter x4, waiting for transfers between devices: 32 us -> 0.03 us  [reduce_dp(): return lax.psum_scatter(part, 'dp', scatter_dimension=0, tiled=True)]
    ppermute x12, waiting for transfers between devices: 208 us -> 179 us  [ring_step(): lax.ppermute(block, 'expert', [(i, (i + 1) % experts) for i in range(expe...]
    ppermute x10, waiting for transfers between devices: 15.2 us -> 38.7 us  [swap(): return lax.ppermute(block, 'dp', [(i, i ^ bit) for i in range(8)])]
    all_to_all x6 -> x7, waiting for transfers between devices: 148 us -> 157 us  [exchange(): lax.all_to_all(packed, 'expert', split_axis=0, concat_axis=0, tiled=True)]
    all_to_all x6 -> x7, starting transfers between devices: 25.4 us -> 30.5 us  [exchange(): lax.all_to_all(packed, 'expert', split_axis=0, concat_axis=0, tiled=True)]
    unnamed x377 -> x389, local copies, waits for them, and re-layouts: 43.6 us -> 46.1 us
  transfers between devices with their start and end apart: 41 -> 42, of which waited for: 23 -> 24; matrix products, arithmetic and copies ran while one was open for 52% -> 55% of each run, Pallas kernels for 0% -> 0%
where the time goes in v5:
time: 1190 us; the launch traced here: 1180 us
  matrix products  446 us (37%)
  waiting for transfers between devices  391 us (33%)
  local copies, waits for them, and re-layouts  134 us (11%)
  other arithmetic  124 us (10%)
  starting transfers between devices  64.8 us (5%)
  between operations  17.7 us (1%)
    ppermute x12, waiting for transfers between devices, ring_step(): lax.ppermute(block, 'expert', [(i, (i + 1) % experts) for i in range(expe...  179 us
    all_to_all x7, waiting for transfers between devices, exchange(): lax.all_to_all(packed, 'expert', split_axis=0, concat_axis=0, tiled=True)  157 us
    dot_general x18, matrix products, mm(): return jnp.dot(left, right, preferred_element_type=f32)  121 us
    dot_general x11, matrix products, mm_tn(): lax.dot_general(left, right, (((0,), (0,)), ((), ())), preferred_element_...  109 us
    dot_general x6, matrix products, mm_nt(): lax.dot_general(left, right, (((1,), (1,)), ((), ())), preferred_element_...  104 us
    unnamed x389, local copies, waits for them, and re-layouts  46.1 us
    ppermute x10, waiting for transfers between devices, swap(): return lax.ppermute(block, 'dp', [(i, i ^ bit) for i in range(8)])  38.7 us
    all_to_all x7, starting transfers between devices, exchange(): lax.all_to_all(packed, 'expert', split_axis=0, concat_axis=0, tiled=True)  30.5 us
  transfers between devices with their start and end apart: 42, of which 24 were waited for; matrix products, arithmetic and copies ran while one was open for 55% of the time, Pallas kernels for 0%

profile of v5, /device:TPU:0, one launch (start us, length us, event | category | flops | bytes accessed | tf_op | source)
XLA Modules:
  0.0 1177.1 jit_solution(3366180518558044289)
XLA Ops:
  38.4 24.9 %collective-permute-done = bf16[256,2176]{1,0:T(8,128)(2,1)} collective-permute-done((bf16[256,2176]{1,0:T(8,128)(2,1)S(1)}, bf16[256,2176]{1,0:T(8,128)(2,1)}, u32[]{:S(2)}, u32[]{:S(2)}) %collective-permute-start) | collective-permute-done | bytes 1114144 | tf_op jit(solution)/shard_map/ppermute | solution.py:159
  68.2 22.1 %collective-permute-done.1 = bf16[256,2176]{1,0:T(8,128)(2,1)} collective-permute-done((bf16[256,2176]{1,0:T(8,128)(2,1)}, bf16[256,2176]{1,0:T(8,128)(2,1)}, u32[]{:S(2)}, u32[]{:S(2)}) %collective-permute-start.1) | collective-permute-done | bytes 1114144 | tf_op jit(solution)/shard_map/ppermute | solution.py:159
  94.2 22.1 %collective-permute-done.2 = bf16[256,2176]{1,0:T(8,128)(2,1)S(1)} collective-permute-done((bf16[256,2176]{1,0:T(8,128)(2,1)}, bf16[256,2176]{1,0:T(8,128)(2,1)S(1)}, u32[]{:S(2)}, u32[]{:S(2)}) %collective-permute-start.2) | collective-permute-done | bytes 1114144 | tf_op jit(solution)/shard_map/ppermute | solution.py:159
  150.4 12.4 %copy.272 = bf16[2048,2048]{1,0:T(8,128)(2,1)} copy(bf16[2048,2048]{0,1:T(8,128)(2,1)} %bitcast.402) | data formatting | bytes 16777216 | tf_op jit(solution)/shard_map/dot_general | solution.py:82
  162.8 10.1 fusion.233
  173.9 20.6 %collective-permute-done.6 = bf16[1024,1024]{0,1:T(8,128)(2,1)} collective-permute-done((bf16[1024,1024]{0,1:T(8,128)(2,1)}, bf16[1024,1024]{0,1:T(8,128)(2,1)}, u32[]{:S(2)}, u32[]{:S(2)}) %collective-permute-start.6) | collective-permute-done | bytes 2097184 | tf_op jit(solution)/shard_map/ppermute | solution.py:159
  223.1 17.2 %collective-permute-done.7 = bf16[1024,1024]{0,1:T(8,128)(2,1)} collective-permute-done((bf16[1024,1024]{0,1:T(8,128)(2,1)}, bf16[1024,1024]{0,1:T(8,128)(2,1)}, u32[]{:S(2)}, u32[]{:S(2)}) %collective-permute-start.7) | collective-permute-done | bytes 2097184 | tf_op jit(solution)/shard_map/ppermute | solution.py:159
  253.7 31.3 %collective-permute-done.8 = bf16[1024,1024]{0,1:T(8,128)(2,1)S(1)} collective-permute-done((bf16[1024,1024]{0,1:T(8,128)(2,1)}, bf16[1024,1024]{0,1:T(8,128)(2,1)S(1)}, u32[]{:S(2)}, u32[]{:S(2)}) %collective-permute-start.8) | collective-permute-done | bytes 2097184 | tf_op jit(solution)/shard_map/ppermute | solution.py:159
  297.7 10.3 fusion.72
  317.2 48.7 %all-to-all-done = bf16[4,160,2048]{2,1,0:T(8,128)(2,1)S(1)} async-done(((bf16[4,160,2048]{2,1,0:T(8,128)(2,1)}), bf16[4,160,2048]{2,1,0:T(8,128)(2,1)S(1)}, u32[]{:S(2)}, u32[]{:S(2)}) %all-to-all-start) | async-done | bytes 2621472 | tf_op jit(solution)/shard_map/all_to_all | solution.py:145
  387.2 51.9 %all-to-all-done.1 = bf16[4,160,2048]{2,1,0:T(8,128)(2,1)} async-done(((bf16[4,160,2048]{2,1,0:T(8,128)(2,1)}), bf16[4,160,2048]{2,1,0:T(8,128)(2,1)}, u32[]{:S(2)}, u32[]{:S(2)}) %all-to-all-start.1) | async-done | bytes 2621472 | tf_op jit(solution)/shard_map/all_to_all | solution.py:145
  442.8 23.7 %fusion.10 = f32[640,5632]{1,0:T(8,128)} fusion(bf16[640,2048]{1,0:T(8,128)(2,1)} %bitcast.47, bf16[1,2048,5632]{2,1,0:T(8,128)(2,1)} %all-gather.18.cloned.1.call-done), kind=kOutput, calls=%fused_computation.10 | convolution fusion | flops 14763950080 | bytes 40108032 | tf_op jit(solution)/shard_map/dot_general | solution.py:82
  466.4 32.2 %multiply_convert_fusion.2 = (bf16[640,5632]{1,0:T(8,128)(2,1)}, f32[640,5632]{1,0:T(8,128)}) fusion(f32[640,5632]{1,0:T(8,128)} %fusion.10, bf16[640,2048]{1,0:T(8,128)(2,1)} %bitcast.47, bf16[1,2048,5632]{2,1,0:T(8,128)(2,1)} %all-gather.20.cloned.1.call-done), kind=kOutput, calls=%fused_computation.18 | convolution fusion | flops 14785576960 | bytes 61734912 | tf_op jit(solution)/shard_map/dot_general | solution.py:82
  507.1 24.9 %convolution_convert_fusion = bf16[5632,2048]{1,0:T(8,128)(2,1)} fusion(bf16[640,5632]{1,0:T(8,128)(2,1)} %get-tuple-element.66, f32[640]{0:T(1024)S(1)} %convert_reduce_fusion.2, bf16[640,2176]{1,0:T(8,128)(2,1)S(1)} %bitcast.392), kind=kOutput, calls=%fused_computation.12 | convolution fusion | flops 14779416576 | bytes 32903168 | tf_op jit(solution)/shard_map/dot_general | solution.py:86
  537.1 38.4 %multiply_convert_fusion.1 = (bf16[640,5632]{1,0:T(8,128)(2,1)}, bf16[640,5632]{1,0:T(8,128)(2,1)}, f32[640]{0:T(1024)S(1)}) fusion(f32[640,5632]{1,0:T(8,128)} %fusion.10, f32[640,5632]{1,0:T(8,128)} %get-tuple-element.199, f32[640]{0:T(1024)S(1)} %convert_reduce_fusion.2, bf16[640,5632]{1,0:T(8,128)(2,1)} %get-tuple-element.66, ...), kind=kOutput, calls=%fused_computation.17 | convolution fusion | flops 14825225216 | bytes 76157952 | tf_op jit(solution)/shard_map/dot_general | solution.py:90
  575.8 20.6 %fusion.4 = f32[640,2048]{1,0:T(8,128)S(1)} fusion(bf16[640,5632]{1,0:T(8,128)(2,1)} %get-tuple-element.62, bf16[1,2048,5632]{2,1,0:T(8,128)(2,1)} %all-gather.20.cloned.1.call-done), kind=kOutput, calls=%fused_computation.4 | convolution fusion | flops 14763950080 | bytes 35520512 | tf_op jit(solution)/shard_map/dot_general | solution.py:90
  596.4 18.8 %add_convert_fusion.1 = bf16[640,2048]{1,0:T(8,128)(2,1)S(1)} fusion(f32[640,2048]{1,0:T(8,128)S(1)} %fusion.4, bf16[640,5632]{1,0:T(8,128)(2,1)S(1)} %copy-done.167, bf16[1,2048,5632]{2,1,0:T(8,128)(2,1)} %all-gather.18.cloned.1.call-done), kind=kOutput, calls=%fused_computation.75 | convolution fusion | flops 14766571520 | bytes 38141952 | tf_op jit(solution)/shard_map/dot_general | solution.py:90
  621.4 25.6 %convolution_convert_fusion.1 = bf16[2048,5632]{1,0:T(8,128)(2,1)} fusion(bf16[640,2048]{1,0:T(8,128)(2,1)} %bitcast.47, bf16[640,5632]{1,0:T(8,128)(2,1)} %get-tuple-element.62), kind=kOutput, calls=%fused_computation.13 | convolution fusion | flops 14775484416 | bytes 32899072 | tf_op jit(solution)/shard_map/dot_general | solution.py:86
  647.0 26.1 %convolution_convert_fusion.2 = bf16[2048,5632]{1,0:T(8,128)(2,1)} fusion(bf16[640,2048]{1,0:T(8,128)(2,1)} %bitcast.47, bf16[640,5632]{1,0:T(8,128)(2,1)} %get-tuple-element.61), kind=kOutput, calls=%fused_computation.14 | convolution fusion | flops 14775484416 | bytes 32899072 | tf_op jit(solution)/shard_map/dot_general | solution.py:86
  673.1 11.3 all-to-all-done.3
  720.4 21.8 %fusion.66 = bf16[640,2048]{1,0:T(8,128)(2,1)} fusion(bf16[640,5632]{1,0:T(8,128)(2,1)} %get-tuple-element.66, bf16[1,5632,2048]{2,1,0:T(8,128)(2,1)} %all-gather.22.cloned.1.call-done), kind=kOutput, calls=%fused_computation.114 | convolution fusion | flops 14765260800 | bytes 32899072 | tf_op jit(solution)/shard_map/dot_general | solution.py:82
  742.2 26.4 %all-to-all-done.4 = bf16[4,160,2048]{2,1,0:T(8,128)(2,1)} async-done(((bf16[4,160,2048]{2,1,0:T(8,128)(2,1)}), bf16[4,160,2048]{2,1,0:T(8,128)(2,1)}, u32[]{:S(2)}, u32[]{:S(2)}) %all-to-all-start.4) | async-done | bytes 2621472 | tf_op jit(solution)/shard_map/all_to_all | solution.py:145
  773.3 10.1 fusion.63
  794.6 8.4 multiply_convert_fusion.5
  816.6 8.5 multiply_convert_fusion.3
  830.8 7.9 multiply_convert_fusion.6
  882.0 9.9 convolution_convert_fusion.4
  949.9 33.6 %collective-permute-done.11 = bf16[1024,1024]{0,1:T(8,128)(2,1)S(1)} collective-permute-done((bf16[1024,1024]{0,1:T(8,128)(2,1)S(1)}, bf16[1024,1024]{0,1:T(8,128)(2,1)S(1)}, u32[]{:S(2)}, u32[]{:S(2)}) %collective-permute-start.11) | collective-permute-done | bytes 2097184 | tf_op jit(solution)/shard_map/ppermute | solution.py:159
  995.8 9.3 fusion.57
  1036.0 9.0 collective-permute-done.14
  1099.4 17.4 %collective-permute-done.21 = bf16[2,256,1024]{2,1,0:T(8,128)(2,1)} collective-permute-done((bf16[2,256,1024]{2,1,0:T(8,128)(2,1)}, bf16[2,256,1024]{2,1,0:T(8,128)(2,1)}, u32[]{:S(2)}, u32[]{:S(2)}) %collective-permute-start.21) | collective-permute-done | bytes 1048608 | tf_op jit(solution)/shard_map/ppermute | solution.py:234
  1154.1 8.1 all-to-all-done.6
  (716 shorter events, 496.1 us)
Async XLA Ops:
  7.2 115.3 %all-gather.12.cloned.1.call-start = ((), (), s32[]{:S(2)}) async-start(), calls=%async_computation.11 | async-start | bytes 5308416 | tf_op jit(solution)/shard_map/all_gather | solution.py:311
  29.2 121.2 %all-gather.14.cloned.1.call-start = ((), (), s32[]{:S(2)}) async-start(), calls=%async_computation.16 | async-start | bytes 9437184 | tf_op jit(solution)/shard_map/all_gather | solution.py:226
  29.9 267.7 %all-gather.16.cloned.1.call-start = ((), (), s32[]{:S(2)}) async-start(), calls=%async_computation.17 | async-start | bytes 9437184 | tf_op jit(solution)/shard_map/all_gather | solution.py:226
  30.7 412.1 %all-gather.18.cloned.1.call-start = ((), (), s32[]{:S(2)}) async-start(), calls=%async_computation.18 | async-start | bytes 25952256 | tf_op jit(solution)/shard_map/all_gather | solution.py:226
  31.3 435.2 %all-gather.20.cloned.1.call-start = ((), (), s32[]{:S(2)}) async-start(), calls=%async_computation.19 | async-start | bytes 25952256 | tf_op jit(solution)/shard_map/all_gather | solution.py:226
  31.8 505.3 %all-gather.22.cloned.1.call-start = ((), (), s32[]{:S(2)}) async-start(), calls=%async_computation.20 | async-start | bytes 25952256 | tf_op jit(solution)/shard_map/all_gather | solution.py:226
  34.7 28.6 %collective-permute-start = (bf16[256,2176]{1,0:T(8,128)(2,1)S(1)}, bf16[256,2176]{1,0:T(8,128)(2,1)}, u32[]{:S(2)}, u32[]{:S(2)}) collective-permute-start(bf16[256,2176]{1,0:T(8,128)(2,1)S(1)} %concatenate.65), channel_id=1, source_target_pairs={{0,1},{1,2},{2,3},{3,0},{4,5},{5,6},{6,7},{7,4},{8,9},{9,10},{10,1... | collective-permute-start | bytes 3342344 | tf_op jit(solution)/shard_map/ppermute | solution.py:159
  63.3 27.0 %collective-permute-start.1 = (bf16[256,2176]{1,0:T(8,128)(2,1)}, bf16[256,2176]{1,0:T(8,128)(2,1)}, u32[]{:S(2)}, u32[]{:S(2)}) collective-permute-start(bf16[256,2176]{1,0:T(8,128)(2,1)} %collective-permute-done), channel_id=1, source_target_pairs={{0,1},{1,2},{2,3},{3,0},{4,5},{5,6},{6,7},{7,4},{8,9},{9,10},{10,1... | collective-permute-start | bytes 3342344 | tf_op jit(solution)/shard_map/ppermute | solution.py:159
  90.3 26.0 %collective-permute-start.2 = (bf16[256,2176]{1,0:T(8,128)(2,1)}, bf16[256,2176]{1,0:T(8,128)(2,1)S(1)}, u32[]{:S(2)}, u32[]{:S(2)}) collective-permute-start(bf16[256,2176]{1,0:T(8,128)(2,1)} %collective-permute-done.1), channel_id=1, source_target_pairs={{0,1},{1,2},{2,3},{3,0},{4,5},{5,6},{6,7},{7,4},{8,9},{9,10},{10,1... | collective-permute-start | bytes 3342344 | tf_op jit(solution)/shard_map/ppermute | solution.py:159
  148.0 46.5 %collective-permute-start.6 = (bf16[1024,1024]{0,1:T(8,128)(2,1)}, bf16[1024,1024]{0,1:T(8,128)(2,1)}, u32[]{:S(2)}, u32[]{:S(2)}) collective-permute-start(bf16[1024,1024]{0,1:T(8,128)(2,1)} %pad_maximum_fusion.5), channel_id=1, source_target_pairs={{0,1},{1,2},{2,3},{3,0},{4,5},{5,6},{6,7},{7,4},{8,9},{9,10},{10,1... | collective-permute-start | bytes 6291464 | tf_op jit(solution)/shard_map/ppermute | solution.py:159
  194.5 45.8 %collective-permute-start.7 = (bf16[1024,1024]{0,1:T(8,128)(2,1)}, bf16[1024,1024]{0,1:T(8,128)(2,1)}, u32[]{:S(2)}, u32[]{:S(2)}) collective-permute-start(bf16[1024,1024]{0,1:T(8,128)(2,1)} %collective-permute-done.6), channel_id=1, source_target_pairs={{0,1},{1,2},{2,3},{3,0},{4,5},{5,6},{6,7},{7,4},{8,9},{9,10},{10,1... | collective-permute-start | bytes 6291464 | tf_op jit(solution)/shard_map/ppermute | solution.py:159
  240.3 44.7 %collective-permute-start.8 = (bf16[1024,1024]{0,1:T(8,128)(2,1)}, bf16[1024,1024]{0,1:T(8,128)(2,1)S(1)}, u32[]{:S(2)}, u32[]{:S(2)}) collective-permute-start(bf16[1024,1024]{0,1:T(8,128)(2,1)} %collective-permute-done.7), channel_id=1, source_target_pairs={{0,1},{1,2},{2,3},{3,0},{4,5},{5,6},{6,7},{7,4},{8,9},{9,10},{10,1... | collective-permute-start | bytes 6291464 | tf_op jit(solution)/shard_map/ppermute | solution.py:159
  308.0 57.9 %all-to-all-start = ((bf16[4,160,2048]{2,1,0:T(8,128)(2,1)}), bf16[4,160,2048]{2,1,0:T(8,128)(2,1)S(1)}, u32[]{:S(2)}, u32[]{:S(2)}) async-start(bf16[4,160,2048]{2,1,0:T(8,128)(2,1)} %bitcast.438), calls=%async_computation | async-start | bytes 5242880 | tf_op jit(solution)/shard_map/all_to_all | solution.py:145
  375.4 63.6 %all-to-all-start.1 = ((bf16[4,160,2048]{2,1,0:T(8,128)(2,1)}), bf16[4,160,2048]{2,1,0:T(8,128)(2,1)}, u32[]{:S(2)}, u32[]{:S(2)}) async-start(bf16[4,160,2048]{2,1,0:T(8,128)(2,1)} %bitcast.46), calls=%async_computation.1 | async-start | bytes 5242880 | tf_op jit(solution)/shard_map/all_to_all | solution.py:145
  439.0 66.1 %all-to-all-start.2 = ((bf16[4,160,2176]{2,1,0:T(8,128)(2,1)}), bf16[4,160,2176]{2,1,0:T(8,128)(2,1)S(1)}, u32[]{:S(2)}, u32[]{:S(2)}) async-start(bf16[4,160,2176]{2,1,0:T(8,128)(2,1)} %pad_maximum_fusion.2), calls=%async_computation.2 | async-start | bytes 5570560 | tf_op jit(solution)/shard_map/all_to_all | solution.py:145
  442.7 330.6 %reduce-scatter.5.cloned.1.call-start = ((), (), s32[]{:S(2)}) async-start(), calls=%async_computation.12 | async-start | bytes 25952256 | tf_op jit(solution)/shard_map/reduce_scatter | solution.py:230
  617.0 67.5 %all-to-all-start.3 = ((bf16[4,160,2176]{2,1,0:T(8,128)(2,1)}), bf16[4,160,2176]{2,1,0:T(8,128)(2,1)S(1)}, u32[]{:S(2)}, u32[]{:S(2)}) async-start(bf16[4,160,2176]{2,1,0:T(8,128)(2,1)} %bitcast.54), calls=%async_computation.3 | async-start | bytes 5570560 | tf_op jit(solution)/shard_map/all_to_all | solution.py:145
  621.4 462.2 %reduce-scatter.11.cloned.1.call-start = ((), (), s32[]{:S(2)}) async-start(), calls=%async_computation.15 | async-start | bytes 25952256 | tf_op jit(solution)/shard_map/reduce_scatter | solution.py:230
  705.1 63.5 %all-to-all-start.4 = ((bf16[4,160,2048]{2,1,0:T(8,128)(2,1)}), bf16[4,160,2048]{2,1,0:T(8,128)(2,1)}, u32[]{:S(2)}, u32[]{:S(2)}) async-start(bf16[4,160,2048]{2,1,0:T(8,128)(2,1)} %bitcast.395), calls=%async_computation.4 | async-start | bytes 5242880 | tf_op jit(solution)/shard_map/all_to_all | solution.py:145
  710.1 414.6 %reduce-scatter.9.cloned.1.call-start = ((), (), s32[]{:S(2)}) async-start(), calls=%async_computation.14 | async-start | bytes 25952256 | tf_op jit(solution)/shard_map/reduce_scatter | solution.py:230
  768.6 108.6 %all-to-all-start.5 = ((bf16[4,160,2048]{2,1,0:T(8,128)(2,1)}), bf16[4,160,2048]{2,1,0:T(8,128)(2,1)}, u32[]{:S(2)}, u32[]{:S(2)}) async-start(bf16[4,160,2048]{2,1,0:T(8,128)(2,1)} %bitcast.76), calls=%async_computation.6 | async-start | bytes 5242880 | tf_op jit(solution)/shard_map/all_to_all | solution.py:145
  773.2 365.2 %reduce-scatter.7.cloned.1.call-start = ((), (), s32[]{:S(2)}) async-start(), calls=%async_computation.13 | async-start | bytes 5308416 | tf_op jit(solution)/shard_map/reduce_scatter | solution.py:230
  811.2 57.3 %collective-permute-start.9 = (bf16[1024,1024]{0,1:T(8,128)(2,1)}, bf16[1024,1024]{0,1:T(8,128)(2,1)}, u32[]{:S(2)}, u32[]{:S(2)}) collective-permute-start(bf16[1024,1024]{0,1:T(8,128)(2,1)} %pad_maximum_fusion.6), channel_id=1, source_target_pairs={{0,1},{1,2},{2,3},{3,0},{4,5},{5,6},{6,7},{7,4},{8,9},{9,10},{10,1... | collective-permute-start | bytes 6291464 | tf_op jit(solution)/shard_map/ppermute | solution.py:159
  879.4 51.2 %collective-permute-start.10 = (bf16[1024,1024]{0,1:T(8,128)(2,1)}, bf16[1024,1024]{0,1:T(8,128)(2,1)}, u32[]{:S(2)}, u32[]{:S(2)}) collective-permute-start(bf16[1024,1024]{0,1:T(8,128)(2,1)} %fusion.54), channel_id=1, source_target_pairs={{0,1},{1,2},{2,3},{3,0},{4,5},{5,6},{6,7},{7,4},{8,9},{9,10},{10,1... | collective-permute-start | bytes 6291464 | tf_op jit(solution)/shard_map/ppermute | solution.py:159
  897.5 114.9 %collective-permute-start.13 = (bf16[2,2,256,2048]{3,2,1,0:T(8,128)(2,1)}, bf16[2,2,256,2048]{3,2,1,0:T(8,128)(2,1)}, u32[]{:S(2)}, u32[]{:S(2)}) collective-permute-start(bf16[2,2,256,2048]{3,2,1,0:T(8,128)(2,1)} %dynamic-slice_bitcast_fusion.1), channel_id=1, source_target_pairs={{0,4},{4,0},{8,12},{12,8},{16,20},{20,16},{24,28},{28,24},{1,5},{5... | collective-permute-start | bytes 12582920 | tf_op jit(solution)/shard_map/ppermute | solution.py:234
  933.4 50.1 %collective-permute-start.11 = (bf16[1024,1024]{0,1:T(8,128)(2,1)S(1)}, bf16[1024,1024]{0,1:T(8,128)(2,1)S(1)}, u32[]{:S(2)}, u32[]{:S(2)}) collective-permute-start(bf16[1024,1024]{0,1:T(8,128)(2,1)S(1)} %fusion.56), channel_id=1, source_target_pairs={{0,1},{1,2},{2,3},{3,0},{4,5},{5,6},{6,7},{7,4},{8,9},{9,10},{10,1... | collective-permute-start | bytes 6291464 | tf_op jit(solution)/shard_map/ppermute | solution.py:159
  949.0 123.3 %collective-permute-start.20 = (bf16[2,2,256,2048]{3,2,1,0:T(8,128)(2,1)}, bf16[2,2,256,2048]{3,2,1,0:T(8,128)(2,1)}, u32[]{:S(2)}, u32[]{:S(2)}) collective-permute-start(bf16[2,2,256,2048]{3,2,1,0:T(8,128)(2,1)} %dynamic-slice_bitcast_fusion), channel_id=1, source_target_pairs={{0,4},{4,0},{8,12},{12,8},{16,20},{20,16},{24,28},{28,24},{1,5},{5... | collective-permute-start | bytes 12582920 | tf_op jit(solution)/shard_map/ppermute | solution.py:234
  1022.0 26.7 %collective-permute-start.16 = (bf16[2,256,1024]{2,1,0:T(8,128)(2,1)}, bf16[2,256,1024]{2,1,0:T(8,128)(2,1)}, u32[]{:S(2)}, u32[]{:S(2)}) collective-permute-start(bf16[2,256,1024]{2,1,0:T(8,128)(2,1)} %dynamic-slice_bitcast_fusion.4), channel_id=1, source_target_pairs={{0,16},{4,20},{8,24},{12,28},{16,0},{20,4},{24,8},{28,12},{1,17},{... | collective-permute-start | bytes 3145736 | tf_op jit(solution)/shard_map/ppermute | solution.py:234
  1024.6 43.4 %collective-permute-start.12 = (bf16[256,2048]{1,0:T(8,128)(2,1)}, bf16[256,2048]{1,0:T(8,128)(2,1)}, u32[]{:S(2)}, u32[]{:S(2)}) collective-permute-start(bf16[256,2048]{1,0:T(8,128)(2,1)} %fusion.101), channel_id=1, source_target_pairs={{0,1},{1,2},{2,3},{3,0},{4,5},{5,6},{6,7},{7,4},{8,9},{9,10},{10,1... | collective-permute-start | bytes 3145736 | tf_op jit(solution)/shard_map/ppermute | solution.py:159
  1080.5 36.3 %collective-permute-start.21 = (bf16[2,256,1024]{2,1,0:T(8,128)(2,1)}, bf16[2,256,1024]{2,1,0:T(8,128)(2,1)}, u32[]{:S(2)}, u32[]{:S(2)}) collective-permute-start(bf16[2,256,1024]{2,1,0:T(8,128)(2,1)} %dynamic-slice_bitcast_fusion.3), channel_id=1, source_target_pairs={{0,8},{4,12},{8,0},{12,4},{16,24},{20,28},{24,16},{28,20},{1,9},{5... | collective-permute-start | bytes 3145736 | tf_op jit(solution)/shard_map/ppermute | solution.py:234
  1082.0 38.8 %collective-permute-start.23 = (bf16[2,256,1024]{2,1,0:T(8,128)(2,1)}, bf16[2,256,1024]{2,1,0:T(8,128)(2,1)}, u32[]{:S(2)}, u32[]{:S(2)}) collective-permute-start(bf16[2,256,1024]{2,1,0:T(8,128)(2,1)} %dynamic-slice_bitcast_fusion.2), channel_id=1, source_target_pairs={{0,16},{4,20},{8,24},{12,28},{16,0},{20,4},{24,8},{28,12},{1,17},{... | collective-permute-start | bytes 3145736 | tf_op jit(solution)/shard_map/ppermute | solution.py:234
  1099.0 39.4 %collective-permute-start.19 = (bf16[256,2048]{1,0:T(8,128)(2,1)}, bf16[256,2048]{1,0:T(8,128)(2,1)}, u32[]{:S(2)}, u32[]{:S(2)}) collective-permute-start(bf16[256,2048]{1,0:T(8,128)(2,1)} %fusion.93), channel_id=1, source_target_pairs={{0,1},{1,2},{2,3},{3,0},{4,5},{5,6},{6,7},{7,4},{8,9},{9,10},{10,1... | collective-permute-start | bytes 3145736 | tf_op jit(solution)/shard_map/ppermute | solution.py:159
  (200 other events, 2074.3 us)
Sparse Core Ops, SparseCore 0:
  29.3 41.1 all-gather.11
  72.3 54.2 all-gather.13
  128.5 54.2 all-gather.15
  184.6 116.3 all-gather.17
  302.6 116.3 all-gather.19
  420.7 116.3 all-gather.21
  540.7 146.3 reduce-scatter.4
  690.7 146.3 reduce-scatter.10
  840.7 146.3 reduce-scatter.8
  1056.6 64.1 reduce-scatter.6

commit v6 on v5

--- a/solution.py
+++ b/solution.py
@@ -436,13 +436,13 @@
     ffn_rows_back = exchange(ffn_rows_grad.reshape(experts, capacity, -1)).reshape(
         experts * capacity, -1
     )
+    ffn_rows_grad, hidden = lax.optimization_barrier((ffn_rows_grad, hidden))
+    ffn_branch = mm(hidden, down_all).astype(bf16)
+    ffn_branch, ffn_rows, gate_grad = lax.optimization_barrier((ffn_branch, ffn_rows, gate_grad))
+    ffn_back = exchange_direct(ffn_branch.reshape(experts, capacity, -1), experts, own)
     gate_part = mm_tn(ffn_rows, gate_grad).astype(bf16)
-    up_part = mm_tn(ffn_rows, up_grad).astype(bf16)
-    gate_part, up_part, ffn_rows_back = lax.optimization_barrier(
-        (gate_part, up_part, ffn_rows_back)
-    )
+    gate_part, ffn_rows_back = lax.optimization_barrier((gate_part, ffn_rows_back))
     gate_sum = reduce_dp(gate_part)
-    up_sum = reduce_dp(up_part)
     gate_pull = jnp.sum(take_back(ffn_place, ffn_rows_back[:, model_width:]), 2).T
     ffn_logit_grad = router_back(ffn_gate, ffn_picks, gate_pull)
     normed_two_grad = mm(ffn_place[0] + ffn_place[1], ffn_rows_back[:, :model_width]) + jnp.dot(
@@ -454,13 +454,17 @@
     att_logit_grad = router_back(
         att_gate, att_picks, jnp.sum(att_picked * mixed_grad[None], 2).T
     )
-    packed_grads, hidden = lax.optimization_barrier(
-        (send_grads(att_place, att_gate, mixed_grad, experts), hidden)
-    )
-    ffn_branch = mm(hidden, down_all).astype(bf16)
-    att_grad_rows, ffn_branch = lax.optimization_barrier((exchange(packed_grads), ffn_branch))
+    packed_grads, up_grad = lax.optimization_barrier(
+        (send_grads(att_place, att_gate, mixed_grad, experts), up_grad)
+    )
+    up_part = mm_tn(ffn_rows, up_grad).astype(bf16)
+    att_grad_rows, up_part, ffn_back = lax.optimization_barrier(
+        (exchange(packed_grads), up_part, ffn_back)
+    )
+    up_sum = reduce_dp(up_part)
     att_grad_rows = att_grad_rows.reshape(-1, model_width)
-    ffn_back = exchange(ffn_branch.reshape(experts, capacity, -1))
+    ffn_picked = take_back(ffn_place, ffn_back)
+    result = mixed_stream + jnp.sum(ffn_gate.T[:, :, None] * ffn_picked, 0)
     att_grad_rows, down_sum = lax.optimization_barrier((att_grad_rows, down_sum))
     attended_grad = mm_nt(att_grad_rows, output_all).astype(bf16)
     query_grad = jnp.zeros(queries.shape, f32)
@@ -469,27 +473,25 @@
         k = step % experts
         start = backs[k] * width
         group_grad = lax.dynamic_slice_in_dim(
-            attended_grad if step < 4 else late_grad, start, width, 1
+            late_grad if k == 0 else attended_grad, start, width, 1
         )
         group_query_grad, key_grad, value_grad = attend_back(*saved[k], group_grad)
         query_grad = lax.dynamic_update_slice_in_dim(query_grad, group_query_grad, start, 1)
         part = jnp.concatenate([key_grad, value_grad], 1)
+        if k == 0:
+            output_sum = reduce_swaps(mm_tn(attended, att_grad_rows).astype(bf16))
+            kv_grad, query_rows = lax.optimization_barrier((kv_grad, query_rows))
         if kv_grad is not None:
             part = part + kv_grad.astype(f32)
         if k == 0:
             kv_grad = part
             continue
         part = part.astype(bf16)
-        if step == 2:
-            part, att_grad_rows, ffn_back, late_grad = lax.optimization_barrier(
-                (part, att_grad_rows, ffn_back, attended_grad)
+        if step == experts - 1:
+            part, late_grad, att_grad_rows = lax.optimization_barrier(
+                (part, attended_grad, att_grad_rows)
             )
-        if step == experts - 1:
-            part, query_rows = lax.optimization_barrier((part, query_rows))
         kv_grad = ring_step(part, experts)
-    ffn_picked = take_back(ffn_place, ffn_back)
-    result = mixed_stream + jnp.sum(ffn_gate.T[:, :, None] * ffn_picked, 0)
-    output_sum = reduce_swaps(mm_tn(attended, att_grad_rows).astype(bf16))
     query_raw_grad = rotate_back(query_grad, query_cos, query_sin).astype(bf16)
     query_sum = reduce_swaps(mm_tn(query_rows, query_raw_grad).astype(bf16))
     att_rows_grad = mm_nt(query_raw_grad, query_all).astype(bf16)
@@ -540,9 +542,10 @@
             normed_one_grad, shared_part = lax.optimization_barrier(
                 (normed_one_grad, reduce_dp(shared_part))
             )
-        if step == 1:
-            normed_one_grad, output_sum = lax.optimization_barrier((normed_one_grad, output_sum))
-    normed_one_grad, query_sum = lax.optimization_barrier((normed_one_grad, query_sum))
+        if k == 0:
+            normed_one_grad, query_sum, output_sum = lax.optimization_barrier(
+                (normed_one_grad, query_sum, output_sum)
+            )
     normed_one_grad = normed_one_grad + router_grad
     input_grad = mixed_grad + norm_back(inputs, inverse_one, gain_first, normed_one_grad)
     shared_sum = exchange(shared_part.reshape(experts, shard_rows, -1)).astype(f32)

time: 1190 us -> 1290 us (1.084)
  waiting for transfers between devices: 391 us -> 474 us
  starting transfers between devices: 64.8 us -> 92.1 us
    ppermute x3 -> x6, waiting for transfers between devices: 8.33 us -> 65.4 us  [exchange_direct(): lax.ppermute(block, 'expert', [(i, (i + k) % experts) for i in range(expe...]
    ppermute x12, starting transfers between devices: 16.2 us -> 42.5 us  [ring_step(): lax.ppermute(block, 'expert', [(i, (i + 1) % experts) for i in range(expe...]
    ppermute x12, waiting for transfers between devices: 179 us -> 205 us  [ring_step(): lax.ppermute(block, 'expert', [(i, (i + 1) % experts) for i in range(expe...]
    ppermute x10, waiting for transfers between devices: 38.7 us -> 64.4 us  [swap(): return lax.ppermute(block, 'dp', [(i, i ^ bit) for i in range(8)])]
    all_to_all x7 -> x6, waiting for transfers between devices: 157 us -> 132 us  [exchange(): lax.all_to_all(packed, 'expert', split_axis=0, concat_axis=0, tiled=True)]
    all_to_all x7 -> x6, starting transfers between devices: 30.5 us -> 26.2 us  [exchange(): lax.all_to_all(packed, 'expert', split_axis=0, concat_axis=0, tiled=True)]
    unnamed x389 -> x375, local copies, waits for them, and re-layouts: 46.1 us -> 45.2 us
  transfers between devices with their start and end apart: 42 -> 44, of which waited for: 24 -> 24; matrix products, arithmetic and copies ran while one was open for 55% -> 50% of each run, Pallas kernels for 0% -> 0%
where the time goes in v6:
time: 1290 us; the launch traced here: 1280 us
  waiting for transfers between devices  474 us (37%)
  matrix products  438 us (34%)
  local copies, waits for them, and re-layouts  132 us (10%)
  other arithmetic  126 us (10%)
  starting transfers between devices  92.1 us (7%)
  between operations  17.5 us (1%)
    ppermute x12, waiting for transfers between devices, ring_step(): lax.ppermute(block, 'expert', [(i, (i + 1) % experts) for i in range(expe...  205 us
    all_to_all x6, waiting for transfers between devices, exchange(): lax.all_to_all(packed, 'expert', split_axis=0, concat_axis=0, tiled=True)  132 us
    dot_general x18, matrix products, mm(): return jnp.dot(left, right, preferred_element_type=f32)  113 us
    dot_general x11, matrix products, mm_tn(): lax.dot_general(left, right, (((0,), (0,)), ((), ())), preferred_element_...  107 us
    dot_general x6, matrix products, mm_nt(): lax.dot_general(left, right, (((1,), (1,)), ((), ())), preferred_element_...  104 us
    ppermute x6, waiting for transfers between devices, exchange_direct(): lax.ppermute(block, 'expert', [(i, (i + k) % experts) for i in range(expe...  65.4 us
    ppermute x10, waiting for transfers between devices, swap(): return lax.ppermute(block, 'dp', [(i, i ^ bit) for i in range(8)])  64.4 us
    unnamed x375, local copies, waits for them, and re-layouts  45.2 us
  transfers between devices with their start and end apart: 44, of which 24 were waited for; matrix products, arithmetic and copies ran while one was open for 50% of the time, Pallas kernels for 0%

profile of v6, /device:TPU:0, one launch (start us, length us, event | category | flops | bytes accessed | tf_op | source)
XLA Modules:
  0.0 1280.2 jit_solution(17194381219248414292)
XLA Ops:
  38.4 24.9 %collective-permute-done = bf16[256,2176]{1,0:T(8,128)(2,1)} collective-permute-done((bf16[256,2176]{1,0:T(8,128)(2,1)S(1)}, bf16[256,2176]{1,0:T(8,128)(2,1)}, u32[]{:S(2)}, u32[]{:S(2)}) %collective-permute-start) | collective-permute-done | bytes 1114144 | tf_op jit(solution)/shard_map/ppermute | solution.py:159
  68.2 22.1 %collective-permute-done.1 = bf16[256,2176]{1,0:T(8,128)(2,1)} collective-permute-done((bf16[256,2176]{1,0:T(8,128)(2,1)}, bf16[256,2176]{1,0:T(8,128)(2,1)}, u32[]{:S(2)}, u32[]{:S(2)}) %collective-permute-start.1) | collective-permute-done | bytes 1114144 | tf_op jit(solution)/shard_map/ppermute | solution.py:159
  94.2 22.1 %collective-permute-done.2 = bf16[256,2176]{1,0:T(8,128)(2,1)S(1)} collective-permute-done((bf16[256,2176]{1,0:T(8,128)(2,1)}, bf16[256,2176]{1,0:T(8,128)(2,1)S(1)}, u32[]{:S(2)}, u32[]{:S(2)}) %collective-permute-start.2) | collective-permute-done | bytes 1114144 | tf_op jit(solution)/shard_map/ppermute | solution.py:159
  150.3 12.4 copy.272
  162.7 10.0 fusion.233
  173.8 20.7 %collective-permute-done.6 = bf16[1024,1024]{0,1:T(8,128)(2,1)} collective-permute-done((bf16[1024,1024]{0,1:T(8,128)(2,1)}, bf16[1024,1024]{0,1:T(8,128)(2,1)}, u32[]{:S(2)}, u32[]{:S(2)}) %collective-permute-start.6) | collective-permute-done | bytes 2097184 | tf_op jit(solution)/shard_map/ppermute | solution.py:159
  223.0 17.3 %collective-permute-done.7 = bf16[1024,1024]{0,1:T(8,128)(2,1)} collective-permute-done((bf16[1024,1024]{0,1:T(8,128)(2,1)}, bf16[1024,1024]{0,1:T(8,128)(2,1)}, u32[]{:S(2)}, u32[]{:S(2)}) %collective-permute-start.7) | collective-permute-done | bytes 2097184 | tf_op jit(solution)/shard_map/ppermute | solution.py:159
  253.8 31.3 %collective-permute-done.8 = bf16[1024,1024]{0,1:T(8,128)(2,1)S(1)} collective-permute-done((bf16[1024,1024]{0,1:T(8,128)(2,1)}, bf16[1024,1024]{0,1:T(8,128)(2,1)S(1)}, u32[]{:S(2)}, u32[]{:S(2)}) %collective-permute-start.8) | collective-permute-done | bytes 2097184 | tf_op jit(solution)/shard_map/ppermute | solution.py:159
  297.7 10.3 fusion.72
  317.2 48.7 %all-to-all-done = bf16[4,160,2048]{2,1,0:T(8,128)(2,1)S(1)} async-done(((bf16[4,160,2048]{2,1,0:T(8,128)(2,1)}), bf16[4,160,2048]{2,1,0:T(8,128)(2,1)S(1)}, u32[]{:S(2)}, u32[]{:S(2)}) %all-to-all-start) | async-done | bytes 2621472 | tf_op jit(solution)/shard_map/all_to_all | solution.py:145
  387.1 51.9 %all-to-all-done.1 = bf16[4,160,2048]{2,1,0:T(8,128)(2,1)} async-done(((bf16[4,160,2048]{2,1,0:T(8,128)(2,1)}), bf16[4,160,2048]{2,1,0:T(8,128)(2,1)}, u32[]{:S(2)}, u32[]{:S(2)}) %all-to-all-start.1) | async-done | bytes 2621472 | tf_op jit(solution)/shard_map/all_to_all | solution.py:145
  442.8 23.6 %fusion.10 = f32[640,5632]{1,0:T(8,128)} fusion(bf16[640,2048]{1,0:T(8,128)(2,1)} %bitcast.47, bf16[1,2048,5632]{2,1,0:T(8,128)(2,1)} %all-gather.18.cloned.1.call-done), kind=kOutput, calls=%fused_computation.10 | convolution fusion | flops 14763950080 | bytes 40108032 | tf_op jit(solution)/shard_map/dot_general | solution.py:82
  466.4 32.1 %multiply_convert_fusion.2 = (bf16[640,5632]{1,0:T(8,128)(2,1)}, f32[640,5632]{1,0:T(8,128)}) fusion(f32[640,5632]{1,0:T(8,128)} %fusion.10, bf16[640,2048]{1,0:T(8,128)(2,1)} %bitcast.47, bf16[1,2048,5632]{2,1,0:T(8,128)(2,1)} %all-gather.20.cloned.1.call-done), kind=kOutput, calls=%fused_computation.18 | convolution fusion | flops 14785576960 | bytes 61734912 | tf_op jit(solution)/shard_map/dot_general | solution.py:82
  507.2 24.9 %convolution_convert_fusion = bf16[5632,2048]{1,0:T(8,128)(2,1)} fusion(bf16[640,5632]{1,0:T(8,128)(2,1)} %get-tuple-element.64, f32[640]{0:T(1024)S(1)} %convert_reduce_fusion.2, bf16[640,2176]{1,0:T(8,128)(2,1)S(1)} %bitcast.395), kind=kOutput, calls=%fused_computation.12 | convolution fusion | flops 14779416576 | bytes 32903168 | tf_op jit(solution)/shard_map/dot_general | solution.py:86
  537.1 38.6 %multiply_convert_fusion.1 = (bf16[640,5632]{1,0:T(8,128)(2,1)}, bf16[640,5632]{1,0:T(8,128)(2,1)}, f32[640]{0:T(1024)S(1)}) fusion(f32[640,5632]{1,0:T(8,128)} %fusion.10, f32[640,5632]{1,0:T(8,128)} %get-tuple-element.207, f32[640]{0:T(1024)S(1)} %convert_reduce_fusion.2, bf16[640,5632]{1,0:T(8,128)(2,1)} %get-tuple-element.64, ...), kind=kOutput, calls=%fused_computation.17 | convolution fusion | flops 14825225216 | bytes 76157952 | tf_op jit(solution)/shard_map/dot_general | solution.py:90
  576.0 20.6 %fusion.4 = f32[640,2048]{1,0:T(8,128)S(1)} fusion(bf16[640,5632]{1,0:T(8,128)(2,1)} %get-tuple-element.71, bf16[1,2048,5632]{2,1,0:T(8,128)(2,1)} %all-gather.20.cloned.1.call-done), kind=kOutput, calls=%fused_computation.4 | convolution fusion | flops 14763950080 | bytes 35520512 | tf_op jit(solution)/shard_map/dot_general | solution.py:90
  596.5 18.7 %add_convert_fusion.1 = bf16[640,2048]{1,0:T(8,128)(2,1)S(1)} fusion(f32[640,2048]{1,0:T(8,128)S(1)} %fusion.4, bf16[640,5632]{1,0:T(8,128)(2,1)S(1)} %copy-done.162, bf16[1,2048,5632]{2,1,0:T(8,128)(2,1)} %all-gather.18.cloned.1.call-done), kind=kOutput, calls=%fused_computation.75 | convolution fusion | flops 14766571520 | bytes 38141952 | tf_op jit(solution)/shard_map/dot_general | solution.py:90
  621.5 21.5 %fusion.66 = bf16[640,2048]{1,0:T(8,128)(2,1)} fusion(bf16[640,5632]{1,0:T(8,128)(2,1)} %get-tuple-element.64, bf16[1,5632,2048]{2,1,0:T(8,128)(2,1)} %all-gather.22.cloned.1.call-done), kind=kOutput, calls=%fused_computation.114 | convolution fusion | flops 14765260800 | bytes 32899072 | tf_op jit(solution)/shard_map/dot_general | solution.py:82
  643.0 25.6 %convolution_convert_fusion.2 = bf16[2048,5632]{1,0:T(8,128)(2,1)} fusion(bf16[640,2048]{1,0:T(8,128)(2,1)} %bitcast.47, bf16[640,5632]{1,0:T(8,128)(2,1)} %get-tuple-element.67), kind=kOutput, calls=%fused_computation.14 | convolution fusion | flops 14775484416 | bytes 32899072 | tf_op jit(solution)/shard_map/dot_general | solution.py:86
  668.6 16.0 %all-to-all-done.3 = bf16[4,160,2176]{2,1,0:T(8,128)(2,1)S(1)} async-done(((bf16[4,160,2176]{2,1,0:T(8,128)(2,1)}), bf16[4,160,2176]{2,1,0:T(8,128)(2,1)S(1)}, u32[]{:S(2)}, u32[]{:S(2)}) %all-to-all-start.3) | async-done | bytes 2785312 | tf_op jit(solution)/shard_map/all_to_all | solution.py:145
  714.7 37.0 %collective-permute-done.10 = bf16[1,160,2048]{2,1,0:T(8,128)(2,1)} collective-permute-done((bf16[1,160,2048]{2,1,0:T(8,128)(2,1)}, bf16[1,160,2048]{2,1,0:T(8,128)(2,1)}, u32[]{:S(2)}, u32[]{:S(2)}) %collective-permute-start.10) | collective-permute-done | bytes 655392 | tf_op jit(solution)/shard_map/ppermute | solution.py:153
  753.7 20.1 %collective-permute-done.11 = bf16[1,160,2048]{2,1,0:T(8,128)(2,1)S(1)} collective-permute-done((bf16[1,160,2048]{2,1,0:T(8,128)(2,1)S(1)}, bf16[1,160,2048]{2,1,0:T(8,128)(2,1)S(1)}, u32[]{:S(2)}, u32[]{:S(2)}) %collective-permute-start.11) | collective-permute-done | bytes 655392 | tf_op jit(solution)/shard_map/ppermute | solution.py:153
  774.7 25.6 %convolution_convert_fusion.1 = bf16[2048,5632]{1,0:T(8,128)(2,1)} fusion(bf16[640,2048]{1,0:T(8,128)(2,1)} %bitcast.47, bf16[640,5632]{1,0:T(8,128)(2,1)} %get-tuple-element.71), kind=kOutput, calls=%fused_computation.13 | convolution fusion | flops 14775484416 | bytes 32899072 | tf_op jit(solution)/shard_map/dot_general | solution.py:86
  821.7 9.7 fusion.63
  853.6 36.1 %collective-permute-start.12 = (bf16[1024,1024]{0,1:T(8,128)(2,1)}, bf16[1024,1024]{0,1:T(8,128)(2,1)}, u32[]{:S(2)}, u32[]{:S(2)}) collective-permute-start(bf16[1024,1024]{0,1:T(8,128)(2,1)} %pad_maximum_fusion.6), channel_id=1, source_target_pairs={{0,1},{1,2},{2,3},{3,0},{4,5},{5,6},{6,7},{7,4},{8,9},{9,10},{10,1... | collective-permute-start | bytes 6291464 | tf_op jit(solution)/shard_map/ppermute | solution.py:159
  957.3 40.5 %collective-permute-done.13 = bf16[1024,1024]{0,1:T(8,128)(2,1)} collective-permute-done((bf16[1024,1024]{0,1:T(8,128)(2,1)}, bf16[1024,1024]{0,1:T(8,128)(2,1)}, u32[]{:S(2)}, u32[]{:S(2)}) %collective-permute-start.13) | collective-permute-done | bytes 2097184 | tf_op jit(solution)/shard_map/ppermute | solution.py:159
  1001.6 9.1 convolution_convert_fusion.3
  1039.2 9.8 fusion.69
  1049.0 20.3 %collective-permute-done.14 = bf16[1024,1024]{0,1:T(8,128)(2,1)} collective-permute-done((bf16[1024,1024]{0,1:T(8,128)(2,1)}, bf16[1024,1024]{0,1:T(8,128)(2,1)}, u32[]{:S(2)}, u32[]{:S(2)}) %collective-permute-start.14) | collective-permute-done | bytes 2097184 | tf_op jit(solution)/shard_map/ppermute | solution.py:159
  1152.9 29.2 %collective-permute-done.24 = bf16[2,256,1024]{2,1,0:T(8,128)(2,1)} collective-permute-done((bf16[2,256,1024]{2,1,0:T(8,128)(2,1)}, bf16[2,256,1024]{2,1,0:T(8,128)(2,1)}, u32[]{:S(2)}, u32[]{:S(2)}) %collective-permute-start.24) | collective-permute-done | bytes 1048608 | tf_op jit(solution)/shard_map/ppermute | solution.py:234
  1202.9 21.0 %collective-permute-done.19 = bf16[2,256,1024]{2,1,0:T(8,128)(2,1)S(1)} collective-permute-done((bf16[2,256,1024]{2,1,0:T(8,128)(2,1)S(1)}, bf16[2,256,1024]{2,1,0:T(8,128)(2,1)S(1)}, u32[]{:S(2)}, u32[]{:S(2)}) %collective-permute-start.19) | collective-permute-done | bytes 1048608 | tf_op jit(solution)/shard_map/ppermute | solution.py:234
  1228.5 9.2 collective-permute-done.20
  (711 shorter events, 501.8 us)
Async XLA Ops:
  7.2 115.2 %all-gather.12.cloned.1.call-start = ((), (), s32[]{:S(2)}) async-start(), calls=%async_computation.10 | async-start | bytes 5308416 | tf_op jit(solution)/shard_map/all_gather | solution.py:311
  29.2 121.1 %all-gather.14.cloned.1.call-start = ((), (), s32[]{:S(2)}) async-start(), calls=%async_computation.15 | async-start | bytes 9437184 | tf_op jit(solution)/shard_map/all_gather | solution.py:226
  29.9 267.7 %all-gather.16.cloned.1.call-start = ((), (), s32[]{:S(2)}) async-start(), calls=%async_computation.16 | async-start | bytes 9437184 | tf_op jit(solution)/shard_map/all_gather | solution.py:226
  30.7 412.1 %all-gather.18.cloned.1.call-start = ((), (), s32[]{:S(2)}) async-start(), calls=%async_computation.17 | async-start | bytes 25952256 | tf_op jit(solution)/shard_map/all_gather | solution.py:226
  31.3 435.1 %all-gather.20.cloned.1.call-start = ((), (), s32[]{:S(2)}) async-start(), calls=%async_computation.18 | async-start | bytes 25952256 | tf_op jit(solution)/shard_map/all_gather | solution.py:226
  31.8 505.3 %all-gather.22.cloned.1.call-start = ((), (), s32[]{:S(2)}) async-start(), calls=%async_computation.19 | async-start | bytes 25952256 | tf_op jit(solution)/shard_map/all_gather | solution.py:226
  34.7 28.6 %collective-permute-start = (bf16[256,2176]{1,0:T(8,128)(2,1)S(1)}, bf16[256,2176]{1,0:T(8,128)(2,1)}, u32[]{:S(2)}, u32[]{:S(2)}) collective-permute-start(bf16[256,2176]{1,0:T(8,128)(2,1)S(1)} %concatenate.65), channel_id=1, source_target_pairs={{0,1},{1,2},{2,3},{3,0},{4,5},{5,6},{6,7},{7,4},{8,9},{9,10},{10,1... | collective-permute-start | bytes 3342344 | tf_op jit(solution)/shard_map/ppermute | solution.py:159
  147.9 46.6 %collective-permute-start.6 = (bf16[1024,1024]{0,1:T(8,128)(2,1)}, bf16[1024,1024]{0,1:T(8,128)(2,1)}, u32[]{:S(2)}, u32[]{:S(2)}) collective-permute-start(bf16[1024,1024]{0,1:T(8,128)(2,1)} %pad_maximum_fusion.5), channel_id=1, source_target_pairs={{0,1},{1,2},{2,3},{3,0},{4,5},{5,6},{6,7},{7,4},{8,9},{9,10},{10,1... | collective-permute-start | bytes 6291464 | tf_op jit(solution)/shard_map/ppermute | solution.py:159
  194.5 45.8 %collective-permute-start.7 = (bf16[1024,1024]{0,1:T(8,128)(2,1)}, bf16[1024,1024]{0,1:T(8,128)(2,1)}, u32[]{:S(2)}, u32[]{:S(2)}) collective-permute-start(bf16[1024,1024]{0,1:T(8,128)(2,1)} %collective-permute-done.6), channel_id=1, source_target_pairs={{0,1},{1,2},{2,3},{3,0},{4,5},{5,6},{6,7},{7,4},{8,9},{9,10},{10,1... | collective-permute-start | bytes 6291464 | tf_op jit(solution)/shard_map/ppermute | solution.py:159
  240.3 44.7 %collective-permute-start.8 = (bf16[1024,1024]{0,1:T(8,128)(2,1)}, bf16[1024,1024]{0,1:T(8,128)(2,1)S(1)}, u32[]{:S(2)}, u32[]{:S(2)}) collective-permute-start(bf16[1024,1024]{0,1:T(8,128)(2,1)} %collective-permute-done.7), channel_id=1, source_target_pairs={{0,1},{1,2},{2,3},{3,0},{4,5},{5,6},{6,7},{7,4},{8,9},{9,10},{10,1... | collective-permute-start | bytes 6291464 | tf_op jit(solution)/shard_map/ppermute | solution.py:159
  308.0 57.9 %all-to-all-start = ((bf16[4,160,2048]{2,1,0:T(8,128)(2,1)}), bf16[4,160,2048]{2,1,0:T(8,128)(2,1)S(1)}, u32[]{:S(2)}, u32[]{:S(2)}) async-start(bf16[4,160,2048]{2,1,0:T(8,128)(2,1)} %bitcast.438), calls=%async_computation | async-start | bytes 5242880 | tf_op jit(solution)/shard_map/all_to_all | solution.py:145
  375.4 63.6 %all-to-all-start.1 = ((bf16[4,160,2048]{2,1,0:T(8,128)(2,1)}), bf16[4,160,2048]{2,1,0:T(8,128)(2,1)}, u32[]{:S(2)}, u32[]{:S(2)}) async-start(bf16[4,160,2048]{2,1,0:T(8,128)(2,1)} %bitcast.46), calls=%async_computation.1 | async-start | bytes 5242880 | tf_op jit(solution)/shard_map/all_to_all | solution.py:145
  439.0 66.1 %all-to-all-start.2 = ((bf16[4,160,2176]{2,1,0:T(8,128)(2,1)}), bf16[4,160,2176]{2,1,0:T(8,128)(2,1)S(1)}, u32[]{:S(2)}, u32[]{:S(2)}) async-start(bf16[4,160,2176]{2,1,0:T(8,128)(2,1)} %pad_maximum_fusion.2), calls=%async_computation.2 | async-start | bytes 5570560 | tf_op jit(solution)/shard_map/all_to_all | solution.py:145
  442.7 379.0 %reduce-scatter.5.cloned.1.call-start = ((), (), s32[]{:S(2)}) async-start(), calls=%async_computation.11 | async-start | bytes 25952256 | tf_op jit(solution)/shard_map/reduce_scatter | solution.py:230
  617.1 67.5 %all-to-all-start.3 = ((bf16[4,160,2176]{2,1,0:T(8,128)(2,1)}), bf16[4,160,2176]{2,1,0:T(8,128)(2,1)S(1)}, u32[]{:S(2)}, u32[]{:S(2)}) async-start(bf16[4,160,2176]{2,1,0:T(8,128)(2,1)} %bitcast.54), calls=%async_computation.3 | async-start | bytes 5570560 | tf_op jit(solution)/shard_map/all_to_all | solution.py:145
  621.5 329.8 %reduce-scatter.9.cloned.1.call-start = ((), (), s32[]{:S(2)}) async-start(), calls=%async_computation.13 | async-start | bytes 25952256 | tf_op jit(solution)/shard_map/reduce_scatter | solution.py:230
  689.7 61.9 %collective-permute-start.10 = (bf16[1,160,2048]{2,1,0:T(8,128)(2,1)}, bf16[1,160,2048]{2,1,0:T(8,128)(2,1)}, u32[]{:S(2)}, u32[]{:S(2)}) collective-permute-start(bf16[1,160,2048]{2,1,0:T(8,128)(2,1)} %get-tuple-element.159), channel_id=1, source_target_pairs={{0,2},{1,3},{2,0},{3,1},{4,6},{5,7},{6,4},{7,5},{8,10},{9,11},{10,... | collective-permute-start | bytes 1966088 | tf_op jit(solution)/shard_map/ppermute | solution.py:153
  704.0 96.4 %all-to-all-start.4 = ((bf16[4,160,2048]{2,1,0:T(8,128)(2,1)}), bf16[4,160,2048]{2,1,0:T(8,128)(2,1)}, u32[]{:S(2)}, u32[]{:S(2)}) async-start(bf16[4,160,2048]{2,1,0:T(8,128)(2,1)} %bitcast.398), calls=%async_computation.4 | async-start | bytes 5242880 | tf_op jit(solution)/shard_map/all_to_all | solution.py:145
  708.6 439.1 %reduce-scatter.11.cloned.1.call-start = ((), (), s32[]{:S(2)}) async-start(), calls=%async_computation.14 | async-start | bytes 25952256 | tf_op jit(solution)/shard_map/reduce_scatter | solution.py:230
  708.7 65.1 %collective-permute-start.11 = (bf16[1,160,2048]{2,1,0:T(8,128)(2,1)S(1)}, bf16[1,160,2048]{2,1,0:T(8,128)(2,1)S(1)}, u32[]{:S(2)}, u32[]{:S(2)}) collective-permute-start(bf16[1,160,2048]{2,1,0:T(8,128)(2,1)S(1)} %get-tuple-element.158), channel_id=1, source_target_pairs={{0,3},{1,0},{2,1},{3,2},{4,7},{5,4},{6,5},{7,6},{8,11},{9,8},{10,9... | collective-permute-start | bytes 1966088 | tf_op jit(solution)/shard_map/ppermute | solution.py:153
  800.4 440.5 %reduce-scatter.7.cloned.1.call-start = ((), (), s32[]{:S(2)}) async-start(), calls=%async_computation.12 | async-start | bytes 5308416 | tf_op jit(solution)/shard_map/reduce_scatter | solution.py:230
  853.6 91.5 %collective-permute-start.12 = (bf16[1024,1024]{0,1:T(8,128)(2,1)}, bf16[1024,1024]{0,1:T(8,128)(2,1)}, u32[]{:S(2)}, u32[]{:S(2)}) collective-permute-start(bf16[1024,1024]{0,1:T(8,128)(2,1)} %pad_maximum_fusion.6), channel_id=1, source_target_pairs={{0,1},{1,2},{2,3},{3,0},{4,5},{5,6},{6,7},{7,4},{8,9},{9,10},{10,1... | collective-permute-start | bytes 6291464 | tf_op jit(solution)/shard_map/ppermute | solution.py:159
  949.1 48.7 %collective-permute-start.13 = (bf16[1024,1024]{0,1:T(8,128)(2,1)}, bf16[1024,1024]{0,1:T(8,128)(2,1)}, u32[]{:S(2)}, u32[]{:S(2)}) collective-permute-start(bf16[1024,1024]{0,1:T(8,128)(2,1)} %fusion.56), channel_id=1, source_target_pairs={{0,1},{1,2},{2,3},{3,0},{4,5},{5,6},{6,7},{7,4},{8,9},{9,10},{10,1... | collective-permute-start | bytes 6291464 | tf_op jit(solution)/shard_map/ppermute | solution.py:159
  1015.5 119.8 %collective-permute-start.23 = (bf16[2,2,256,2048]{3,2,1,0:T(8,128)(2,1)}, bf16[2,2,256,2048]{3,2,1,0:T(8,128)(2,1)}, u32[]{:S(2)}, u32[]{:S(2)}) collective-permute-start(bf16[2,2,256,2048]{3,2,1,0:T(8,128)(2,1)} %dynamic-slice_bitcast_fusion), channel_id=1, source_target_pairs={{0,4},{4,0},{8,12},{12,8},{16,20},{20,16},{24,28},{28,24},{1,5},{5... | collective-permute-start | bytes 12582920 | tf_op jit(solution)/shard_map/ppermute | solution.py:234
  1018.9 50.4 %collective-permute-start.14 = (bf16[1024,1024]{0,1:T(8,128)(2,1)}, bf16[1024,1024]{0,1:T(8,128)(2,1)}, u32[]{:S(2)}, u32[]{:S(2)}) collective-permute-start(bf16[1024,1024]{0,1:T(8,128)(2,1)} %fusion.55), channel_id=1, source_target_pairs={{0,1},{1,2},{2,3},{3,0},{4,5},{5,6},{6,7},{7,4},{8,9},{9,10},{10,1... | collective-permute-start | bytes 6291464 | tf_op jit(solution)/shard_map/ppermute | solution.py:159
  1087.4 100.7 %collective-permute-start.18 = (bf16[2,2,256,2048]{3,2,1,0:T(8,128)(2,1)}, bf16[2,2,256,2048]{3,2,1,0:T(8,128)(2,1)}, u32[]{:S(2)}, u32[]{:S(2)}) collective-permute-start(bf16[2,2,256,2048]{3,2,1,0:T(8,128)(2,1)} %dynamic-slice_bitcast_fusion.1), channel_id=1, source_target_pairs={{0,4},{4,0},{8,12},{12,8},{16,20},{20,16},{24,28},{28,24},{1,5},{5... | collective-permute-start | bytes 12582920 | tf_op jit(solution)/shard_map/ppermute | solution.py:234
  1135.3 61.3 %collective-permute-start.16 = (bf16[256,2048]{1,0:T(8,128)(2,1)S(1)}, bf16[256,2048]{1,0:T(8,128)(2,1)}, u32[]{:S(2)}, u32[]{:S(2)}) collective-permute-start(bf16[256,2048]{1,0:T(8,128)(2,1)S(1)} %fusion.92), channel_id=1, source_target_pairs={{0,1},{1,2},{2,3},{3,0},{4,5},{5,6},{6,7},{7,4},{8,9},{9,10},{10,1... | collective-permute-start | bytes 3145736 | tf_op jit(solution)/shard_map/ppermute | solution.py:159
  1144.3 37.8 %collective-permute-start.24 = (bf16[2,256,1024]{2,1,0:T(8,128)(2,1)}, bf16[2,256,1024]{2,1,0:T(8,128)(2,1)}, u32[]{:S(2)}, u32[]{:S(2)}) collective-permute-start(bf16[2,256,1024]{2,1,0:T(8,128)(2,1)} %dynamic-slice_bitcast_fusion.3), channel_id=1, source_target_pairs={{0,8},{4,12},{8,0},{12,4},{16,24},{20,28},{24,16},{28,20},{1,9},{5... | collective-permute-start | bytes 3145736 | tf_op jit(solution)/shard_map/ppermute | solution.py:234
  1146.9 38.2 %collective-permute-start.26 = (bf16[2,256,1024]{2,1,0:T(8,128)(2,1)}, bf16[2,256,1024]{2,1,0:T(8,128)(2,1)}, u32[]{:S(2)}, u32[]{:S(2)}) collective-permute-start(bf16[2,256,1024]{2,1,0:T(8,128)(2,1)} %dynamic-slice_bitcast_fusion.2), channel_id=1, source_target_pairs={{0,16},{4,20},{8,24},{12,28},{16,0},{20,4},{24,8},{28,12},{1,17},{... | collective-permute-start | bytes 3145736 | tf_op jit(solution)/shard_map/ppermute | solution.py:234
  1194.3 29.6 %collective-permute-start.19 = (bf16[2,256,1024]{2,1,0:T(8,128)(2,1)S(1)}, bf16[2,256,1024]{2,1,0:T(8,128)(2,1)S(1)}, u32[]{:S(2)}, u32[]{:S(2)}) collective-permute-start(bf16[2,256,1024]{2,1,0:T(8,128)(2,1)S(1)} %dynamic-slice_bitcast_fusion.5), channel_id=1, source_target_pairs={{0,8},{4,12},{8,0},{12,4},{16,24},{20,28},{24,16},{28,20},{1,9},{5... | collective-permute-start | bytes 3145736 | tf_op jit(solution)/shard_map/ppermute | solution.py:234
  1195.2 30.7 %collective-permute-start.21 = (bf16[2,256,1024]{2,1,0:T(8,128)(2,1)S(1)}, bf16[2,256,1024]{2,1,0:T(8,128)(2,1)S(1)}, u32[]{:S(2)}, u32[]{:S(2)}) collective-permute-start(bf16[2,256,1024]{2,1,0:T(8,128)(2,1)S(1)} %dynamic-slice_bitcast_fusion.4), channel_id=1, source_target_pairs={{0,16},{4,20},{8,24},{12,28},{16,0},{20,4},{24,8},{28,12},{1,17},{... | collective-permute-start | bytes 3145736 | tf_op jit(solution)/shard_map/ppermute | solution.py:234
  1198.8 42.1 %collective-permute-start.17 = (bf16[256,2048]{1,0:T(8,128)(2,1)S(1)}, bf16[256,2048]{1,0:T(8,128)(2,1)S(1)}, u32[]{:S(2)}, u32[]{:S(2)}) collective-permute-start(bf16[256,2048]{1,0:T(8,128)(2,1)S(1)} %fusion.93), channel_id=1, source_target_pairs={{0,1},{1,2},{2,3},{3,0},{4,5},{5,6},{6,7},{7,4},{8,9},{9,10},{10,1... | collective-permute-start | bytes 3145736 | tf_op jit(solution)/shard_map/ppermute | solution.py:159
  (196 other events, 2197.8 us)
Sparse Core Ops, SparseCore 0:
  29.3 41.1 all-gather.11
  72.3 54.2 all-gather.13
  128.5 54.2 all-gather.15
  184.6 116.3 all-gather.17
  302.6 116.3 all-gather.19
  420.7 116.3 all-gather.21
  540.7 146.3 reduce-scatter.4
  690.7 146.3 reduce-scatter.8
  840.7 146.4 reduce-scatter.10
  1127.5 68.9 reduce-scatter.6

commit v7 on v5

--- a/solution.py
+++ b/solution.py
@@ -428,24 +428,27 @@
         hidden_grad * up_value * sigmoid_gate * (1.0 + gate_value * (1.0 - sigmoid_gate))
     ).astype(bf16)
     up_grad = (hidden_grad * gate_value * sigmoid_gate).astype(bf16)
-    ffn_rows_grad = (mm_nt(gate_grad, gate_all) + mm_nt(up_grad, up_all)).astype(bf16)
-    ffn_rows_grad = jnp.concatenate([ffn_rows_grad, as_columns(row_pull)], 1)
-    ffn_rows_grad, gate_grad, up_grad = lax.optimization_barrier(
-        (ffn_rows_grad, gate_grad, up_grad)
-    )
-    ffn_rows_back = exchange(ffn_rows_grad.reshape(experts, capacity, -1)).reshape(
-        experts * capacity, -1
-    )
+    half = model_width // 2
+    left_grad = (mm_nt(gate_grad, gate_all[:half]) + mm_nt(up_grad, up_all[:half])).astype(bf16)
+    left_grad = jnp.concatenate([left_grad, as_columns(row_pull)], 1)
+    left_grad, gate_grad, up_grad = lax.optimization_barrier((left_grad, gate_grad, up_grad))
+    left_back = exchange(left_grad.reshape(experts, capacity, -1))
+    right_grad = (mm_nt(gate_grad, gate_all[half:]) + mm_nt(up_grad, up_all[half:])).astype(bf16)
+    left_back, right_grad, gate_grad, up_grad = lax.optimization_barrier(
+        (left_back, right_grad, gate_grad, up_grad)
+    )
+    right_back = exchange(right_grad.reshape(experts, capacity, -1))
     gate_part = mm_tn(ffn_rows, gate_grad).astype(bf16)
-    up_part = mm_tn(ffn_rows, up_grad).astype(bf16)
-    gate_part, up_part, ffn_rows_back = lax.optimization_barrier(
-        (gate_part, up_part, ffn_rows_back)
-    )
+    gate_part, right_back = lax.optimization_barrier((gate_part, right_back))
+    left_back = left_back.reshape(experts * capacity, -1)
+    right_back = right_back.reshape(experts * capacity, -1)
     gate_sum = reduce_dp(gate_part)
-    up_sum = reduce_dp(up_part)
-    gate_pull = jnp.sum(take_back(ffn_place, ffn_rows_back[:, model_width:]), 2).T
+    gate_pull = jnp.sum(take_back(ffn_place, left_back[:, half:]), 2).T
     ffn_logit_grad = router_back(ffn_gate, ffn_picks, gate_pull)
-    normed_two_grad = mm(ffn_place[0] + ffn_place[1], ffn_rows_back[:, :model_width]) + jnp.dot(
+    ffn_slots = ffn_place[0] + ffn_place[1]
+    normed_two_grad = jnp.concatenate(
+        [mm(ffn_slots, left_back[:, :half]), mm(ffn_slots, right_back)], 1
+    ) + jnp.dot(
         ffn_logit_grad, ffn_all.astype(f32).T, precision=highest
     )
     gain_two_part = jnp.sum(normed_two_grad * mixed_stream * inverse_two, 0)
@@ -454,11 +457,15 @@
     att_logit_grad = router_back(
         att_gate, att_picks, jnp.sum(att_picked * mixed_grad[None], 2).T
     )
-    packed_grads, hidden = lax.optimization_barrier(
-        (send_grads(att_place, att_gate, mixed_grad, experts), hidden)
+    packed_grads, hidden, up_grad = lax.optimization_barrier(
+        (send_grads(att_place, att_gate, mixed_grad, experts), hidden, up_grad)
     )
     ffn_branch = mm(hidden, down_all).astype(bf16)
-    att_grad_rows, ffn_branch = lax.optimization_barrier((exchange(packed_grads), ffn_branch))
+    up_part = mm_tn(ffn_rows, up_grad).astype(bf16)
+    att_grad_rows, ffn_branch, up_part = lax.optimization_barrier(
+        (exchange(packed_grads), ffn_branch, up_part)
+    )
+    up_sum = reduce_dp(up_part)
     att_grad_rows = att_grad_rows.reshape(-1, model_width)
     ffn_back = exchange(ffn_branch.reshape(experts, capacity, -1))
     att_grad_rows, down_sum = lax.optimization_barrier((att_grad_rows, down_sum))
@@ -474,6 +481,8 @@
         group_query_grad, key_grad, value_grad = attend_back(*saved[k], group_grad)
         query_grad = lax.dynamic_update_slice_in_dim(query_grad, group_query_grad, start, 1)
         part = jnp.concatenate([key_grad, value_grad], 1)
+        if k == 0:
+            kv_grad, output_sum = lax.optimization_barrier((kv_grad, output_sum))
         if kv_grad is not None:
             part = part + kv_grad.astype(f32)
         if k == 0:
@@ -484,12 +493,12 @@
             part, att_grad_rows, ffn_back, late_grad = lax.optimization_barrier(
                 (part, att_grad_rows, ffn_back, attended_grad)
             )
+            output_sum = reduce_swaps(mm_tn(attended, att_grad_rows).astype(bf16))
         if step == experts - 1:
             part, query_rows = lax.optimization_barrier((part, query_rows))
         kv_grad = ring_step(part, experts)
     ffn_picked = take_back(ffn_place, ffn_back)
     result = mixed_stream + jnp.sum(ffn_gate.T[:, :, None] * ffn_picked, 0)
-    output_sum = reduce_swaps(mm_tn(attended, att_grad_rows).astype(bf16))
     query_raw_grad = rotate_back(query_grad, query_cos, query_sin).astype(bf16)
     query_sum = reduce_swaps(mm_tn(query_rows, query_raw_grad).astype(bf16))
     att_rows_grad = mm_nt(query_raw_grad, query_all).astype(bf16)
@@ -540,9 +549,8 @@
             normed_one_grad, shared_part = lax.optimization_barrier(
                 (normed_one_grad, reduce_dp(shared_part))
             )
-        if step == 1:
-            normed_one_grad, output_sum = lax.optimization_barrier((normed_one_grad, output_sum))
-    normed_one_grad, query_sum = lax.optimization_barrier((normed_one_grad, query_sum))
+        if step == 2:
+            normed_one_grad, query_sum = lax.optimization_barrier((normed_one_grad, query_sum))
     normed_one_grad = normed_one_grad + router_grad
     input_grad = mixed_grad + norm_back(inputs, inverse_one, gain_first, normed_one_grad)
     shared_sum = exchange(shared_part.reshape(experts, shard_rows, -1)).astype(f32)

time: 1190 us -> 1170 us (0.983)
  local copies, waits for them, and re-layouts: 134 us -> 115 us
  waiting for transfers between devices: 391 us -> 404 us
    ppermute x10, waiting for transfers between devices: 38.7 us -> 82.1 us  [swap(): return lax.ppermute(block, 'dp', [(i, i ^ bit) for i in range(8)])]
    ppermute x12, waiting for transfers between devices: 179 us -> 161 us  [ring_step(): lax.ppermute(block, 'expert', [(i, (i + 1) % experts) for i in range(expe...]
    all_to_all x7 -> x8, waiting for transfers between devices: 157 us -> 144 us  [exchange(): lax.all_to_all(packed, 'expert', split_axis=0, concat_axis=0, tiled=True)]
    unnamed x389 -> x363, local copies, waits for them, and re-layouts: 46.1 us -> 33.7 us
    dot_general x6 -> x8, matrix products: 104 us -> 113 us  [mm_nt(): lax.dot_general(left, right, (((1,), (1,)), ((), ())), preferred_element_...]
    dot_general x18 -> x19, matrix products: 121 us -> 116 us  [mm(): return jnp.dot(left, right, preferred_element_type=f32)]
    all_to_all x7 -> x8, starting transfers between devices: 30.5 us -> 33.8 us  [exchange(): lax.all_to_all(packed, 'expert', split_axis=0, concat_axis=0, tiled=True)]
  transfers between devices with their start and end apart: 42 -> 43, of which waited for: 24 -> 25; matrix products, arithmetic and copies ran while one was open for 55% -> 55% of each run, Pallas kernels for 0% -> 0%
where the time goes in v7:
time: 1170 us; the launch traced here: 1160 us
  matrix products  440 us (38%)
  waiting for transfers between devices  404 us (35%)
  local copies, waits for them, and re-layouts  115 us (10%)
  other arithmetic  114 us (10%)
  starting transfers between devices  67.5 us (6%)
  between operations  17.8 us (2%)
    ppermute x12, waiting for transfers between devices, ring_step(): lax.ppermute(block, 'expert', [(i, (i + 1) % experts) for i in range(expe...  161 us
    all_to_all x8, waiting for transfers between devices, exchange(): lax.all_to_all(packed, 'expert', split_axis=0, concat_axis=0, tiled=True)  144 us
    dot_general x19, matrix products, mm(): return jnp.dot(left, right, preferred_element_type=f32)  116 us
    dot_general x8, matrix products, mm_nt(): lax.dot_general(left, right, (((1,), (1,)), ((), ())), preferred_element_...  113 us
    dot_general x11, matrix products, mm_tn(): lax.dot_general(left, right, (((0,), (0,)), ((), ())), preferred_element_...  112 us
    ppermute x10, waiting for transfers between devices, swap(): return lax.ppermute(block, 'dp', [(i, i ^ bit) for i in range(8)])  82.1 us
    all_to_all x8, starting transfers between devices, exchange(): lax.all_to_all(packed, 'expert', split_axis=0, concat_axis=0, tiled=True)  33.8 us
    unnamed x363, local copies, waits for them, and re-layouts  33.7 us
  transfers between devices with their start and end apart: 43, of which 25 were waited for; matrix products, arithmetic and copies ran while one was open for 55% of the time, Pallas kernels for 0%

profile of v7, /device:TPU:0, one launch (start us, length us, event | category | flops | bytes accessed | tf_op | source)
XLA Modules:
  0.0 1159.2 jit_solution(17503617652929909289)
XLA Ops:
  38.4 24.9 %collective-permute-done = bf16[256,2176]{1,0:T(8,128)(2,1)} collective-permute-done((bf16[256,2176]{1,0:T(8,128)(2,1)S(1)}, bf16[256,2176]{1,0:T(8,128)(2,1)}, u32[]{:S(2)}, u32[]{:S(2)}) %collective-permute-start) | collective-permute-done | bytes 1114144 | tf_op jit(solution)/shard_map/ppermute | solution.py:159
  68.2 22.1 %collective-permute-done.1 = bf16[256,2176]{1,0:T(8,128)(2,1)} collective-permute-done((bf16[256,2176]{1,0:T(8,128)(2,1)}, bf16[256,2176]{1,0:T(8,128)(2,1)}, u32[]{:S(2)}, u32[]{:S(2)}) %collective-permute-start.1) | collective-permute-done | bytes 1114144 | tf_op jit(solution)/shard_map/ppermute | solution.py:159
  94.2 22.1 %collective-permute-done.2 = bf16[256,2176]{1,0:T(8,128)(2,1)S(1)} collective-permute-done((bf16[256,2176]{1,0:T(8,128)(2,1)}, bf16[256,2176]{1,0:T(8,128)(2,1)S(1)}, u32[]{:S(2)}, u32[]{:S(2)}) %collective-permute-start.2) | collective-permute-done | bytes 1114144 | tf_op jit(solution)/shard_map/ppermute | solution.py:159
  150.3 12.4 %copy.272 = bf16[2048,2048]{1,0:T(8,128)(2,1)} copy(bf16[2048,2048]{0,1:T(8,128)(2,1)} %bitcast.423) | data formatting | bytes 16777216 | tf_op jit(solution)/shard_map/dot_general | solution.py:82
  162.7 10.0 fusion.230
  173.7 20.7 %collective-permute-done.6 = bf16[1024,1024]{0,1:T(8,128)(2,1)} collective-permute-done((bf16[1024,1024]{0,1:T(8,128)(2,1)}, bf16[1024,1024]{0,1:T(8,128)(2,1)}, u32[]{:S(2)}, u32[]{:S(2)}) %collective-permute-start.6) | collective-permute-done | bytes 2097184 | tf_op jit(solution)/shard_map/ppermute | solution.py:159
  223.0 17.2 %collective-permute-done.7 = bf16[1024,1024]{0,1:T(8,128)(2,1)} collective-permute-done((bf16[1024,1024]{0,1:T(8,128)(2,1)}, bf16[1024,1024]{0,1:T(8,128)(2,1)}, u32[]{:S(2)}, u32[]{:S(2)}) %collective-permute-start.7) | collective-permute-done | bytes 2097184 | tf_op jit(solution)/shard_map/ppermute | solution.py:159
  253.6 31.3 %collective-permute-done.8 = bf16[1024,1024]{0,1:T(8,128)(2,1)S(1)} collective-permute-done((bf16[1024,1024]{0,1:T(8,128)(2,1)}, bf16[1024,1024]{0,1:T(8,128)(2,1)S(1)}, u32[]{:S(2)}, u32[]{:S(2)}) %collective-permute-start.8) | collective-permute-done | bytes 2097184 | tf_op jit(solution)/shard_map/ppermute | solution.py:159
  297.4 10.3 fusion.69
  315.9 49.6 %all-to-all-done = bf16[4,160,2048]{2,1,0:T(8,128)(2,1)S(1)} async-done(((bf16[4,160,2048]{2,1,0:T(8,128)(2,1)}), bf16[4,160,2048]{2,1,0:T(8,128)(2,1)S(1)}, u32[]{:S(2)}, u32[]{:S(2)}) %all-to-all-start) | async-done | bytes 2621472 | tf_op jit(solution)/shard_map/all_to_all | solution.py:145
  386.0 51.9 %all-to-all-done.1 = bf16[4,160,2048]{2,1,0:T(8,128)(2,1)} async-done(((bf16[4,160,2048]{2,1,0:T(8,128)(2,1)}), bf16[4,160,2048]{2,1,0:T(8,128)(2,1)}, u32[]{:S(2)}, u32[]{:S(2)}) %all-to-all-start.1) | async-done | bytes 2621472 | tf_op jit(solution)/shard_map/all_to_all | solution.py:145
  441.6 23.6 %fusion.6 = f32[640,5632]{1,0:T(8,128)} fusion(bf16[640,2048]{1,0:T(8,128)(2,1)} %bitcast.47, bf16[1,2048,5632]{2,1,0:T(8,128)(2,1)} %all-gather.18.cloned.1.call-done), kind=kOutput, calls=%fused_computation.6 | convolution fusion | flops 14763950080 | bytes 40108032 | tf_op jit(solution)/shard_map/dot_general | solution.py:82
  465.2 32.0 %multiply_convert_fusion.2 = (bf16[640,5632]{1,0:T(8,128)(2,1)}, f32[640,5632]{1,0:T(8,128)}) fusion(f32[640,5632]{1,0:T(8,128)} %fusion.6, bf16[640,2048]{1,0:T(8,128)(2,1)} %bitcast.47, bf16[1,2048,5632]{2,1,0:T(8,128)(2,1)} %all-gather.20.cloned.1.call-done), kind=kOutput, calls=%fused_computation.14 | convolution fusion | flops 14785576960 | bytes 61734912 | tf_op jit(solution)/shard_map/dot_general | solution.py:82
  506.0 24.9 %convolution_convert_fusion = bf16[5632,2048]{1,0:T(8,128)(2,1)} fusion(bf16[640,5632]{1,0:T(8,128)(2,1)} %get-tuple-element.75, f32[640]{0:T(1024)S(1)} %convert_reduce_fusion.2, bf16[640,2176]{1,0:T(8,128)(2,1)S(1)} %bitcast.414), kind=kOutput, calls=%fused_computation.8 | convolution fusion | flops 14779416576 | bytes 32903168 | tf_op jit(solution)/shard_map/dot_general | solution.py:86
  537.1 38.5 %multiply_convert_fusion.1 = (bf16[640,5632]{1,0:T(8,128)(2,1)}, bf16[640,5632]{1,0:T(8,128)(2,1)}, f32[640]{0:T(1024)S(1)}) fusion(f32[640,5632]{1,0:T(8,128)} %fusion.6, f32[640,5632]{1,0:T(8,128)} %get-tuple-element.209, f32[640]{0:T(1024)S(1)} %convert_reduce_fusion.2, bf16[640,5632]{1,0:T(8,128)(2,1)} %get-tuple-element.75, ...), kind=kOutput, calls=%fused_computation.13 | convolution fusion | flops 14825225216 | bytes 76157952 | tf_op jit(solution)/shard_map/dot_general | solution.py:90
  575.9 12.7 %fusion.10 = f32[640,1024]{1,0:T(8,128)S(1)} fusion(bf16[640,5632]{1,0:T(8,128)(2,1)} %get-tuple-element.76, bf16[1,2048,5632]{2,1,0:T(8,128)(2,1)} %all-gather.20.cloned.1.call-done), kind=kOutput, calls=%fused_computation.24 | convolution fusion | flops 7381975040 | bytes 21364736 | tf_op jit(solution)/shard_map/dot_general | solution.py:90
  588.6 11.0 add_convert_fusion.3
  605.3 13.0 %fusion.8 = f32[640,1024]{1,0:T(8,128)S(1)} fusion(bf16[640,5632]{1,0:T(8,128)(2,1)} %get-tuple-element.76, bf16[1,2048,5632]{2,1,0:T(8,128)(2,1)} %all-gather.20.cloned.1.call-done), kind=kOutput, calls=%fused_computation.20 | convolution fusion | flops 7381975040 | bytes 21364736 | tf_op jit(solution)/shard_map/dot_general | solution.py:90
  618.2 13.8 %add_convert_fusion.2 = bf16[640,1024]{1,0:T(8,128)(2,1)} fusion(f32[640,1024]{1,0:T(8,128)S(1)} %fusion.8, bf16[640,5632]{1,0:T(8,128)(2,1)} %get-tuple-element.70, bf16[1,2048,5632]{2,1,0:T(8,128)(2,1)} %all-gather.18.cloned.1.call-done), kind=kOutput, calls=%fused_computation.136 | convolution fusion | flops 7383285760 | bytes 22675456 | tf_op jit(solution)/shard_map/dot_general | solution.py:90
  632.0 8.2 all-to-all-done.3
  643.8 26.3 %convolution_convert_fusion.2 = bf16[2048,5632]{1,0:T(8,128)(2,1)} fusion(bf16[640,2048]{1,0:T(8,128)(2,1)} %bitcast.47, bf16[640,5632]{1,0:T(8,128)(2,1)} %get-tuple-element.70), kind=kOutput, calls=%fused_computation.10 | convolution fusion | flops 14775484416 | bytes 32899072 | tf_op jit(solution)/shard_map/dot_general | solution.py:86
  691.1 28.5 %convolution_convert_fusion.1 = bf16[2048,5632]{1,0:T(8,128)(2,1)} fusion(bf16[640,2048]{1,0:T(8,128)(2,1)} %bitcast.47, bf16[640,5632]{1,0:T(8,128)(2,1)} %get-tuple-element.76), kind=kOutput, calls=%fused_computation.9 | convolution fusion | flops 14775484416 | bytes 32899072 | tf_op jit(solution)/shard_map/dot_general | solution.py:86
  719.6 22.1 %fusion.63 = bf16[640,2048]{1,0:T(8,128)(2,1)} fusion(bf16[640,5632]{1,0:T(8,128)(2,1)} %get-tuple-element.75, bf16[1,5632,2048]{2,1,0:T(8,128)(2,1)} %all-gather.22.cloned.1.call-done), kind=kOutput, calls=%fused_computation.115 | convolution fusion | flops 14765260800 | bytes 32899072 | tf_op jit(solution)/shard_map/dot_general | solution.py:82
  741.9 8.3 all-to-all-done.5
  764.9 10.2 fusion.60
  784.3 8.4 multiply_convert_fusion.5
  860.2 8.6 all-to-all-done.6
  875.6 9.3 convolution_convert_fusion.4
  942.5 27.7 %collective-permute-done.15 = bf16[2,256,1024]{2,1,0:T(8,128)(2,1)S(1)} collective-permute-done((bf16[2,256,1024]{2,1,0:T(8,128)(2,1)S(1)}, bf16[2,256,1024]{2,1,0:T(8,128)(2,1)S(1)}, u32[]{:S(2)}, u32[]{:S(2)}) %collective-permute-start.15) | collective-permute-done | bytes 1048608 | tf_op jit(solution)/shard_map/ppermute | solution.py:234
  975.6 20.8 %collective-permute-done.16 = bf16[256,1024]{1,0:T(8,128)(2,1)S(1)} collective-permute-done((bf16[256,1024]{1,0:T(8,128)(2,1)S(1)}, bf16[256,1024]{1,0:T(8,128)(2,1)S(1)}, u32[]{:S(2)}, u32[]{:S(2)}) %collective-permute-start.16) | collective-permute-done | bytes 524320 | tf_op jit(solution)/shard_map/ppermute | solution.py:234
  1051.3 25.4 %collective-permute-done.22 = bf16[2,256,1024]{2,1,0:T(8,128)(2,1)S(1)} collective-permute-done((bf16[2,256,1024]{2,1,0:T(8,128)(2,1)S(1)}, bf16[2,256,1024]{2,1,0:T(8,128)(2,1)S(1)}, u32[]{:S(2)}, u32[]{:S(2)}) %collective-permute-start.22) | collective-permute-done | bytes 1048608 | tf_op jit(solution)/shard_map/ppermute | solution.py:234
  1105.9 18.4 %collective-permute-done.24 = bf16[256,2048]{1,0:T(8,128)(2,1)} collective-permute-done((bf16[256,2048]{1,0:T(8,128)(2,1)}, bf16[256,2048]{1,0:T(8,128)(2,1)}, u32[]{:S(2)}, u32[]{:S(2)}) %collective-permute-start.24) | collective-permute-done | bytes 1048608 | tf_op jit(solution)/shard_map/ppermute | solution.py:159
  (695 shorter events, 477.3 us)
Async XLA Ops:
  7.2 115.3 %all-gather.12.cloned.1.call-start = ((), (), s32[]{:S(2)}) async-start(), calls=%async_computation.12 | async-start | bytes 5308416 | tf_op jit(solution)/shard_map/all_gather | solution.py:311
  29.2 121.1 %all-gather.14.cloned.1.call-start = ((), (), s32[]{:S(2)}) async-start(), calls=%async_computation.17 | async-start | bytes 9437184 | tf_op jit(solution)/shard_map/all_gather | solution.py:226
  30.0 267.4 %all-gather.16.cloned.1.call-start = ((), (), s32[]{:S(2)}) async-start(), calls=%async_computation.18 | async-start | bytes 9437184 | tf_op jit(solution)/shard_map/all_gather | solution.py:226
  30.7 410.9 %all-gather.18.cloned.1.call-start = ((), (), s32[]{:S(2)}) async-start(), calls=%async_computation.19 | async-start | bytes 25952256 | tf_op jit(solution)/shard_map/all_gather | solution.py:226
  31.3 433.9 %all-gather.20.cloned.1.call-start = ((), (), s32[]{:S(2)}) async-start(), calls=%async_computation.20 | async-start | bytes 25952256 | tf_op jit(solution)/shard_map/all_gather | solution.py:226
  31.9 505.3 %all-gather.22.cloned.1.call-start = ((), (), s32[]{:S(2)}) async-start(), calls=%async_computation.21 | async-start | bytes 25952256 | tf_op jit(solution)/shard_map/all_gather | solution.py:226
  34.7 28.6 %collective-permute-start = (bf16[256,2176]{1,0:T(8,128)(2,1)S(1)}, bf16[256,2176]{1,0:T(8,128)(2,1)}, u32[]{:S(2)}, u32[]{:S(2)}) collective-permute-start(bf16[256,2176]{1,0:T(8,128)(2,1)S(1)} %concatenate.68), channel_id=1, source_target_pairs={{0,1},{1,2},{2,3},{3,0},{4,5},{5,6},{6,7},{7,4},{8,9},{9,10},{10,1... | collective-permute-start | bytes 3342344 | tf_op jit(solution)/shard_map/ppermute | solution.py:159
  63.3 27.0 %collective-permute-start.1 = (bf16[256,2176]{1,0:T(8,128)(2,1)}, bf16[256,2176]{1,0:T(8,128)(2,1)}, u32[]{:S(2)}, u32[]{:S(2)}) collective-permute-start(bf16[256,2176]{1,0:T(8,128)(2,1)} %collective-permute-done), channel_id=1, source_target_pairs={{0,1},{1,2},{2,3},{3,0},{4,5},{5,6},{6,7},{7,4},{8,9},{9,10},{10,1... | collective-permute-start | bytes 3342344 | tf_op jit(solution)/shard_map/ppermute | solution.py:159
  147.9 46.5 %collective-permute-start.6 = (bf16[1024,1024]{0,1:T(8,128)(2,1)}, bf16[1024,1024]{0,1:T(8,128)(2,1)}, u32[]{:S(2)}, u32[]{:S(2)}) collective-permute-start(bf16[1024,1024]{0,1:T(8,128)(2,1)} %pad_maximum_fusion.5), channel_id=1, source_target_pairs={{0,1},{1,2},{2,3},{3,0},{4,5},{5,6},{6,7},{7,4},{8,9},{9,10},{10,1... | collective-permute-start | bytes 6291464 | tf_op jit(solution)/shard_map/ppermute | solution.py:159
  194.4 45.8 %collective-permute-start.7 = (bf16[1024,1024]{0,1:T(8,128)(2,1)}, bf16[1024,1024]{0,1:T(8,128)(2,1)}, u32[]{:S(2)}, u32[]{:S(2)}) collective-permute-start(bf16[1024,1024]{0,1:T(8,128)(2,1)} %collective-permute-done.6), channel_id=1, source_target_pairs={{0,1},{1,2},{2,3},{3,0},{4,5},{5,6},{6,7},{7,4},{8,9},{9,10},{10,1... | collective-permute-start | bytes 6291464 | tf_op jit(solution)/shard_map/ppermute | solution.py:159
  240.2 44.7 %collective-permute-start.8 = (bf16[1024,1024]{0,1:T(8,128)(2,1)}, bf16[1024,1024]{0,1:T(8,128)(2,1)S(1)}, u32[]{:S(2)}, u32[]{:S(2)}) collective-permute-start(bf16[1024,1024]{0,1:T(8,128)(2,1)} %collective-permute-done.7), channel_id=1, source_target_pairs={{0,1},{1,2},{2,3},{3,0},{4,5},{5,6},{6,7},{7,4},{8,9},{9,10},{10,1... | collective-permute-start | bytes 6291464 | tf_op jit(solution)/shard_map/ppermute | solution.py:159
  307.7 57.8 %all-to-all-start = ((bf16[4,160,2048]{2,1,0:T(8,128)(2,1)}), bf16[4,160,2048]{2,1,0:T(8,128)(2,1)S(1)}, u32[]{:S(2)}, u32[]{:S(2)}) async-start(bf16[4,160,2048]{2,1,0:T(8,128)(2,1)} %bitcast.465), calls=%async_computation | async-start | bytes 5242880 | tf_op jit(solution)/shard_map/all_to_all | solution.py:145
  374.2 63.6 %all-to-all-start.1 = ((bf16[4,160,2048]{2,1,0:T(8,128)(2,1)}), bf16[4,160,2048]{2,1,0:T(8,128)(2,1)}, u32[]{:S(2)}, u32[]{:S(2)}) async-start(bf16[4,160,2048]{2,1,0:T(8,128)(2,1)} %bitcast.46), calls=%async_computation.1 | async-start | bytes 5242880 | tf_op jit(solution)/shard_map/all_to_all | solution.py:145
  437.8 66.1 %all-to-all-start.2 = ((bf16[4,160,2176]{2,1,0:T(8,128)(2,1)}), bf16[4,160,2176]{2,1,0:T(8,128)(2,1)S(1)}, u32[]{:S(2)}, u32[]{:S(2)}) async-start(bf16[4,160,2176]{2,1,0:T(8,128)(2,1)} %pad_maximum_fusion.2), calls=%async_computation.2 | async-start | bytes 5570560 | tf_op jit(solution)/shard_map/all_to_all | solution.py:145
  441.5 323.4 %reduce-scatter.5.cloned.1.call-start = ((), (), s32[]{:S(2)}) async-start(), calls=%async_computation.13 | async-start | bytes 25952256 | tf_op jit(solution)/shard_map/reduce_scatter | solution.py:230
  600.8 39.4 %all-to-all-start.3 = ((bf16[4,160,1152]{2,1,0:T(8,128)(2,1)}), bf16[4,160,1152]{2,1,0:T(8,128)(2,1)S(1)}, u32[]{:S(2)}, u32[]{:S(2)}) async-start(bf16[4,160,1152]{2,1,0:T(8,128)(2,1)} %bitcast.56), calls=%async_computation.3 | async-start | bytes 2949120 | tf_op jit(solution)/shard_map/all_to_all | solution.py:145
  640.2 34.4 %all-to-all-start.4 = ((bf16[4,160,1024]{2,1,0:T(8,128)(2,1)}), bf16[4,160,1024]{2,1,0:T(8,128)(2,1)S(1)}, u32[]{:S(2)}, u32[]{:S(2)}) async-start(bf16[4,160,1024]{2,1,0:T(8,128)(2,1)} %bitcast.489), calls=%async_computation.4 | async-start | bytes 2621440 | tf_op jit(solution)/shard_map/all_to_all | solution.py:145
  643.8 437.6 %reduce-scatter.9.cloned.1.call-start = ((), (), s32[]{:S(2)}) async-start(), calls=%async_computation.15 | async-start | bytes 25952256 | tf_op jit(solution)/shard_map/reduce_scatter | solution.py:230
  686.5 63.6 %all-to-all-start.5 = ((bf16[4,160,2048]{2,1,0:T(8,128)(2,1)}), bf16[4,160,2048]{2,1,0:T(8,128)(2,1)}, u32[]{:S(2)}, u32[]{:S(2)}) async-start(bf16[4,160,2048]{2,1,0:T(8,128)(2,1)} %bitcast.68), calls=%async_computation.5 | async-start | bytes 5242880 | tf_op jit(solution)/shard_map/all_to_all | solution.py:145
  691.1 409.8 %reduce-scatter.11.cloned.1.call-start = ((), (), s32[]{:S(2)}) async-start(), calls=%async_computation.16 | async-start | bytes 25952256 | tf_op jit(solution)/shard_map/reduce_scatter | solution.py:230
  760.2 108.6 %all-to-all-start.6 = ((bf16[4,160,2048]{2,1,0:T(8,128)(2,1)}), bf16[4,160,2048]{2,1,0:T(8,128)(2,1)}, u32[]{:S(2)}, u32[]{:S(2)}) async-start(bf16[4,160,2048]{2,1,0:T(8,128)(2,1)} %bitcast.462), calls=%async_computation.7 | async-start | bytes 5242880 | tf_op jit(solution)/shard_map/all_to_all | solution.py:145
  764.9 359.4 %reduce-scatter.7.cloned.1.call-start = ((), (), s32[]{:S(2)}) async-start(), calls=%async_computation.14 | async-start | bytes 5308416 | tf_op jit(solution)/shard_map/reduce_scatter | solution.py:230
  799.8 56.0 %collective-permute-start.9 = (bf16[1024,1024]{0,1:T(8,128)(2,1)}, bf16[1024,1024]{0,1:T(8,128)(2,1)}, u32[]{:S(2)}, u32[]{:S(2)}) collective-permute-start(bf16[1024,1024]{0,1:T(8,128)(2,1)} %pad_maximum_fusion.6), channel_id=1, source_target_pairs={{0,1},{1,2},{2,3},{3,0},{4,5},{5,6},{6,7},{7,4},{8,9},{9,10},{10,1... | collective-permute-start | bytes 6291464 | tf_op jit(solution)/shard_map/ppermute | solution.py:159
  872.3 50.6 %collective-permute-start.10 = (bf16[1024,1024]{0,1:T(8,128)(2,1)}, bf16[1024,1024]{0,1:T(8,128)(2,1)}, u32[]{:S(2)}, u32[]{:S(2)}) collective-permute-start(bf16[1024,1024]{0,1:T(8,128)(2,1)} %fusion.53), channel_id=1, source_target_pairs={{0,1},{1,2},{2,3},{3,0},{4,5},{5,6},{6,7},{7,4},{8,9},{9,10},{10,1... | collective-permute-start | bytes 6291464 | tf_op jit(solution)/shard_map/ppermute | solution.py:159
  889.6 38.7 %collective-permute-start.12 = (bf16[2,2,256,2048]{3,2,1,0:T(8,128)(2,1)}, bf16[2,2,256,2048]{3,2,1,0:T(8,128)(2,1)}, u32[]{:S(2)}, u32[]{:S(2)}) collective-permute-start(bf16[2,2,256,2048]{3,2,1,0:T(8,128)(2,1)} %dynamic-slice_bitcast_fusion.1), channel_id=1, source_target_pairs={{0,4},{4,0},{8,12},{12,8},{16,20},{20,16},{24,28},{28,24},{1,5},{5... | collective-permute-start | bytes 12582920 | tf_op jit(solution)/shard_map/ppermute | solution.py:234
  925.5 74.5 %collective-permute-start.11 = (bf16[1024,1024]{0,1:T(8,128)(2,1)S(1)}, bf16[1024,1024]{0,1:T(8,128)(2,1)S(1)}, u32[]{:S(2)}, u32[]{:S(2)}) collective-permute-start(bf16[1024,1024]{0,1:T(8,128)(2,1)S(1)} %fusion.55), channel_id=1, source_target_pairs={{0,1},{1,2},{2,3},{3,0},{4,5},{5,6},{6,7},{7,4},{8,9},{9,10},{10,1... | collective-permute-start | bytes 6291464 | tf_op jit(solution)/shard_map/ppermute | solution.py:159
  933.2 37.0 %collective-permute-start.15 = (bf16[2,256,1024]{2,1,0:T(8,128)(2,1)S(1)}, bf16[2,256,1024]{2,1,0:T(8,128)(2,1)S(1)}, u32[]{:S(2)}, u32[]{:S(2)}) collective-permute-start(bf16[2,256,1024]{2,1,0:T(8,128)(2,1)S(1)} %dynamic-slice_bitcast_fusion.4), channel_id=1, source_target_pairs={{0,16},{4,20},{8,24},{12,28},{16,0},{20,4},{24,8},{28,12},{1,17},{... | collective-permute-start | bytes 3145736 | tf_op jit(solution)/shard_map/ppermute | solution.py:234
  934.4 37.8 %collective-permute-start.13 = (bf16[2,256,1024]{2,1,0:T(8,128)(2,1)S(1)}, bf16[2,256,1024]{2,1,0:T(8,128)(2,1)S(1)}, u32[]{:S(2)}, u32[]{:S(2)}) collective-permute-start(bf16[2,256,1024]{2,1,0:T(8,128)(2,1)S(1)} %dynamic-slice_bitcast_fusion.5), channel_id=1, source_target_pairs={{0,8},{4,12},{8,0},{12,4},{16,24},{20,28},{24,16},{28,20},{1,9},{5... | collective-permute-start | bytes 3145736 | tf_op jit(solution)/shard_map/ppermute | solution.py:234
  975.6 61.8 %collective-permute-start.19 = (bf16[2,2,256,2048]{3,2,1,0:T(8,128)(2,1)}, bf16[2,2,256,2048]{3,2,1,0:T(8,128)(2,1)}, u32[]{:S(2)}, u32[]{:S(2)}) collective-permute-start(bf16[2,2,256,2048]{3,2,1,0:T(8,128)(2,1)} %dynamic-slice_bitcast_fusion), channel_id=1, source_target_pairs={{0,4},{4,0},{8,12},{12,8},{16,20},{20,16},{24,28},{28,24},{1,5},{5... | collective-permute-start | bytes 12582920 | tf_op jit(solution)/shard_map/ppermute | solution.py:234
  1043.5 33.2 %collective-permute-start.22 = (bf16[2,256,1024]{2,1,0:T(8,128)(2,1)S(1)}, bf16[2,256,1024]{2,1,0:T(8,128)(2,1)S(1)}, u32[]{:S(2)}, u32[]{:S(2)}) collective-permute-start(bf16[2,256,1024]{2,1,0:T(8,128)(2,1)S(1)} %dynamic-slice_bitcast_fusion.2), channel_id=1, source_target_pairs={{0,16},{4,20},{8,24},{12,28},{16,0},{20,4},{24,8},{28,12},{1,17},{... | collective-permute-start | bytes 3145736 | tf_op jit(solution)/shard_map/ppermute | solution.py:234
  1044.2 34.7 %collective-permute-start.20 = (bf16[2,256,1024]{2,1,0:T(8,128)(2,1)S(1)}, bf16[2,256,1024]{2,1,0:T(8,128)(2,1)S(1)}, u32[]{:S(2)}, u32[]{:S(2)}) collective-permute-start(bf16[2,256,1024]{2,1,0:T(8,128)(2,1)S(1)} %dynamic-slice_bitcast_fusion.3), channel_id=1, source_target_pairs={{0,8},{4,12},{8,0},{12,4},{16,24},{20,28},{24,16},{28,20},{1,9},{5... | collective-permute-start | bytes 3145736 | tf_op jit(solution)/shard_map/ppermute | solution.py:234
  1049.4 46.4 %collective-permute-start.18 = (bf16[256,2048]{1,0:T(8,128)(2,1)S(1)}, bf16[256,2048]{1,0:T(8,128)(2,1)}, u32[]{:S(2)}, u32[]{:S(2)}) collective-permute-start(bf16[256,2048]{1,0:T(8,128)(2,1)S(1)} %fusion.87), channel_id=1, source_target_pairs={{0,1},{1,2},{2,3},{3,0},{4,5},{5,6},{6,7},{7,4},{8,9},{9,10},{10,1... | collective-permute-start | bytes 3145736 | tf_op jit(solution)/shard_map/ppermute | solution.py:159
  (188 other events, 2201.5 us)
Sparse Core Ops, SparseCore 0:
  29.3 41.1 all-gather.11
  72.4 54.2 all-gather.13
  128.5 54.2 all-gather.15
  184.6 116.3 all-gather.17
  302.7 116.3 all-gather.19
  420.8 116.3 all-gather.21
  540.7 146.3 reduce-scatter.4
  690.7 146.3 reduce-scatter.8
  840.8 171.0 reduce-scatter.10
  1037.5 63.1 reduce-scatter.6

commit v8 on v7

--- a/solution.py
+++ b/solution.py
@@ -250,11 +250,21 @@
     return kept + swap(sent, bit).astype(f32)
 
 
-def reduce_swaps(part):
-    if lax.axis_size("dp") != 8:
-        return reduce_dp(part).astype(f32)
+def swaps_fit():
+    return lax.axis_size("dp") == 8
+
+
+def reduce_core(part):
+    if not swaps_fit():
+        return part
     rows, columns = part.shape
-    grid = fold(part.reshape(2, 2, 2, rows // 8, columns), 2, 1).astype(bf16)
+    return fold(part.reshape(2, 2, 2, rows // 8, columns), 2, 1).astype(bf16)
+
+
+def reduce_chips(grid):
+    if not swaps_fit():
+        return reduce_dp(grid).astype(f32)
+    columns = grid.shape[-1]
     left, right = grid[..., : columns // 2], grid[..., columns // 2 :]
     left = fold(fold(left, 1, 2).astype(bf16), 0, 4)
     right = fold(fold(right, 0, 4).astype(bf16), 0, 2)
@@ -470,6 +480,9 @@
     ffn_back = exchange(ffn_branch.reshape(experts, capacity, -1))
     att_grad_rows, down_sum = lax.optimization_barrier((att_grad_rows, down_sum))
     attended_grad = mm_nt(att_grad_rows, output_all).astype(bf16)
+    output_part = mm_tn(attended, att_grad_rows).astype(bf16)
+    attended_grad, output_part = lax.optimization_barrier((attended_grad, output_part))
+    output_core = reduce_core(output_part)
     query_grad = jnp.zeros(queries.shape, f32)
     kv_grad = None
     for step in range(1, experts + 1):
@@ -483,6 +496,14 @@
         part = jnp.concatenate([key_grad, value_grad], 1)
         if k == 0:
             kv_grad, output_sum = lax.optimization_barrier((kv_grad, output_sum))
+        if step == 2:
+            kv_grad, output_core = lax.optimization_barrier((kv_grad, output_core))
+            output_sum = reduce_chips(output_core)
+        if step == experts - 1:
+            kv_grad, output_sum = lax.optimization_barrier((kv_grad, output_sum))
+        if k == 0:
+            query_raw_grad = rotate_back(query_grad, query_cos, query_sin).astype(bf16)
+            query_core = reduce_core(mm_tn(query_rows, query_raw_grad).astype(bf16))
         if kv_grad is not None:
             part = part + kv_grad.astype(f32)
         if k == 0:
@@ -490,17 +511,12 @@
             continue
         part = part.astype(bf16)
         if step == 2:
-            part, att_grad_rows, ffn_back, late_grad = lax.optimization_barrier(
-                (part, att_grad_rows, ffn_back, attended_grad)
-            )
-            output_sum = reduce_swaps(mm_tn(attended, att_grad_rows).astype(bf16))
+            part, ffn_back, late_grad = lax.optimization_barrier((part, ffn_back, attended_grad))
         if step == experts - 1:
             part, query_rows = lax.optimization_barrier((part, query_rows))
         kv_grad = ring_step(part, experts)
     ffn_picked = take_back(ffn_place, ffn_back)
     result = mixed_stream + jnp.sum(ffn_gate.T[:, :, None] * ffn_picked, 0)
-    query_raw_grad = rotate_back(query_grad, query_cos, query_sin).astype(bf16)
-    query_sum = reduce_swaps(mm_tn(query_rows, query_raw_grad).astype(bf16))
     att_rows_grad = mm_nt(query_raw_grad, query_all).astype(bf16)
     kv_raw_grad = jnp.concatenate(
         [rotate_back(kv_grad[:, :width], tree_cos, tree_sin), kv_grad[:, width:]], 1
@@ -549,7 +565,10 @@
             normed_one_grad, shared_part = lax.optimization_barrier(
                 (normed_one_grad, reduce_dp(shared_part))
             )
-        if step == 2:
+        if step == 1:
+            normed_one_grad, query_core = lax.optimization_barrier((normed_one_grad, query_core))
+            query_sum = reduce_chips(query_core)
+        if k == 0:
             normed_one_grad, query_sum = lax.optimization_barrier((normed_one_grad, query_sum))
     normed_one_grad = normed_one_grad + router_grad
     input_grad = mixed_grad + norm_back(inputs, inverse_one, gain_first, normed_one_grad)

time: 1170 us -> 1190 us (1.017)
  matrix products: 440 us -> 456 us
  waiting for transfers between devices: 404 us -> 416 us
    ppermute x12, waiting for transfers between devices: 161 us -> 205 us  [ring_step(): lax.ppermute(block, 'expert', [(i, (i + 1) % experts) for i in range(expe...]
    ppermute x10, waiting for transfers between devices: 82.1 us -> 55.6 us  [swap(): return lax.ppermute(block, 'dp', [(i, i ^ bit) for i in range(8)])]
    unnamed x363 -> x377, local copies, waits for them, and re-layouts: 33.7 us -> 33.1 us
where the time goes in v8:
time: 1190 us; the launch traced here: 1180 us
  matrix products  456 us (38%)
  waiting for transfers between devices  416 us (35%)
  local copies, waits for them, and re-layouts  117 us (10%)
  other arithmetic  116 us (10%)
  starting transfers between devices  61.3 us (5%)
  between operations  17.8 us (1%)
    ppermute x12, waiting for transfers between devices, ring_step(): lax.ppermute(block, 'expert', [(i, (i + 1) % experts) for i in range(expe...  205 us
    all_to_all x8, waiting for transfers between devices, exchange(): lax.all_to_all(packed, 'expert', split_axis=0, concat_axis=0, tiled=True)  137 us
    dot_general x19, matrix products, mm(): return jnp.dot(left, right, preferred_element_type=f32)  117 us
    dot_general x8, matrix products, mm_nt(): lax.dot_general(left, right, (((1,), (1,)), ((), ())), preferred_element_...  116 us
    dot_general x11, matrix products, mm_tn(): lax.dot_general(left, right, (((0,), (0,)), ((), ())), preferred_element_...  114 us
    ppermute x10, waiting for transfers between devices, swap(): return lax.ppermute(block, 'dp', [(i, i ^ bit) for i in range(8)])  55.6 us
    all_to_all x8, starting transfers between devices, exchange(): lax.all_to_all(packed, 'expert', split_axis=0, concat_axis=0, tiled=True)  34.3 us
    unnamed x377, local copies, waits for them, and re-layouts  33.1 us
  transfers between devices with their start and end apart: 43, of which 25 were waited for; matrix products, arithmetic and copies ran while one was open for 55% of the time, Pallas kernels for 0%

profile of v8, /device:TPU:0, one launch (start us, length us, event | category | flops | bytes accessed | tf_op | source)
XLA Modules:
  0.0 1183.1 jit_solution(1137479178416724442)
XLA Ops:
  38.4 24.9 %collective-permute-done = bf16[256,2176]{1,0:T(8,128)(2,1)} collective-permute-done((bf16[256,2176]{1,0:T(8,128)(2,1)S(1)}, bf16[256,2176]{1,0:T(8,128)(2,1)}, u32[]{:S(2)}, u32[]{:S(2)}) %collective-permute-start) | collective-permute-done | bytes 1114144 | tf_op jit(solution)/shard_map/ppermute | solution.py:159
  68.2 22.1 %collective-permute-done.1 = bf16[256,2176]{1,0:T(8,128)(2,1)} collective-permute-done((bf16[256,2176]{1,0:T(8,128)(2,1)}, bf16[256,2176]{1,0:T(8,128)(2,1)}, u32[]{:S(2)}, u32[]{:S(2)}) %collective-permute-start.1) | collective-permute-done | bytes 1114144 | tf_op jit(solution)/shard_map/ppermute | solution.py:159
  94.2 22.1 %collective-permute-done.2 = bf16[256,2176]{1,0:T(8,128)(2,1)S(1)} collective-permute-done((bf16[256,2176]{1,0:T(8,128)(2,1)}, bf16[256,2176]{1,0:T(8,128)(2,1)S(1)}, u32[]{:S(2)}, u32[]{:S(2)}) %collective-permute-start.2) | collective-permute-done | bytes 1114144 | tf_op jit(solution)/shard_map/ppermute | solution.py:159
  150.2 12.4 %copy.272 = bf16[2048,2048]{1,0:T(8,128)(2,1)} copy(bf16[2048,2048]{0,1:T(8,128)(2,1)} %bitcast.417) | data formatting | bytes 16777216 | tf_op jit(solution)/shard_map/dot_general | solution.py:82
  162.6 10.0 fusion.228
  173.7 20.6 %collective-permute-done.6 = bf16[1024,1024]{0,1:T(8,128)(2,1)} collective-permute-done((bf16[1024,1024]{0,1:T(8,128)(2,1)}, bf16[1024,1024]{0,1:T(8,128)(2,1)}, u32[]{:S(2)}, u32[]{:S(2)}) %collective-permute-start.6) | collective-permute-done | bytes 2097184 | tf_op jit(solution)/shard_map/ppermute | solution.py:159
  222.7 17.3 %collective-permute-done.7 = bf16[1024,1024]{0,1:T(8,128)(2,1)} collective-permute-done((bf16[1024,1024]{0,1:T(8,128)(2,1)}, bf16[1024,1024]{0,1:T(8,128)(2,1)}, u32[]{:S(2)}, u32[]{:S(2)}) %collective-permute-start.7) | collective-permute-done | bytes 2097184 | tf_op jit(solution)/shard_map/ppermute | solution.py:159
  253.5 31.2 %collective-permute-done.8 = bf16[1024,1024]{0,1:T(8,128)(2,1)S(1)} collective-permute-done((bf16[1024,1024]{0,1:T(8,128)(2,1)}, bf16[1024,1024]{0,1:T(8,128)(2,1)S(1)}, u32[]{:S(2)}, u32[]{:S(2)}) %collective-permute-start.8) | collective-permute-done | bytes 2097184 | tf_op jit(solution)/shard_map/ppermute | solution.py:159
  297.1 10.3 fusion.69
  315.7 49.7 %all-to-all-done = bf16[4,160,2048]{2,1,0:T(8,128)(2,1)S(1)} async-done(((bf16[4,160,2048]{2,1,0:T(8,128)(2,1)}), bf16[4,160,2048]{2,1,0:T(8,128)(2,1)S(1)}, u32[]{:S(2)}, u32[]{:S(2)}) %all-to-all-start) | async-done | bytes 2621472 | tf_op jit(solution)/shard_map/all_to_all | solution.py:145
  385.7 51.9 %all-to-all-done.1 = bf16[4,160,2048]{2,1,0:T(8,128)(2,1)} async-done(((bf16[4,160,2048]{2,1,0:T(8,128)(2,1)}), bf16[4,160,2048]{2,1,0:T(8,128)(2,1)}, u32[]{:S(2)}, u32[]{:S(2)}) %all-to-all-start.1) | async-done | bytes 2621472 | tf_op jit(solution)/shard_map/all_to_all | solution.py:145
  441.4 23.7 %fusion.6 = f32[640,5632]{1,0:T(8,128)} fusion(bf16[640,2048]{1,0:T(8,128)(2,1)} %bitcast.47, bf16[1,2048,5632]{2,1,0:T(8,128)(2,1)} %all-gather.18.cloned.1.call-done), kind=kOutput, calls=%fused_computation.6 | convolution fusion | flops 14763950080 | bytes 40108032 | tf_op jit(solution)/shard_map/dot_general | solution.py:82
  465.0 31.9 %multiply_convert_fusion.2 = (bf16[640,5632]{1,0:T(8,128)(2,1)}, f32[640,5632]{1,0:T(8,128)}) fusion(f32[640,5632]{1,0:T(8,128)} %fusion.6, bf16[640,2048]{1,0:T(8,128)(2,1)} %bitcast.47, bf16[1,2048,5632]{2,1,0:T(8,128)(2,1)} %all-gather.20.cloned.1.call-done), kind=kOutput, calls=%fused_computation.14 | convolution fusion | flops 14785576960 | bytes 61734912 | tf_op jit(solution)/shard_map/dot_general | solution.py:82
  505.8 24.9 %convolution_convert_fusion = bf16[5632,2048]{1,0:T(8,128)(2,1)} fusion(bf16[640,5632]{1,0:T(8,128)(2,1)} %get-tuple-element.82, f32[640]{0:T(1024)S(1)} %convert_reduce_fusion.2, bf16[640,2176]{1,0:T(8,128)(2,1)S(1)} %bitcast.408), kind=kOutput, calls=%fused_computation.8 | convolution fusion | flops 14779416576 | bytes 32903168 | tf_op jit(solution)/shard_map/dot_general | solution.py:86
  537.2 38.5 %multiply_convert_fusion.1 = (bf16[640,5632]{1,0:T(8,128)(2,1)}, bf16[640,5632]{1,0:T(8,128)(2,1)}, f32[640]{0:T(1024)S(1)}) fusion(f32[640,5632]{1,0:T(8,128)} %fusion.6, f32[640,5632]{1,0:T(8,128)} %get-tuple-element.223, f32[640]{0:T(1024)S(1)} %convert_reduce_fusion.2, bf16[640,5632]{1,0:T(8,128)(2,1)} %get-tuple-element.82, ...), kind=kOutput, calls=%fused_computation.13 | convolution fusion | flops 14825225216 | bytes 76157952 | tf_op jit(solution)/shard_map/dot_general | solution.py:90
  575.9 12.7 %fusion.10 = f32[640,1024]{1,0:T(8,128)S(1)} fusion(bf16[640,5632]{1,0:T(8,128)(2,1)} %get-tuple-element.83, bf16[1,2048,5632]{2,1,0:T(8,128)(2,1)} %all-gather.20.cloned.1.call-done), kind=kOutput, calls=%fused_computation.24 | convolution fusion | flops 7381975040 | bytes 21364736 | tf_op jit(solution)/shard_map/dot_general | solution.py:90
  588.7 11.0 add_convert_fusion.3
  605.3 12.9 %fusion.8 = f32[640,1024]{1,0:T(8,128)S(1)} fusion(bf16[640,5632]{1,0:T(8,128)(2,1)} %get-tuple-element.83, bf16[1,2048,5632]{2,1,0:T(8,128)(2,1)} %all-gather.20.cloned.1.call-done), kind=kOutput, calls=%fused_computation.20 | convolution fusion | flops 7381975040 | bytes 21364736 | tf_op jit(solution)/shard_map/dot_general | solution.py:90
  618.3 13.8 %add_convert_fusion.2 = bf16[640,1024]{1,0:T(8,128)(2,1)} fusion(f32[640,1024]{1,0:T(8,128)S(1)} %fusion.8, bf16[640,5632]{1,0:T(8,128)(2,1)} %get-tuple-element.77, bf16[1,2048,5632]{2,1,0:T(8,128)(2,1)} %all-gather.18.cloned.1.call-done), kind=kOutput, calls=%fused_computation.136 | convolution fusion | flops 7383285760 | bytes 22675456 | tf_op jit(solution)/shard_map/dot_general | solution.py:90
  643.9 26.3 %convolution_convert_fusion.2 = bf16[2048,5632]{1,0:T(8,128)(2,1)} fusion(bf16[640,2048]{1,0:T(8,128)(2,1)} %bitcast.47, bf16[640,5632]{1,0:T(8,128)(2,1)} %get-tuple-element.77), kind=kOutput, calls=%fused_computation.10 | convolution fusion | flops 14775484416 | bytes 32899072 | tf_op jit(solution)/shard_map/dot_general | solution.py:86
  691.1 28.5 %convolution_convert_fusion.1 = bf16[2048,5632]{1,0:T(8,128)(2,1)} fusion(bf16[640,2048]{1,0:T(8,128)(2,1)} %bitcast.47, bf16[640,5632]{1,0:T(8,128)(2,1)} %get-tuple-element.83), kind=kOutput, calls=%fused_computation.9 | convolution fusion | flops 14775484416 | bytes 32899072 | tf_op jit(solution)/shard_map/dot_general | solution.py:86
  719.6 22.3 %fusion.63 = bf16[640,2048]{1,0:T(8,128)(2,1)} fusion(bf16[640,5632]{1,0:T(8,128)(2,1)} %get-tuple-element.82, bf16[1,5632,2048]{2,1,0:T(8,128)(2,1)} %all-gather.22.cloned.1.call-done), kind=kOutput, calls=%fused_computation.115 | convolution fusion | flops 14765260800 | bytes 32899072 | tf_op jit(solution)/shard_map/dot_general | solution.py:82
  765.0 11.4 convolution_convert_fusion.4
  776.3 10.4 fusion.60
  795.7 8.4 multiply_convert_fusion.5
  911.0 9.8 fusion.66
  920.8 20.7 %collective-permute-done.14 = bf16[2,256,1024]{2,1,0:T(8,128)(2,1)} collective-permute-done((bf16[2,256,1024]{2,1,0:T(8,128)(2,1)}, bf16[2,256,1024]{2,1,0:T(8,128)(2,1)}, u32[]{:S(2)}, u32[]{:S(2)}) %collective-permute-start.14) | collective-permute-done | bytes 1048608 | tf_op jit(solution)/shard_map/ppermute | solution.py:234
  950.7 18.0 %collective-permute-done.15 = bf16[256,1024]{1,0:T(8,128)(2,1)S(1)} collective-permute-done((bf16[256,1024]{1,0:T(8,128)(2,1)S(1)}, bf16[256,1024]{1,0:T(8,128)(2,1)S(1)}, u32[]{:S(2)}, u32[]{:S(2)}) %collective-permute-start.15) | collective-permute-done | bytes 524320 | tf_op jit(solution)/shard_map/ppermute | solution.py:234
  990.6 33.3 %collective-permute-done.16 = bf16[1024,1024]{0,1:T(8,128)(2,1)S(1)} collective-permute-done((bf16[1024,1024]{0,1:T(8,128)(2,1)S(1)}, bf16[1024,1024]{0,1:T(8,128)(2,1)S(1)}, u32[]{:S(2)}, u32[]{:S(2)}) %collective-permute-start.16) | collective-permute-done | bytes 2097184 | tf_op jit(solution)/shard_map/ppermute | solution.py:159
  1077.8 14.8 %collective-permute-done.17 = bf16[256,2048]{1,0:T(8,128)(2,1)S(1)} collective-permute-done((bf16[256,2048]{1,0:T(8,128)(2,1)}, bf16[256,2048]{1,0:T(8,128)(2,1)S(1)}, u32[]{:S(2)}, u32[]{:S(2)}) %collective-permute-start.17) | collective-permute-done | bytes 1048608 | tf_op jit(solution)/shard_map/ppermute | solution.py:159
  1097.1 18.9 %collective-permute-done.19 = bf16[256,2048]{1,0:T(8,128)(2,1)S(1)} collective-permute-done((bf16[256,2048]{1,0:T(8,128)(2,1)S(1)}, bf16[256,2048]{1,0:T(8,128)(2,1)S(1)}, u32[]{:S(2)}, u32[]{:S(2)}) %collective-permute-start.19) | collective-permute-done | bytes 1048608 | tf_op jit(solution)/shard_map/ppermute | solution.py:159
  1160.1 8.2 all-to-all-done.7
  (712 shorter events, 492.4 us)
Async XLA Ops:
  7.2 115.3 %all-gather.12.cloned.1.call-start = ((), (), s32[]{:S(2)}) async-start(), calls=%async_computation.12 | async-start | bytes 5308416 | tf_op jit(solution)/shard_map/all_gather | solution.py:321
  29.2 121.0 %all-gather.14.cloned.1.call-start = ((), (), s32[]{:S(2)}) async-start(), calls=%async_computation.17 | async-start | bytes 9437184 | tf_op jit(solution)/shard_map/all_gather | solution.py:226
  30.0 267.2 %all-gather.16.cloned.1.call-start = ((), (), s32[]{:S(2)}) async-start(), calls=%async_computation.18 | async-start | bytes 9437184 | tf_op jit(solution)/shard_map/all_gather | solution.py:226
  30.7 410.7 %all-gather.18.cloned.1.call-start = ((), (), s32[]{:S(2)}) async-start(), calls=%async_computation.19 | async-start | bytes 25952256 | tf_op jit(solution)/shard_map/all_gather | solution.py:226
  31.3 433.8 %all-gather.20.cloned.1.call-start = ((), (), s32[]{:S(2)}) async-start(), calls=%async_computation.20 | async-start | bytes 25952256 | tf_op jit(solution)/shard_map/all_gather | solution.py:226
  31.8 505.3 %all-gather.22.cloned.1.call-start = ((), (), s32[]{:S(2)}) async-start(), calls=%async_computation.21 | async-start | bytes 25952256 | tf_op jit(solution)/shard_map/all_gather | solution.py:226
  34.7 28.6 %collective-permute-start = (bf16[256,2176]{1,0:T(8,128)(2,1)S(1)}, bf16[256,2176]{1,0:T(8,128)(2,1)}, u32[]{:S(2)}, u32[]{:S(2)}) collective-permute-start(bf16[256,2176]{1,0:T(8,128)(2,1)S(1)} %concatenate.68), channel_id=1, source_target_pairs={{0,1},{1,2},{2,3},{3,0},{4,5},{5,6},{6,7},{7,4},{8,9},{9,10},{10,1... | collective-permute-start | bytes 3342344 | tf_op jit(solution)/shard_map/ppermute | solution.py:159
  63.3 27.0 %collective-permute-start.1 = (bf16[256,2176]{1,0:T(8,128)(2,1)}, bf16[256,2176]{1,0:T(8,128)(2,1)}, u32[]{:S(2)}, u32[]{:S(2)}) collective-permute-start(bf16[256,2176]{1,0:T(8,128)(2,1)} %collective-permute-done), channel_id=1, source_target_pairs={{0,1},{1,2},{2,3},{3,0},{4,5},{5,6},{6,7},{7,4},{8,9},{9,10},{10,1... | collective-permute-start | bytes 3342344 | tf_op jit(solution)/shard_map/ppermute | solution.py:159
  147.8 46.5 %collective-permute-start.6 = (bf16[1024,1024]{0,1:T(8,128)(2,1)}, bf16[1024,1024]{0,1:T(8,128)(2,1)}, u32[]{:S(2)}, u32[]{:S(2)}) collective-permute-start(bf16[1024,1024]{0,1:T(8,128)(2,1)} %pad_maximum_fusion.5), channel_id=1, source_target_pairs={{0,1},{1,2},{2,3},{3,0},{4,5},{5,6},{6,7},{7,4},{8,9},{9,10},{10,1... | collective-permute-start | bytes 6291464 | tf_op jit(solution)/shard_map/ppermute | solution.py:159
  194.3 45.8 %collective-permute-start.7 = (bf16[1024,1024]{0,1:T(8,128)(2,1)}, bf16[1024,1024]{0,1:T(8,128)(2,1)}, u32[]{:S(2)}, u32[]{:S(2)}) collective-permute-start(bf16[1024,1024]{0,1:T(8,128)(2,1)} %collective-permute-done.6), channel_id=1, source_target_pairs={{0,1},{1,2},{2,3},{3,0},{4,5},{5,6},{6,7},{7,4},{8,9},{9,10},{10,1... | collective-permute-start | bytes 6291464 | tf_op jit(solution)/shard_map/ppermute | solution.py:159
  240.1 44.6 %collective-permute-start.8 = (bf16[1024,1024]{0,1:T(8,128)(2,1)}, bf16[1024,1024]{0,1:T(8,128)(2,1)S(1)}, u32[]{:S(2)}, u32[]{:S(2)}) collective-permute-start(bf16[1024,1024]{0,1:T(8,128)(2,1)} %collective-permute-done.7), channel_id=1, source_target_pairs={{0,1},{1,2},{2,3},{3,0},{4,5},{5,6},{6,7},{7,4},{8,9},{9,10},{10,1... | collective-permute-start | bytes 6291464 | tf_op jit(solution)/shard_map/ppermute | solution.py:159
  307.4 57.9 %all-to-all-start = ((bf16[4,160,2048]{2,1,0:T(8,128)(2,1)}), bf16[4,160,2048]{2,1,0:T(8,128)(2,1)S(1)}, u32[]{:S(2)}, u32[]{:S(2)}) async-start(bf16[4,160,2048]{2,1,0:T(8,128)(2,1)} %bitcast.461), calls=%async_computation | async-start | bytes 5242880 | tf_op jit(solution)/shard_map/all_to_all | solution.py:145
  374.0 63.6 %all-to-all-start.1 = ((bf16[4,160,2048]{2,1,0:T(8,128)(2,1)}), bf16[4,160,2048]{2,1,0:T(8,128)(2,1)}, u32[]{:S(2)}, u32[]{:S(2)}) async-start(bf16[4,160,2048]{2,1,0:T(8,128)(2,1)} %bitcast.46), calls=%async_computation.1 | async-start | bytes 5242880 | tf_op jit(solution)/shard_map/all_to_all | solution.py:145
  437.6 66.1 %all-to-all-start.2 = ((bf16[4,160,2176]{2,1,0:T(8,128)(2,1)}), bf16[4,160,2176]{2,1,0:T(8,128)(2,1)S(1)}, u32[]{:S(2)}, u32[]{:S(2)}) async-start(bf16[4,160,2176]{2,1,0:T(8,128)(2,1)} %pad_maximum_fusion.2), calls=%async_computation.2 | async-start | bytes 5570560 | tf_op jit(solution)/shard_map/all_to_all | solution.py:145
  441.3 323.7 %reduce-scatter.5.cloned.1.call-start = ((), (), s32[]{:S(2)}) async-start(), calls=%async_computation.13 | async-start | bytes 25952256 | tf_op jit(solution)/shard_map/reduce_scatter | solution.py:230
  600.9 39.4 %all-to-all-start.3 = ((bf16[4,160,1152]{2,1,0:T(8,128)(2,1)}), bf16[4,160,1152]{2,1,0:T(8,128)(2,1)S(1)}, u32[]{:S(2)}, u32[]{:S(2)}) async-start(bf16[4,160,1152]{2,1,0:T(8,128)(2,1)} %bitcast.56), calls=%async_computation.3 | async-start | bytes 2949120 | tf_op jit(solution)/shard_map/all_to_all | solution.py:145
  640.3 34.4 %all-to-all-start.4 = ((bf16[4,160,1024]{2,1,0:T(8,128)(2,1)}), bf16[4,160,1024]{2,1,0:T(8,128)(2,1)S(1)}, u32[]{:S(2)}, u32[]{:S(2)}) async-start(bf16[4,160,1024]{2,1,0:T(8,128)(2,1)} %bitcast.485), calls=%async_computation.4 | async-start | bytes 2621440 | tf_op jit(solution)/shard_map/all_to_all | solution.py:145
  643.8 224.4 %reduce-scatter.9.cloned.1.call-start = ((), (), s32[]{:S(2)}) async-start(), calls=%async_computation.15 | async-start | bytes 25952256 | tf_op jit(solution)/shard_map/reduce_scatter | solution.py:230
  686.5 63.6 %all-to-all-start.5 = ((bf16[4,160,2048]{2,1,0:T(8,128)(2,1)}), bf16[4,160,2048]{2,1,0:T(8,128)(2,1)}, u32[]{:S(2)}, u32[]{:S(2)}) async-start(bf16[4,160,2048]{2,1,0:T(8,128)(2,1)} %bitcast.68), calls=%async_computation.5 | async-start | bytes 5242880 | tf_op jit(solution)/shard_map/all_to_all | solution.py:145
  691.1 438.0 %reduce-scatter.11.cloned.1.call-start = ((), (), s32[]{:S(2)}) async-start(), calls=%async_computation.16 | async-start | bytes 25952256 | tf_op jit(solution)/shard_map/reduce_scatter | solution.py:230
  760.2 125.8 %all-to-all-start.6 = ((bf16[4,160,2048]{2,1,0:T(8,128)(2,1)}), bf16[4,160,2048]{2,1,0:T(8,128)(2,1)}, u32[]{:S(2)}, u32[]{:S(2)}) async-start(bf16[4,160,2048]{2,1,0:T(8,128)(2,1)} %bitcast.458), calls=%async_computation.7 | async-start | bytes 5242880 | tf_op jit(solution)/shard_map/all_to_all | solution.py:145
  764.9 379.0 %reduce-scatter.7.cloned.1.call-start = ((), (), s32[]{:S(2)}) async-start(), calls=%async_computation.14 | async-start | bytes 5308416 | tf_op jit(solution)/shard_map/reduce_scatter | solution.py:230
  811.4 70.5 %collective-permute-start.9 = (bf16[1024,1024]{0,1:T(8,128)(2,1)}, bf16[1024,1024]{0,1:T(8,128)(2,1)}, u32[]{:S(2)}, u32[]{:S(2)}) collective-permute-start(bf16[1024,1024]{0,1:T(8,128)(2,1)} %pad_maximum_fusion.6), channel_id=1, source_target_pairs={{0,1},{1,2},{2,3},{3,0},{4,5},{5,6},{6,7},{7,4},{8,9},{9,10},{10,1... | collective-permute-start | bytes 6291464 | tf_op jit(solution)/shard_map/ppermute | solution.py:159
  815.8 58.2 %collective-permute-start.10 = (bf16[2,2,256,2048]{3,2,1,0:T(8,128)(2,1)}, bf16[2,2,256,2048]{3,2,1,0:T(8,128)(2,1)}, u32[]{:S(2)}, u32[]{:S(2)}) collective-permute-start(bf16[2,2,256,2048]{3,2,1,0:T(8,128)(2,1)} %dynamic-slice_bitcast_fusion.1), channel_id=1, source_target_pairs={{0,4},{4,0},{8,12},{12,8},{16,20},{20,16},{24,28},{28,24},{1,5},{5... | collective-permute-start | bytes 12582920 | tf_op jit(solution)/shard_map/ppermute | solution.py:234
  887.5 86.1 %collective-permute-start.11 = (bf16[1024,1024]{0,1:T(8,128)(2,1)}, bf16[1024,1024]{0,1:T(8,128)(2,1)}, u32[]{:S(2)}, u32[]{:S(2)}) collective-permute-start(bf16[1024,1024]{0,1:T(8,128)(2,1)} %fusion.53), channel_id=1, source_target_pairs={{0,1},{1,2},{2,3},{3,0},{4,5},{5,6},{6,7},{7,4},{8,9},{9,10},{10,1... | collective-permute-start | bytes 6291464 | tf_op jit(solution)/shard_map/ppermute | solution.py:159
  893.0 48.5 %collective-permute-start.14 = (bf16[2,256,1024]{2,1,0:T(8,128)(2,1)}, bf16[2,256,1024]{2,1,0:T(8,128)(2,1)}, u32[]{:S(2)}, u32[]{:S(2)}) collective-permute-start(bf16[2,256,1024]{2,1,0:T(8,128)(2,1)} %dynamic-slice_bitcast_fusion.4), channel_id=1, source_target_pairs={{0,16},{4,20},{8,24},{12,28},{16,0},{20,4},{24,8},{28,12},{1,17},{... | collective-permute-start | bytes 3145736 | tf_op jit(solution)/shard_map/ppermute | solution.py:234
  894.2 50.6 %collective-permute-start.12 = (bf16[2,256,1024]{2,1,0:T(8,128)(2,1)S(1)}, bf16[2,256,1024]{2,1,0:T(8,128)(2,1)}, u32[]{:S(2)}, u32[]{:S(2)}) collective-permute-start(bf16[2,256,1024]{2,1,0:T(8,128)(2,1)S(1)} %dynamic-slice_bitcast_fusion.5), channel_id=1, source_target_pairs={{0,8},{4,12},{8,0},{12,4},{16,24},{20,28},{24,16},{28,20},{1,9},{5... | collective-permute-start | bytes 3145736 | tf_op jit(solution)/shard_map/ppermute | solution.py:234
  976.1 47.8 %collective-permute-start.16 = (bf16[1024,1024]{0,1:T(8,128)(2,1)S(1)}, bf16[1024,1024]{0,1:T(8,128)(2,1)S(1)}, u32[]{:S(2)}, u32[]{:S(2)}) collective-permute-start(bf16[1024,1024]{0,1:T(8,128)(2,1)S(1)} %fusion.55), channel_id=1, source_target_pairs={{0,1},{1,2},{2,3},{3,0},{4,5},{5,6},{6,7},{7,4},{8,9},{9,10},{10,1... | collective-permute-start | bytes 6291464 | tf_op jit(solution)/shard_map/ppermute | solution.py:159
  990.6 82.6 %collective-permute-start.18 = (bf16[2,2,256,2048]{3,2,1,0:T(8,128)(2,1)}, bf16[2,2,256,2048]{3,2,1,0:T(8,128)(2,1)}, u32[]{:S(2)}, u32[]{:S(2)}) collective-permute-start(bf16[2,2,256,2048]{3,2,1,0:T(8,128)(2,1)} %dynamic-slice_bitcast_fusion), channel_id=1, source_target_pairs={{0,4},{4,0},{8,12},{12,8},{16,20},{20,16},{24,28},{28,24},{1,5},{5... | collective-permute-start | bytes 12582920 | tf_op jit(solution)/shard_map/ppermute | solution.py:234
  1093.7 30.9 %collective-permute-start.23 = (bf16[2,256,1024]{2,1,0:T(8,128)(2,1)S(1)}, bf16[2,256,1024]{2,1,0:T(8,128)(2,1)S(1)}, u32[]{:S(2)}, u32[]{:S(2)}) collective-permute-start(bf16[2,256,1024]{2,1,0:T(8,128)(2,1)S(1)} %dynamic-slice_bitcast_fusion.2), channel_id=1, source_target_pairs={{0,16},{4,20},{8,24},{12,28},{16,0},{20,4},{24,8},{28,12},{1,17},{... | collective-permute-start | bytes 3145736 | tf_op jit(solution)/shard_map/ppermute | solution.py:234
  1094.9 32.4 %collective-permute-start.21 = (bf16[2,256,1024]{2,1,0:T(8,128)(2,1)S(1)}, bf16[2,256,1024]{2,1,0:T(8,128)(2,1)S(1)}, u32[]{:S(2)}, u32[]{:S(2)}) collective-permute-start(bf16[2,256,1024]{2,1,0:T(8,128)(2,1)S(1)} %dynamic-slice_bitcast_fusion.3), channel_id=1, source_target_pairs={{0,8},{4,12},{8,0},{12,4},{16,24},{20,28},{24,16},{28,20},{1,9},{5... | collective-permute-start | bytes 3145736 | tf_op jit(solution)/shard_map/ppermute | solution.py:234
  1116.4 27.5 %collective-permute-start.20 = (bf16[256,2048]{1,0:T(8,128)(2,1)S(1)}, bf16[256,2048]{1,0:T(8,128)(2,1)}, u32[]{:S(2)}, u32[]{:S(2)}) collective-permute-start(bf16[256,2048]{1,0:T(8,128)(2,1)S(1)} %fusion.88), channel_id=1, source_target_pairs={{0,1},{1,2},{2,3},{3,0},{4,5},{5,6},{6,7},{7,4},{8,9},{9,10},{10,1... | collective-permute-start | bytes 3145736 | tf_op jit(solution)/shard_map/ppermute | solution.py:159
  (195 other events, 2256.0 us)
Sparse Core Ops, SparseCore 0:
  29.3 41.1 all-gather.11
  72.4 54.2 all-gather.13
  128.5 54.2 all-gather.15
  184.6 116.3 all-gather.17
  302.7 116.3 all-gather.19
  420.8 116.3 all-gather.21
  540.8 146.3 reduce-scatter.4
  690.8 146.3 reduce-scatter.8
  840.8 180.0 reduce-scatter.10
  1061.4 61.0 reduce-scatter.6

commit v9 on v8

--- a/solution.py
+++ b/solution.py
@@ -261,14 +261,18 @@
     return fold(part.reshape(2, 2, 2, rows // 8, columns), 2, 1).astype(bf16)
 
 
-def reduce_chips(grid):
+def reduce_first(grid):
     if not swaps_fit():
-        return reduce_dp(grid).astype(f32)
+        return (grid,)
     columns = grid.shape[-1]
     left, right = grid[..., : columns // 2], grid[..., columns // 2 :]
-    left = fold(fold(left, 1, 2).astype(bf16), 0, 4)
-    right = fold(fold(right, 0, 4).astype(bf16), 0, 2)
-    return jnp.concatenate([left, right], 1)
+    return (fold(left, 1, 2).astype(bf16), fold(right, 0, 4).astype(bf16))
+
+
+def reduce_last(halved):
+    if not swaps_fit():
+        return reduce_dp(halved[0]).astype(f32)
+    return jnp.concatenate([fold(halved[0], 0, 4), fold(halved[1], 0, 2)], 1)
 
 
 def body(
@@ -498,8 +502,11 @@
             kv_grad, output_sum = lax.optimization_barrier((kv_grad, output_sum))
         if step == 2:
             kv_grad, output_core = lax.optimization_barrier((kv_grad, output_core))
-            output_sum = reduce_chips(output_core)
+            output_core = reduce_first(output_core)
         if step == experts - 1:
+            kv_grad, output_core = lax.optimization_barrier((kv_grad, output_core))
+            output_sum = reduce_last(output_core)
+        if k == 0:
             kv_grad, output_sum = lax.optimization_barrier((kv_grad, output_sum))
         if k == 0:
             query_raw_grad = rotate_back(query_grad, query_cos, query_sin).astype(bf16)
@@ -515,8 +522,6 @@
         if step == experts - 1:
             part, query_rows = lax.optimization_barrier((part, query_rows))
         kv_grad = ring_step(part, experts)
-    ffn_picked = take_back(ffn_place, ffn_back)
-    result = mixed_stream + jnp.sum(ffn_gate.T[:, :, None] * ffn_picked, 0)
     att_rows_grad = mm_nt(query_raw_grad, query_all).astype(bf16)
     kv_raw_grad = jnp.concatenate(
         [rotate_back(kv_grad[:, :width], tree_cos, tree_sin), kv_grad[:, width:]], 1
@@ -566,11 +571,18 @@
                 (normed_one_grad, reduce_dp(shared_part))
             )
         if step == 1:
+            normed_one_grad, query_core, ffn_back = lax.optimization_barrier(
+                (normed_one_grad, query_core, ffn_back)
+            )
+            query_core = reduce_first(query_core)
+        if step == 2:
             normed_one_grad, query_core = lax.optimization_barrier((normed_one_grad, query_core))
-            query_sum = reduce_chips(query_core)
+            query_sum = reduce_last(query_core)
         if k == 0:
             normed_one_grad, query_sum = lax.optimization_barrier((normed_one_grad, query_sum))
     normed_one_grad = normed_one_grad + router_grad
+    ffn_picked = take_back(ffn_place, ffn_back)
+    result = mixed_stream + jnp.sum(ffn_gate.T[:, :, None] * ffn_picked, 0)
     input_grad = mixed_grad + norm_back(inputs, inverse_one, gain_first, normed_one_grad)
     shared_sum = exchange(shared_part.reshape(experts, shard_rows, -1)).astype(f32)
     kv_sum = (

time: 1190 us -> 1170 us (0.983)
  waiting for transfers between devices: 416 us -> 394 us
    ppermute x12, waiting for transfers between devices: 205 us -> 179 us  [ring_step(): lax.ppermute(block, 'expert', [(i, (i + 1) % experts) for i in range(expe...]
    unnamed x377 -> x371, local copies, waits for them, and re-layouts: 33.1 us -> 31.1 us
  transfers between devices with their start and end apart: 43 -> 43, of which waited for: 25 -> 25; matrix products, arithmetic and copies ran while one was open for 55% -> 56% of each run, Pallas kernels for 0% -> 0%
where the time goes in v9:
time: 1170 us; the launch traced here: 1160 us
  matrix products  456 us (39%)
  waiting for transfers between devices  394 us (34%)
  other arithmetic  115 us (10%)
  local copies, waits for them, and re-layouts  112 us (10%)
  starting transfers between devices  64.3 us (5%)
  between operations  17.8 us (2%)
    ppermute x12, waiting for transfers between devices, ring_step(): lax.ppermute(block, 'expert', [(i, (i + 1) % experts) for i in range(expe...  179 us
    all_to_all x8, waiting for transfers between devices, exchange(): lax.all_to_all(packed, 'expert', split_axis=0, concat_axis=0, tiled=True)  137 us
    dot_general x19, matrix products, mm(): return jnp.dot(left, right, preferred_element_type=f32)  116 us
    dot_general x8, matrix products, mm_nt(): lax.dot_general(left, right, (((1,), (1,)), ((), ())), preferred_element_...  116 us
    dot_general x11, matrix products, mm_tn(): lax.dot_general(left, right, (((0,), (0,)), ((), ())), preferred_element_...  114 us
    ppermute x10, waiting for transfers between devices, swap(): return lax.ppermute(block, 'dp', [(i, i ^ bit) for i in range(8)])  61.5 us
    all_to_all x8, starting transfers between devices, exchange(): lax.all_to_all(packed, 'expert', split_axis=0, concat_axis=0, tiled=True)  33.8 us
    unnamed x371, local copies, waits for them, and re-layouts  31.1 us
  transfers between devices with their start and end apart: 43, of which 25 were waited for; matrix products, arithmetic and copies ran while one was open for 56% of the time, Pallas kernels for 0%

profile of v9, /device:TPU:0, one launch (start us, length us, event | category | flops | bytes accessed | tf_op | source)
XLA Modules:
  0.0 1158.6 jit_solution(5252466244508557937)
XLA Ops:
  38.4 24.9 %collective-permute-done = bf16[256,2176]{1,0:T(8,128)(2,1)} collective-permute-done((bf16[256,2176]{1,0:T(8,128)(2,1)S(1)}, bf16[256,2176]{1,0:T(8,128)(2,1)}, u32[]{:S(2)}, u32[]{:S(2)}) %collective-permute-start) | collective-permute-done | bytes 1114144 | tf_op jit(solution)/shard_map/ppermute | solution.py:159
  68.2 22.1 %collective-permute-done.1 = bf16[256,2176]{1,0:T(8,128)(2,1)} collective-permute-done((bf16[256,2176]{1,0:T(8,128)(2,1)}, bf16[256,2176]{1,0:T(8,128)(2,1)}, u32[]{:S(2)}, u32[]{:S(2)}) %collective-permute-start.1) | collective-permute-done | bytes 1114144 | tf_op jit(solution)/shard_map/ppermute | solution.py:159
  94.2 22.1 %collective-permute-done.2 = bf16[256,2176]{1,0:T(8,128)(2,1)S(1)} collective-permute-done((bf16[256,2176]{1,0:T(8,128)(2,1)}, bf16[256,2176]{1,0:T(8,128)(2,1)S(1)}, u32[]{:S(2)}, u32[]{:S(2)}) %collective-permute-start.2) | collective-permute-done | bytes 1114144 | tf_op jit(solution)/shard_map/ppermute | solution.py:159
  150.2 12.4 %copy.272 = bf16[2048,2048]{1,0:T(8,128)(2,1)} copy(bf16[2048,2048]{0,1:T(8,128)(2,1)} %bitcast.417) | data formatting | bytes 16777216 | tf_op jit(solution)/shard_map/dot_general | solution.py:82
  162.6 10.0 fusion.228
  173.7 20.6 %collective-permute-done.6 = bf16[1024,1024]{0,1:T(8,128)(2,1)} collective-permute-done((bf16[1024,1024]{0,1:T(8,128)(2,1)}, bf16[1024,1024]{0,1:T(8,128)(2,1)}, u32[]{:S(2)}, u32[]{:S(2)}) %collective-permute-start.6) | collective-permute-done | bytes 2097184 | tf_op jit(solution)/shard_map/ppermute | solution.py:159
  222.8 17.3 %collective-permute-done.7 = bf16[1024,1024]{0,1:T(8,128)(2,1)} collective-permute-done((bf16[1024,1024]{0,1:T(8,128)(2,1)}, bf16[1024,1024]{0,1:T(8,128)(2,1)}, u32[]{:S(2)}, u32[]{:S(2)}) %collective-permute-start.7) | collective-permute-done | bytes 2097184 | tf_op jit(solution)/shard_map/ppermute | solution.py:159
  253.5 31.2 %collective-permute-done.8 = bf16[1024,1024]{0,1:T(8,128)(2,1)S(1)} collective-permute-done((bf16[1024,1024]{0,1:T(8,128)(2,1)}, bf16[1024,1024]{0,1:T(8,128)(2,1)S(1)}, u32[]{:S(2)}, u32[]{:S(2)}) %collective-permute-start.8) | collective-permute-done | bytes 2097184 | tf_op jit(solution)/shard_map/ppermute | solution.py:159
  297.1 10.3 fusion.69
  315.6 49.7 %all-to-all-done = bf16[4,160,2048]{2,1,0:T(8,128)(2,1)S(1)} async-done(((bf16[4,160,2048]{2,1,0:T(8,128)(2,1)}), bf16[4,160,2048]{2,1,0:T(8,128)(2,1)S(1)}, u32[]{:S(2)}, u32[]{:S(2)}) %all-to-all-start) | async-done | bytes 2621472 | tf_op jit(solution)/shard_map/all_to_all | solution.py:145
  385.7 51.9 %all-to-all-done.1 = bf16[4,160,2048]{2,1,0:T(8,128)(2,1)} async-done(((bf16[4,160,2048]{2,1,0:T(8,128)(2,1)}), bf16[4,160,2048]{2,1,0:T(8,128)(2,1)}, u32[]{:S(2)}, u32[]{:S(2)}) %all-to-all-start.1) | async-done | bytes 2621472 | tf_op jit(solution)/shard_map/all_to_all | solution.py:145
  441.4 23.6 %fusion.6 = f32[640,5632]{1,0:T(8,128)} fusion(bf16[640,2048]{1,0:T(8,128)(2,1)} %bitcast.47, bf16[1,2048,5632]{2,1,0:T(8,128)(2,1)} %all-gather.18.cloned.1.call-done), kind=kOutput, calls=%fused_computation.6 | convolution fusion | flops 14763950080 | bytes 40108032 | tf_op jit(solution)/shard_map/dot_general | solution.py:82
  465.0 31.8 %multiply_convert_fusion.2 = (bf16[640,5632]{1,0:T(8,128)(2,1)}, f32[640,5632]{1,0:T(8,128)}) fusion(f32[640,5632]{1,0:T(8,128)} %fusion.6, bf16[640,2048]{1,0:T(8,128)(2,1)} %bitcast.47, bf16[1,2048,5632]{2,1,0:T(8,128)(2,1)} %all-gather.20.cloned.1.call-done), kind=kOutput, calls=%fused_computation.14 | convolution fusion | flops 14785576960 | bytes 61734912 | tf_op jit(solution)/shard_map/dot_general | solution.py:82
  505.7 24.9 %convolution_convert_fusion = bf16[5632,2048]{1,0:T(8,128)(2,1)} fusion(bf16[640,5632]{1,0:T(8,128)(2,1)} %get-tuple-element.87, f32[640]{0:T(1024)S(1)} %convert_reduce_fusion.2, bf16[640,2176]{1,0:T(8,128)(2,1)S(1)} %bitcast.408), kind=kOutput, calls=%fused_computation.8 | convolution fusion | flops 14779416576 | bytes 32903168 | tf_op jit(solution)/shard_map/dot_general | solution.py:86
  537.2 38.4 %multiply_convert_fusion.1 = (bf16[640,5632]{1,0:T(8,128)(2,1)}, bf16[640,5632]{1,0:T(8,128)(2,1)}, f32[640]{0:T(1024)S(1)}) fusion(f32[640,5632]{1,0:T(8,128)} %fusion.6, f32[640,5632]{1,0:T(8,128)} %get-tuple-element.233, f32[640]{0:T(1024)S(1)} %convert_reduce_fusion.2, bf16[640,5632]{1,0:T(8,128)(2,1)} %get-tuple-element.87, ...), kind=kOutput, calls=%fused_computation.13 | convolution fusion | flops 14825225216 | bytes 76157952 | tf_op jit(solution)/shard_map/dot_general | solution.py:90
  575.8 12.7 %fusion.10 = f32[640,1024]{1,0:T(8,128)S(1)} fusion(bf16[640,5632]{1,0:T(8,128)(2,1)} %get-tuple-element.88, bf16[1,2048,5632]{2,1,0:T(8,128)(2,1)} %all-gather.20.cloned.1.call-done), kind=kOutput, calls=%fused_computation.24 | convolution fusion | flops 7381975040 | bytes 21364736 | tf_op jit(solution)/shard_map/dot_general | solution.py:90
  588.6 11.0 add_convert_fusion.3
  605.3 13.0 %fusion.8 = f32[640,1024]{1,0:T(8,128)S(1)} fusion(bf16[640,5632]{1,0:T(8,128)(2,1)} %get-tuple-element.88, bf16[1,2048,5632]{2,1,0:T(8,128)(2,1)} %all-gather.20.cloned.1.call-done), kind=kOutput, calls=%fused_computation.20 | convolution fusion | flops 7381975040 | bytes 21364736 | tf_op jit(solution)/shard_map/dot_general | solution.py:90
  618.2 13.8 %add_convert_fusion.2 = bf16[640,1024]{1,0:T(8,128)(2,1)} fusion(f32[640,1024]{1,0:T(8,128)S(1)} %fusion.8, bf16[640,5632]{1,0:T(8,128)(2,1)} %get-tuple-element.82, bf16[1,2048,5632]{2,1,0:T(8,128)(2,1)} %all-gather.18.cloned.1.call-done), kind=kOutput, calls=%fused_computation.136 | convolution fusion | flops 7383285760 | bytes 22675456 | tf_op jit(solution)/shard_map/dot_general | solution.py:90
  643.8 26.3 %convolution_convert_fusion.2 = bf16[2048,5632]{1,0:T(8,128)(2,1)} fusion(bf16[640,2048]{1,0:T(8,128)(2,1)} %bitcast.47, bf16[640,5632]{1,0:T(8,128)(2,1)} %get-tuple-element.82), kind=kOutput, calls=%fused_computation.10 | convolution fusion | flops 14775484416 | bytes 32899072 | tf_op jit(solution)/shard_map/dot_general | solution.py:86
  691.1 28.5 %convolution_convert_fusion.1 = bf16[2048,5632]{1,0:T(8,128)(2,1)} fusion(bf16[640,2048]{1,0:T(8,128)(2,1)} %bitcast.47, bf16[640,5632]{1,0:T(8,128)(2,1)} %get-tuple-element.88), kind=kOutput, calls=%fused_computation.9 | convolution fusion | flops 14775484416 | bytes 32899072 | tf_op jit(solution)/shard_map/dot_general | solution.py:86
  719.6 22.4 %fusion.63 = bf16[640,2048]{1,0:T(8,128)(2,1)} fusion(bf16[640,5632]{1,0:T(8,128)(2,1)} %get-tuple-element.87, bf16[1,5632,2048]{2,1,0:T(8,128)(2,1)} %all-gather.22.cloned.1.call-done), kind=kOutput, calls=%fused_computation.115 | convolution fusion | flops 14765260800 | bytes 32899072 | tf_op jit(solution)/shard_map/dot_general | solution.py:82
  764.9 11.4 convolution_convert_fusion.4
  776.3 10.4 fusion.60
  795.6 8.4 multiply_convert_fusion.5
  911.1 10.2 fusion.66
  925.6 15.9 %collective-permute-done.12 = bf16[2,256,1024]{2,1,0:T(8,128)(2,1)} collective-permute-done((bf16[2,256,1024]{2,1,0:T(8,128)(2,1)}, bf16[2,256,1024]{2,1,0:T(8,128)(2,1)}, u32[]{:S(2)}, u32[]{:S(2)}) %collective-permute-start.12) | collective-permute-done | bytes 1048608 | tf_op jit(solution)/shard_map/ppermute | solution.py:234
  963.6 11.0 collective-permute-done.16
  977.9 18.3 %collective-permute-done.14 = bf16[1024,1024]{0,1:T(8,128)(2,1)S(1)} collective-permute-done((bf16[1024,1024]{0,1:T(8,128)(2,1)S(1)}, bf16[1024,1024]{0,1:T(8,128)(2,1)S(1)}, u32[]{:S(2)}, u32[]{:S(2)}) %collective-permute-start.14) | collective-permute-done | bytes 2097184 | tf_op jit(solution)/shard_map/ppermute | solution.py:159
  1047.7 13.0 %collective-permute-done.17 = bf16[256,2048]{1,0:T(8,128)(2,1)S(1)} collective-permute-done((bf16[256,2048]{1,0:T(8,128)(2,1)S(1)}, bf16[256,2048]{1,0:T(8,128)(2,1)S(1)}, u32[]{:S(2)}, u32[]{:S(2)}) %collective-permute-start.17) | collective-permute-done | bytes 1048608 | tf_op jit(solution)/shard_map/ppermute | solution.py:159
  1070.6 24.8 %collective-permute-done.20 = bf16[2,256,1024]{2,1,0:T(8,128)(2,1)S(1)} collective-permute-done((bf16[2,256,1024]{2,1,0:T(8,128)(2,1)S(1)}, bf16[2,256,1024]{2,1,0:T(8,128)(2,1)S(1)}, u32[]{:S(2)}, u32[]{:S(2)}) %collective-permute-start.20) | collective-permute-done | bytes 1048608 | tf_op jit(solution)/shard_map/ppermute | solution.py:234
  1112.0 9.2 collective-permute-done.22
  (705 shorter events, 489.1 us)
Async XLA Ops:
  7.2 115.3 %all-gather.12.cloned.1.call-start = ((), (), s32[]{:S(2)}) async-start(), calls=%async_computation.12 | async-start | bytes 5308416 | tf_op jit(solution)/shard_map/all_gather | solution.py:325
  29.2 121.0 %all-gather.14.cloned.1.call-start = ((), (), s32[]{:S(2)}) async-start(), calls=%async_computation.17 | async-start | bytes 9437184 | tf_op jit(solution)/shard_map/all_gather | solution.py:226
  30.0 267.2 %all-gather.16.cloned.1.call-start = ((), (), s32[]{:S(2)}) async-start(), calls=%async_computation.18 | async-start | bytes 9437184 | tf_op jit(solution)/shard_map/all_gather | solution.py:226
  30.7 410.7 %all-gather.18.cloned.1.call-start = ((), (), s32[]{:S(2)}) async-start(), calls=%async_computation.19 | async-start | bytes 25952256 | tf_op jit(solution)/shard_map/all_gather | solution.py:226
  31.3 433.7 %all-gather.20.cloned.1.call-start = ((), (), s32[]{:S(2)}) async-start(), calls=%async_computation.20 | async-start | bytes 25952256 | tf_op jit(solution)/shard_map/all_gather | solution.py:226
  31.8 505.3 %all-gather.22.cloned.1.call-start = ((), (), s32[]{:S(2)}) async-start(), calls=%async_computation.21 | async-start | bytes 25952256 | tf_op jit(solution)/shard_map/all_gather | solution.py:226
  34.7 28.6 %collective-permute-start = (bf16[256,2176]{1,0:T(8,128)(2,1)S(1)}, bf16[256,2176]{1,0:T(8,128)(2,1)}, u32[]{:S(2)}, u32[]{:S(2)}) collective-permute-start(bf16[256,2176]{1,0:T(8,128)(2,1)S(1)} %concatenate.68), channel_id=1, source_target_pairs={{0,1},{1,2},{2,3},{3,0},{4,5},{5,6},{6,7},{7,4},{8,9},{9,10},{10,1... | collective-permute-start | bytes 3342344 | tf_op jit(solution)/shard_map/ppermute | solution.py:159
  63.3 27.0 %collective-permute-start.1 = (bf16[256,2176]{1,0:T(8,128)(2,1)}, bf16[256,2176]{1,0:T(8,128)(2,1)}, u32[]{:S(2)}, u32[]{:S(2)}) collective-permute-start(bf16[256,2176]{1,0:T(8,128)(2,1)} %collective-permute-done), channel_id=1, source_target_pairs={{0,1},{1,2},{2,3},{3,0},{4,5},{5,6},{6,7},{7,4},{8,9},{9,10},{10,1... | collective-permute-start | bytes 3342344 | tf_op jit(solution)/shard_map/ppermute | solution.py:159
  147.8 46.5 %collective-permute-start.6 = (bf16[1024,1024]{0,1:T(8,128)(2,1)}, bf16[1024,1024]{0,1:T(8,128)(2,1)}, u32[]{:S(2)}, u32[]{:S(2)}) collective-permute-start(bf16[1024,1024]{0,1:T(8,128)(2,1)} %pad_maximum_fusion.5), channel_id=1, source_target_pairs={{0,1},{1,2},{2,3},{3,0},{4,5},{5,6},{6,7},{7,4},{8,9},{9,10},{10,1... | collective-permute-start | bytes 6291464 | tf_op jit(solution)/shard_map/ppermute | solution.py:159
  194.3 45.8 %collective-permute-start.7 = (bf16[1024,1024]{0,1:T(8,128)(2,1)}, bf16[1024,1024]{0,1:T(8,128)(2,1)}, u32[]{:S(2)}, u32[]{:S(2)}) collective-permute-start(bf16[1024,1024]{0,1:T(8,128)(2,1)} %collective-permute-done.6), channel_id=1, source_target_pairs={{0,1},{1,2},{2,3},{3,0},{4,5},{5,6},{6,7},{7,4},{8,9},{9,10},{10,1... | collective-permute-start | bytes 6291464 | tf_op jit(solution)/shard_map/ppermute | solution.py:159
  240.1 44.6 %collective-permute-start.8 = (bf16[1024,1024]{0,1:T(8,128)(2,1)}, bf16[1024,1024]{0,1:T(8,128)(2,1)S(1)}, u32[]{:S(2)}, u32[]{:S(2)}) collective-permute-start(bf16[1024,1024]{0,1:T(8,128)(2,1)} %collective-permute-done.7), channel_id=1, source_target_pairs={{0,1},{1,2},{2,3},{3,0},{4,5},{5,6},{6,7},{7,4},{8,9},{9,10},{10,1... | collective-permute-start | bytes 6291464 | tf_op jit(solution)/shard_map/ppermute | solution.py:159
  307.4 57.9 %all-to-all-start = ((bf16[4,160,2048]{2,1,0:T(8,128)(2,1)}), bf16[4,160,2048]{2,1,0:T(8,128)(2,1)S(1)}, u32[]{:S(2)}, u32[]{:S(2)}) async-start(bf16[4,160,2048]{2,1,0:T(8,128)(2,1)} %bitcast.459), calls=%async_computation | async-start | bytes 5242880 | tf_op jit(solution)/shard_map/all_to_all | solution.py:145
  374.0 63.6 %all-to-all-start.1 = ((bf16[4,160,2048]{2,1,0:T(8,128)(2,1)}), bf16[4,160,2048]{2,1,0:T(8,128)(2,1)}, u32[]{:S(2)}, u32[]{:S(2)}) async-start(bf16[4,160,2048]{2,1,0:T(8,128)(2,1)} %bitcast.46), calls=%async_computation.1 | async-start | bytes 5242880 | tf_op jit(solution)/shard_map/all_to_all | solution.py:145
  437.6 66.1 %all-to-all-start.2 = ((bf16[4,160,2176]{2,1,0:T(8,128)(2,1)}), bf16[4,160,2176]{2,1,0:T(8,128)(2,1)S(1)}, u32[]{:S(2)}, u32[]{:S(2)}) async-start(bf16[4,160,2176]{2,1,0:T(8,128)(2,1)} %pad_maximum_fusion.2), calls=%async_computation.2 | async-start | bytes 5570560 | tf_op jit(solution)/shard_map/all_to_all | solution.py:145
  441.3 323.6 %reduce-scatter.5.cloned.1.call-start = ((), (), s32[]{:S(2)}) async-start(), calls=%async_computation.13 | async-start | bytes 25952256 | tf_op jit(solution)/shard_map/reduce_scatter | solution.py:230
  600.8 39.4 %all-to-all-start.3 = ((bf16[4,160,1152]{2,1,0:T(8,128)(2,1)}), bf16[4,160,1152]{2,1,0:T(8,128)(2,1)S(1)}, u32[]{:S(2)}, u32[]{:S(2)}) async-start(bf16[4,160,1152]{2,1,0:T(8,128)(2,1)} %bitcast.56), calls=%async_computation.3 | async-start | bytes 2949120 | tf_op jit(solution)/shard_map/all_to_all | solution.py:145
  640.2 34.4 %all-to-all-start.4 = ((bf16[4,160,1024]{2,1,0:T(8,128)(2,1)}), bf16[4,160,1024]{2,1,0:T(8,128)(2,1)S(1)}, u32[]{:S(2)}, u32[]{:S(2)}) async-start(bf16[4,160,1024]{2,1,0:T(8,128)(2,1)} %bitcast.483), calls=%async_computation.4 | async-start | bytes 2621440 | tf_op jit(solution)/shard_map/all_to_all | solution.py:145
  643.8 224.5 %reduce-scatter.9.cloned.1.call-start = ((), (), s32[]{:S(2)}) async-start(), calls=%async_computation.15 | async-start | bytes 25952256 | tf_op jit(solution)/shard_map/reduce_scatter | solution.py:230
  686.5 63.6 %all-to-all-start.5 = ((bf16[4,160,2048]{2,1,0:T(8,128)(2,1)}), bf16[4,160,2048]{2,1,0:T(8,128)(2,1)}, u32[]{:S(2)}, u32[]{:S(2)}) async-start(bf16[4,160,2048]{2,1,0:T(8,128)(2,1)} %bitcast.68), calls=%async_computation.5 | async-start | bytes 5242880 | tf_op jit(solution)/shard_map/all_to_all | solution.py:145
  691.1 344.5 %reduce-scatter.11.cloned.1.call-start = ((), (), s32[]{:S(2)}) async-start(), calls=%async_computation.16 | async-start | bytes 25952256 | tf_op jit(solution)/shard_map/reduce_scatter | solution.py:230
  760.2 125.9 %all-to-all-start.6 = ((bf16[4,160,2048]{2,1,0:T(8,128)(2,1)}), bf16[4,160,2048]{2,1,0:T(8,128)(2,1)}, u32[]{:S(2)}, u32[]{:S(2)}) async-start(bf16[4,160,2048]{2,1,0:T(8,128)(2,1)} %bitcast.456), calls=%async_computation.7 | async-start | bytes 5242880 | tf_op jit(solution)/shard_map/all_to_all | solution.py:145
  764.9 356.3 %reduce-scatter.7.cloned.1.call-start = ((), (), s32[]{:S(2)}) async-start(), calls=%async_computation.14 | async-start | bytes 5308416 | tf_op jit(solution)/shard_map/reduce_scatter | solution.py:230
  811.4 70.6 %collective-permute-start.9 = (bf16[1024,1024]{0,1:T(8,128)(2,1)}, bf16[1024,1024]{0,1:T(8,128)(2,1)}, u32[]{:S(2)}, u32[]{:S(2)}) collective-permute-start(bf16[1024,1024]{0,1:T(8,128)(2,1)} %pad_maximum_fusion.6), channel_id=1, source_target_pairs={{0,1},{1,2},{2,3},{3,0},{4,5},{5,6},{6,7},{7,4},{8,9},{9,10},{10,1... | collective-permute-start | bytes 6291464 | tf_op jit(solution)/shard_map/ppermute | solution.py:159
  815.8 58.3 %collective-permute-start.10 = (bf16[2,2,256,2048]{3,2,1,0:T(8,128)(2,1)}, bf16[2,2,256,2048]{3,2,1,0:T(8,128)(2,1)}, u32[]{:S(2)}, u32[]{:S(2)}) collective-permute-start(bf16[2,2,256,2048]{3,2,1,0:T(8,128)(2,1)} %dynamic-slice_bitcast_fusion.1), channel_id=1, source_target_pairs={{0,4},{4,0},{8,12},{12,8},{16,20},{20,16},{24,28},{28,24},{1,5},{5... | collective-permute-start | bytes 12582920 | tf_op jit(solution)/shard_map/ppermute | solution.py:234
  887.5 57.3 %collective-permute-start.11 = (bf16[1024,1024]{0,1:T(8,128)(2,1)}, bf16[1024,1024]{0,1:T(8,128)(2,1)}, u32[]{:S(2)}, u32[]{:S(2)}) collective-permute-start(bf16[1024,1024]{0,1:T(8,128)(2,1)} %fusion.53), channel_id=1, source_target_pairs={{0,1},{1,2},{2,3},{3,0},{4,5},{5,6},{6,7},{7,4},{8,9},{9,10},{10,1... | collective-permute-start | bytes 6291464 | tf_op jit(solution)/shard_map/ppermute | solution.py:159
  893.0 48.5 %collective-permute-start.12 = (bf16[2,256,1024]{2,1,0:T(8,128)(2,1)}, bf16[2,256,1024]{2,1,0:T(8,128)(2,1)}, u32[]{:S(2)}, u32[]{:S(2)}) collective-permute-start(bf16[2,256,1024]{2,1,0:T(8,128)(2,1)} %dynamic-slice_bitcast_fusion.5), channel_id=1, source_target_pairs={{0,8},{4,12},{8,0},{12,4},{16,24},{20,28},{24,16},{28,20},{1,9},{5... | collective-permute-start | bytes 3145736 | tf_op jit(solution)/shard_map/ppermute | solution.py:234
  894.5 48.6 %collective-permute-start.13 = (bf16[2,256,1024]{2,1,0:T(8,128)(2,1)S(1)}, bf16[2,256,1024]{2,1,0:T(8,128)(2,1)}, u32[]{:S(2)}, u32[]{:S(2)}) collective-permute-start(bf16[2,256,1024]{2,1,0:T(8,128)(2,1)S(1)} %dynamic-slice_bitcast_fusion.4), channel_id=1, source_target_pairs={{0,16},{4,20},{8,24},{12,28},{16,0},{20,4},{24,8},{28,12},{1,17},{... | collective-permute-start | bytes 3145736 | tf_op jit(solution)/shard_map/ppermute | solution.py:234
  947.5 48.7 %collective-permute-start.14 = (bf16[1024,1024]{0,1:T(8,128)(2,1)S(1)}, bf16[1024,1024]{0,1:T(8,128)(2,1)S(1)}, u32[]{:S(2)}, u32[]{:S(2)}) collective-permute-start(bf16[1024,1024]{0,1:T(8,128)(2,1)S(1)} %fusion.54), channel_id=1, source_target_pairs={{0,1},{1,2},{2,3},{3,0},{4,5},{5,6},{6,7},{7,4},{8,9},{9,10},{10,1... | collective-permute-start | bytes 6291464 | tf_op jit(solution)/shard_map/ppermute | solution.py:159
  963.6 77.7 %collective-permute-start.18 = (bf16[2,2,256,2048]{3,2,1,0:T(8,128)(2,1)}, bf16[2,2,256,2048]{3,2,1,0:T(8,128)(2,1)}, u32[]{:S(2)}, u32[]{:S(2)}) collective-permute-start(bf16[2,2,256,2048]{3,2,1,0:T(8,128)(2,1)} %dynamic-slice_bitcast_fusion), channel_id=1, source_target_pairs={{0,4},{4,0},{8,12},{12,8},{16,20},{20,16},{24,28},{28,24},{1,5},{5... | collective-permute-start | bytes 12582920 | tf_op jit(solution)/shard_map/ppermute | solution.py:234
  1061.3 34.2 %collective-permute-start.20 = (bf16[2,256,1024]{2,1,0:T(8,128)(2,1)S(1)}, bf16[2,256,1024]{2,1,0:T(8,128)(2,1)S(1)}, u32[]{:S(2)}, u32[]{:S(2)}) collective-permute-start(bf16[2,256,1024]{2,1,0:T(8,128)(2,1)S(1)} %dynamic-slice_bitcast_fusion.3), channel_id=1, source_target_pairs={{0,8},{4,12},{8,0},{12,4},{16,24},{20,28},{24,16},{28,20},{1,9},{5... | collective-permute-start | bytes 3145736 | tf_op jit(solution)/shard_map/ppermute | solution.py:234
  1063.6 32.7 %collective-permute-start.19 = (bf16[256,2048]{1,0:T(8,128)(2,1)S(1)}, bf16[256,2048]{1,0:T(8,128)(2,1)S(1)}, u32[]{:S(2)}, u32[]{:S(2)}) collective-permute-start(bf16[256,2048]{1,0:T(8,128)(2,1)S(1)} %fusion.87), channel_id=1, source_target_pairs={{0,1},{1,2},{2,3},{3,0},{4,5},{5,6},{6,7},{7,4},{8,9},{9,10},{10,1... | collective-permute-start | bytes 3145736 | tf_op jit(solution)/shard_map/ppermute | solution.py:159
  1063.7 32.2 %collective-permute-start.21 = (bf16[2,256,1024]{2,1,0:T(8,128)(2,1)S(1)}, bf16[2,256,1024]{2,1,0:T(8,128)(2,1)S(1)}, u32[]{:S(2)}, u32[]{:S(2)}) collective-permute-start(bf16[2,256,1024]{2,1,0:T(8,128)(2,1)S(1)} %dynamic-slice_bitcast_fusion.2), channel_id=1, source_target_pairs={{0,16},{4,20},{8,24},{12,28},{16,0},{20,4},{24,8},{28,12},{1,17},{... | collective-permute-start | bytes 3145736 | tf_op jit(solution)/shard_map/ppermute | solution.py:234
  (192 other events, 2198.7 us)
Sparse Core Ops, SparseCore 0:
  29.3 41.1 all-gather.11
  72.4 54.2 all-gather.13
  128.5 54.2 all-gather.15
  184.6 116.3 all-gather.17
  302.7 116.3 all-gather.19
  420.8 116.3 all-gather.21
  540.8 146.3 reduce-scatter.4
  690.8 146.3 reduce-scatter.8
  840.8 180.0 reduce-scatter.10
  1033.9 64.9 reduce-scatter.6

commit v10 on v9

--- a/solution.py
+++ b/solution.py
@@ -501,7 +501,7 @@
         if k == 0:
             kv_grad, output_sum = lax.optimization_barrier((kv_grad, output_sum))
         if step == 2:
-            kv_grad, output_core = lax.optimization_barrier((kv_grad, output_core))
+            _, output_core = lax.optimization_barrier((kv_grad, output_core))
             output_core = reduce_first(output_core)
         if step == experts - 1:
             kv_grad, output_core = lax.optimization_barrier((kv_grad, output_core))

time: 1170 us -> 1190 us (1.017)
  waiting for transfers between devices: 394 us -> 420 us
  matrix products: 456 us -> 444 us
    ppermute x10, waiting for transfers between devices: 61.5 us -> 86.9 us  [swap(): return lax.ppermute(block, 'dp', [(i, i ^ bit) for i in range(8)])]
  transfers between devices with their start and end apart: 43 -> 43, of which waited for: 25 -> 24; matrix products, arithmetic and copies ran while one was open for 56% -> 54% of each run, Pallas kernels for 0% -> 0%
where the time goes in v10:
time: 1190 us; the launch traced here: 1180 us
  matrix products  444 us (37%)
  waiting for transfers between devices  420 us (35%)
  local copies, waits for them, and re-layouts  122 us (10%)
  other arithmetic  115 us (10%)
  starting transfers between devices  60.9 us (5%)
  between operations  17.9 us (2%)
    ppermute x12, waiting for transfers between devices, ring_step(): lax.ppermute(block, 'expert', [(i, (i + 1) % experts) for i in range(expe...  179 us
    all_to_all x8, waiting for transfers between devices, exchange(): lax.all_to_all(packed, 'expert', split_axis=0, concat_axis=0, tiled=True)  136 us
    dot_general x19, matrix products, mm(): return jnp.dot(left, right, preferred_element_type=f32)  116 us
    dot_general x8, matrix products, mm_nt(): lax.dot_general(left, right, (((1,), (1,)), ((), ())), preferred_element_...  115 us
    dot_general x11, matrix products, mm_tn(): lax.dot_general(left, right, (((0,), (0,)), ((), ())), preferred_element_...  114 us
    ppermute x10, waiting for transfers between devices, swap(): return lax.ppermute(block, 'dp', [(i, i ^ bit) for i in range(8)])  86.9 us
    unnamed x371, local copies, waits for them, and re-layouts  37.6 us
    all_to_all x8, starting transfers between devices, exchange(): lax.all_to_all(packed, 'expert', split_axis=0, concat_axis=0, tiled=True)  33.8 us
  transfers between devices with their start and end apart: 43, of which 24 were waited for; matrix products, arithmetic and copies ran while one was open for 54% of the time, Pallas kernels for 0%

profile of v10, /device:TPU:0, one launch (start us, length us, event | category | flops | bytes accessed | tf_op | source)
XLA Modules:
  0.0 1180.2 jit_solution(15989748898773350402)
XLA Ops:
  38.4 24.9 %collective-permute-done = bf16[256,2176]{1,0:T(8,128)(2,1)} collective-permute-done((bf16[256,2176]{1,0:T(8,128)(2,1)S(1)}, bf16[256,2176]{1,0:T(8,128)(2,1)}, u32[]{:S(2)}, u32[]{:S(2)}) %collective-permute-start) | collective-permute-done | bytes 1114144 | tf_op jit(solution)/shard_map/ppermute | solution.py:159
  68.2 22.1 %collective-permute-done.1 = bf16[256,2176]{1,0:T(8,128)(2,1)} collective-permute-done((bf16[256,2176]{1,0:T(8,128)(2,1)}, bf16[256,2176]{1,0:T(8,128)(2,1)}, u32[]{:S(2)}, u32[]{:S(2)}) %collective-permute-start.1) | collective-permute-done | bytes 1114144 | tf_op jit(solution)/shard_map/ppermute | solution.py:159
  94.2 22.1 %collective-permute-done.2 = bf16[256,2176]{1,0:T(8,128)(2,1)S(1)} collective-permute-done((bf16[256,2176]{1,0:T(8,128)(2,1)}, bf16[256,2176]{1,0:T(8,128)(2,1)S(1)}, u32[]{:S(2)}, u32[]{:S(2)}) %collective-permute-start.2) | collective-permute-done | bytes 1114144 | tf_op jit(solution)/shard_map/ppermute | solution.py:159
  150.3 12.4 %copy.272 = bf16[2048,2048]{1,0:T(8,128)(2,1)} copy(bf16[2048,2048]{0,1:T(8,128)(2,1)} %bitcast.417) | data formatting | bytes 16777216 | tf_op jit(solution)/shard_map/dot_general | solution.py:82
  162.7 10.0 fusion.228
  173.7 20.6 %collective-permute-done.6 = bf16[1024,1024]{0,1:T(8,128)(2,1)} collective-permute-done((bf16[1024,1024]{0,1:T(8,128)(2,1)}, bf16[1024,1024]{0,1:T(8,128)(2,1)}, u32[]{:S(2)}, u32[]{:S(2)}) %collective-permute-start.6) | collective-permute-done | bytes 2097184 | tf_op jit(solution)/shard_map/ppermute | solution.py:159
  222.8 17.3 %collective-permute-done.7 = bf16[1024,1024]{0,1:T(8,128)(2,1)} collective-permute-done((bf16[1024,1024]{0,1:T(8,128)(2,1)}, bf16[1024,1024]{0,1:T(8,128)(2,1)}, u32[]{:S(2)}, u32[]{:S(2)}) %collective-permute-start.7) | collective-permute-done | bytes 2097184 | tf_op jit(solution)/shard_map/ppermute | solution.py:159
  253.6 31.2 %collective-permute-done.8 = bf16[1024,1024]{0,1:T(8,128)(2,1)S(1)} collective-permute-done((bf16[1024,1024]{0,1:T(8,128)(2,1)}, bf16[1024,1024]{0,1:T(8,128)(2,1)S(1)}, u32[]{:S(2)}, u32[]{:S(2)}) %collective-permute-start.8) | collective-permute-done | bytes 2097184 | tf_op jit(solution)/shard_map/ppermute | solution.py:159
  297.4 10.3 fusion.69
  315.8 49.6 %all-to-all-done = bf16[4,160,2048]{2,1,0:T(8,128)(2,1)S(1)} async-done(((bf16[4,160,2048]{2,1,0:T(8,128)(2,1)}), bf16[4,160,2048]{2,1,0:T(8,128)(2,1)S(1)}, u32[]{:S(2)}, u32[]{:S(2)}) %all-to-all-start) | async-done | bytes 2621472 | tf_op jit(solution)/shard_map/all_to_all | solution.py:145
  385.8 51.9 %all-to-all-done.1 = bf16[4,160,2048]{2,1,0:T(8,128)(2,1)} async-done(((bf16[4,160,2048]{2,1,0:T(8,128)(2,1)}), bf16[4,160,2048]{2,1,0:T(8,128)(2,1)}, u32[]{:S(2)}, u32[]{:S(2)}) %all-to-all-start.1) | async-done | bytes 2621472 | tf_op jit(solution)/shard_map/all_to_all | solution.py:145
  441.4 23.6 %fusion.6 = f32[640,5632]{1,0:T(8,128)} fusion(bf16[640,2048]{1,0:T(8,128)(2,1)} %bitcast.47, bf16[1,2048,5632]{2,1,0:T(8,128)(2,1)} %all-gather.18.cloned.1.call-done), kind=kOutput, calls=%fused_computation.6 | convolution fusion | flops 14763950080 | bytes 40108032 | tf_op jit(solution)/shard_map/dot_general | solution.py:82
  465.0 31.9 %multiply_convert_fusion.2 = (bf16[640,5632]{1,0:T(8,128)(2,1)}, f32[640,5632]{1,0:T(8,128)}) fusion(f32[640,5632]{1,0:T(8,128)} %fusion.6, bf16[640,2048]{1,0:T(8,128)(2,1)} %bitcast.47, bf16[1,2048,5632]{2,1,0:T(8,128)(2,1)} %all-gather.20.cloned.1.call-done), kind=kOutput, calls=%fused_computation.14 | convolution fusion | flops 14785576960 | bytes 61734912 | tf_op jit(solution)/shard_map/dot_general | solution.py:82
  505.8 24.9 %convolution_convert_fusion = bf16[5632,2048]{1,0:T(8,128)(2,1)} fusion(bf16[640,5632]{1,0:T(8,128)(2,1)} %get-tuple-element.86, f32[640]{0:T(1024)S(1)} %convert_reduce_fusion.2, bf16[640,2176]{1,0:T(8,128)(2,1)S(1)} %bitcast.408), kind=kOutput, calls=%fused_computation.8 | convolution fusion | flops 14779416576 | bytes 32903168 | tf_op jit(solution)/shard_map/dot_general | solution.py:86
  537.2 38.4 %multiply_convert_fusion.1 = (bf16[640,5632]{1,0:T(8,128)(2,1)}, bf16[640,5632]{1,0:T(8,128)(2,1)}, f32[640]{0:T(1024)S(1)}) fusion(f32[640,5632]{1,0:T(8,128)} %fusion.6, f32[640,5632]{1,0:T(8,128)} %get-tuple-element.231, f32[640]{0:T(1024)S(1)} %convert_reduce_fusion.2, bf16[640,5632]{1,0:T(8,128)(2,1)} %get-tuple-element.86, ...), kind=kOutput, calls=%fused_computation.13 | convolution fusion | flops 14825225216 | bytes 76157952 | tf_op jit(solution)/shard_map/dot_general | solution.py:90
  575.8 12.7 %fusion.10 = f32[640,1024]{1,0:T(8,128)S(1)} fusion(bf16[640,5632]{1,0:T(8,128)(2,1)} %get-tuple-element.87, bf16[1,2048,5632]{2,1,0:T(8,128)(2,1)} %all-gather.20.cloned.1.call-done), kind=kOutput, calls=%fused_computation.24 | convolution fusion | flops 7381975040 | bytes 21364736 | tf_op jit(solution)/shard_map/dot_general | solution.py:90
  588.6 11.0 add_convert_fusion.3
  605.3 13.0 %fusion.8 = f32[640,1024]{1,0:T(8,128)S(1)} fusion(bf16[640,5632]{1,0:T(8,128)(2,1)} %get-tuple-element.87, bf16[1,2048,5632]{2,1,0:T(8,128)(2,1)} %all-gather.20.cloned.1.call-done), kind=kOutput, calls=%fused_computation.20 | convolution fusion | flops 7381975040 | bytes 21364736 | tf_op jit(solution)/shard_map/dot_general | solution.py:90
  618.3 13.8 %add_convert_fusion.2 = bf16[640,1024]{1,0:T(8,128)(2,1)} fusion(f32[640,1024]{1,0:T(8,128)S(1)} %fusion.8, bf16[640,5632]{1,0:T(8,128)(2,1)} %get-tuple-element.81, bf16[1,2048,5632]{2,1,0:T(8,128)(2,1)} %all-gather.18.cloned.1.call-done), kind=kOutput, calls=%fused_computation.136 | convolution fusion | flops 7383285760 | bytes 22675456 | tf_op jit(solution)/shard_map/dot_general | solution.py:90
  643.9 26.3 %convolution_convert_fusion.2 = bf16[2048,5632]{1,0:T(8,128)(2,1)} fusion(bf16[640,2048]{1,0:T(8,128)(2,1)} %bitcast.47, bf16[640,5632]{1,0:T(8,128)(2,1)} %get-tuple-element.81), kind=kOutput, calls=%fused_computation.10 | convolution fusion | flops 14775484416 | bytes 32899072 | tf_op jit(solution)/shard_map/dot_general | solution.py:86
  691.1 28.5 %convolution_convert_fusion.1 = bf16[2048,5632]{1,0:T(8,128)(2,1)} fusion(bf16[640,2048]{1,0:T(8,128)(2,1)} %bitcast.47, bf16[640,5632]{1,0:T(8,128)(2,1)} %get-tuple-element.87), kind=kOutput, calls=%fused_computation.9 | convolution fusion | flops 14775484416 | bytes 32899072 | tf_op jit(solution)/shard_map/dot_general | solution.py:86
  719.6 22.3 %fusion.63 = bf16[640,2048]{1,0:T(8,128)(2,1)} fusion(bf16[640,5632]{1,0:T(8,128)(2,1)} %get-tuple-element.86, bf16[1,5632,2048]{2,1,0:T(8,128)(2,1)} %all-gather.22.cloned.1.call-done), kind=kOutput, calls=%fused_computation.115 | convolution fusion | flops 14765260800 | bytes 32899072 | tf_op jit(solution)/shard_map/dot_general | solution.py:82
  765.0 11.4 convolution_convert_fusion.4
  776.3 10.4 fusion.60
  795.7 8.4 multiply_convert_fusion.5
  901.3 9.1 fusion.66
  924.5 41.5 %collective-permute-done.12 = bf16[2,256,1024]{2,1,0:T(8,128)(2,1)} collective-permute-done((bf16[2,256,1024]{2,1,0:T(8,128)(2,1)}, bf16[2,256,1024]{2,1,0:T(8,128)(2,1)}, u32[]{:S(2)}, u32[]{:S(2)}) %collective-permute-start.12) | collective-permute-done | bytes 1048608 | tf_op jit(solution)/shard_map/ppermute | solution.py:234
  986.7 10.9 collective-permute-done.16
  1001.7 19.0 %collective-permute-done.14 = bf16[1024,1024]{0,1:T(8,128)(2,1)S(1)} collective-permute-done((bf16[1024,1024]{0,1:T(8,128)(2,1)S(1)}, bf16[1024,1024]{0,1:T(8,128)(2,1)S(1)}, u32[]{:S(2)}, u32[]{:S(2)}) %collective-permute-start.14) | collective-permute-done | bytes 2097184 | tf_op jit(solution)/shard_map/ppermute | solution.py:159
  1071.7 13.4 %collective-permute-done.17 = bf16[256,2048]{1,0:T(8,128)(2,1)S(1)} collective-permute-done((bf16[256,2048]{1,0:T(8,128)(2,1)S(1)}, bf16[256,2048]{1,0:T(8,128)(2,1)S(1)}, u32[]{:S(2)}, u32[]{:S(2)}) %collective-permute-start.17) | collective-permute-done | bytes 1048608 | tf_op jit(solution)/shard_map/ppermute | solution.py:159
  1093.7 24.0 %collective-permute-done.20 = bf16[2,256,1024]{2,1,0:T(8,128)(2,1)S(1)} collective-permute-done((bf16[2,256,1024]{2,1,0:T(8,128)(2,1)S(1)}, bf16[2,256,1024]{2,1,0:T(8,128)(2,1)S(1)}, u32[]{:S(2)}, u32[]{:S(2)}) %collective-permute-start.20) | collective-permute-done | bytes 1048608 | tf_op jit(solution)/shard_map/ppermute | solution.py:234
  1134.4 8.7 collective-permute-done.22
  (705 shorter events, 486.7 us)
Async XLA Ops:
  7.2 115.3 %all-gather.12.cloned.1.call-start = ((), (), s32[]{:S(2)}) async-start(), calls=%async_computation.12 | async-start | bytes 5308416 | tf_op jit(solution)/shard_map/all_gather | solution.py:325
  29.2 121.1 %all-gather.14.cloned.1.call-start = ((), (), s32[]{:S(2)}) async-start(), calls=%async_computation.17 | async-start | bytes 9437184 | tf_op jit(solution)/shard_map/all_gather | solution.py:226
  30.0 267.4 %all-gather.16.cloned.1.call-start = ((), (), s32[]{:S(2)}) async-start(), calls=%async_computation.18 | async-start | bytes 9437184 | tf_op jit(solution)/shard_map/all_gather | solution.py:226
  30.7 410.7 %all-gather.18.cloned.1.call-start = ((), (), s32[]{:S(2)}) async-start(), calls=%async_computation.19 | async-start | bytes 25952256 | tf_op jit(solution)/shard_map/all_gather | solution.py:226
  31.3 433.8 %all-gather.20.cloned.1.call-start = ((), (), s32[]{:S(2)}) async-start(), calls=%async_computation.20 | async-start | bytes 25952256 | tf_op jit(solution)/shard_map/all_gather | solution.py:226
  31.8 505.4 %all-gather.22.cloned.1.call-start = ((), (), s32[]{:S(2)}) async-start(), calls=%async_computation.21 | async-start | bytes 25952256 | tf_op jit(solution)/shard_map/all_gather | solution.py:226
  34.7 28.6 %collective-permute-start = (bf16[256,2176]{1,0:T(8,128)(2,1)S(1)}, bf16[256,2176]{1,0:T(8,128)(2,1)}, u32[]{:S(2)}, u32[]{:S(2)}) collective-permute-start(bf16[256,2176]{1,0:T(8,128)(2,1)S(1)} %concatenate.68), channel_id=1, source_target_pairs={{0,1},{1,2},{2,3},{3,0},{4,5},{5,6},{6,7},{7,4},{8,9},{9,10},{10,1... | collective-permute-start | bytes 3342344 | tf_op jit(solution)/shard_map/ppermute | solution.py:159
  63.3 27.0 %collective-permute-start.1 = (bf16[256,2176]{1,0:T(8,128)(2,1)}, bf16[256,2176]{1,0:T(8,128)(2,1)}, u32[]{:S(2)}, u32[]{:S(2)}) collective-permute-start(bf16[256,2176]{1,0:T(8,128)(2,1)} %collective-permute-done), channel_id=1, source_target_pairs={{0,1},{1,2},{2,3},{3,0},{4,5},{5,6},{6,7},{7,4},{8,9},{9,10},{10,1... | collective-permute-start | bytes 3342344 | tf_op jit(solution)/shard_map/ppermute | solution.py:159
  147.9 46.5 %collective-permute-start.6 = (bf16[1024,1024]{0,1:T(8,128)(2,1)}, bf16[1024,1024]{0,1:T(8,128)(2,1)}, u32[]{:S(2)}, u32[]{:S(2)}) collective-permute-start(bf16[1024,1024]{0,1:T(8,128)(2,1)} %pad_maximum_fusion.5), channel_id=1, source_target_pairs={{0,1},{1,2},{2,3},{3,0},{4,5},{5,6},{6,7},{7,4},{8,9},{9,10},{10,1... | collective-permute-start | bytes 6291464 | tf_op jit(solution)/shard_map/ppermute | solution.py:159
  194.3 45.8 %collective-permute-start.7 = (bf16[1024,1024]{0,1:T(8,128)(2,1)}, bf16[1024,1024]{0,1:T(8,128)(2,1)}, u32[]{:S(2)}, u32[]{:S(2)}) collective-permute-start(bf16[1024,1024]{0,1:T(8,128)(2,1)} %collective-permute-done.6), channel_id=1, source_target_pairs={{0,1},{1,2},{2,3},{3,0},{4,5},{5,6},{6,7},{7,4},{8,9},{9,10},{10,1... | collective-permute-start | bytes 6291464 | tf_op jit(solution)/shard_map/ppermute | solution.py:159
  240.1 44.7 %collective-permute-start.8 = (bf16[1024,1024]{0,1:T(8,128)(2,1)}, bf16[1024,1024]{0,1:T(8,128)(2,1)S(1)}, u32[]{:S(2)}, u32[]{:S(2)}) collective-permute-start(bf16[1024,1024]{0,1:T(8,128)(2,1)} %collective-permute-done.7), channel_id=1, source_target_pairs={{0,1},{1,2},{2,3},{3,0},{4,5},{5,6},{6,7},{7,4},{8,9},{9,10},{10,1... | collective-permute-start | bytes 6291464 | tf_op jit(solution)/shard_map/ppermute | solution.py:159
  307.6 57.8 %all-to-all-start = ((bf16[4,160,2048]{2,1,0:T(8,128)(2,1)}), bf16[4,160,2048]{2,1,0:T(8,128)(2,1)S(1)}, u32[]{:S(2)}, u32[]{:S(2)}) async-start(bf16[4,160,2048]{2,1,0:T(8,128)(2,1)} %bitcast.459), calls=%async_computation | async-start | bytes 5242880 | tf_op jit(solution)/shard_map/all_to_all | solution.py:145
  374.1 63.6 %all-to-all-start.1 = ((bf16[4,160,2048]{2,1,0:T(8,128)(2,1)}), bf16[4,160,2048]{2,1,0:T(8,128)(2,1)}, u32[]{:S(2)}, u32[]{:S(2)}) async-start(bf16[4,160,2048]{2,1,0:T(8,128)(2,1)} %bitcast.46), calls=%async_computation.1 | async-start | bytes 5242880 | tf_op jit(solution)/shard_map/all_to_all | solution.py:145
  437.7 66.1 %all-to-all-start.2 = ((bf16[4,160,2176]{2,1,0:T(8,128)(2,1)}), bf16[4,160,2176]{2,1,0:T(8,128)(2,1)S(1)}, u32[]{:S(2)}, u32[]{:S(2)}) async-start(bf16[4,160,2176]{2,1,0:T(8,128)(2,1)} %pad_maximum_fusion.2), calls=%async_computation.2 | async-start | bytes 5570560 | tf_op jit(solution)/shard_map/all_to_all | solution.py:145
  441.4 323.6 %reduce-scatter.5.cloned.1.call-start = ((), (), s32[]{:S(2)}) async-start(), calls=%async_computation.13 | async-start | bytes 25952256 | tf_op jit(solution)/shard_map/reduce_scatter | solution.py:230
  600.8 39.4 %all-to-all-start.3 = ((bf16[4,160,1152]{2,1,0:T(8,128)(2,1)}), bf16[4,160,1152]{2,1,0:T(8,128)(2,1)S(1)}, u32[]{:S(2)}, u32[]{:S(2)}) async-start(bf16[4,160,1152]{2,1,0:T(8,128)(2,1)} %bitcast.56), calls=%async_computation.3 | async-start | bytes 2949120 | tf_op jit(solution)/shard_map/all_to_all | solution.py:145
  640.3 34.4 %all-to-all-start.4 = ((bf16[4,160,1024]{2,1,0:T(8,128)(2,1)}), bf16[4,160,1024]{2,1,0:T(8,128)(2,1)S(1)}, u32[]{:S(2)}, u32[]{:S(2)}) async-start(bf16[4,160,1024]{2,1,0:T(8,128)(2,1)} %bitcast.483), calls=%async_computation.4 | async-start | bytes 2621440 | tf_op jit(solution)/shard_map/all_to_all | solution.py:145
  643.8 275.2 %reduce-scatter.9.cloned.1.call-start = ((), (), s32[]{:S(2)}) async-start(), calls=%async_computation.15 | async-start | bytes 25952256 | tf_op jit(solution)/shard_map/reduce_scatter | solution.py:230
  686.5 63.6 %all-to-all-start.5 = ((bf16[4,160,2048]{2,1,0:T(8,128)(2,1)}), bf16[4,160,2048]{2,1,0:T(8,128)(2,1)}, u32[]{:S(2)}, u32[]{:S(2)}) async-start(bf16[4,160,2048]{2,1,0:T(8,128)(2,1)} %bitcast.68), calls=%async_computation.5 | async-start | bytes 5242880 | tf_op jit(solution)/shard_map/all_to_all | solution.py:145
  691.1 368.6 %reduce-scatter.11.cloned.1.call-start = ((), (), s32[]{:S(2)}) async-start(), calls=%async_computation.16 | async-start | bytes 25952256 | tf_op jit(solution)/shard_map/reduce_scatter | solution.py:230
  760.2 112.7 %all-to-all-start.6 = ((bf16[4,160,2048]{2,1,0:T(8,128)(2,1)}), bf16[4,160,2048]{2,1,0:T(8,128)(2,1)}, u32[]{:S(2)}, u32[]{:S(2)}) async-start(bf16[4,160,2048]{2,1,0:T(8,128)(2,1)} %bitcast.456), calls=%async_computation.7 | async-start | bytes 5242880 | tf_op jit(solution)/shard_map/all_to_all | solution.py:145
  764.9 378.1 %reduce-scatter.7.cloned.1.call-start = ((), (), s32[]{:S(2)}) async-start(), calls=%async_computation.14 | async-start | bytes 5308416 | tf_op jit(solution)/shard_map/reduce_scatter | solution.py:230
  811.2 57.2 %collective-permute-start.9 = (bf16[1024,1024]{0,1:T(8,128)(2,1)}, bf16[1024,1024]{0,1:T(8,128)(2,1)}, u32[]{:S(2)}, u32[]{:S(2)}) collective-permute-start(bf16[1024,1024]{0,1:T(8,128)(2,1)} %pad_maximum_fusion.6), channel_id=1, source_target_pairs={{0,1},{1,2},{2,3},{3,0},{4,5},{5,6},{6,7},{7,4},{8,9},{9,10},{10,1... | collective-permute-start | bytes 6291464 | tf_op jit(solution)/shard_map/ppermute | solution.py:159
  820.4 90.0 %collective-permute-start.11 = (bf16[2,2,256,2048]{3,2,1,0:T(8,128)(2,1)}, bf16[2,2,256,2048]{3,2,1,0:T(8,128)(2,1)}, u32[]{:S(2)}, u32[]{:S(2)}) collective-permute-start(bf16[2,2,256,2048]{3,2,1,0:T(8,128)(2,1)} %dynamic-slice_bitcast_fusion.1), channel_id=1, source_target_pairs={{0,4},{4,0},{8,12},{12,8},{16,20},{20,16},{24,28},{28,24},{1,5},{5... | collective-permute-start | bytes 12582920 | tf_op jit(solution)/shard_map/ppermute | solution.py:234
  876.3 93.0 %collective-permute-start.10 = (bf16[1024,1024]{0,1:T(8,128)(2,1)}, bf16[1024,1024]{0,1:T(8,128)(2,1)}, u32[]{:S(2)}, u32[]{:S(2)}) collective-permute-start(bf16[1024,1024]{0,1:T(8,128)(2,1)} %fusion.53), channel_id=1, source_target_pairs={{0,1},{1,2},{2,3},{3,0},{4,5},{5,6},{6,7},{7,4},{8,9},{9,10},{10,1... | collective-permute-start | bytes 6291464 | tf_op jit(solution)/shard_map/ppermute | solution.py:159
  917.4 48.5 %collective-permute-start.12 = (bf16[2,256,1024]{2,1,0:T(8,128)(2,1)}, bf16[2,256,1024]{2,1,0:T(8,128)(2,1)}, u32[]{:S(2)}, u32[]{:S(2)}) collective-permute-start(bf16[2,256,1024]{2,1,0:T(8,128)(2,1)} %dynamic-slice_bitcast_fusion.5), channel_id=1, source_target_pairs={{0,8},{4,12},{8,0},{12,4},{16,24},{20,28},{24,16},{28,20},{1,9},{5... | collective-permute-start | bytes 3145736 | tf_op jit(solution)/shard_map/ppermute | solution.py:234
  918.9 48.7 %collective-permute-start.13 = (bf16[2,256,1024]{2,1,0:T(8,128)(2,1)S(1)}, bf16[2,256,1024]{2,1,0:T(8,128)(2,1)}, u32[]{:S(2)}, u32[]{:S(2)}) collective-permute-start(bf16[2,256,1024]{2,1,0:T(8,128)(2,1)S(1)} %dynamic-slice_bitcast_fusion.4), channel_id=1, source_target_pairs={{0,16},{4,20},{8,24},{12,28},{16,0},{20,4},{24,8},{28,12},{1,17},{... | collective-permute-start | bytes 3145736 | tf_op jit(solution)/shard_map/ppermute | solution.py:234
  971.9 48.7 %collective-permute-start.14 = (bf16[1024,1024]{0,1:T(8,128)(2,1)S(1)}, bf16[1024,1024]{0,1:T(8,128)(2,1)S(1)}, u32[]{:S(2)}, u32[]{:S(2)}) collective-permute-start(bf16[1024,1024]{0,1:T(8,128)(2,1)S(1)} %fusion.54), channel_id=1, source_target_pairs={{0,1},{1,2},{2,3},{3,0},{4,5},{5,6},{6,7},{7,4},{8,9},{9,10},{10,1... | collective-permute-start | bytes 6291464 | tf_op jit(solution)/shard_map/ppermute | solution.py:159
  986.7 78.7 %collective-permute-start.18 = (bf16[2,2,256,2048]{3,2,1,0:T(8,128)(2,1)}, bf16[2,2,256,2048]{3,2,1,0:T(8,128)(2,1)}, u32[]{:S(2)}, u32[]{:S(2)}) collective-permute-start(bf16[2,2,256,2048]{3,2,1,0:T(8,128)(2,1)} %dynamic-slice_bitcast_fusion), channel_id=1, source_target_pairs={{0,4},{4,0},{8,12},{12,8},{16,20},{20,16},{24,28},{28,24},{1,5},{5... | collective-permute-start | bytes 12582920 | tf_op jit(solution)/shard_map/ppermute | solution.py:234
  1085.6 32.1 %collective-permute-start.20 = (bf16[2,256,1024]{2,1,0:T(8,128)(2,1)S(1)}, bf16[2,256,1024]{2,1,0:T(8,128)(2,1)S(1)}, u32[]{:S(2)}, u32[]{:S(2)}) collective-permute-start(bf16[2,256,1024]{2,1,0:T(8,128)(2,1)S(1)} %dynamic-slice_bitcast_fusion.3), channel_id=1, source_target_pairs={{0,8},{4,12},{8,0},{12,4},{16,24},{20,28},{24,16},{28,20},{1,9},{5... | collective-permute-start | bytes 3145736 | tf_op jit(solution)/shard_map/ppermute | solution.py:234
  1087.6 30.9 %collective-permute-start.19 = (bf16[256,2048]{1,0:T(8,128)(2,1)S(1)}, bf16[256,2048]{1,0:T(8,128)(2,1)S(1)}, u32[]{:S(2)}, u32[]{:S(2)}) collective-permute-start(bf16[256,2048]{1,0:T(8,128)(2,1)S(1)} %fusion.87), channel_id=1, source_target_pairs={{0,1},{1,2},{2,3},{3,0},{4,5},{5,6},{6,7},{7,4},{8,9},{9,10},{10,1... | collective-permute-start | bytes 3145736 | tf_op jit(solution)/shard_map/ppermute | solution.py:159
  1087.7 30.4 %collective-permute-start.21 = (bf16[2,256,1024]{2,1,0:T(8,128)(2,1)S(1)}, bf16[2,256,1024]{2,1,0:T(8,128)(2,1)S(1)}, u32[]{:S(2)}, u32[]{:S(2)}) collective-permute-start(bf16[2,256,1024]{2,1,0:T(8,128)(2,1)S(1)} %dynamic-slice_bitcast_fusion.2), channel_id=1, source_target_pairs={{0,16},{4,20},{8,24},{12,28},{16,0},{20,4},{24,8},{28,12},{1,17},{... | collective-permute-start | bytes 3145736 | tf_op jit(solution)/shard_map/ppermute | solution.py:234
  (192 other events, 2231.4 us)
Sparse Core Ops, SparseCore 0:
  29.3 41.1 all-gather.11
  72.4 54.2 all-gather.13
  128.5 54.2 all-gather.15
  184.6 116.3 all-gather.17
  302.7 116.4 all-gather.19
  420.8 116.3 all-gather.21
  540.8 146.3 reduce-scatter.4
  690.8 146.3 reduce-scatter.8
  840.9 179.5 reduce-scatter.10
  1058.0 64.9 reduce-scatter.6
